TPU v7x, 256 devices: a whole 4x4x8 slice. The times are simulated.
256 devices in a mesh: layer: 64 (over y_hi, z, x), shot: 4 (over y_lo, core).
Axes of the slice: x: 4, y: 4 (y_hi: 2, y_lo: 2; y = y_hi * 2 + y_lo), z: 8, core: 2. Of those that a mesh axis runs over, the one named last changes fastest.
Arguments:
- down_state: bfloat16 [64, 1024, 2048], P('layer', None, 'shot'), may hold values from -6 to 6
- up_state: bfloat16 [64, 1024, 2048], P('layer', None, 'shot'), may hold values from -6 to 6
- down_op: bfloat16 [64, 1024, 1024], P('layer', 'shot'), may hold values from -0.1875 to 0.1875
- up_op: bfloat16 [64, 1024, 1024], P('layer', 'shot'), may hold values from -0.1875 to 0.1875
- reflect_op: bfloat16 [64, 1024, 1024], P('layer', 'shot'), may hold values from -0.125 to 0.125
- source_bank: bfloat16 [64, 2, 1024, 2048], P('layer', None, None, 'shot'), may hold values from -4 to 4
- plan: int32 [4, 64], P(None, 'layer'), may hold values from 0 to 1
- layer_source: int32 [64], P('layer'), may hold values from 0 to 1
Outputs:
- down_out: bfloat16 [64, 1024, 2048], P('layer', None, 'shot')
- up_out: bfloat16 [64, 1024, 2048], P('layer', None, 'shot')
All inputs are finite; a program needn't handle non-finite values.
Results may differ from a plain program's by a relative error of at most 0.008.
Values may be sent and summed in bfloat16 or wider, within the bound.
No kernel may reach another device: no remote copies, remote signals or barrier semaphores. Data moves between devices by JAX's collectives and lax.ppermute only.
A program may use at most 64 MiB of HBM per device.

v0:
```python
import functools

import jax
import jax.numpy as jnp
from jax import lax
from jax.experimental import pallas as pl
from jax.experimental.pallas import tpu as pltpu
from jax.sharding import PartitionSpec as P


TICKS = 4
CHUNKS = 2
WHOLE = pl.BlockSpec(memory_space=pltpu.VMEM)
SCALARS = pl.BlockSpec(memory_space=pltpu.SMEM)
F32, BF16 = jnp.float32, jnp.bfloat16


def dot(a, b):
    return jnp.dot(a, b, preferred_element_type=F32)


def place():
    spot = lax.axis_index("shot")
    return spot // 2, spot % 2


def band(index, height):
    return pl.ds(pl.multiple_of(index * height, height), height)


def injected(received, source):
    return (received.astype(F32) + source.astype(F32)).astype(BF16)


def first_down_kernel(plan, own, near, received, sources, new, down_in):
    _, core = place()
    down_in[...] = injected(received[...], sources[plan[0, 0]])
    for k, block in enumerate((own, near)):
        new[band(core ^ k, block.shape[0]), :] = dot(block[...], down_in[...]).astype(BF16)


def other_down_kernel(far, diagonal, down_in, new):
    _, core = place()
    for k, block in enumerate((far, diagonal)):
        new[band(core ^ k, block.shape[0]), :] = dot(block[...], down_in[...]).astype(BF16)


def half_up_kernel(half, pick, u0, u1, r0, r1, received, down_in, sources, new):
    side, core = place()
    for k, (up, reflect) in enumerate(((u0, r0), (u1, r1))):
        height = up.shape[0]
        total = dot(up[...], received[...]) + dot(reflect[...], down_in[...])
        rows = band((side ^ half) * 2 + (core ^ k), height)
        total = total + sources[pick[0], rows, :].astype(F32)
        new[band(core ^ k, height), :] = total.astype(BF16)


def stage_kernel(*refs):
    n = (len(refs) - 1) // 2
    copies = [pltpu.make_async_copy(refs[i], refs[n + i], refs[-1].at[i]) for i in range(n)]
    for copy in copies:
        copy.start()
    for copy in copies:
        copy.wait()


def staged(*arrays):
    n = len(arrays)
    return pl.pallas_call(
        stage_kernel,
        name="stage",
        in_specs=[pl.BlockSpec(memory_space=pl.ANY)] * n,
        out_specs=[WHOLE] * n,
        out_shape=[jax.ShapeDtypeStruct(a.shape, a.dtype) for a in arrays],
        scratch_shapes=[pltpu.SemaphoreType.DMA((n,))],
        cost_estimate=pl.CostEstimate(flops=0, transcendentals=0, bytes_accessed=2**20),
        compiler_params=pltpu.CompilerParams(vmem_limit_bytes=16 * 2**20),
    )(*arrays)


def late_kernel(_, down, up, reflect, after, pair):
    high = down.shape[0]
    top = lax.axis_index("layer") == 0
    pair[:high, :] = jnp.where(top, up[...], down[...])
    pair[high:, :] = jnp.where(top, reflect[...], up[...])


def columns(chunk, width):
    return slice(chunk * width, (chunk + 1) * width)


def halves(refs):
    side, _ = place()
    return tuple((band(side ^ k, ref.shape[0]), ref) for k, ref in enumerate(refs))


def down_kernel(moment, chunk, n, last, *refs):
    plan, *blocks = refs[:5]
    received, sources = refs[5 : 5 + n], refs[5 + n]
    late = refs[6 + n : 8 + n] if last else ()
    end = lax.axis_index("layer") == lax.axis_size("layer") - 1
    new, down_in = refs[-2:]
    side, core = place()
    _, width = down_in.shape
    picked, cols = plan[0, moment], columns(chunk, width)
    if n == 1:
        down_in[...] = injected(received[0][...], sources[picked, :, cols])
    else:
        for rows, ref in halves(received):
            down_in[rows, :] = injected(ref[:, cols], sources[picked, rows, cols])
    for k, block in enumerate(blocks):
        high = block.shape[0]
        value = block[...]
        if last and k >= 2:
            value = jnp.where(end, late[k - 2][:high, :], value)
        new[band((side * 2 + core) ^ k, high), :] = dot(value, down_in[...]).astype(BF16)


def up_kernel(chunk, n, last, *refs):
    pick, *blocks = refs[:9]
    received, (down_in, sources) = refs[9 : 9 + n], refs[9 + n : 11 + n]
    late = refs[11 + n : 13 + n] if last else ()
    top = lax.axis_index("layer") == 0
    end = lax.axis_index("layer") == lax.axis_size("layer") - 1
    side, core = place()
    _, width = down_in.shape
    cols = columns(chunk, width)
    if n == 1:
        new, gathered = refs[-1], received[0]
    else:
        new, gathered = refs[-2:]
        for rows, ref in halves(received):
            gathered[rows, :] = ref[:, cols]
    for k in range(4):
        up, reflect = blocks[k][...], blocks[4 + k][...]
        high = up.shape[0]
        if last and k >= 2:
            first, second = late[k - 2][:high, :], late[k - 2][high:, :]
            up = jnp.where(top, first, jnp.where(end, second, up))
            reflect = jnp.where(top, second, reflect)
        rows = band((side * 2 + core) ^ k, high)
        total = dot(up, gathered[...]) + dot(reflect, down_in[...])
        total = total + sources[pick[0], rows, cols].astype(F32)
        new[rows, :] = total.astype(BF16)


def call(kernel, scalars, arrays, out_shape, flops, scratch=(), full=None, into=None, more=()):
    out_specs = [WHOLE] * len(out_shape)
    in_specs = [SCALARS] + [WHOLE] * len(arrays)
    args = [scalars, *arrays]
    in_specs += [WHOLE] * len(more)
    args += more
    aliases = {}
    if full is not None:
        chunk, wide = full
        height, width = out_shape[0]
        out_shape = [(height, wide), *out_shape[1:]]
        out_specs[0] = pl.BlockSpec((height, width), lambda i: (0, chunk))
        if into is not None:
            in_specs.append(pl.BlockSpec(memory_space=pl.ANY))
            aliases = {len(args): 0}
            args.append(into)
            kernel = without(kernel, len(args) - 1)
    return pl.pallas_call(
        kernel,
        grid=(1,),
        in_specs=in_specs,
        out_specs=out_specs,
        out_shape=[jax.ShapeDtypeStruct(s, BF16) for s in out_shape],
        scratch_shapes=list(scratch),
        input_output_aliases=aliases,
        cost_estimate=pl.CostEstimate(flops=flops, transcendentals=0, bytes_accessed=2**20),
        compiler_params=pltpu.CompilerParams(vmem_limit_bytes=16 * 2**20),
    )(*args)


def without(kernel, at):
    def inner(*refs):
        kernel(*refs[:at], *refs[at + 1 :])

    return inner


def sent(value, pairs):
    return lax.ppermute(value, ("layer", "shot"), pairs)


def steps(down_state, up_state, down_op, up_op, reflect_op, source_bank, plan, layer_source):
    layers, shots = lax.axis_size("layer"), lax.axis_size("shot")
    height, wide = down_state.shape[1:]
    width = wide // CHUNKS
    one = 2 * height * height * width
    down_op, up_op, reflect_op = down_op[0], up_op[0], reflect_op[0]

    def at(layer, shot):
        return layer * shots + shot

    every = range(layers)

    def shift(value, steps):
        return sent(value, [
            (at(l, s), at(l + steps, s)) for l in every for s in range(shots) if 0 <= l + steps < layers
        ])

    def swap(value, bit, members):
        return sent(value, [(at(l, s), at(l, s ^ bit)) for l in members for s in range(shots)])

    middle = [l for l in every if 0 < l < layers - 1]
    down_0 = shift(down_state[0], 1)
    far_d = swap(down_op, 2, [0] + middle)
    up_0 = shift(up_state[0], -1)
    near_d = swap(down_op, 1, every)
    far_u = swap(up_op, 2, middle)
    far_r = swap(reflect_op, 2, middle + [layers - 1])
    near_u = swap(up_op, 1, every)
    near_r = swap(reflect_op, 1, every)
    cross_d = swap(far_d, 1, every)
    cross_u = swap(far_u, 1, every)
    cross_r = swap(far_r, 1, every)

    plan = plan.T
    down_op, up_op, reflect_op, sources = staged(down_op, up_op, reflect_op, source_bank[0])
    half = (height // 2, wide)
    new, down_in = call(
        first_down_kernel, plan, [down_op, near_d, down_0, sources],
        [half, (height, wide)], one,
    )
    downs = [shift(new, 1)]
    (new,) = call(
        functools.partial(half_up_kernel, 0), layer_source,
        [up_op, near_u, reflect_op, near_r, up_0, down_in, sources], [half], 2 * one,
    )
    up_near = new
    ups = [shift(new, -1)]
    make = pl.pallas_call(
        other_down_kernel, name="down_far", in_specs=[WHOLE] * 3, out_specs=[WHOLE],
        out_shape=[jax.ShapeDtypeStruct(half, BF16)],
        cost_estimate=pl.CostEstimate(flops=one, transcendentals=0, bytes_accessed=2**20),
        compiler_params=pltpu.CompilerParams(vmem_limit_bytes=16 * 2**20),
    )
    (new,) = make(far_d, cross_d, down_in)
    downs.append(shift(new, 1))
    (new,) = call(
        functools.partial(half_up_kernel, 1), layer_source,
        [far_u, cross_u, far_r, cross_r, up_0, down_in, sources], [half], 2 * one,
    )
    ups.append(shift(new, -1))

    d_blocks = [down_op, near_d, far_d, cross_d]
    u_blocks = [up_op, near_u, far_u, cross_u, reflect_op, near_r, far_r, cross_r]
    late = ()
    for moment in range(1, TICKS):
        last = moment == TICKS - 1
        if moment == 1:
            (pair,) = call(
                late_kernel, layer_source, [down_op, up_op, reflect_op, up_near],
                [(height // 2, height)], one // 8,
            )
            ends = ((0, layers - 4), (layers - 1, 3))
            pair = sent(pair, [(at(a, s), at(b, s)) for a, b in ends for s in range(shots)])
            pair = sent(pair, [(at(b, s), at(a, s ^ 2)) for a, b in ends for s in range(shots)])
            late = (pair, swap(pair, 1, (0, layers - 1)))
        new_downs, new_ups = [], []
        n = len(downs) if moment == 1 else 1
        for chunk in range(CHUNKS):
            full = (chunk, wide) if last else None
            received = downs if moment == 1 else [downs[chunk]]
            new, down_in = call(
                functools.partial(down_kernel, moment, chunk, n, last), plan,
                [*d_blocks, *received, sources], [(height, width)] * 2, one,
                full=full, into=new_downs[-1] if last and chunk else None, more=late if last else (),
            )
            new_downs.append(new)
            received = ups if moment == 1 else [ups[chunk]]
            (new,) = call(
                functools.partial(up_kernel, chunk, n, last), layer_source,
                [*u_blocks, *received, down_in, sources], [(height, width)], 2 * one,
                scratch=[pltpu.VMEM((height, width), BF16)] if n > 1 else [],
                full=full, into=new_ups[-1] if last and chunk else None, more=late if last else (),
            )
            new_ups.append(new)
        if last:
            return (new_downs[-1][None], new_ups[-1][None])
        downs = [shift(a, 1) for a in new_downs]
        ups = [shift(a, -1) for a in new_ups]


def solution(mesh):
    placed = (
        P("layer", None, "shot"),
        P("layer", None, "shot"),
        P("layer", "shot", None),
        P("layer", "shot", None),
        P("layer", "shot", None),
        P("layer", None, None, "shot"),
        P(None, "layer"),
        P("layer"),
    )
    return jax.shard_map(
        steps,
        mesh=mesh,
        in_specs=placed,
        out_specs=(P("layer", None, "shot"), P("layer", None, "shot")),
        check_vma=False,
    )
```

profile of v0, /device:TPU:22, one launch (start us, length us, event | category | flops | bytes accessed | tf_op | source)
XLA Modules:
  0.0 191.2 jit_solution(17601910140371014586)
XLA Ops:
  0.6 3.7 %collective-permute-start.3 = (bf16[1024,512]{1,0:T(8,128)(2,1)}, bf16[1024,512]{1,0:T(8,128)(2,1)S(1)}, u32[]{:S(2)}, u32[]{:S(2)}) collective-permute-start(bf16[1024,512]{1,0:T(8,128)(2,1)} %bitcast.28), channel_id=1, source_target_pairs={{0,4},{1,5},{2,6},{3,7},{4,8},{5,9},{6,10},{7,11},{8,12},{9,13},{1... | collective-permute-start | bytes 3145736 | tf_op jit(solution)/shard_map/ppermute | solution.py:185
  4.4 2.1 %collective-permute-start.10 = (bf16[1024,512]{1,0:T(8,128)(2,1)}, bf16[1024,512]{1,0:T(8,128)(2,1)S(1)}, u32[]{:S(2)}, u32[]{:S(2)}) collective-permute-start(bf16[1024,512]{1,0:T(8,128)(2,1)} %bitcast.29), channel_id=1, source_target_pairs={{4,0},{5,1},{6,2},{7,3},{8,4},{9,5},{10,6},{11,7},{12,8},{13,9},{1... | collective-permute-start | bytes 3145736 | tf_op jit(solution)/shard_map/ppermute | solution.py:185
  7.9 1.6 copy-done
  9.4 1.0 copy-done.1
  10.5 1.0 copy-done.3
  11.5 1.0 copy-done.5
  12.9 14.8 %collective-permute-done.3.received = bf16[1024,512]{1,0:T(8,128)(2,1)S(1)} collective-permute-done((bf16[1024,512]{1,0:T(8,128)(2,1)}, bf16[1024,512]{1,0:T(8,128)(2,1)S(1)}, u32[]{:S(2)}, u32[]{:S(2)}) %collective-permute-start.3) | collective-permute-done | bytes 1048608 | tf_op jit(solution)/shard_map/ppermute | solution.py:185
  27.6 1.3 shard_map.95
  29.0 4.2 %collective-permute-done.10.received = bf16[1024,512]{1,0:T(8,128)(2,1)S(1)} collective-permute-done((bf16[1024,512]{1,0:T(8,128)(2,1)}, bf16[1024,512]{1,0:T(8,128)(2,1)S(1)}, u32[]{:S(2)}, u32[]{:S(2)}) %collective-permute-start.10) | collective-permute-done | bytes 1048608 | tf_op jit(solution)/shard_map/ppermute | solution.py:185
  33.2 1.2 shard_map.98.after
  34.6 0.9 collective-permute-start.11
  35.5 3.2 %collective-permute-start.1 = (bf16[256,1024]{1,0:T(8,128)(2,1)S(1)}, bf16[256,1024]{1,0:T(8,128)(2,1)S(1)}, u32[]{:S(2)}, u32[]{:S(2)}) collective-permute-start(bf16[256,1024]{1,0:T(8,128)(2,1)S(1)} %bitcast.12), channel_id=1, source_target_pairs={{0,2},{1,3},{2,0},{3,1},{4,6},{5,7},{6,4},{7,5},{8,10},{9,11},{10,... | collective-permute-start | bytes 1572872 | tf_op jit(solution)/shard_map/ppermute | solution.py:185
  38.7 2.7 %collective-permute-start.16 = (bf16[256,1024]{1,0:T(8,128)(2,1)S(1)}, bf16[256,1024]{1,0:T(8,128)(2,1)S(1)}, u32[]{:S(2)}, u32[]{:S(2)}) collective-permute-start(bf16[256,1024]{1,0:T(8,128)(2,1)S(1)} %bitcast.15), channel_id=1, source_target_pairs={{4,6},{5,7},{6,4},{7,5},{8,10},{9,11},{10,8},{11,9},{12,14},{13,15... | collective-permute-start | bytes 1572872 | tf_op jit(solution)/shard_map/ppermute | solution.py:185
  41.4 3.2 %collective-permute-start.18 = (bf16[256,1024]{1,0:T(8,128)(2,1)S(1)}, bf16[256,1024]{1,0:T(8,128)(2,1)S(1)}, u32[]{:S(2)}, u32[]{:S(2)}) collective-permute-start(bf16[256,1024]{1,0:T(8,128)(2,1)S(1)} %bitcast.18), channel_id=1, source_target_pairs={{4,6},{5,7},{6,4},{7,5},{8,10},{9,11},{10,8},{11,9},{12,14},{13,15... | collective-permute-start | bytes 1572872 | tf_op jit(solution)/shard_map/ppermute | solution.py:185
  44.6 29.8 %collective-permute-done.1.far.refs_3_ = bf16[256,1024]{1,0:T(8,128)(2,1)S(1)} collective-permute-done((bf16[256,1024]{1,0:T(8,128)(2,1)S(1)}, bf16[256,1024]{1,0:T(8,128)(2,1)S(1)}, u32[]{:S(2)}, u32[]{:S(2)}) %collective-permute-start.1) | collective-permute-done | bytes 524320 | tf_op jit(solution)/shard_map/ppermute | solution.py:185
  74.4 11.2 %collective-permute-done.16.u0.refs_3_ = bf16[256,1024]{1,0:T(8,128)(2,1)S(1)} collective-permute-done((bf16[256,1024]{1,0:T(8,128)(2,1)S(1)}, bf16[256,1024]{1,0:T(8,128)(2,1)S(1)}, u32[]{:S(2)}, u32[]{:S(2)}) %collective-permute-start.16) | collective-permute-done | bytes 524320 | tf_op jit(solution)/shard_map/ppermute | solution.py:185
  85.6 9.3 %collective-permute-done.18.r0.refs_7_ = bf16[256,1024]{1,0:T(8,128)(2,1)S(1)} collective-permute-done((bf16[256,1024]{1,0:T(8,128)(2,1)S(1)}, bf16[256,1024]{1,0:T(8,128)(2,1)S(1)}, u32[]{:S(2)}, u32[]{:S(2)}) %collective-permute-start.18) | collective-permute-done | bytes 524320 | tf_op jit(solution)/shard_map/ppermute | solution.py:185
  96.3 1.9 %collective-permute-start.5 = (bf16[512,512]{1,0:T(8,128)(2,1)S(1)}, bf16[512,512]{1,0:T(8,128)(2,1)S(1)}, u32[]{:S(2)}, u32[]{:S(2)}) collective-permute-start(bf16[512,512]{1,0:T(8,128)(2,1)S(1)} %down_far.1), channel_id=1, source_target_pairs={{0,4},{1,5},{2,6},{3,7},{4,8},{5,9},{6,10},{7,11},{8,12},{9,13},{1... | collective-permute-start | bytes 1572872 | tf_op jit(solution)/shard_map/ppermute | solution.py:185
  98.3 1.9 %collective-permute-start.4 = (bf16[512,512]{1,0:T(8,128)(2,1)S(1)}, bf16[512,512]{1,0:T(8,128)(2,1)S(1)}, u32[]{:S(2)}, u32[]{:S(2)}) collective-permute-start(bf16[512,512]{1,0:T(8,128)(2,1)S(1)} %get-tuple-element.22), channel_id=1, source_target_pairs={{0,4},{1,5},{2,6},{3,7},{4,8},{5,9},{6,10},{7,11},{8,12},{9,13},{1... | collective-permute-start | bytes 1572872 | tf_op jit(solution)/shard_map/ppermute | solution.py:185
  100.2 1.2 shard_map.104
  101.5 3.9 %collective-permute-start.21 = (bf16[512,512]{1,0:T(8,128)(2,1)S(1)}, bf16[512,512]{1,0:T(8,128)(2,1)S(1)}, u32[]{:S(2)}, u32[]{:S(2)}) collective-permute-start(bf16[512,512]{1,0:T(8,128)(2,1)S(1)} %shard_map.104), channel_id=1, source_target_pairs={{4,0},{5,1},{6,2},{7,3},{8,4},{9,5},{10,6},{11,7},{12,8},{13,9},{1... | collective-permute-start | bytes 1572872 | tf_op jit(solution)/shard_map/ppermute | solution.py:185
  105.4 3.9 %collective-permute-start.20 = (bf16[512,512]{1,0:T(8,128)(2,1)S(1)}, bf16[512,512]{1,0:T(8,128)(2,1)S(1)}, u32[]{:S(2)}, u32[]{:S(2)}) collective-permute-start(bf16[512,512]{1,0:T(8,128)(2,1)S(1)} %shard_map.98.after), channel_id=1, source_target_pairs={{4,0},{5,1},{6,2},{7,3},{8,4},{9,5},{10,6},{11,7},{12,8},{13,9},{1... | collective-permute-start | bytes 1572872 | tf_op jit(solution)/shard_map/ppermute | solution.py:185
  109.3 3.7 %collective-permute-done.5.refs_6_ = bf16[512,512]{1,0:T(8,128)(2,1)S(1)} collective-permute-done((bf16[512,512]{1,0:T(8,128)(2,1)S(1)}, bf16[512,512]{1,0:T(8,128)(2,1)S(1)}, u32[]{:S(2)}, u32[]{:S(2)}) %collective-permute-start.5) | collective-permute-done | bytes 524320 | tf_op jit(solution)/shard_map/ppermute | solution.py:185
  113.0 10.8 %collective-permute-done.4.refs_5_ = bf16[512,512]{1,0:T(8,128)(2,1)S(1)} collective-permute-done((bf16[512,512]{1,0:T(8,128)(2,1)S(1)}, bf16[512,512]{1,0:T(8,128)(2,1)S(1)}, u32[]{:S(2)}, u32[]{:S(2)}) %collective-permute-start.4) | collective-permute-done | bytes 524320 | tf_op jit(solution)/shard_map/ppermute | solution.py:185
  123.8 1.5 shard_map.96
  125.3 4.3 %collective-permute-start.6 = (bf16[1024,256]{1,0:T(8,128)(2,1)S(1)}, bf16[1024,256]{1,0:T(8,128)(2,1)S(1)}, u32[]{:S(2)}, u32[]{:S(2)}) collective-permute-start(bf16[1024,256]{1,0:T(8,128)(2,1)S(1)} %get-tuple-element.24), channel_id=1, source_target_pairs={{0,4},{1,5},{2,6},{3,7},{4,8},{5,9},{6,10},{7,11},{8,12},{9,13},{1... | collective-permute-start | bytes 1572872 | tf_op jit(solution)/shard_map/ppermute | solution.py:185
  129.6 1.5 shard_map.100
  131.1 1.9 %collective-permute-start.14 = (bf16[1024,256]{1,0:T(8,128)(2,1)S(1)}, bf16[1024,256]{1,0:T(8,128)(2,1)S(1)}, u32[]{:S(2)}, u32[]{:S(2)}) collective-permute-start(bf16[1024,256]{1,0:T(8,128)(2,1)S(1)} %get-tuple-element.28), channel_id=1, source_target_pairs={{0,4},{1,5},{2,6},{3,7},{4,8},{5,9},{6,10},{7,11},{8,12},{9,13},{1... | collective-permute-start | bytes 1572872 | tf_op jit(solution)/shard_map/ppermute | solution.py:185
  133.1 1.3 shard_map.107
  135.2 3.9 %collective-permute-start.24 = (bf16[1024,256]{1,0:T(8,128)(2,1)S(1)}, bf16[1024,256]{1,0:T(8,128)(2,1)S(1)}, u32[]{:S(2)}, u32[]{:S(2)}) collective-permute-start(bf16[1024,256]{1,0:T(8,128)(2,1)S(1)} %shard_map.107), channel_id=1, source_target_pairs={{4,0},{5,1},{6,2},{7,3},{8,4},{9,5},{10,6},{11,7},{12,8},{13,9},{1... | collective-permute-start | bytes 1572872 | tf_op jit(solution)/shard_map/ppermute | solution.py:185
  139.1 1.3 shard_map.105
  140.4 2.1 %collective-permute-start.22 = (bf16[1024,256]{1,0:T(8,128)(2,1)S(1)}, bf16[1024,256]{1,0:T(8,128)(2,1)S(1)}, u32[]{:S(2)}, u32[]{:S(2)}) collective-permute-start(bf16[1024,256]{1,0:T(8,128)(2,1)S(1)} %shard_map.105), channel_id=1, source_target_pairs={{4,0},{5,1},{6,2},{7,3},{8,4},{9,5},{10,6},{11,7},{12,8},{13,9},{1... | collective-permute-start | bytes 1572872 | tf_op jit(solution)/shard_map/ppermute | solution.py:185
  142.5 1.3 shard_map.97
  143.8 5.9 %collective-permute-start.7 = (bf16[1024,256]{1,0:T(8,128)(2,1)S(1)}, bf16[1024,256]{1,0:T(8,128)(2,1)S(1)}, u32[]{:S(2)}, u32[]{:S(2)}) collective-permute-start(bf16[1024,256]{1,0:T(8,128)(2,1)S(1)} %get-tuple-element.25), channel_id=1, source_target_pairs={{0,4},{1,5},{2,6},{3,7},{4,8},{5,9},{6,10},{7,11},{8,12},{9,13},{1... | collective-permute-start | bytes 1572872 | tf_op jit(solution)/shard_map/ppermute | solution.py:185
  149.7 3.5 %collective-permute-done.14.refs_5_ = bf16[1024,256]{1,0:T(8,128)(2,1)S(1)} collective-permute-done((bf16[1024,256]{1,0:T(8,128)(2,1)S(1)}, bf16[1024,256]{1,0:T(8,128)(2,1)S(1)}, u32[]{:S(2)}, u32[]{:S(2)}) %collective-permute-start.14) | collective-permute-done | bytes 524320 | tf_op jit(solution)/shard_map/ppermute | solution.py:185
  153.2 1.3 shard_map.101
  154.5 6.4 %collective-permute-start.15 = (bf16[1024,256]{1,0:T(8,128)(2,1)S(1)}, bf16[1024,256]{1,0:T(8,128)(2,1)S(1)}, u32[]{:S(2)}, u32[]{:S(2)}) collective-permute-start(bf16[1024,256]{1,0:T(8,128)(2,1)S(1)} %get-tuple-element.29), channel_id=1, source_target_pairs={{0,4},{1,5},{2,6},{3,7},{4,8},{5,9},{6,10},{7,11},{8,12},{9,13},{1... | collective-permute-start | bytes 1572872 | tf_op jit(solution)/shard_map/ppermute | solution.py:185
  161.0 1.3 shard_map.108
  162.3 1.9 %collective-permute-start.25 = (bf16[1024,256]{1,0:T(8,128)(2,1)S(1)}, bf16[1024,256]{1,0:T(8,128)(2,1)S(1)}, u32[]{:S(2)}, u32[]{:S(2)}) collective-permute-start(bf16[1024,256]{1,0:T(8,128)(2,1)S(1)} %shard_map.108), channel_id=1, source_target_pairs={{4,0},{5,1},{6,2},{7,3},{8,4},{9,5},{10,6},{11,7},{12,8},{13,9},{1... | collective-permute-start | bytes 1572872 | tf_op jit(solution)/shard_map/ppermute | solution.py:185
  164.2 1.3 shard_map.106
  165.5 1.9 %collective-permute-start.23 = (bf16[1024,256]{1,0:T(8,128)(2,1)S(1)}, bf16[1024,256]{1,0:T(8,128)(2,1)S(1)}, u32[]{:S(2)}, u32[]{:S(2)}) collective-permute-start(bf16[1024,256]{1,0:T(8,128)(2,1)S(1)} %shard_map.106), channel_id=1, source_target_pairs={{4,0},{5,1},{6,2},{7,3},{8,4},{9,5},{10,6},{11,7},{12,8},{13,9},{1... | collective-permute-start | bytes 1572872 | tf_op jit(solution)/shard_map/ppermute | solution.py:185
  167.4 7.2 %collective-permute-done.15.refs_5_ = bf16[1024,256]{1,0:T(8,128)(2,1)S(1)} collective-permute-done((bf16[1024,256]{1,0:T(8,128)(2,1)S(1)}, bf16[1024,256]{1,0:T(8,128)(2,1)S(1)}, u32[]{:S(2)}, u32[]{:S(2)}) %collective-permute-start.15) | collective-permute-done | bytes 524320 | tf_op jit(solution)/shard_map/ppermute | solution.py:185
  174.6 2.1 %shard_map.102 = (bf16[1024,512]{1,0:T(8,128)(2,1)}, bf16[1024,256]{1,0:T(8,128)(2,1)S(1)}) custom-call(s32[1,4]{1,0:T(1,128)S(1)} %bitcast.24, bf16[256,1024]{1,0:T(8,128)(2,1)S(1)} %get-tuple-element.20.own.refs_1_.down, bf16[256,1024]{1,0:T(8,128)(2,1)S(1)} %collective-permute-done.near.refs_2_, bf16[256,1024]{1,0:T(8,128)(2,1)S(1)} %collective-permute-done.1.far.refs_3_, ...), custom_call_target="tpu_custom_call" | custom-call | flops 536870912 | bytes 1048576 | tf_op jit(solution)/shard_map/pallas_call | solution.py:164
  176.7 2.1 %shard_map.103 = (bf16[1024,512]{1,0:T(8,128)(2,1)}, bf16[1024,256]{1,0:T(8,128)(2,1)S(1)}) custom-call(s32[1,4]{1,0:T(1,128)S(1)} %bitcast.25, bf16[256,1024]{1,0:T(8,128)(2,1)S(1)} %get-tuple-element.20.own.refs_1_.down, bf16[256,1024]{1,0:T(8,128)(2,1)S(1)} %collective-permute-done.near.refs_2_, ...), custom_call_target="tpu_custom_call", output_to_operand_aliasing={{0}: (9, {})} | custom-call | flops 536870912 | bytes 1048576 | tf_op jit(solution)/shard_map/pallas_call | solution.py:164
  178.7 2.3 %collective-permute-done.25.refs_9_ = bf16[1024,256]{1,0:T(8,128)(2,1)S(1)} collective-permute-done((bf16[1024,256]{1,0:T(8,128)(2,1)S(1)}, bf16[1024,256]{1,0:T(8,128)(2,1)S(1)}, u32[]{:S(2)}, u32[]{:S(2)}) %collective-permute-start.25) | collective-permute-done | bytes 524320 | tf_op jit(solution)/shard_map/ppermute | solution.py:185
  181.1 2.1 %shard_map.109.refs_14_ = bf16[1024,512]{1,0:T(8,128)(2,1)} custom-call(s32[1]{0:T(128)S(6)} %copy.14.pick._.refs_0_, bf16[256,1024]{1,0:T(8,128)(2,1)S(1)} %get-tuple-element.26.u0.up.refs_1_, bf16[256,1024]{1,0:T(8,128)(2,1)S(1)} %collective-permute-done.8.u1.refs_2_, bf16[256,1024]{1,0:T(8,128)(2,1)S(1)} %collective-permute-done.16.u0.refs_3_, ...), custom_call_target="tpu_custom_call" | custom-call | flops 1073741824 | bytes 1048576 | tf_op jit(solution)/shard_map/pallas_call | solution.py:164
  183.2 5.9 %collective-permute-done.23.refs_9_ = bf16[1024,256]{1,0:T(8,128)(2,1)S(1)} collective-permute-done((bf16[1024,256]{1,0:T(8,128)(2,1)S(1)}, bf16[1024,256]{1,0:T(8,128)(2,1)S(1)}, u32[]{:S(2)}, u32[]{:S(2)}) %collective-permute-start.23) | collective-permute-done | bytes 524320 | tf_op jit(solution)/shard_map/ppermute | solution.py:185
  189.1 2.2 %shard_map.110 = bf16[1024,512]{1,0:T(8,128)(2,1)} custom-call(s32[1]{0:T(128)S(6)} %copy.14.pick._.refs_0_, bf16[256,1024]{1,0:T(8,128)(2,1)S(1)} %get-tuple-element.26.u0.up.refs_1_, bf16[256,1024]{1,0:T(8,128)(2,1)S(1)} %collective-permute-done.8.u1.refs_2_, ...), custom_call_target="tpu_custom_call", output_to_operand_aliasing={{}: (14, {})} | custom-call | flops 1073741824 | bytes 1048576 | tf_op jit(solution)/shard_map/pallas_call | solution.py:164
  (38 shorter events, 3.3 us)
Async XLA Ops:
  0.6 27.0 %copy-start.7 = (s32[4,1]{0,1:T(1,128)S(1)}, s32[4,1]{0,1:T(1,128)}, u32[]{:S(2)}) copy-start(s32[4,1]{0,1:T(1,128)} %param.14) | copy-start | bytes 52
  0.6 27.0 %collective-permute-start.3 = (bf16[1024,512]{1,0:T(8,128)(2,1)}, bf16[1024,512]{1,0:T(8,128)(2,1)S(1)}, u32[]{:S(2)}, u32[]{:S(2)}) collective-permute-start(bf16[1024,512]{1,0:T(8,128)(2,1)} %bitcast.28), channel_id=1, source_target_pairs={{0,4},{1,5},{2,6},{3,7},{4,8},{5,9},{6,10},{7,11},{8,12},{9,13},{1... | collective-permute-start | bytes 3145736 | tf_op jit(solution)/shard_map/ppermute | solution.py:185
  4.4 28.8 %collective-permute-start.10 = (bf16[1024,512]{1,0:T(8,128)(2,1)}, bf16[1024,512]{1,0:T(8,128)(2,1)S(1)}, u32[]{:S(2)}, u32[]{:S(2)}) collective-permute-start(bf16[1024,512]{1,0:T(8,128)(2,1)} %bitcast.29), channel_id=1, source_target_pairs={{4,0},{5,1},{6,2},{7,3},{8,4},{9,5},{10,6},{11,7},{12,8},{13,9},{1... | collective-permute-start | bytes 3145736 | tf_op jit(solution)/shard_map/ppermute | solution.py:185
  6.5 6.4 %collective-permute-start = (bf16[256,1024]{1,0:T(8,128)(2,1)}, bf16[256,1024]{1,0:T(8,128)(2,1)S(1)}, u32[]{:S(2)}, u32[]{:S(2)}) collective-permute-start(bf16[256,1024]{1,0:T(8,128)(2,1)} %bitcast.10), channel_id=1, source_target_pairs={{0,1},{1,0},{2,3},{3,2},{4,5},{5,4},{6,7},{7,6},{8,9},{9,8},{10,11... | collective-permute-start | bytes 1572872 | tf_op jit(solution)/shard_map/ppermute | solution.py:185
  6.6 22.4 %collective-permute-start.8 = (bf16[256,1024]{1,0:T(8,128)(2,1)}, bf16[256,1024]{1,0:T(8,128)(2,1)S(1)}, u32[]{:S(2)}, u32[]{:S(2)}) collective-permute-start(bf16[256,1024]{1,0:T(8,128)(2,1)} %bitcast.13), channel_id=1, source_target_pairs={{0,1},{1,0},{2,3},{3,2},{4,5},{5,4},{6,7},{7,6},{8,9},{9,8},{10,11... | collective-permute-start | bytes 1572872 | tf_op jit(solution)/shard_map/ppermute | solution.py:185
  7.1 21.9 %collective-permute-start.9 = (bf16[256,1024]{1,0:T(8,128)(2,1)}, bf16[256,1024]{1,0:T(8,128)(2,1)S(1)}, u32[]{:S(2)}, u32[]{:S(2)}) collective-permute-start(bf16[256,1024]{1,0:T(8,128)(2,1)} %bitcast.16), channel_id=1, source_target_pairs={{0,1},{1,0},{2,3},{3,2},{4,5},{5,4},{6,7},{7,6},{8,9},{9,8},{10,11... | collective-permute-start | bytes 1572872 | tf_op jit(solution)/shard_map/ppermute | solution.py:185
  7.8 1.6 copy-start
  9.4 1.0 copy-start.1
  10.5 1.0 copy-start.3
  11.5 1.0 copy-start.5
  34.5 1.0 copy-start.2
  34.5 4.2 %copy-start.4 = (bf16[1,256,1024]{2,1,0:T(8,128)(2,1)S(1)}, bf16[1,256,1024]{2,1,0:T(8,128)(2,1)}, u32[]{:S(2)}) copy-start(bf16[1,256,1024]{2,1,0:T(8,128)(2,1)} %param.11) | copy-start | bytes 1572868
  34.5 6.9 %copy-start.6 = (bf16[1,256,1024]{2,1,0:T(8,128)(2,1)S(1)}, bf16[1,256,1024]{2,1,0:T(8,128)(2,1)}, u32[]{:S(2)}) copy-start(bf16[1,256,1024]{2,1,0:T(8,128)(2,1)} %param.12) | copy-start | bytes 1572868
  34.6 60.2 %collective-permute-start.11 = (bf16[512,1024]{1,0:T(8,128)(2,1)S(1)}, bf16[512,1024]{1,0:T(8,128)(2,1)S(1)}, u32[]{:S(2)}, u32[]{:S(2)}) collective-permute-start(bf16[512,1024]{1,0:T(8,128)(2,1)S(1)} %shard_map.99), channel_id=1, source_target_pairs={{0,240},{1,241},{2,242},{3,243},{252,12},{253,13},{254,14},{255,15}} | collective-permute-start | bytes 3145736 | tf_op jit(solution)/shard_map/ppermute | solution.py:185
  35.5 38.8 %collective-permute-start.1 = (bf16[256,1024]{1,0:T(8,128)(2,1)S(1)}, bf16[256,1024]{1,0:T(8,128)(2,1)S(1)}, u32[]{:S(2)}, u32[]{:S(2)}) collective-permute-start(bf16[256,1024]{1,0:T(8,128)(2,1)S(1)} %bitcast.12), channel_id=1, source_target_pairs={{0,2},{1,3},{2,0},{3,1},{4,6},{5,7},{6,4},{7,5},{8,10},{9,11},{10,... | collective-permute-start | bytes 1572872 | tf_op jit(solution)/shard_map/ppermute | solution.py:185
  38.7 46.9 %collective-permute-start.16 = (bf16[256,1024]{1,0:T(8,128)(2,1)S(1)}, bf16[256,1024]{1,0:T(8,128)(2,1)S(1)}, u32[]{:S(2)}, u32[]{:S(2)}) collective-permute-start(bf16[256,1024]{1,0:T(8,128)(2,1)S(1)} %bitcast.15), channel_id=1, source_target_pairs={{4,6},{5,7},{6,4},{7,5},{8,10},{9,11},{10,8},{11,9},{12,14},{13,15... | collective-permute-start | bytes 1572872 | tf_op jit(solution)/shard_map/ppermute | solution.py:185
  41.4 53.5 %collective-permute-start.18 = (bf16[256,1024]{1,0:T(8,128)(2,1)S(1)}, bf16[256,1024]{1,0:T(8,128)(2,1)S(1)}, u32[]{:S(2)}, u32[]{:S(2)}) collective-permute-start(bf16[256,1024]{1,0:T(8,128)(2,1)S(1)} %bitcast.18), channel_id=1, source_target_pairs={{4,6},{5,7},{6,4},{7,5},{8,10},{9,11},{10,8},{11,9},{12,14},{13,15... | collective-permute-start | bytes 1572872 | tf_op jit(solution)/shard_map/ppermute | solution.py:185
  74.4 21.3 %collective-permute-start.2 = (bf16[256,1024]{1,0:T(8,128)(2,1)S(1)}, bf16[256,1024]{1,0:T(8,128)(2,1)S(1)}, u32[]{:S(2)}, u32[]{:S(2)}) collective-permute-start(bf16[256,1024]{1,0:T(8,128)(2,1)S(1)} %collective-permute-done.1.far.refs_3_), channel_id=1, source_target_pairs={{0,1},{1,0},{2,3},{3,2},{4,5},{5,4},{6,7},{7,6},{8,9},{9,8},{10,11... | collective-permute-start | bytes 1572872 | tf_op jit(solution)/shard_map/ppermute | solution.py:185
  85.6 14.6 %collective-permute-start.17 = (bf16[256,1024]{1,0:T(8,128)(2,1)S(1)}, bf16[256,1024]{1,0:T(8,128)(2,1)S(1)}, u32[]{:S(2)}, u32[]{:S(2)}) collective-permute-start(bf16[256,1024]{1,0:T(8,128)(2,1)S(1)} %collective-permute-done.16.u0.refs_3_), channel_id=1, source_target_pairs={{0,1},{1,0},{2,3},{3,2},{4,5},{5,4},{6,7},{7,6},{8,9},{9,8},{10,11... | collective-permute-start | bytes 1572872 | tf_op jit(solution)/shard_map/ppermute | solution.py:185
  94.9 5.3 %collective-permute-start.19 = (bf16[256,1024]{1,0:T(8,128)(2,1)S(1)}, bf16[256,1024]{1,0:T(8,128)(2,1)S(1)}, u32[]{:S(2)}, u32[]{:S(2)}) collective-permute-start(bf16[256,1024]{1,0:T(8,128)(2,1)S(1)} %collective-permute-done.18.r0.refs_7_), channel_id=1, source_target_pairs={{0,1},{1,0},{2,3},{3,2},{4,5},{5,4},{6,7},{7,6},{8,9},{9,8},{10,11... | collective-permute-start | bytes 1572872 | tf_op jit(solution)/shard_map/ppermute | solution.py:185
  94.9 39.5 %collective-permute-start.12 = (bf16[512,1024]{1,0:T(8,128)(2,1)S(1)}, bf16[512,1024]{1,0:T(8,128)(2,1)S(1)}, u32[]{:S(2)}, u32[]{:S(2)}) collective-permute-start(bf16[512,1024]{1,0:T(8,128)(2,1)S(1)} %collective-permute-done.11), channel_id=1, source_target_pairs={{240,2},{241,3},{242,0},{243,1},{12,254},{13,255},{14,252},{15,253}} | collective-permute-start | bytes 3145736 | tf_op jit(solution)/shard_map/ppermute | solution.py:185
  96.3 16.7 %collective-permute-start.5 = (bf16[512,512]{1,0:T(8,128)(2,1)S(1)}, bf16[512,512]{1,0:T(8,128)(2,1)S(1)}, u32[]{:S(2)}, u32[]{:S(2)}) collective-permute-start(bf16[512,512]{1,0:T(8,128)(2,1)S(1)} %down_far.1), channel_id=1, source_target_pairs={{0,4},{1,5},{2,6},{3,7},{4,8},{5,9},{6,10},{7,11},{8,12},{9,13},{1... | collective-permute-start | bytes 1572872 | tf_op jit(solution)/shard_map/ppermute | solution.py:185
  98.3 25.5 %collective-permute-start.4 = (bf16[512,512]{1,0:T(8,128)(2,1)S(1)}, bf16[512,512]{1,0:T(8,128)(2,1)S(1)}, u32[]{:S(2)}, u32[]{:S(2)}) collective-permute-start(bf16[512,512]{1,0:T(8,128)(2,1)S(1)} %get-tuple-element.22), channel_id=1, source_target_pairs={{0,4},{1,5},{2,6},{3,7},{4,8},{5,9},{6,10},{7,11},{8,12},{9,13},{1... | collective-permute-start | bytes 1572872 | tf_op jit(solution)/shard_map/ppermute | solution.py:185
  101.5 31.6 %collective-permute-start.21 = (bf16[512,512]{1,0:T(8,128)(2,1)S(1)}, bf16[512,512]{1,0:T(8,128)(2,1)S(1)}, u32[]{:S(2)}, u32[]{:S(2)}) collective-permute-start(bf16[512,512]{1,0:T(8,128)(2,1)S(1)} %shard_map.104), channel_id=1, source_target_pairs={{4,0},{5,1},{6,2},{7,3},{8,4},{9,5},{10,6},{11,7},{12,8},{13,9},{1... | collective-permute-start | bytes 1572872 | tf_op jit(solution)/shard_map/ppermute | solution.py:185
  105.4 27.7 %collective-permute-start.20 = (bf16[512,512]{1,0:T(8,128)(2,1)S(1)}, bf16[512,512]{1,0:T(8,128)(2,1)S(1)}, u32[]{:S(2)}, u32[]{:S(2)}) collective-permute-start(bf16[512,512]{1,0:T(8,128)(2,1)S(1)} %shard_map.98.after), channel_id=1, source_target_pairs={{4,0},{5,1},{6,2},{7,3},{8,4},{9,5},{10,6},{11,7},{12,8},{13,9},{1... | collective-permute-start | bytes 1572872 | tf_op jit(solution)/shard_map/ppermute | solution.py:185
  125.3 17.2 %collective-permute-start.6 = (bf16[1024,256]{1,0:T(8,128)(2,1)S(1)}, bf16[1024,256]{1,0:T(8,128)(2,1)S(1)}, u32[]{:S(2)}, u32[]{:S(2)}) collective-permute-start(bf16[1024,256]{1,0:T(8,128)(2,1)S(1)} %get-tuple-element.24), channel_id=1, source_target_pairs={{0,4},{1,5},{2,6},{3,7},{4,8},{5,9},{6,10},{7,11},{8,12},{9,13},{1... | collective-permute-start | bytes 1572872 | tf_op jit(solution)/shard_map/ppermute | solution.py:185
  131.1 22.1 %collective-permute-start.14 = (bf16[1024,256]{1,0:T(8,128)(2,1)S(1)}, bf16[1024,256]{1,0:T(8,128)(2,1)S(1)}, u32[]{:S(2)}, u32[]{:S(2)}) collective-permute-start(bf16[1024,256]{1,0:T(8,128)(2,1)S(1)} %get-tuple-element.28), channel_id=1, source_target_pairs={{0,4},{1,5},{2,6},{3,7},{4,8},{5,9},{6,10},{7,11},{8,12},{9,13},{1... | collective-permute-start | bytes 1572872 | tf_op jit(solution)/shard_map/ppermute | solution.py:185
  134.4 40.2 %collective-permute-start.13 = (bf16[512,1024]{1,0:T(8,128)(2,1)S(1)}, bf16[512,1024]{1,0:T(8,128)(2,1)S(1)}, u32[]{:S(2)}, u32[]{:S(2)}) collective-permute-start(bf16[512,1024]{1,0:T(8,128)(2,1)S(1)} %collective-permute-done.12.refs_7_.refs_12_), channel_id=1, source_target_pairs={{0,1},{1,0},{2,3},{3,2},{252,253},{253,252},{254,255},{255,254}} | collective-permute-start | bytes 3145736 | tf_op jit(solution)/shard_map/ppermute | solution.py:185
  135.2 25.8 %collective-permute-start.24 = (bf16[1024,256]{1,0:T(8,128)(2,1)S(1)}, bf16[1024,256]{1,0:T(8,128)(2,1)S(1)}, u32[]{:S(2)}, u32[]{:S(2)}) collective-permute-start(bf16[1024,256]{1,0:T(8,128)(2,1)S(1)} %shard_map.107), channel_id=1, source_target_pairs={{4,0},{5,1},{6,2},{7,3},{8,4},{9,5},{10,6},{11,7},{12,8},{13,9},{1... | collective-permute-start | bytes 1572872 | tf_op jit(solution)/shard_map/ppermute | solution.py:185
  140.4 23.8 %collective-permute-start.22 = (bf16[1024,256]{1,0:T(8,128)(2,1)S(1)}, bf16[1024,256]{1,0:T(8,128)(2,1)S(1)}, u32[]{:S(2)}, u32[]{:S(2)}) collective-permute-start(bf16[1024,256]{1,0:T(8,128)(2,1)S(1)} %shard_map.105), channel_id=1, source_target_pairs={{4,0},{5,1},{6,2},{7,3},{8,4},{9,5},{10,6},{11,7},{12,8},{13,9},{1... | collective-permute-start | bytes 1572872 | tf_op jit(solution)/shard_map/ppermute | solution.py:185
  143.8 32.8 %collective-permute-start.7 = (bf16[1024,256]{1,0:T(8,128)(2,1)S(1)}, bf16[1024,256]{1,0:T(8,128)(2,1)S(1)}, u32[]{:S(2)}, u32[]{:S(2)}) collective-permute-start(bf16[1024,256]{1,0:T(8,128)(2,1)S(1)} %get-tuple-element.25), channel_id=1, source_target_pairs={{0,4},{1,5},{2,6},{3,7},{4,8},{5,9},{6,10},{7,11},{8,12},{9,13},{1... | collective-permute-start | bytes 1572872 | tf_op jit(solution)/shard_map/ppermute | solution.py:185
  154.5 20.1 %collective-permute-start.15 = (bf16[1024,256]{1,0:T(8,128)(2,1)S(1)}, bf16[1024,256]{1,0:T(8,128)(2,1)S(1)}, u32[]{:S(2)}, u32[]{:S(2)}) collective-permute-start(bf16[1024,256]{1,0:T(8,128)(2,1)S(1)} %get-tuple-element.29), channel_id=1, source_target_pairs={{0,4},{1,5},{2,6},{3,7},{4,8},{5,9},{6,10},{7,11},{8,12},{9,13},{1... | collective-permute-start | bytes 1572872 | tf_op jit(solution)/shard_map/ppermute | solution.py:185
  162.3 18.8 %collective-permute-start.25 = (bf16[1024,256]{1,0:T(8,128)(2,1)S(1)}, bf16[1024,256]{1,0:T(8,128)(2,1)S(1)}, u32[]{:S(2)}, u32[]{:S(2)}) collective-permute-start(bf16[1024,256]{1,0:T(8,128)(2,1)S(1)} %shard_map.108), channel_id=1, source_target_pairs={{4,0},{5,1},{6,2},{7,3},{8,4},{9,5},{10,6},{11,7},{12,8},{13,9},{1... | collective-permute-start | bytes 1572872 | tf_op jit(solution)/shard_map/ppermute | solution.py:185
  165.5 23.6 %collective-permute-start.23 = (bf16[1024,256]{1,0:T(8,128)(2,1)S(1)}, bf16[1024,256]{1,0:T(8,128)(2,1)S(1)}, u32[]{:S(2)}, u32[]{:S(2)}) collective-permute-start(bf16[1024,256]{1,0:T(8,128)(2,1)S(1)} %shard_map.106), channel_id=1, source_target_pairs={{4,0},{5,1},{6,2},{7,3},{8,4},{9,5},{10,6},{11,7},{12,8},{13,9},{1... | collective-permute-start | bytes 1572872 | tf_op jit(solution)/shard_map/ppermute | solution.py:185
where the time goes:
time: 192 us; the launch traced here: 191 us
  waiting for transfers between devices  103 us (54%)
  starting transfers between devices  58 us (30%)
  Pallas kernels  24.1 us (13%)
  local copies, waits for them, and re-layouts  4.75 us (2%)
    ppermute x26, waiting for transfers between devices, sent(): return lax.ppermute(value, ('layer', 'shot'), pairs)  103 us
    ppermute x26, starting transfers between devices, sent(): return lax.ppermute(value, ('layer', 'shot'), pairs)  58 us
    pallas_call x16, Pallas kernels, call(): pl.pallas_call(kernel, grid=(1,), in_specs=in_specs, out_specs=out_specs,...  23.1 us
    unnamed x16, local copies, waits for them, and re-layouts  4.75 us
  transfers between devices with their start and end apart: 26, of which 11 were waited for; matrix products, arithmetic and copies ran while one was open for 0% of the time, Pallas kernels for 11%

commit v1 on v0

v1 whole, which is shorter than its diff:
```python
import functools

import jax
import jax.numpy as jnp
from jax import lax
from jax.experimental import pallas as pl
from jax.experimental.pallas import tpu as pltpu
from jax.sharding import PartitionSpec as P


TICKS = 4
CHUNKS = 2
WHOLE = pl.BlockSpec(memory_space=pltpu.VMEM)
SCALARS = pl.BlockSpec(memory_space=pltpu.SMEM)
F32, BF16 = jnp.float32, jnp.bfloat16


def dot(a, b):
    return jnp.dot(a, b, preferred_element_type=F32)


def band(index, height):
    return pl.ds(pl.multiple_of(index * height, height), height)


def injected(received, source):
    return (received.astype(F32) + source.astype(F32)).astype(BF16)


def stage_kernel(*refs):
    n = (len(refs) - 1) // 2
    copies = [pltpu.make_async_copy(refs[i], refs[n + i], refs[-1].at[i]) for i in range(n)]
    for copy in copies:
        copy.start()
    for copy in copies:
        copy.wait()


def staged(*arrays):
    n = len(arrays)
    return pl.pallas_call(
        stage_kernel,
        name="stage",
        in_specs=[pl.BlockSpec(memory_space=pl.ANY)] * n,
        out_specs=[WHOLE] * n,
        out_shape=[jax.ShapeDtypeStruct(a.shape, a.dtype) for a in arrays],
        scratch_shapes=[pltpu.SemaphoreType.DMA((n,))],
        cost_estimate=pl.CostEstimate(flops=0, transcendentals=0, bytes_accessed=2**20),
        compiler_params=pltpu.CompilerParams(vmem_limit_bytes=16 * 2**20),
    )(*arrays)


def late_kernel(_, after, down, up, reflect, pair):
    high = down.shape[0]
    top = lax.axis_index("layer") == 0
    pair[:high, :] = jnp.where(top, up[...], down[...])
    pair[high:, :] = jnp.where(top, reflect[...], up[...])


def columns(ref, chunk, width):
    return slice(chunk * width, (chunk + 1) * width) if ref.shape[-1] > width else slice(None)


def down_kernel(moment, chunk, last, plan, b0, b1, b2, b3, received, sources, *rest):
    late, (new, down_in) = rest[:-2], rest[-2:]
    end = lax.axis_index("layer") == lax.axis_size("layer") - 1
    spot = lax.axis_index("shot")
    width = down_in.shape[1]
    source = sources[plan[0, moment], :, columns(sources, chunk, width)]
    down_in[...] = injected(received[:, columns(received, chunk, width)], source)
    for k, block in enumerate((b0, b1, b2, b3)):
        high, value = block.shape[0], block[...]
        if last and k >= 2:
            value = jnp.where(end, late[k - 2][:high, :], value)
        new[band(spot ^ k, high), :] = dot(value, down_in[...]).astype(BF16)


def up_kernel(chunk, last, *refs):
    pick, *blocks = refs[:9]
    received, down_in, sources = refs[9:12]
    late, new = refs[12:-1], refs[-1]
    top = lax.axis_index("layer") == 0
    end = lax.axis_index("layer") == lax.axis_size("layer") - 1
    spot = lax.axis_index("shot")
    width = down_in.shape[1]
    gathered = received[:, columns(received, chunk, width)]
    for k in range(4):
        up, reflect = blocks[k][...], blocks[4 + k][...]
        high = up.shape[0]
        if last and k >= 2:
            first, second = late[k - 2][:high, :], late[k - 2][high:, :]
            up = jnp.where(top, first, jnp.where(end, second, up))
            reflect = jnp.where(top, second, reflect)
        rows = band(spot ^ k, high)
        total = dot(up, gathered) + dot(reflect, down_in[...])
        total = total + sources[pick[0], rows, columns(sources, chunk, width)].astype(F32)
        new[rows, :] = total.astype(BF16)


def call(kernel, scalars, arrays, out_shape, flops, full=None, into=None, more=()):
    out_specs = [WHOLE] * len(out_shape)
    in_specs = [SCALARS] + [WHOLE] * len(arrays)
    args = [scalars, *arrays]
    in_specs += [WHOLE] * len(more)
    args += more
    aliases = {}
    if full is not None:
        chunk, wide = full
        height, width = out_shape[0]
        out_shape = [(height, wide), *out_shape[1:]]
        out_specs[0] = pl.BlockSpec((height, width), lambda i: (0, chunk))
        if into is not None:
            in_specs.append(pl.BlockSpec(memory_space=pl.ANY))
            aliases = {len(args): 0}
            args.append(into)
            kernel = without(kernel, len(args) - 1)
    return pl.pallas_call(
        kernel,
        grid=(1,),
        in_specs=in_specs,
        out_specs=out_specs,
        out_shape=[jax.ShapeDtypeStruct(s, BF16) for s in out_shape],
        input_output_aliases=aliases,
        cost_estimate=pl.CostEstimate(flops=flops, transcendentals=0, bytes_accessed=2**20),
        compiler_params=pltpu.CompilerParams(vmem_limit_bytes=16 * 2**20),
    )(*args)


def without(kernel, at):
    def inner(*refs):
        kernel(*refs[:at], *refs[at + 1 :])

    return inner


def sent(value, pairs):
    return lax.ppermute(value, ("layer", "shot"), pairs)


def steps(down_state, up_state, down_op, up_op, reflect_op, source_bank, plan, layer_source):
    layers, shots = lax.axis_size("layer"), lax.axis_size("shot")
    height, wide = down_state.shape[1:]
    width = wide // CHUNKS
    one = 2 * height * height * width
    down_op, up_op, reflect_op = down_op[0], up_op[0], reflect_op[0]

    def at(layer, shot):
        return layer * shots + shot

    every = range(layers)

    def shift(value, steps):
        return sent(value, [
            (at(l, s), at(l + steps, s)) for l in every for s in range(shots) if 0 <= l + steps < layers
        ])

    def swap(value, bit, members):
        return sent(value, [(at(l, s), at(l, s ^ bit)) for l in members for s in range(shots)])

    middle = [l for l in every if 0 < l < layers - 1]
    down_0 = shift(down_state[0], 1)
    far_d = swap(down_op, 2, [0] + middle)
    up_0 = shift(up_state[0], -1)
    near_d = swap(down_op, 1, every)
    far_u = swap(up_op, 2, middle)
    far_r = swap(reflect_op, 2, middle + [layers - 1])
    near_u = swap(up_op, 1, every)
    near_r = swap(reflect_op, 1, every)
    cross_d = swap(far_d, 1, every)
    cross_u = swap(far_u, 1, every)
    cross_r = swap(far_r, 1, every)

    plan = plan.T
    down_op, up_op, reflect_op, sources = staged(down_op, up_op, reflect_op, source_bank[0])
    d_blocks = [down_op, near_d, far_d, cross_d]
    u_blocks = [up_op, near_u, far_u, cross_u, reflect_op, near_r, far_r, cross_r]
    downs, ups = [down_0] * CHUNKS, [up_0] * CHUNKS
    late = ()
    for moment in range(TICKS):
        last = moment == TICKS - 1
        if moment == 1:
            (pair,) = call(
                late_kernel, layer_source, [down_in_0, down_op, up_op, reflect_op],
                [(height // 2, height)], one // 8,
            )
            ends = ((0, layers - 4), (layers - 1, 3))
            pair = sent(pair, [(at(a, s), at(b, s)) for a, b in ends for s in range(shots)])
            pair = sent(pair, [(at(b, s), at(a, s ^ 2)) for a, b in ends for s in range(shots)])
            late = (pair, swap(pair, 1, (0, layers - 1)))
        new_downs, new_ups, new, up = [], [], None, None
        for chunk in range(CHUNKS):
            full = (chunk, wide) if last else None
            more = late if last else ()
            new, down_in = call(
                functools.partial(down_kernel, moment, chunk, last), plan,
                [*d_blocks, downs[chunk], sources], [(height, width)] * 2, one,
                full=full, into=new if last else None, more=more,
            )
            (up,) = call(
                functools.partial(up_kernel, chunk, last), layer_source,
                [*u_blocks, ups[chunk], down_in, sources], [(height, width)], 2 * one,
                full=full, into=up if last else None, more=more,
            )
            if moment == 0 and chunk == CHUNKS - 1:
                down_in_0 = down_in
            new_downs.append(new)
            new_ups.append(up)
        if last:
            return (new[None], up[None])
        downs = [shift(a, 1) for a in new_downs]
        ups = [shift(a, -1) for a in new_ups]


def solution(mesh):
    placed = (
        P("layer", None, "shot"),
        P("layer", None, "shot"),
        P("layer", "shot", None),
        P("layer", "shot", None),
        P("layer", "shot", None),
        P("layer", None, None, "shot"),
        P(None, "layer"),
        P("layer"),
    )
    return jax.shard_map(
        steps,
        mesh=mesh,
        in_specs=placed,
        out_specs=(P("layer", None, "shot"), P("layer", None, "shot")),
        check_vma=False,
    )
```

time: 192 us -> 175 us (0.911)
  the two profiles are of different devices: /device:TPU:22 before, /device:TPU:198 now
where the time goes in v1:
time: 175 us; the launch traced here: 174 us
  starting transfers between devices  86.4 us (49%)
  waiting for transfers between devices  56.8 us (32%)
  Pallas kernels  25.1 us (14%)
  local copies, waits for them, and re-layouts  3.68 us (2%)
    ppermute x26, starting transfers between devices, sent(): return lax.ppermute(value, ('layer', 'shot'), pairs)  86.4 us
    ppermute x26, waiting for transfers between devices, sent(): return lax.ppermute(value, ('layer', 'shot'), pairs)  56.8 us
    pallas_call x17, Pallas kernels, call(): pl.pallas_call(kernel, grid=(1,), in_specs=in_specs, out_specs=out_specs,...  24 us
    unnamed x12, local copies, waits for them, and re-layouts  3.68 us
  transfers between devices with their start and end apart: 26, of which 10 were waited for; matrix products, arithmetic and copies ran while one was open for 0% of the time, Pallas kernels for 12%

profile of v1, /device:TPU:198, one launch (start us, length us, event | category | flops | bytes accessed | tf_op | source)
XLA Modules:
  0.0 173.8 jit_solution(7308758681395812473)
XLA Ops:
  0.6 3.5 %collective-permute-start.1 = (bf16[256,1024]{1,0:T(8,128)(2,1)}, bf16[256,1024]{1,0:T(8,128)(2,1)S(1)}, u32[]{:S(2)}, u32[]{:S(2)}) collective-permute-start(bf16[256,1024]{1,0:T(8,128)(2,1)} %bitcast.10), channel_id=1, source_target_pairs={{0,2},{1,3},{2,0},{3,1},{4,6},{5,7},{6,4},{7,5},{8,10},{9,11},{10,... | collective-permute-start | bytes 1572872 | tf_op jit(solution)/shard_map/ppermute | solution.py:137
  4.1 2.8 %collective-permute-start.3 = (bf16[1024,512]{1,0:T(8,128)(2,1)}, bf16[1024,512]{1,0:T(8,128)(2,1)S(1)}, u32[]{:S(2)}, u32[]{:S(2)}) collective-permute-start(bf16[1024,512]{1,0:T(8,128)(2,1)} %bitcast.26), channel_id=1, source_target_pairs={{0,4},{1,5},{2,6},{3,7},{4,8},{5,9},{6,10},{7,11},{8,12},{9,13},{1... | collective-permute-start | bytes 3145736 | tf_op jit(solution)/shard_map/ppermute | solution.py:137
  7.1 9.3 %collective-permute-done.1.b2.refs_3_ = bf16[256,1024]{1,0:T(8,128)(2,1)S(1)} collective-permute-done((bf16[256,1024]{1,0:T(8,128)(2,1)}, bf16[256,1024]{1,0:T(8,128)(2,1)S(1)}, u32[]{:S(2)}, u32[]{:S(2)}) %collective-permute-start.1) | collective-permute-done | bytes 524320 | tf_op jit(solution)/shard_map/ppermute | solution.py:137
  17.1 1.6 copy-done
  18.7 1.0 copy-done.1
  19.7 1.0 copy-done.2
  20.7 1.1 stage.1
  21.9 9.0 %collective-permute-done.3.received = bf16[1024,512]{1,0:T(8,128)(2,1)S(1)} collective-permute-done((bf16[1024,512]{1,0:T(8,128)(2,1)}, bf16[1024,512]{1,0:T(8,128)(2,1)S(1)}, u32[]{:S(2)}, u32[]{:S(2)}) %collective-permute-start.3) | collective-permute-done | bytes 1048608 | tf_op jit(solution)/shard_map/ppermute | solution.py:137
  30.9 1.3 shard_map.95
  32.3 0.9 collective-permute-start.7
  33.2 2.4 %collective-permute-start.14 = (bf16[256,1024]{1,0:T(8,128)(2,1)}, bf16[256,1024]{1,0:T(8,128)(2,1)S(1)}, u32[]{:S(2)}, u32[]{:S(2)}) collective-permute-start(bf16[256,1024]{1,0:T(8,128)(2,1)} %bitcast.2.refs_1_), channel_id=1, source_target_pairs={{4,6},{5,7},{6,4},{7,5},{8,10},{9,11},{10,8},{11,9},{12,14},{13,15... | collective-permute-start | bytes 1572872 | tf_op jit(solution)/shard_map/ppermute | solution.py:137
  35.6 3.5 %collective-permute-start.17 = (bf16[256,1024]{1,0:T(8,128)(2,1)S(1)}, bf16[256,1024]{1,0:T(8,128)(2,1)S(1)}, u32[]{:S(2)}, u32[]{:S(2)}) collective-permute-start(bf16[256,1024]{1,0:T(8,128)(2,1)S(1)} %bitcast.14), channel_id=1, source_target_pairs={{4,6},{5,7},{6,4},{7,5},{8,10},{9,11},{10,8},{11,9},{12,14},{13,15... | collective-permute-start | bytes 1572872 | tf_op jit(solution)/shard_map/ppermute | solution.py:137
  39.1 2.7 %collective-permute-start.19 = (bf16[1024,512]{1,0:T(8,128)(2,1)S(1)}, bf16[1024,512]{1,0:T(8,128)(2,1)S(1)}, u32[]{:S(2)}, u32[]{:S(2)}) collective-permute-start(bf16[1024,512]{1,0:T(8,128)(2,1)S(1)} %bitcast.27), channel_id=1, source_target_pairs={{4,0},{5,1},{6,2},{7,3},{8,4},{9,5},{10,6},{11,7},{12,8},{13,9},{1... | collective-permute-start | bytes 3145736 | tf_op jit(solution)/shard_map/ppermute | solution.py:137
  41.9 8.2 %collective-permute-done.14.refs_3_ = bf16[256,1024]{1,0:T(8,128)(2,1)S(1)} collective-permute-done((bf16[256,1024]{1,0:T(8,128)(2,1)}, bf16[256,1024]{1,0:T(8,128)(2,1)S(1)}, u32[]{:S(2)}, u32[]{:S(2)}) %collective-permute-start.14) | collective-permute-done | bytes 524320 | tf_op jit(solution)/shard_map/ppermute | solution.py:137
  50.6 8.5 %collective-permute-done.17.refs_7_ = bf16[256,1024]{1,0:T(8,128)(2,1)S(1)} collective-permute-done((bf16[256,1024]{1,0:T(8,128)(2,1)S(1)}, bf16[256,1024]{1,0:T(8,128)(2,1)S(1)}, u32[]{:S(2)}, u32[]{:S(2)}) %collective-permute-start.17) | collective-permute-done | bytes 524320 | tf_op jit(solution)/shard_map/ppermute | solution.py:137
  59.8 1.3 shard_map.99
  61.1 27.4 %collective-permute-start.4 = (bf16[1024,256]{1,0:T(8,128)(2,1)S(1)}, bf16[1024,256]{1,0:T(8,128)(2,1)S(1)}, u32[]{:S(2)}, u32[]{:S(2)}) collective-permute-start(bf16[1024,256]{1,0:T(8,128)(2,1)S(1)} %get-tuple-element.24), channel_id=1, source_target_pairs={{0,4},{1,5},{2,6},{3,7},{4,8},{5,9},{6,10},{7,11},{8,12},{9,13},{1... | collective-permute-start | bytes 1572872 | tf_op jit(solution)/shard_map/ppermute | solution.py:137
  88.5 1.9 %collective-permute-start.10 = (bf16[1024,256]{1,0:T(8,128)(2,1)S(1)}, bf16[1024,256]{1,0:T(8,128)(2,1)S(1)}, u32[]{:S(2)}, u32[]{:S(2)}) collective-permute-start(bf16[1024,256]{1,0:T(8,128)(2,1)S(1)} %get-tuple-element.30), channel_id=1, source_target_pairs={{0,4},{1,5},{2,6},{3,7},{4,8},{5,9},{6,10},{7,11},{8,12},{9,13},{1... | collective-permute-start | bytes 1572872 | tf_op jit(solution)/shard_map/ppermute | solution.py:137
  90.5 1.3 shard_map.107
  91.7 3.9 %collective-permute-start.23 = (bf16[1024,256]{1,0:T(8,128)(2,1)S(1)}, bf16[1024,256]{1,0:T(8,128)(2,1)S(1)}, u32[]{:S(2)}, u32[]{:S(2)}) collective-permute-start(bf16[1024,256]{1,0:T(8,128)(2,1)S(1)} %shard_map.107), channel_id=1, source_target_pairs={{4,0},{5,1},{6,2},{7,3},{8,4},{9,5},{10,6},{11,7},{12,8},{13,9},{1... | collective-permute-start | bytes 1572872 | tf_op jit(solution)/shard_map/ppermute | solution.py:137
  95.7 1.3 shard_map.104
  96.9 1.9 %collective-permute-start.20 = (bf16[1024,256]{1,0:T(8,128)(2,1)S(1)}, bf16[1024,256]{1,0:T(8,128)(2,1)S(1)}, u32[]{:S(2)}, u32[]{:S(2)}) collective-permute-start(bf16[1024,256]{1,0:T(8,128)(2,1)S(1)} %shard_map.104), channel_id=1, source_target_pairs={{4,0},{5,1},{6,2},{7,3},{8,4},{9,5},{10,6},{11,7},{12,8},{13,9},{1... | collective-permute-start | bytes 1572872 | tf_op jit(solution)/shard_map/ppermute | solution.py:137
  98.9 1.9 %collective-permute-done.4.received = bf16[1024,256]{1,0:T(8,128)(2,1)S(1)} collective-permute-done((bf16[1024,256]{1,0:T(8,128)(2,1)S(1)}, bf16[1024,256]{1,0:T(8,128)(2,1)S(1)}, u32[]{:S(2)}, u32[]{:S(2)}) %collective-permute-start.4) | collective-permute-done | bytes 524320 | tf_op jit(solution)/shard_map/ppermute | solution.py:137
  100.8 1.3 shard_map.96
  102.1 6.5 %collective-permute-start.5 = (bf16[1024,256]{1,0:T(8,128)(2,1)S(1)}, bf16[1024,256]{1,0:T(8,128)(2,1)S(1)}, u32[]{:S(2)}, u32[]{:S(2)}) collective-permute-start(bf16[1024,256]{1,0:T(8,128)(2,1)S(1)} %get-tuple-element.25), channel_id=1, source_target_pairs={{0,4},{1,5},{2,6},{3,7},{4,8},{5,9},{6,10},{7,11},{8,12},{9,13},{1... | collective-permute-start | bytes 1572872 | tf_op jit(solution)/shard_map/ppermute | solution.py:137
  108.6 3.4 %collective-permute-done.10.received = bf16[1024,256]{1,0:T(8,128)(2,1)S(1)} collective-permute-done((bf16[1024,256]{1,0:T(8,128)(2,1)S(1)}, bf16[1024,256]{1,0:T(8,128)(2,1)S(1)}, u32[]{:S(2)}, u32[]{:S(2)}) %collective-permute-start.10) | collective-permute-done | bytes 524320 | tf_op jit(solution)/shard_map/ppermute | solution.py:137
  112.0 1.3 shard_map.100
  113.3 6.5 %collective-permute-start.11 = (bf16[1024,256]{1,0:T(8,128)(2,1)S(1)}, bf16[1024,256]{1,0:T(8,128)(2,1)S(1)}, u32[]{:S(2)}, u32[]{:S(2)}) collective-permute-start(bf16[1024,256]{1,0:T(8,128)(2,1)S(1)} %get-tuple-element.31), channel_id=1, source_target_pairs={{0,4},{1,5},{2,6},{3,7},{4,8},{5,9},{6,10},{7,11},{8,12},{9,13},{1... | collective-permute-start | bytes 1572872 | tf_op jit(solution)/shard_map/ppermute | solution.py:137
  119.8 1.3 shard_map.108
  121.1 1.9 %collective-permute-start.24 = (bf16[1024,256]{1,0:T(8,128)(2,1)S(1)}, bf16[1024,256]{1,0:T(8,128)(2,1)S(1)}, u32[]{:S(2)}, u32[]{:S(2)}) collective-permute-start(bf16[1024,256]{1,0:T(8,128)(2,1)S(1)} %shard_map.108), channel_id=1, source_target_pairs={{4,0},{5,1},{6,2},{7,3},{8,4},{9,5},{10,6},{11,7},{12,8},{13,9},{1... | collective-permute-start | bytes 1572872 | tf_op jit(solution)/shard_map/ppermute | solution.py:137
  123.8 1.3 shard_map.105
  125.1 2.1 %collective-permute-start.21 = (bf16[1024,256]{1,0:T(8,128)(2,1)S(1)}, bf16[1024,256]{1,0:T(8,128)(2,1)S(1)}, u32[]{:S(2)}, u32[]{:S(2)}) collective-permute-start(bf16[1024,256]{1,0:T(8,128)(2,1)S(1)} %shard_map.105), channel_id=1, source_target_pairs={{4,0},{5,1},{6,2},{7,3},{8,4},{9,5},{10,6},{11,7},{12,8},{13,9},{1... | collective-permute-start | bytes 1572872 | tf_op jit(solution)/shard_map/ppermute | solution.py:137
  127.2 1.3 shard_map.97
  128.5 6.0 %collective-permute-start.6 = (bf16[1024,256]{1,0:T(8,128)(2,1)S(1)}, bf16[1024,256]{1,0:T(8,128)(2,1)S(1)}, u32[]{:S(2)}, u32[]{:S(2)}) collective-permute-start(bf16[1024,256]{1,0:T(8,128)(2,1)S(1)} %get-tuple-element.26), channel_id=1, source_target_pairs={{0,4},{1,5},{2,6},{3,7},{4,8},{5,9},{6,10},{7,11},{8,12},{9,13},{1... | collective-permute-start | bytes 1572872 | tf_op jit(solution)/shard_map/ppermute | solution.py:137
  134.6 1.3 shard_map.101
  135.9 6.4 %collective-permute-start.12 = (bf16[1024,256]{1,0:T(8,128)(2,1)S(1)}, bf16[1024,256]{1,0:T(8,128)(2,1)S(1)}, u32[]{:S(2)}, u32[]{:S(2)}) collective-permute-start(bf16[1024,256]{1,0:T(8,128)(2,1)S(1)} %get-tuple-element.32), channel_id=1, source_target_pairs={{0,4},{1,5},{2,6},{3,7},{4,8},{5,9},{6,10},{7,11},{8,12},{9,13},{1... | collective-permute-start | bytes 1572872 | tf_op jit(solution)/shard_map/ppermute | solution.py:137
  142.3 1.3 shard_map.109
  143.6 1.9 %collective-permute-start.25 = (bf16[1024,256]{1,0:T(8,128)(2,1)S(1)}, bf16[1024,256]{1,0:T(8,128)(2,1)S(1)}, u32[]{:S(2)}, u32[]{:S(2)}) collective-permute-start(bf16[1024,256]{1,0:T(8,128)(2,1)S(1)} %shard_map.109), channel_id=1, source_target_pairs={{4,0},{5,1},{6,2},{7,3},{8,4},{9,5},{10,6},{11,7},{12,8},{13,9},{1... | collective-permute-start | bytes 1572872 | tf_op jit(solution)/shard_map/ppermute | solution.py:137
  145.5 3.6 %collective-permute-done.21.refs_9_ = bf16[1024,256]{1,0:T(8,128)(2,1)S(1)} collective-permute-done((bf16[1024,256]{1,0:T(8,128)(2,1)S(1)}, bf16[1024,256]{1,0:T(8,128)(2,1)S(1)}, u32[]{:S(2)}, u32[]{:S(2)}) %collective-permute-start.21) | collective-permute-done | bytes 524320 | tf_op jit(solution)/shard_map/ppermute | solution.py:137
  149.1 1.3 shard_map.106
  150.4 1.9 %collective-permute-start.22 = (bf16[1024,256]{1,0:T(8,128)(2,1)S(1)}, bf16[1024,256]{1,0:T(8,128)(2,1)S(1)}, u32[]{:S(2)}, u32[]{:S(2)}) collective-permute-start(bf16[1024,256]{1,0:T(8,128)(2,1)S(1)} %shard_map.106), channel_id=1, source_target_pairs={{4,0},{5,1},{6,2},{7,3},{8,4},{9,5},{10,6},{11,7},{12,8},{13,9},{1... | collective-permute-start | bytes 1572872 | tf_op jit(solution)/shard_map/ppermute | solution.py:137
  152.3 4.2 %collective-permute-done.12.received = bf16[1024,256]{1,0:T(8,128)(2,1)S(1)} collective-permute-done((bf16[1024,256]{1,0:T(8,128)(2,1)S(1)}, bf16[1024,256]{1,0:T(8,128)(2,1)S(1)}, u32[]{:S(2)}, u32[]{:S(2)}) %collective-permute-start.12) | collective-permute-done | bytes 524320 | tf_op jit(solution)/shard_map/ppermute | solution.py:137
  156.5 2.1 %shard_map.102 = (bf16[1024,512]{1,0:T(8,128)(2,1)}, bf16[1024,256]{1,0:T(8,128)(2,1)S(1)}) custom-call(s32[1,4]{1,0:T(1,128)S(1)} %bitcast.22, bf16[256,1024]{1,0:T(8,128)(2,1)S(1)} %get-tuple-element.22.b0.down.refs_1_, bf16[256,1024]{1,0:T(8,128)(2,1)S(1)} %collective-permute-done.b1.refs_2_, bf16[256,1024]{1,0:T(8,128)(2,1)S(1)} %collective-permute-done.1.b2.refs_3_, ...), custom_call_target="tpu_custom_call" | custom-call | flops 536870912 | bytes 1048576 | tf_op jit(solution)/shard_map/pallas_call | solution.py:117
  158.6 2.1 %shard_map.103 = (bf16[1024,512]{1,0:T(8,128)(2,1)}, bf16[1024,256]{1,0:T(8,128)(2,1)S(1)}) custom-call(s32[1,4]{1,0:T(1,128)S(1)} %bitcast.23, bf16[256,1024]{1,0:T(8,128)(2,1)S(1)} %get-tuple-element.22.b0.down.refs_1_, bf16[256,1024]{1,0:T(8,128)(2,1)S(1)} %collective-permute-done.b1.refs_2_, ...), custom_call_target="tpu_custom_call", output_to_operand_aliasing={{0}: (9, {})} | custom-call | flops 536870912 | bytes 1048576 | tf_op jit(solution)/shard_map/pallas_call | solution.py:117
  160.7 1.7 collective-permute-done.25.refs_9_
  162.4 2.1 %shard_map.110.refs_14_ = bf16[1024,512]{1,0:T(8,128)(2,1)} custom-call(s32[1]{0:T(128)S(6)} %copy.14._.refs_0_, bf16[256,1024]{1,0:T(8,128)(2,1)S(1)} %get-tuple-element.28.up.refs_1_, bf16[256,1024]{1,0:T(8,128)(2,1)S(1)} %collective-permute-done.13.refs_2_, bf16[256,1024]{1,0:T(8,128)(2,1)S(1)} %collective-permute-done.14.refs_3_, ...), custom_call_target="tpu_custom_call" | custom-call | flops 1073741824 | bytes 1048576 | tf_op jit(solution)/shard_map/pallas_call | solution.py:117
  164.5 7.0 %collective-permute-done.22.refs_9_ = bf16[1024,256]{1,0:T(8,128)(2,1)S(1)} collective-permute-done((bf16[1024,256]{1,0:T(8,128)(2,1)S(1)}, bf16[1024,256]{1,0:T(8,128)(2,1)S(1)}, u32[]{:S(2)}, u32[]{:S(2)}) %collective-permute-start.22) | collective-permute-done | bytes 524320 | tf_op jit(solution)/shard_map/ppermute | solution.py:137
  171.6 2.2 %shard_map.111 = bf16[1024,512]{1,0:T(8,128)(2,1)} custom-call(s32[1]{0:T(128)S(6)} %copy.14._.refs_0_, bf16[256,1024]{1,0:T(8,128)(2,1)S(1)} %get-tuple-element.28.up.refs_1_, bf16[256,1024]{1,0:T(8,128)(2,1)S(1)} %collective-permute-done.13.refs_2_, bf16[256,1024]{1,0:T(8,128)(2,1)S(1)} %collective-permute-done.14.refs_3_, ...), custom_call_target="tpu_custom_call", output_to_operand_aliasing={{}: (14, {})} | custom-call | flops 1073741824 | bytes 1048576 | tf_op jit(solution)/shard_map/pallas_call | solution.py:117
  (34 shorter events, 2.3 us)
Async XLA Ops:
  0.6 30.2 %copy-start.4 = (s32[4,1]{0,1:T(1,128)S(1)}, s32[4,1]{0,1:T(1,128)}, u32[]{:S(2)}) copy-start(s32[4,1]{0,1:T(1,128)} %param.14) | copy-start | bytes 52
  0.6 15.8 %collective-permute-start.1 = (bf16[256,1024]{1,0:T(8,128)(2,1)}, bf16[256,1024]{1,0:T(8,128)(2,1)S(1)}, u32[]{:S(2)}, u32[]{:S(2)}) collective-permute-start(bf16[256,1024]{1,0:T(8,128)(2,1)} %bitcast.10), channel_id=1, source_target_pairs={{0,2},{1,3},{2,0},{3,1},{4,6},{5,7},{6,4},{7,5},{8,10},{9,11},{10,... | collective-permute-start | bytes 1572872 | tf_op jit(solution)/shard_map/ppermute | solution.py:137
  4.1 26.7 %collective-permute-start.3 = (bf16[1024,512]{1,0:T(8,128)(2,1)}, bf16[1024,512]{1,0:T(8,128)(2,1)S(1)}, u32[]{:S(2)}, u32[]{:S(2)}) collective-permute-start(bf16[1024,512]{1,0:T(8,128)(2,1)} %bitcast.26), channel_id=1, source_target_pairs={{0,4},{1,5},{2,6},{3,7},{4,8},{5,9},{6,10},{7,11},{8,12},{9,13},{1... | collective-permute-start | bytes 3145736 | tf_op jit(solution)/shard_map/ppermute | solution.py:137
  7.0 14.9 %collective-permute-start = (bf16[256,1024]{1,0:T(8,128)(2,1)}, bf16[256,1024]{1,0:T(8,128)(2,1)S(1)}, u32[]{:S(2)}, u32[]{:S(2)}) collective-permute-start(bf16[256,1024]{1,0:T(8,128)(2,1)} %bitcast.11), channel_id=1, source_target_pairs={{0,1},{1,0},{2,3},{3,2},{4,5},{5,4},{6,7},{7,6},{8,9},{9,8},{10,11... | collective-permute-start | bytes 1572872 | tf_op jit(solution)/shard_map/ppermute | solution.py:137
  16.4 5.5 %collective-permute-start.2 = (bf16[256,1024]{1,0:T(8,128)(2,1)S(1)}, bf16[256,1024]{1,0:T(8,128)(2,1)S(1)}, u32[]{:S(2)}, u32[]{:S(2)}) collective-permute-start(bf16[256,1024]{1,0:T(8,128)(2,1)S(1)} %collective-permute-done.1.b2.refs_3_), channel_id=1, source_target_pairs={{0,1},{1,0},{2,3},{3,2},{4,5},{5,4},{6,7},{7,6},{8,9},{9,8},{10,11... | collective-permute-start | bytes 1572872 | tf_op jit(solution)/shard_map/ppermute | solution.py:137
  17.1 1.6 copy-start
  18.7 1.0 copy-start.1
  19.7 1.0 copy-start.2
  32.1 3.5 %copy-start.3 = (bf16[1,256,1024]{2,1,0:T(8,128)(2,1)S(1)}, bf16[1,256,1024]{2,1,0:T(8,128)(2,1)}, u32[]{:S(2)}) copy-start(bf16[1,256,1024]{2,1,0:T(8,128)(2,1)} %param.12) | copy-start | bytes 1572868
  32.2 7.0 %copy-start.5 = (bf16[1,1024,512]{2,1,0:T(8,128)(2,1)S(1)}, bf16[1,1024,512]{2,1,0:T(8,128)(2,1)}, u32[]{:S(2)}) copy-start(bf16[1,1024,512]{2,1,0:T(8,128)(2,1)} %param.9) | copy-start | bytes 3145732
  32.3 26.7 %collective-permute-start.7 = (bf16[512,1024]{1,0:T(8,128)(2,1)S(1)}, bf16[512,1024]{1,0:T(8,128)(2,1)S(1)}, u32[]{:S(2)}, u32[]{:S(2)}) collective-permute-start(bf16[512,1024]{1,0:T(8,128)(2,1)S(1)} %shard_map.98), channel_id=1, source_target_pairs={{0,240},{1,241},{2,242},{3,243},{252,12},{253,13},{254,14},{255,15}} | collective-permute-start | bytes 3145736 | tf_op jit(solution)/shard_map/ppermute | solution.py:137
  33.2 16.9 %collective-permute-start.14 = (bf16[256,1024]{1,0:T(8,128)(2,1)}, bf16[256,1024]{1,0:T(8,128)(2,1)S(1)}, u32[]{:S(2)}, u32[]{:S(2)}) collective-permute-start(bf16[256,1024]{1,0:T(8,128)(2,1)} %bitcast.2.refs_1_), channel_id=1, source_target_pairs={{4,6},{5,7},{6,4},{7,5},{8,10},{9,11},{10,8},{11,9},{12,14},{13,15... | collective-permute-start | bytes 1572872 | tf_op jit(solution)/shard_map/ppermute | solution.py:137
  35.5 14.5 %collective-permute-start.13 = (bf16[256,1024]{1,0:T(8,128)(2,1)}, bf16[256,1024]{1,0:T(8,128)(2,1)S(1)}, u32[]{:S(2)}, u32[]{:S(2)}) collective-permute-start(bf16[256,1024]{1,0:T(8,128)(2,1)} %bitcast.2.refs_1_), channel_id=1, source_target_pairs={{0,1},{1,0},{2,3},{3,2},{4,5},{5,4},{6,7},{7,6},{8,9},{9,8},{10,11... | collective-permute-start | bytes 1572872 | tf_op jit(solution)/shard_map/ppermute | solution.py:137
  35.6 23.4 %collective-permute-start.17 = (bf16[256,1024]{1,0:T(8,128)(2,1)S(1)}, bf16[256,1024]{1,0:T(8,128)(2,1)S(1)}, u32[]{:S(2)}, u32[]{:S(2)}) collective-permute-start(bf16[256,1024]{1,0:T(8,128)(2,1)S(1)} %bitcast.14), channel_id=1, source_target_pairs={{4,6},{5,7},{6,4},{7,5},{8,10},{9,11},{10,8},{11,9},{12,14},{13,15... | collective-permute-start | bytes 1572872 | tf_op jit(solution)/shard_map/ppermute | solution.py:137
  39.1 51.3 %collective-permute-start.19 = (bf16[1024,512]{1,0:T(8,128)(2,1)S(1)}, bf16[1024,512]{1,0:T(8,128)(2,1)S(1)}, u32[]{:S(2)}, u32[]{:S(2)}) collective-permute-start(bf16[1024,512]{1,0:T(8,128)(2,1)S(1)} %bitcast.27), channel_id=1, source_target_pairs={{4,0},{5,1},{6,2},{7,3},{8,4},{9,5},{10,6},{11,7},{12,8},{13,9},{1... | collective-permute-start | bytes 3145736 | tf_op jit(solution)/shard_map/ppermute | solution.py:137
  50.1 11.0 %collective-permute-start.16 = (bf16[256,1024]{1,0:T(8,128)(2,1)S(1)}, bf16[256,1024]{1,0:T(8,128)(2,1)S(1)}, u32[]{:S(2)}, u32[]{:S(2)}) collective-permute-start(bf16[256,1024]{1,0:T(8,128)(2,1)S(1)} %bitcast.15), channel_id=1, source_target_pairs={{0,1},{1,0},{2,3},{3,2},{4,5},{5,4},{6,7},{7,6},{8,9},{9,8},{10,11... | collective-permute-start | bytes 1572872 | tf_op jit(solution)/shard_map/ppermute | solution.py:137
  50.1 38.4 %collective-permute-start.15 = (bf16[256,1024]{1,0:T(8,128)(2,1)S(1)}, bf16[256,1024]{1,0:T(8,128)(2,1)S(1)}, u32[]{:S(2)}, u32[]{:S(2)}) collective-permute-start(bf16[256,1024]{1,0:T(8,128)(2,1)S(1)} %collective-permute-done.14.refs_3_), channel_id=1, source_target_pairs={{0,1},{1,0},{2,3},{3,2},{4,5},{5,4},{6,7},{7,6},{8,9},{9,8},{10,11... | collective-permute-start | bytes 1572872 | tf_op jit(solution)/shard_map/ppermute | solution.py:137
  59.0 31.4 %collective-permute-start.18 = (bf16[256,1024]{1,0:T(8,128)(2,1)S(1)}, bf16[256,1024]{1,0:T(8,128)(2,1)S(1)}, u32[]{:S(2)}, u32[]{:S(2)}) collective-permute-start(bf16[256,1024]{1,0:T(8,128)(2,1)S(1)} %collective-permute-done.17.refs_7_), channel_id=1, source_target_pairs={{0,1},{1,0},{2,3},{3,2},{4,5},{5,4},{6,7},{7,6},{8,9},{9,8},{10,11... | collective-permute-start | bytes 1572872 | tf_op jit(solution)/shard_map/ppermute | solution.py:137
  59.0 64.0 %collective-permute-start.8 = (bf16[512,1024]{1,0:T(8,128)(2,1)S(1)}, bf16[512,1024]{1,0:T(8,128)(2,1)S(1)}, u32[]{:S(2)}, u32[]{:S(2)}) collective-permute-start(bf16[512,1024]{1,0:T(8,128)(2,1)S(1)} %collective-permute-done.7), channel_id=1, source_target_pairs={{240,2},{241,3},{242,0},{243,1},{12,254},{13,255},{14,252},{15,253}} | collective-permute-start | bytes 3145736 | tf_op jit(solution)/shard_map/ppermute | solution.py:137
  61.1 39.7 %collective-permute-start.4 = (bf16[1024,256]{1,0:T(8,128)(2,1)S(1)}, bf16[1024,256]{1,0:T(8,128)(2,1)S(1)}, u32[]{:S(2)}, u32[]{:S(2)}) collective-permute-start(bf16[1024,256]{1,0:T(8,128)(2,1)S(1)} %get-tuple-element.24), channel_id=1, source_target_pairs={{0,4},{1,5},{2,6},{3,7},{4,8},{5,9},{6,10},{7,11},{8,12},{9,13},{1... | collective-permute-start | bytes 1572872 | tf_op jit(solution)/shard_map/ppermute | solution.py:137
  88.5 23.5 %collective-permute-start.10 = (bf16[1024,256]{1,0:T(8,128)(2,1)S(1)}, bf16[1024,256]{1,0:T(8,128)(2,1)S(1)}, u32[]{:S(2)}, u32[]{:S(2)}) collective-permute-start(bf16[1024,256]{1,0:T(8,128)(2,1)S(1)} %get-tuple-element.30), channel_id=1, source_target_pairs={{0,4},{1,5},{2,6},{3,7},{4,8},{5,9},{6,10},{7,11},{8,12},{9,13},{1... | collective-permute-start | bytes 1572872 | tf_op jit(solution)/shard_map/ppermute | solution.py:137
  91.7 28.1 %collective-permute-start.23 = (bf16[1024,256]{1,0:T(8,128)(2,1)S(1)}, bf16[1024,256]{1,0:T(8,128)(2,1)S(1)}, u32[]{:S(2)}, u32[]{:S(2)}) collective-permute-start(bf16[1024,256]{1,0:T(8,128)(2,1)S(1)} %shard_map.107), channel_id=1, source_target_pairs={{4,0},{5,1},{6,2},{7,3},{8,4},{9,5},{10,6},{11,7},{12,8},{13,9},{1... | collective-permute-start | bytes 1572872 | tf_op jit(solution)/shard_map/ppermute | solution.py:137
  96.9 26.9 %collective-permute-start.20 = (bf16[1024,256]{1,0:T(8,128)(2,1)S(1)}, bf16[1024,256]{1,0:T(8,128)(2,1)S(1)}, u32[]{:S(2)}, u32[]{:S(2)}) collective-permute-start(bf16[1024,256]{1,0:T(8,128)(2,1)S(1)} %shard_map.104), channel_id=1, source_target_pairs={{4,0},{5,1},{6,2},{7,3},{8,4},{9,5},{10,6},{11,7},{12,8},{13,9},{1... | collective-permute-start | bytes 1572872 | tf_op jit(solution)/shard_map/ppermute | solution.py:137
  102.1 25.1 %collective-permute-start.5 = (bf16[1024,256]{1,0:T(8,128)(2,1)S(1)}, bf16[1024,256]{1,0:T(8,128)(2,1)S(1)}, u32[]{:S(2)}, u32[]{:S(2)}) collective-permute-start(bf16[1024,256]{1,0:T(8,128)(2,1)S(1)} %get-tuple-element.25), channel_id=1, source_target_pairs={{0,4},{1,5},{2,6},{3,7},{4,8},{5,9},{6,10},{7,11},{8,12},{9,13},{1... | collective-permute-start | bytes 1572872 | tf_op jit(solution)/shard_map/ppermute | solution.py:137
  113.3 21.2 %collective-permute-start.11 = (bf16[1024,256]{1,0:T(8,128)(2,1)S(1)}, bf16[1024,256]{1,0:T(8,128)(2,1)S(1)}, u32[]{:S(2)}, u32[]{:S(2)}) collective-permute-start(bf16[1024,256]{1,0:T(8,128)(2,1)S(1)} %get-tuple-element.31), channel_id=1, source_target_pairs={{0,4},{1,5},{2,6},{3,7},{4,8},{5,9},{6,10},{7,11},{8,12},{9,13},{1... | collective-permute-start | bytes 1572872 | tf_op jit(solution)/shard_map/ppermute | solution.py:137
  121.1 21.2 %collective-permute-start.24 = (bf16[1024,256]{1,0:T(8,128)(2,1)S(1)}, bf16[1024,256]{1,0:T(8,128)(2,1)S(1)}, u32[]{:S(2)}, u32[]{:S(2)}) collective-permute-start(bf16[1024,256]{1,0:T(8,128)(2,1)S(1)} %shard_map.108), channel_id=1, source_target_pairs={{4,0},{5,1},{6,2},{7,3},{8,4},{9,5},{10,6},{11,7},{12,8},{13,9},{1... | collective-permute-start | bytes 1572872 | tf_op jit(solution)/shard_map/ppermute | solution.py:137
  123.1 33.5 %collective-permute-start.9 = (bf16[512,1024]{1,0:T(8,128)(2,1)S(1)}, bf16[512,1024]{1,0:T(8,128)(2,1)S(1)}, u32[]{:S(2)}, u32[]{:S(2)}) collective-permute-start(bf16[512,1024]{1,0:T(8,128)(2,1)S(1)} %collective-permute-done.8.rest_0_.refs_7_.refs_12_), channel_id=1, source_target_pairs={{0,1},{1,0},{2,3},{3,2},{252,253},{253,252},{254,255},{255,254}} | collective-permute-start | bytes 3145736 | tf_op jit(solution)/shard_map/ppermute | solution.py:137
  125.1 24.1 %collective-permute-start.21 = (bf16[1024,256]{1,0:T(8,128)(2,1)S(1)}, bf16[1024,256]{1,0:T(8,128)(2,1)S(1)}, u32[]{:S(2)}, u32[]{:S(2)}) collective-permute-start(bf16[1024,256]{1,0:T(8,128)(2,1)S(1)} %shard_map.105), channel_id=1, source_target_pairs={{4,0},{5,1},{6,2},{7,3},{8,4},{9,5},{10,6},{11,7},{12,8},{13,9},{1... | collective-permute-start | bytes 1572872 | tf_op jit(solution)/shard_map/ppermute | solution.py:137
  128.5 30.1 %collective-permute-start.6 = (bf16[1024,256]{1,0:T(8,128)(2,1)S(1)}, bf16[1024,256]{1,0:T(8,128)(2,1)S(1)}, u32[]{:S(2)}, u32[]{:S(2)}) collective-permute-start(bf16[1024,256]{1,0:T(8,128)(2,1)S(1)} %get-tuple-element.26), channel_id=1, source_target_pairs={{0,4},{1,5},{2,6},{3,7},{4,8},{5,9},{6,10},{7,11},{8,12},{9,13},{1... | collective-permute-start | bytes 1572872 | tf_op jit(solution)/shard_map/ppermute | solution.py:137
  135.9 20.7 %collective-permute-start.12 = (bf16[1024,256]{1,0:T(8,128)(2,1)S(1)}, bf16[1024,256]{1,0:T(8,128)(2,1)S(1)}, u32[]{:S(2)}, u32[]{:S(2)}) collective-permute-start(bf16[1024,256]{1,0:T(8,128)(2,1)S(1)} %get-tuple-element.32), channel_id=1, source_target_pairs={{0,4},{1,5},{2,6},{3,7},{4,8},{5,9},{6,10},{7,11},{8,12},{9,13},{1... | collective-permute-start | bytes 1572872 | tf_op jit(solution)/shard_map/ppermute | solution.py:137
  143.6 18.8 %collective-permute-start.25 = (bf16[1024,256]{1,0:T(8,128)(2,1)S(1)}, bf16[1024,256]{1,0:T(8,128)(2,1)S(1)}, u32[]{:S(2)}, u32[]{:S(2)}) collective-permute-start(bf16[1024,256]{1,0:T(8,128)(2,1)S(1)} %shard_map.109), channel_id=1, source_target_pairs={{4,0},{5,1},{6,2},{7,3},{8,4},{9,5},{10,6},{11,7},{12,8},{13,9},{1... | collective-permute-start | bytes 1572872 | tf_op jit(solution)/shard_map/ppermute | solution.py:137
  150.4 21.2 %collective-permute-start.22 = (bf16[1024,256]{1,0:T(8,128)(2,1)S(1)}, bf16[1024,256]{1,0:T(8,128)(2,1)S(1)}, u32[]{:S(2)}, u32[]{:S(2)}) collective-permute-start(bf16[1024,256]{1,0:T(8,128)(2,1)S(1)} %shard_map.106), channel_id=1, source_target_pairs={{4,0},{5,1},{6,2},{7,3},{8,4},{9,5},{10,6},{11,7},{12,8},{13,9},{1... | collective-permute-start | bytes 1572872 | tf_op jit(solution)/shard_map/ppermute | solution.py:137

commit v2 on v1

--- a/solution.py
+++ b/solution.py
@@ -50,28 +50,45 @@
     )(*arrays)
 
 
-def late_kernel(_, after, down, up, reflect, pair):
-    high = down.shape[0]
+def late_kernel(_, after, down, up, reflect, first, second):
     top = lax.axis_index("layer") == 0
-    pair[:high, :] = jnp.where(top, up[...], down[...])
-    pair[high:, :] = jnp.where(top, reflect[...], up[...])
+    first[...] = jnp.where(top, up[...], down[...])
+    second[...] = jnp.where(top, reflect[...], up[...])
+
+
+def near_kernel(plan, own, near, received, sources, new, down_in):
+    core = lax.axis_index("shot") % 2
+    down_in[...] = injected(received[...], sources[plan[0, 0]])
+    for k, block in enumerate((own, near)):
+        new[band(core ^ k, block.shape[0]), :] = dot(block[...], down_in[...]).astype(BF16)
+
+
+def far_kernel(_, far, cross, down_in, *new):
+    core = lax.axis_index("shot") % 2
+    for k, block in enumerate((far, cross)):
+        rows = band(core ^ k, block.shape[0])
+        for chunk, ref in enumerate(new):
+            cols = columns(down_in, chunk, ref.shape[1])
+            ref[rows, :] = dot(block[...], down_in[:, cols]).astype(BF16)
 
 
 def columns(ref, chunk, width):
     return slice(chunk * width, (chunk + 1) * width) if ref.shape[-1] > width else slice(None)
 
 
-def down_kernel(moment, chunk, last, plan, b0, b1, b2, b3, received, sources, *rest):
-    late, (new, down_in) = rest[:-2], rest[-2:]
+def down_kernel(moment, chunk, n, last, plan, b0, b1, b2, b3, *rest):
+    received, sources, late, (new, down_in) = rest[:n], rest[n], rest[n + 1 : -2], rest[-2:]
     end = lax.axis_index("layer") == lax.axis_size("layer") - 1
     spot = lax.axis_index("shot")
     width = down_in.shape[1]
-    source = sources[plan[0, moment], :, columns(sources, chunk, width)]
-    down_in[...] = injected(received[:, columns(received, chunk, width)], source)
+    cols, picked = columns(sources, chunk, width), plan[0, moment]
+    for k, ref in enumerate(received):
+        rows = band((spot // 2) ^ k, ref.shape[0]) if n > 1 else slice(None)
+        down_in[rows, :] = injected(ref[:, columns(ref, chunk, width)], sources[picked, rows, cols])
     for k, block in enumerate((b0, b1, b2, b3)):
         high, value = block.shape[0], block[...]
         if last and k >= 2:
-            value = jnp.where(end, late[k - 2][:high, :], value)
+            value = jnp.where(end, late[k - 2][...], value)
         new[band(spot ^ k, high), :] = dot(value, down_in[...]).astype(BF16)
 
 
@@ -82,17 +99,18 @@
     top = lax.axis_index("layer") == 0
     end = lax.axis_index("layer") == lax.axis_size("layer") - 1
     spot = lax.axis_index("shot")
-    width = down_in.shape[1]
+    width = new.shape[1]
     gathered = received[:, columns(received, chunk, width)]
+    injection = down_in[:, columns(down_in, chunk, width)]
     for k in range(4):
         up, reflect = blocks[k][...], blocks[4 + k][...]
         high = up.shape[0]
         if last and k >= 2:
-            first, second = late[k - 2][:high, :], late[k - 2][high:, :]
+            first, second = late[k - 2][...], late[k][...]
             up = jnp.where(top, first, jnp.where(end, second, up))
             reflect = jnp.where(top, second, reflect)
         rows = band(spot ^ k, high)
-        total = dot(up, gathered) + dot(reflect, down_in[...])
+        total = dot(up, gathered) + dot(reflect, injection)
         total = total + sources[pick[0], rows, columns(sources, chunk, width)].astype(F32)
         new[rows, :] = total.astype(BF16)
 
@@ -149,9 +167,9 @@
 
     every = range(layers)
 
-    def shift(value, steps):
+    def shift(value, steps, lowest=0):
         return sent(value, [
-            (at(l, s), at(l + steps, s)) for l in every for s in range(shots) if 0 <= l + steps < layers
+            (at(l, s), at(l + steps, s)) for l in every for s in range(shots) if lowest <= l + steps < layers
         ])
 
     def swap(value, bit, members):
@@ -160,7 +178,7 @@
     middle = [l for l in every if 0 < l < layers - 1]
     down_0 = shift(down_state[0], 1)
     far_d = swap(down_op, 2, [0] + middle)
-    up_0 = shift(up_state[0], -1)
+    up_0 = shift(up_state[0], -1, 1)
     near_d = swap(down_op, 1, every)
     far_u = swap(up_op, 2, middle)
     far_r = swap(reflect_op, 2, middle + [layers - 1])
@@ -174,41 +192,48 @@
     down_op, up_op, reflect_op, sources = staged(down_op, up_op, reflect_op, source_bank[0])
     d_blocks = [down_op, near_d, far_d, cross_d]
     u_blocks = [up_op, near_u, far_u, cross_u, reflect_op, near_r, far_r, cross_r]
-    downs, ups = [down_0] * CHUNKS, [up_0] * CHUNKS
-    late = ()
+    ends = ((0, layers - 4), (layers - 1, 3))
+    out = [(at(a, s), at(b, s)) for a, b in ends for s in range(shots)]
+    back = [(at(b, s), at(a, s ^ 2)) for a, b in ends for s in range(shots)]
+    half = height // 2
+    near, down_in = call(near_kernel, plan, [down_op, near_d, down_0, sources], [(half, wide), (height, wide)], one)
+    far = call(far_kernel, layer_source, [far_d, cross_d, down_in], [(half, width)] * CHUNKS, one)
+    near = shift(near, 1)
+    downs = [[near, shift(a, 1)] for a in far]
+    pair = call(
+        late_kernel, layer_source, [far[-1], down_op, up_op, reflect_op],
+        [down_op.shape] * 2, one // 8,
+    )
+    late = []
+    for a in pair:
+        a = sent(sent(a, out), back)
+        late += [a, swap(a, 1, (0, layers - 1))]
+    ups = [up_0] * CHUNKS
     for moment in range(TICKS):
         last = moment == TICKS - 1
-        if moment == 1:
-            (pair,) = call(
-                late_kernel, layer_source, [down_in_0, down_op, up_op, reflect_op],
-                [(height // 2, height)], one // 8,
-            )
-            ends = ((0, layers - 4), (layers - 1, 3))
-            pair = sent(pair, [(at(a, s), at(b, s)) for a, b in ends for s in range(shots)])
-            pair = sent(pair, [(at(b, s), at(a, s ^ 2)) for a, b in ends for s in range(shots)])
-            late = (pair, swap(pair, 1, (0, layers - 1)))
         new_downs, new_ups, new, up = [], [], None, None
         for chunk in range(CHUNKS):
             full = (chunk, wide) if last else None
-            more = late if last else ()
-            new, down_in = call(
-                functools.partial(down_kernel, moment, chunk, last), plan,
-                [*d_blocks, downs[chunk], sources], [(height, width)] * 2, one,
-                full=full, into=new if last else None, more=more,
-            )
+            if moment:
+                new, down_in = call(
+                    functools.partial(down_kernel, moment, chunk, len(downs[chunk]), last),
+                    plan, [*d_blocks, *downs[chunk], sources],
+                    [(height, width)] * 2, one,
+                    full=full, into=new if last else None, more=late[:2] if last else (),
+                )
+                new_downs.append(new)
             (up,) = call(
                 functools.partial(up_kernel, chunk, last), layer_source,
                 [*u_blocks, ups[chunk], down_in, sources], [(height, width)], 2 * one,
-                full=full, into=up if last else None, more=more,
+                full=full, into=up if last else None, more=late if last else (),
             )
-            if moment == 0 and chunk == CHUNKS - 1:
-                down_in_0 = down_in
-            new_downs.append(new)
             new_ups.append(up)
         if last:
             return (new[None], up[None])
-        downs = [shift(a, 1) for a in new_downs]
-        ups = [shift(a, -1) for a in new_ups]
+        if moment:
+            downs = [[shift(a, 1)] for a in new_downs]
+        lowest = 0 if moment == TICKS - 2 else 1
+        ups = [shift(a, -1, lowest) for a in new_ups]
 
 
 def solution(mesh):

time: 175 us -> 150 us (0.86)
  the two profiles are of different devices: /device:TPU:198 before, /device:TPU:24 now
where the time goes in v2:
time: 150 us; the launch traced here: 149 us
  starting transfers between devices  87.5 us (58%)
  waiting for transfers between devices  30.7 us (20%)
  Pallas kernels  24.2 us (16%)
  local copies, waits for them, and re-layouts  4.72 us (3%)
  between operations  1.77 us (1%)
    ppermute x30, starting transfers between devices, sent(): return lax.ppermute(value, ('layer', 'shot'), pairs)  87.5 us
    ppermute x30, waiting for transfers between devices, sent(): return lax.ppermute(value, ('layer', 'shot'), pairs)  30.7 us
    pallas_call x17, Pallas kernels, call(): pl.pallas_call(kernel, grid=(1,), in_specs=in_specs, out_specs=out_specs,...  23.9 us
    unnamed x10, local copies, waits for them, and re-layouts  4.72 us
  transfers between devices with their start and end apart: 30, of which 9 were waited for; matrix products, arithmetic and copies ran while one was open for 0% of the time, Pallas kernels for 15%

profile of v2, /device:TPU:24, one launch (start us, length us, event | category | flops | bytes accessed | tf_op | source)
XLA Modules:
  0.0 148.9 jit_solution(2119591917113016266)
XLA Ops:
  0.6 2.7 %collective-permute-start.1 = (bf16[256,1024]{1,0:T(8,128)(2,1)}, bf16[256,1024]{1,0:T(8,128)(2,1)S(1)}, u32[]{:S(2)}, u32[]{:S(2)}) collective-permute-start(bf16[256,1024]{1,0:T(8,128)(2,1)} %bitcast.10), channel_id=1, source_target_pairs={{0,2},{1,3},{2,0},{3,1},{4,6},{5,7},{6,4},{7,5},{8,10},{9,11},{10,... | collective-permute-start | bytes 1572872 | tf_op jit(solution)/shard_map/ppermute | solution.py:155
  3.4 3.4 %collective-permute-start.3 = (bf16[1024,512]{1,0:T(8,128)(2,1)}, bf16[1024,512]{1,0:T(8,128)(2,1)S(1)}, u32[]{:S(2)}, u32[]{:S(2)}) collective-permute-start(bf16[1024,512]{1,0:T(8,128)(2,1)} %bitcast.28), channel_id=1, source_target_pairs={{0,4},{1,5},{2,6},{3,7},{4,8},{5,9},{6,10},{7,11},{8,12},{9,13},{1... | collective-permute-start | bytes 3145736 | tf_op jit(solution)/shard_map/ppermute | solution.py:155
  6.8 3.2 %collective-permute-start.15 = (bf16[256,1024]{1,0:T(8,128)(2,1)}, bf16[256,1024]{1,0:T(8,128)(2,1)S(1)}, u32[]{:S(2)}, u32[]{:S(2)}) collective-permute-start(bf16[256,1024]{1,0:T(8,128)(2,1)} %bitcast.13), channel_id=1, source_target_pairs={{4,6},{5,7},{6,4},{7,5},{8,10},{9,11},{10,8},{11,9},{12,14},{13,15... | collective-permute-start | bytes 1572872 | tf_op jit(solution)/shard_map/ppermute | solution.py:155
  10.1 7.4 %collective-permute-done.1.far.b2.refs_3_ = bf16[256,1024]{1,0:T(8,128)(2,1)S(1)} collective-permute-done((bf16[256,1024]{1,0:T(8,128)(2,1)}, bf16[256,1024]{1,0:T(8,128)(2,1)S(1)}, u32[]{:S(2)}, u32[]{:S(2)}) %collective-permute-start.1) | collective-permute-done | bytes 524320 | tf_op jit(solution)/shard_map/ppermute | solution.py:155
  17.5 2.6 %collective-permute-start.18 = (bf16[256,1024]{1,0:T(8,128)(2,1)}, bf16[256,1024]{1,0:T(8,128)(2,1)S(1)}, u32[]{:S(2)}, u32[]{:S(2)}) collective-permute-start(bf16[256,1024]{1,0:T(8,128)(2,1)} %bitcast.16), channel_id=1, source_target_pairs={{4,6},{5,7},{6,4},{7,5},{8,10},{9,11},{10,8},{11,9},{12,14},{13,15... | collective-permute-start | bytes 1572872 | tf_op jit(solution)/shard_map/ppermute | solution.py:155
  20.2 10.3 %collective-permute-start.20 = (bf16[1024,512]{1,0:T(8,128)(2,1)}, bf16[1024,512]{1,0:T(8,128)(2,1)S(1)}, u32[]{:S(2)}, u32[]{:S(2)}) collective-permute-start(bf16[1024,512]{1,0:T(8,128)(2,1)} %bitcast.29), channel_id=1, source_target_pairs={{8,4},{9,5},{10,6},{11,7},{12,8},{13,9},{14,10},{15,11},{16,12},{1... | collective-permute-start | bytes 3145736 | tf_op jit(solution)/shard_map/ppermute | solution.py:155
  31.2 7.7 %collective-permute-done.18.refs_7_ = bf16[256,1024]{1,0:T(8,128)(2,1)S(1)} collective-permute-done((bf16[256,1024]{1,0:T(8,128)(2,1)}, bf16[256,1024]{1,0:T(8,128)(2,1)S(1)}, u32[]{:S(2)}, u32[]{:S(2)}) %collective-permute-start.18) | collective-permute-done | bytes 524320 | tf_op jit(solution)/shard_map/ppermute | solution.py:155
  39.4 1.6 %copy-done = bf16[1,2,1024,512]{3,2,1,0:T(8,128)(2,1)S(1)} copy-done((bf16[1,2,1024,512]{3,2,1,0:T(8,128)(2,1)S(1)}, bf16[1,2,1024,512]{3,2,1,0:T(8,128)(2,1)}, u32[]{:S(2)}) %copy-start) | copy-done | bytes 2097176
  41.0 1.0 copy-done.1
  42.0 1.0 copy-done.2
  43.1 1.0 copy-done.3
  44.4 1.3 shard_map.95
  45.8 3.4 %collective-permute-start.4 = (bf16[512,512]{1,0:T(8,128)(2,1)S(1)}, bf16[512,512]{1,0:T(8,128)(2,1)S(1)}, u32[]{:S(2)}, u32[]{:S(2)}) collective-permute-start(bf16[512,512]{1,0:T(8,128)(2,1)S(1)} %get-tuple-element.26), channel_id=1, source_target_pairs={{0,4},{1,5},{2,6},{3,7},{4,8},{5,9},{6,10},{7,11},{8,12},{9,13},{1... | collective-permute-start | bytes 1572872 | tf_op jit(solution)/shard_map/ppermute | solution.py:155
  49.8 1.1 collective-permute-done.20.refs_9_
  51.0 1.3 shard_map.107
  52.3 10.0 %collective-permute-start.27 = (bf16[1024,256]{1,0:T(8,128)(2,1)S(1)}, bf16[1024,256]{1,0:T(8,128)(2,1)S(1)}, u32[]{:S(2)}, u32[]{:S(2)}) collective-permute-start(bf16[1024,256]{1,0:T(8,128)(2,1)S(1)} %shard_map.107), channel_id=1, source_target_pairs={{8,4},{9,5},{10,6},{11,7},{12,8},{13,9},{14,10},{15,11},{16,12},{1... | collective-permute-start | bytes 1572872 | tf_op jit(solution)/shard_map/ppermute | solution.py:155
  62.3 0.7 shard_map.96
  63.0 1.9 %collective-permute-start.11 = (bf16[512,256]{1,0:T(8,128)(2,1)S(1)}, bf16[512,256]{1,0:T(8,128)(2,1)S(1)}, u32[]{:S(2)}, u32[]{:S(2)}) collective-permute-start(bf16[512,256]{1,0:T(8,128)(2,1)S(1)} %get-tuple-element.34), channel_id=1, source_target_pairs={{0,4},{1,5},{2,6},{3,7},{4,8},{5,9},{6,10},{7,11},{8,12},{9,13},{1... | collective-permute-start | bytes 786440 | tf_op jit(solution)/shard_map/ppermute | solution.py:155
  65.0 1.9 %collective-permute-start.5 = (bf16[512,256]{1,0:T(8,128)(2,1)S(1)}, bf16[512,256]{1,0:T(8,128)(2,1)S(1)}, u32[]{:S(2)}, u32[]{:S(2)}) collective-permute-start(bf16[512,256]{1,0:T(8,128)(2,1)S(1)} %get-tuple-element.28.after), channel_id=1, source_target_pairs={{0,4},{1,5},{2,6},{3,7},{4,8},{5,9},{6,10},{7,11},{8,12},{9,13},{1... | collective-permute-start | bytes 786440 | tf_op jit(solution)/shard_map/ppermute | solution.py:155
  67.0 1.3 shard_map.104
  68.3 9.6 %collective-permute-start.21 = (bf16[1024,256]{1,0:T(8,128)(2,1)S(1)}, bf16[1024,256]{1,0:T(8,128)(2,1)S(1)}, u32[]{:S(2)}, u32[]{:S(2)}) collective-permute-start(bf16[1024,256]{1,0:T(8,128)(2,1)S(1)} %shard_map.104), channel_id=1, source_target_pairs={{8,4},{9,5},{10,6},{11,7},{12,8},{13,9},{14,10},{15,11},{16,12},{1... | collective-permute-start | bytes 1572872 | tf_op jit(solution)/shard_map/ppermute | solution.py:155
  78.0 1.4 collective-permute-done.11.rest_1_
  80.1 0.7 collective-permute-start.24
  80.8 1.5 %shard_map.100 = (bf16[1024,256]{1,0:T(8,128)(2,1)S(1)}, bf16[1024,256]{1,0:T(8,128)(2,1)S(1)}) custom-call(s32[1,4]{1,0:T(1,128)S(1)} %bitcast.20, bf16[256,1024]{1,0:T(8,128)(2,1)S(1)} %get-tuple-element.24.own.b0.down.refs_1_, bf16[256,1024]{1,0:T(8,128)(2,1)S(1)} %collective-permute-done.near.b1.refs_2_, ...), custom_call_target="tpu_custom_call" | custom-call | flops 536870912 | bytes 1048576 | tf_op jit(solution)/shard_map/pallas_call | solution.py:135
  82.4 1.9 %collective-permute-start.12 = (bf16[1024,256]{1,0:T(8,128)(2,1)S(1)}, bf16[1024,256]{1,0:T(8,128)(2,1)S(1)}, u32[]{:S(2)}, u32[]{:S(2)}) collective-permute-start(bf16[1024,256]{1,0:T(8,128)(2,1)S(1)} %get-tuple-element.35), channel_id=1, source_target_pairs={{0,4},{1,5},{2,6},{3,7},{4,8},{5,9},{6,10},{7,11},{8,12},{9,13},{1... | collective-permute-start | bytes 1572872 | tf_op jit(solution)/shard_map/ppermute | solution.py:155
  84.3 1.5 %shard_map.97 = (bf16[1024,256]{1,0:T(8,128)(2,1)S(1)}, bf16[1024,256]{1,0:T(8,128)(2,1)S(1)}) custom-call(s32[1,4]{1,0:T(1,128)S(1)} %bitcast.21, bf16[256,1024]{1,0:T(8,128)(2,1)S(1)} %get-tuple-element.24.own.b0.down.refs_1_, bf16[256,1024]{1,0:T(8,128)(2,1)S(1)} %collective-permute-done.near.b1.refs_2_, ...), custom_call_target="tpu_custom_call" | custom-call | flops 536870912 | bytes 1048576 | tf_op jit(solution)/shard_map/pallas_call | solution.py:135
  85.8 1.9 %collective-permute-start.6 = (bf16[1024,256]{1,0:T(8,128)(2,1)S(1)}, bf16[1024,256]{1,0:T(8,128)(2,1)S(1)}, u32[]{:S(2)}, u32[]{:S(2)}) collective-permute-start(bf16[1024,256]{1,0:T(8,128)(2,1)S(1)} %get-tuple-element.29), channel_id=1, source_target_pairs={{0,4},{1,5},{2,6},{3,7},{4,8},{5,9},{6,10},{7,11},{8,12},{9,13},{1... | collective-permute-start | bytes 1572872 | tf_op jit(solution)/shard_map/ppermute | solution.py:155
  87.7 1.3 shard_map.108
  89.0 9.6 %collective-permute-start.28 = (bf16[1024,256]{1,0:T(8,128)(2,1)S(1)}, bf16[1024,256]{1,0:T(8,128)(2,1)S(1)}, u32[]{:S(2)}, u32[]{:S(2)}) collective-permute-start(bf16[1024,256]{1,0:T(8,128)(2,1)S(1)} %shard_map.108), channel_id=1, source_target_pairs={{8,4},{9,5},{10,6},{11,7},{12,8},{13,9},{14,10},{15,11},{16,12},{1... | collective-permute-start | bytes 1572872 | tf_op jit(solution)/shard_map/ppermute | solution.py:155
  99.4 1.3 shard_map.105
  100.7 3.9 %collective-permute-start.22 = (bf16[1024,256]{1,0:T(8,128)(2,1)S(1)}, bf16[1024,256]{1,0:T(8,128)(2,1)S(1)}, u32[]{:S(2)}, u32[]{:S(2)}) collective-permute-start(bf16[1024,256]{1,0:T(8,128)(2,1)S(1)} %shard_map.105), channel_id=1, source_target_pairs={{8,4},{9,5},{10,6},{11,7},{12,8},{13,9},{14,10},{15,11},{16,12},{1... | collective-permute-start | bytes 1572872 | tf_op jit(solution)/shard_map/ppermute | solution.py:155
  104.8 0.9 collective-permute-start.25
  105.6 1.3 shard_map.101
  106.9 4.8 %collective-permute-done.6.rest_0_ = bf16[1024,256]{1,0:T(8,128)(2,1)S(1)} collective-permute-done((bf16[1024,256]{1,0:T(8,128)(2,1)S(1)}, bf16[1024,256]{1,0:T(8,128)(2,1)S(1)}, u32[]{:S(2)}, u32[]{:S(2)}) %collective-permute-start.6) | collective-permute-done | bytes 524320 | tf_op jit(solution)/shard_map/ppermute | solution.py:155
  111.8 1.9 %collective-permute-start.13 = (bf16[1024,256]{1,0:T(8,128)(2,1)S(1)}, bf16[1024,256]{1,0:T(8,128)(2,1)S(1)}, u32[]{:S(2)}, u32[]{:S(2)}) collective-permute-start(bf16[1024,256]{1,0:T(8,128)(2,1)S(1)} %get-tuple-element.36), channel_id=1, source_target_pairs={{0,4},{1,5},{2,6},{3,7},{4,8},{5,9},{6,10},{7,11},{8,12},{9,13},{1... | collective-permute-start | bytes 1572872 | tf_op jit(solution)/shard_map/ppermute | solution.py:155
  113.7 1.3 shard_map.98
  115.0 1.9 %collective-permute-start.7 = (bf16[1024,256]{1,0:T(8,128)(2,1)S(1)}, bf16[1024,256]{1,0:T(8,128)(2,1)S(1)}, u32[]{:S(2)}, u32[]{:S(2)}) collective-permute-start(bf16[1024,256]{1,0:T(8,128)(2,1)S(1)} %get-tuple-element.30), channel_id=1, source_target_pairs={{0,4},{1,5},{2,6},{3,7},{4,8},{5,9},{6,10},{7,11},{8,12},{9,13},{1... | collective-permute-start | bytes 1572872 | tf_op jit(solution)/shard_map/ppermute | solution.py:155
  117.6 1.3 shard_map.109
  118.9 9.6 %collective-permute-start.29 = (bf16[1024,256]{1,0:T(8,128)(2,1)S(1)}, bf16[1024,256]{1,0:T(8,128)(2,1)S(1)}, u32[]{:S(2)}, u32[]{:S(2)}) collective-permute-start(bf16[1024,256]{1,0:T(8,128)(2,1)S(1)} %shard_map.109), channel_id=1, source_target_pairs={{4,0},{5,1},{6,2},{7,3},{8,4},{9,5},{10,6},{11,7},{12,8},{13,9},{1... | collective-permute-start | bytes 1572872 | tf_op jit(solution)/shard_map/ppermute | solution.py:155
  129.3 1.3 shard_map.106
  130.5 3.6 %collective-permute-done.13.rest_0_ = bf16[1024,256]{1,0:T(8,128)(2,1)S(1)} collective-permute-done((bf16[1024,256]{1,0:T(8,128)(2,1)S(1)}, bf16[1024,256]{1,0:T(8,128)(2,1)S(1)}, u32[]{:S(2)}, u32[]{:S(2)}) %collective-permute-start.13) | collective-permute-done | bytes 524320 | tf_op jit(solution)/shard_map/ppermute | solution.py:155
  134.2 1.9 %collective-permute-start.23 = (bf16[1024,256]{1,0:T(8,128)(2,1)S(1)}, bf16[1024,256]{1,0:T(8,128)(2,1)S(1)}, u32[]{:S(2)}, u32[]{:S(2)}) collective-permute-start(bf16[1024,256]{1,0:T(8,128)(2,1)S(1)} %shard_map.106), channel_id=1, source_target_pairs={{4,0},{5,1},{6,2},{7,3},{8,4},{9,5},{10,6},{11,7},{12,8},{13,9},{1... | collective-permute-start | bytes 1572872 | tf_op jit(solution)/shard_map/ppermute | solution.py:155
  136.1 2.1 %shard_map.102 = (bf16[1024,512]{1,0:T(8,128)(2,1)}, bf16[1024,256]{1,0:T(8,128)(2,1)S(1)}) custom-call(s32[1,4]{1,0:T(1,128)S(1)} %bitcast.24, bf16[256,1024]{1,0:T(8,128)(2,1)S(1)} %get-tuple-element.24.own.b0.down.refs_1_, bf16[256,1024]{1,0:T(8,128)(2,1)S(1)} %collective-permute-done.near.b1.refs_2_, ...), custom_call_target="tpu_custom_call" | custom-call | flops 536870912 | bytes 1048576 | tf_op jit(solution)/shard_map/pallas_call | solution.py:135
  138.2 2.1 %collective-permute-done.7.refs_5_ = bf16[1024,256]{1,0:T(8,128)(2,1)S(1)} collective-permute-done((bf16[1024,256]{1,0:T(8,128)(2,1)S(1)}, bf16[1024,256]{1,0:T(8,128)(2,1)S(1)}, u32[]{:S(2)}, u32[]{:S(2)}) %collective-permute-start.7) | collective-permute-done | bytes 524320 | tf_op jit(solution)/shard_map/ppermute | solution.py:155
  140.3 2.1 %shard_map.103 = (bf16[1024,512]{1,0:T(8,128)(2,1)}, bf16[1024,256]{1,0:T(8,128)(2,1)S(1)}) custom-call(s32[1,4]{1,0:T(1,128)S(1)} %bitcast.25, bf16[256,1024]{1,0:T(8,128)(2,1)S(1)} %get-tuple-element.24.own.b0.down.refs_1_, bf16[256,1024]{1,0:T(8,128)(2,1)S(1)} %collective-permute-done.near.b1.refs_2_, ...), custom_call_target="tpu_custom_call", output_to_operand_aliasing={{0}: (9, {})} | custom-call | flops 536870912 | bytes 1048576 | tf_op jit(solution)/shard_map/pallas_call | solution.py:135
  142.4 2.2 %shard_map.110.refs_16_ = bf16[1024,512]{1,0:T(8,128)(2,1)} custom-call(s32[1]{0:T(128)S(6)} %copy.14._.refs_0_, bf16[256,1024]{1,0:T(8,128)(2,1)S(1)} %get-tuple-element.31.up.refs_1_, bf16[256,1024]{1,0:T(8,128)(2,1)S(1)} %collective-permute-done.14.refs_2_, bf16[256,1024]{1,0:T(8,128)(2,1)S(1)} %collective-permute-done.15.refs_3_, ...), custom_call_target="tpu_custom_call" | custom-call | flops 1073741824 | bytes 1048576 | tf_op jit(solution)/shard_map/pallas_call | solution.py:135
  144.6 2.1 %collective-permute-done.23.refs_9_ = bf16[1024,256]{1,0:T(8,128)(2,1)S(1)} collective-permute-done((bf16[1024,256]{1,0:T(8,128)(2,1)S(1)}, bf16[1024,256]{1,0:T(8,128)(2,1)S(1)}, u32[]{:S(2)}, u32[]{:S(2)}) %collective-permute-start.23) | collective-permute-done | bytes 524320 | tf_op jit(solution)/shard_map/ppermute | solution.py:155
  146.7 2.2 %shard_map.111 = bf16[1024,512]{1,0:T(8,128)(2,1)} custom-call(s32[1]{0:T(128)S(6)} %copy.14._.refs_0_, bf16[256,1024]{1,0:T(8,128)(2,1)S(1)} %get-tuple-element.31.up.refs_1_, bf16[256,1024]{1,0:T(8,128)(2,1)S(1)} %collective-permute-done.14.refs_2_, bf16[256,1024]{1,0:T(8,128)(2,1)S(1)} %collective-permute-done.15.refs_3_, ...), custom_call_target="tpu_custom_call", output_to_operand_aliasing={{}: (16, {})} | custom-call | flops 1073741824 | bytes 1048576 | tf_op jit(solution)/shard_map/pallas_call | solution.py:135
  (40 shorter events, 4.7 us)
Async XLA Ops:
  0.6 43.8 %copy-start.4 = (s32[4,1]{0,1:T(1,128)S(1)}, s32[4,1]{0,1:T(1,128)}, u32[]{:S(2)}) copy-start(s32[4,1]{0,1:T(1,128)} %param.14) | copy-start | bytes 52
  0.6 16.9 %collective-permute-start.1 = (bf16[256,1024]{1,0:T(8,128)(2,1)}, bf16[256,1024]{1,0:T(8,128)(2,1)S(1)}, u32[]{:S(2)}, u32[]{:S(2)}) collective-permute-start(bf16[256,1024]{1,0:T(8,128)(2,1)} %bitcast.10), channel_id=1, source_target_pairs={{0,2},{1,3},{2,0},{3,1},{4,6},{5,7},{6,4},{7,5},{8,10},{9,11},{10,... | collective-permute-start | bytes 1572872 | tf_op jit(solution)/shard_map/ppermute | solution.py:155
  3.3 16.9 %collective-permute-start = (bf16[256,1024]{1,0:T(8,128)(2,1)}, bf16[256,1024]{1,0:T(8,128)(2,1)S(1)}, u32[]{:S(2)}, u32[]{:S(2)}) collective-permute-start(bf16[256,1024]{1,0:T(8,128)(2,1)} %bitcast.11), channel_id=1, source_target_pairs={{0,1},{1,0},{2,3},{3,2},{4,5},{5,4},{6,7},{7,6},{8,9},{9,8},{10,11... | collective-permute-start | bytes 1572872 | tf_op jit(solution)/shard_map/ppermute | solution.py:155
  3.4 35.5 %collective-permute-start.3 = (bf16[1024,512]{1,0:T(8,128)(2,1)}, bf16[1024,512]{1,0:T(8,128)(2,1)S(1)}, u32[]{:S(2)}, u32[]{:S(2)}) collective-permute-start(bf16[1024,512]{1,0:T(8,128)(2,1)} %bitcast.28), channel_id=1, source_target_pairs={{0,4},{1,5},{2,6},{3,7},{4,8},{5,9},{6,10},{7,11},{8,12},{9,13},{1... | collective-permute-start | bytes 3145736 | tf_op jit(solution)/shard_map/ppermute | solution.py:155
  6.8 23.7 %collective-permute-start.15 = (bf16[256,1024]{1,0:T(8,128)(2,1)}, bf16[256,1024]{1,0:T(8,128)(2,1)S(1)}, u32[]{:S(2)}, u32[]{:S(2)}) collective-permute-start(bf16[256,1024]{1,0:T(8,128)(2,1)} %bitcast.13), channel_id=1, source_target_pairs={{4,6},{5,7},{6,4},{7,5},{8,10},{9,11},{10,8},{11,9},{12,14},{13,15... | collective-permute-start | bytes 1572872 | tf_op jit(solution)/shard_map/ppermute | solution.py:155
  10.0 20.6 %collective-permute-start.14 = (bf16[256,1024]{1,0:T(8,128)(2,1)}, bf16[256,1024]{1,0:T(8,128)(2,1)S(1)}, u32[]{:S(2)}, u32[]{:S(2)}) collective-permute-start(bf16[256,1024]{1,0:T(8,128)(2,1)} %bitcast.14), channel_id=1, source_target_pairs={{0,1},{1,0},{2,3},{3,2},{4,5},{5,4},{6,7},{7,6},{8,9},{9,8},{10,11... | collective-permute-start | bytes 1572872 | tf_op jit(solution)/shard_map/ppermute | solution.py:155
  17.5 21.3 %collective-permute-start.18 = (bf16[256,1024]{1,0:T(8,128)(2,1)}, bf16[256,1024]{1,0:T(8,128)(2,1)S(1)}, u32[]{:S(2)}, u32[]{:S(2)}) collective-permute-start(bf16[256,1024]{1,0:T(8,128)(2,1)} %bitcast.16), channel_id=1, source_target_pairs={{4,6},{5,7},{6,4},{7,5},{8,10},{9,11},{10,8},{11,9},{12,14},{13,15... | collective-permute-start | bytes 1572872 | tf_op jit(solution)/shard_map/ppermute | solution.py:155
  20.2 30.8 %collective-permute-start.20 = (bf16[1024,512]{1,0:T(8,128)(2,1)}, bf16[1024,512]{1,0:T(8,128)(2,1)S(1)}, u32[]{:S(2)}, u32[]{:S(2)}) collective-permute-start(bf16[1024,512]{1,0:T(8,128)(2,1)} %bitcast.29), channel_id=1, source_target_pairs={{8,4},{9,5},{10,6},{11,7},{12,8},{13,9},{14,10},{15,11},{16,12},{1... | collective-permute-start | bytes 3145736 | tf_op jit(solution)/shard_map/ppermute | solution.py:155
  30.6 15.2 %collective-permute-start.17 = (bf16[256,1024]{1,0:T(8,128)(2,1)}, bf16[256,1024]{1,0:T(8,128)(2,1)S(1)}, u32[]{:S(2)}, u32[]{:S(2)}) collective-permute-start(bf16[256,1024]{1,0:T(8,128)(2,1)} %bitcast.17), channel_id=1, source_target_pairs={{0,1},{1,0},{2,3},{3,2},{4,5},{5,4},{6,7},{7,6},{8,9},{9,8},{10,11... | collective-permute-start | bytes 1572872 | tf_op jit(solution)/shard_map/ppermute | solution.py:155
  30.7 19.2 %collective-permute-start.16 = (bf16[256,1024]{1,0:T(8,128)(2,1)S(1)}, bf16[256,1024]{1,0:T(8,128)(2,1)S(1)}, u32[]{:S(2)}, u32[]{:S(2)}) collective-permute-start(bf16[256,1024]{1,0:T(8,128)(2,1)S(1)} %collective-permute-done.15.refs_3_), channel_id=1, source_target_pairs={{0,1},{1,0},{2,3},{3,2},{4,5},{5,4},{6,7},{7,6},{8,9},{9,8},{10,11... | collective-permute-start | bytes 1572872 | tf_op jit(solution)/shard_map/ppermute | solution.py:155
  38.9 11.0 %collective-permute-start.19 = (bf16[256,1024]{1,0:T(8,128)(2,1)S(1)}, bf16[256,1024]{1,0:T(8,128)(2,1)S(1)}, u32[]{:S(2)}, u32[]{:S(2)}) collective-permute-start(bf16[256,1024]{1,0:T(8,128)(2,1)S(1)} %collective-permute-done.18.refs_7_), channel_id=1, source_target_pairs={{0,1},{1,0},{2,3},{3,2},{4,5},{5,4},{6,7},{7,6},{8,9},{9,8},{10,11... | collective-permute-start | bytes 1572872 | tf_op jit(solution)/shard_map/ppermute | solution.py:155
  38.9 23.4 %collective-permute-start.2 = (bf16[256,1024]{1,0:T(8,128)(2,1)S(1)}, bf16[256,1024]{1,0:T(8,128)(2,1)S(1)}, u32[]{:S(2)}, u32[]{:S(2)}) collective-permute-start(bf16[256,1024]{1,0:T(8,128)(2,1)S(1)} %collective-permute-done.1.far.b2.refs_3_), channel_id=1, source_target_pairs={{0,1},{1,0},{2,3},{3,2},{4,5},{5,4},{6,7},{7,6},{8,9},{9,8},{10,11... | collective-permute-start | bytes 1572872 | tf_op jit(solution)/shard_map/ppermute | solution.py:155
  39.4 1.6 %copy-start = (bf16[1,2,1024,512]{3,2,1,0:T(8,128)(2,1)S(1)}, bf16[1,2,1024,512]{3,2,1,0:T(8,128)(2,1)}, u32[]{:S(2)}) copy-start(bf16[1,2,1024,512]{3,2,1,0:T(8,128)(2,1)} %param.13) | copy-start | bytes 6291460
  41.0 1.0 copy-start.1
  42.0 1.0 copy-start.2
  43.1 1.0 copy-start.3
  45.8 34.3 %collective-permute-start.4 = (bf16[512,512]{1,0:T(8,128)(2,1)S(1)}, bf16[512,512]{1,0:T(8,128)(2,1)S(1)}, u32[]{:S(2)}, u32[]{:S(2)}) collective-permute-start(bf16[512,512]{1,0:T(8,128)(2,1)S(1)} %get-tuple-element.26), channel_id=1, source_target_pairs={{0,4},{1,5},{2,6},{3,7},{4,8},{5,9},{6,10},{7,11},{8,12},{9,13},{1... | collective-permute-start | bytes 1572872 | tf_op jit(solution)/shard_map/ppermute | solution.py:155
  52.3 33.5 %collective-permute-start.27 = (bf16[1024,256]{1,0:T(8,128)(2,1)S(1)}, bf16[1024,256]{1,0:T(8,128)(2,1)S(1)}, u32[]{:S(2)}, u32[]{:S(2)}) collective-permute-start(bf16[1024,256]{1,0:T(8,128)(2,1)S(1)} %shard_map.107), channel_id=1, source_target_pairs={{8,4},{9,5},{10,6},{11,7},{12,8},{13,9},{14,10},{15,11},{16,12},{1... | collective-permute-start | bytes 1572872 | tf_op jit(solution)/shard_map/ppermute | solution.py:155
  63.0 16.4 %collective-permute-start.11 = (bf16[512,256]{1,0:T(8,128)(2,1)S(1)}, bf16[512,256]{1,0:T(8,128)(2,1)S(1)}, u32[]{:S(2)}, u32[]{:S(2)}) collective-permute-start(bf16[512,256]{1,0:T(8,128)(2,1)S(1)} %get-tuple-element.34), channel_id=1, source_target_pairs={{0,4},{1,5},{2,6},{3,7},{4,8},{5,9},{6,10},{7,11},{8,12},{9,13},{1... | collective-permute-start | bytes 786440 | tf_op jit(solution)/shard_map/ppermute | solution.py:155
  65.0 17.4 %collective-permute-start.5 = (bf16[512,256]{1,0:T(8,128)(2,1)S(1)}, bf16[512,256]{1,0:T(8,128)(2,1)S(1)}, u32[]{:S(2)}, u32[]{:S(2)}) collective-permute-start(bf16[512,256]{1,0:T(8,128)(2,1)S(1)} %get-tuple-element.28.after), channel_id=1, source_target_pairs={{0,4},{1,5},{2,6},{3,7},{4,8},{5,9},{6,10},{7,11},{8,12},{9,13},{1... | collective-permute-start | bytes 786440 | tf_op jit(solution)/shard_map/ppermute | solution.py:155
  68.3 20.7 %collective-permute-start.21 = (bf16[1024,256]{1,0:T(8,128)(2,1)S(1)}, bf16[1024,256]{1,0:T(8,128)(2,1)S(1)}, u32[]{:S(2)}, u32[]{:S(2)}) collective-permute-start(bf16[1024,256]{1,0:T(8,128)(2,1)S(1)} %shard_map.104), channel_id=1, source_target_pairs={{8,4},{9,5},{10,6},{11,7},{12,8},{13,9},{14,10},{15,11},{16,12},{1... | collective-permute-start | bytes 1572872 | tf_op jit(solution)/shard_map/ppermute | solution.py:155
  79.4 19.3 %collective-permute-start.8 = (bf16[256,1024]{1,0:T(8,128)(2,1)S(1)}, bf16[256,1024]{1,0:T(8,128)(2,1)S(1)}, u32[]{:S(2)}, u32[]{:S(2)}) collective-permute-start(bf16[256,1024]{1,0:T(8,128)(2,1)S(1)} %get-tuple-element.33), channel_id=1, source_target_pairs={{0,240},{1,241},{2,242},{3,243},{252,12},{253,13},{254,14},{255,15}} | collective-permute-start | bytes 1572872 | tf_op jit(solution)/shard_map/ppermute | solution.py:155
  80.1 20.5 %collective-permute-start.24 = (bf16[256,1024]{1,0:T(8,128)(2,1)S(1)}, bf16[256,1024]{1,0:T(8,128)(2,1)S(1)}, u32[]{:S(2)}, u32[]{:S(2)}) collective-permute-start(bf16[256,1024]{1,0:T(8,128)(2,1)S(1)} %get-tuple-element.42), channel_id=1, source_target_pairs={{0,240},{1,241},{2,242},{3,243},{252,12},{253,13},{254,14},{255,15}} | collective-permute-start | bytes 1572872 | tf_op jit(solution)/shard_map/ppermute | solution.py:155
  82.4 22.4 %collective-permute-start.12 = (bf16[1024,256]{1,0:T(8,128)(2,1)S(1)}, bf16[1024,256]{1,0:T(8,128)(2,1)S(1)}, u32[]{:S(2)}, u32[]{:S(2)}) collective-permute-start(bf16[1024,256]{1,0:T(8,128)(2,1)S(1)} %get-tuple-element.35), channel_id=1, source_target_pairs={{0,4},{1,5},{2,6},{3,7},{4,8},{5,9},{6,10},{7,11},{8,12},{9,13},{1... | collective-permute-start | bytes 1572872 | tf_op jit(solution)/shard_map/ppermute | solution.py:155
  85.8 26.0 %collective-permute-start.6 = (bf16[1024,256]{1,0:T(8,128)(2,1)S(1)}, bf16[1024,256]{1,0:T(8,128)(2,1)S(1)}, u32[]{:S(2)}, u32[]{:S(2)}) collective-permute-start(bf16[1024,256]{1,0:T(8,128)(2,1)S(1)} %get-tuple-element.29), channel_id=1, source_target_pairs={{0,4},{1,5},{2,6},{3,7},{4,8},{5,9},{6,10},{7,11},{8,12},{9,13},{1... | collective-permute-start | bytes 1572872 | tf_op jit(solution)/shard_map/ppermute | solution.py:155
  89.0 26.0 %collective-permute-start.28 = (bf16[1024,256]{1,0:T(8,128)(2,1)S(1)}, bf16[1024,256]{1,0:T(8,128)(2,1)S(1)}, u32[]{:S(2)}, u32[]{:S(2)}) collective-permute-start(bf16[1024,256]{1,0:T(8,128)(2,1)S(1)} %shard_map.108), channel_id=1, source_target_pairs={{8,4},{9,5},{10,6},{11,7},{12,8},{13,9},{14,10},{15,11},{16,12},{1... | collective-permute-start | bytes 1572872 | tf_op jit(solution)/shard_map/ppermute | solution.py:155
  98.7 18.2 %collective-permute-start.9 = (bf16[256,1024]{1,0:T(8,128)(2,1)S(1)}, bf16[256,1024]{1,0:T(8,128)(2,1)S(1)}, u32[]{:S(2)}, u32[]{:S(2)}) collective-permute-start(bf16[256,1024]{1,0:T(8,128)(2,1)S(1)} %collective-permute-done.8), channel_id=1, source_target_pairs={{240,2},{241,3},{242,0},{243,1},{12,254},{13,255},{14,252},{15,253}} | collective-permute-start | bytes 1572872 | tf_op jit(solution)/shard_map/ppermute | solution.py:155
  100.7 18.2 %collective-permute-start.22 = (bf16[1024,256]{1,0:T(8,128)(2,1)S(1)}, bf16[1024,256]{1,0:T(8,128)(2,1)S(1)}, u32[]{:S(2)}, u32[]{:S(2)}) collective-permute-start(bf16[1024,256]{1,0:T(8,128)(2,1)S(1)} %shard_map.105), channel_id=1, source_target_pairs={{8,4},{9,5},{10,6},{11,7},{12,8},{13,9},{14,10},{15,11},{16,12},{1... | collective-permute-start | bytes 1572872 | tf_op jit(solution)/shard_map/ppermute | solution.py:155
  104.8 23.8 %collective-permute-start.25 = (bf16[256,1024]{1,0:T(8,128)(2,1)S(1)}, bf16[256,1024]{1,0:T(8,128)(2,1)S(1)}, u32[]{:S(2)}, u32[]{:S(2)}) collective-permute-start(bf16[256,1024]{1,0:T(8,128)(2,1)S(1)} %collective-permute-done.24), channel_id=1, source_target_pairs={{240,2},{241,3},{242,0},{243,1},{12,254},{13,255},{14,252},{15,253}} | collective-permute-start | bytes 1572872 | tf_op jit(solution)/shard_map/ppermute | solution.py:155
  111.8 22.4 %collective-permute-start.13 = (bf16[1024,256]{1,0:T(8,128)(2,1)S(1)}, bf16[1024,256]{1,0:T(8,128)(2,1)S(1)}, u32[]{:S(2)}, u32[]{:S(2)}) collective-permute-start(bf16[1024,256]{1,0:T(8,128)(2,1)S(1)} %get-tuple-element.36), channel_id=1, source_target_pairs={{0,4},{1,5},{2,6},{3,7},{4,8},{5,9},{6,10},{7,11},{8,12},{9,13},{1... | collective-permute-start | bytes 1572872 | tf_op jit(solution)/shard_map/ppermute | solution.py:155
  115.0 25.3 %collective-permute-start.7 = (bf16[1024,256]{1,0:T(8,128)(2,1)S(1)}, bf16[1024,256]{1,0:T(8,128)(2,1)S(1)}, u32[]{:S(2)}, u32[]{:S(2)}) collective-permute-start(bf16[1024,256]{1,0:T(8,128)(2,1)S(1)} %get-tuple-element.30), channel_id=1, source_target_pairs={{0,4},{1,5},{2,6},{3,7},{4,8},{5,9},{6,10},{7,11},{8,12},{9,13},{1... | collective-permute-start | bytes 1572872 | tf_op jit(solution)/shard_map/ppermute | solution.py:155
  116.9 19.2 %collective-permute-start.10 = (bf16[256,1024]{1,0:T(8,128)(2,1)S(1)}, bf16[256,1024]{1,0:T(8,128)(2,1)S(1)}, u32[]{:S(2)}, u32[]{:S(2)}) collective-permute-start(bf16[256,1024]{1,0:T(8,128)(2,1)S(1)} %collective-permute-done.9.rest_2_.refs_7_.refs_12_), channel_id=1, source_target_pairs={{0,1},{1,0},{2,3},{3,2},{252,253},{253,252},{254,255},{255,254}} | collective-permute-start | bytes 1572872 | tf_op jit(solution)/shard_map/ppermute | solution.py:155
  118.9 23.5 %collective-permute-start.29 = (bf16[1024,256]{1,0:T(8,128)(2,1)S(1)}, bf16[1024,256]{1,0:T(8,128)(2,1)S(1)}, u32[]{:S(2)}, u32[]{:S(2)}) collective-permute-start(bf16[1024,256]{1,0:T(8,128)(2,1)S(1)} %shard_map.109), channel_id=1, source_target_pairs={{4,0},{5,1},{6,2},{7,3},{8,4},{9,5},{10,6},{11,7},{12,8},{13,9},{1... | collective-permute-start | bytes 1572872 | tf_op jit(solution)/shard_map/ppermute | solution.py:155
  128.6 13.9 %collective-permute-start.26 = (bf16[256,1024]{1,0:T(8,128)(2,1)S(1)}, bf16[256,1024]{1,0:T(8,128)(2,1)S(1)}, u32[]{:S(2)}, u32[]{:S(2)}) collective-permute-start(bf16[256,1024]{1,0:T(8,128)(2,1)S(1)} %collective-permute-done.25.refs_14_), channel_id=1, source_target_pairs={{0,1},{1,0},{2,3},{3,2},{252,253},{253,252},{254,255},{255,254}} | collective-permute-start | bytes 1572872 | tf_op jit(solution)/shard_map/ppermute | solution.py:155
  134.2 12.6 %collective-permute-start.23 = (bf16[1024,256]{1,0:T(8,128)(2,1)S(1)}, bf16[1024,256]{1,0:T(8,128)(2,1)S(1)}, u32[]{:S(2)}, u32[]{:S(2)}) collective-permute-start(bf16[1024,256]{1,0:T(8,128)(2,1)S(1)} %shard_map.106), channel_id=1, source_target_pairs={{4,0},{5,1},{6,2},{7,3},{8,4},{9,5},{10,6},{11,7},{12,8},{13,9},{1... | collective-permute-start | bytes 1572872 | tf_op jit(solution)/shard_map/ppermute | solution.py:155

commit v3 on v2

--- a/solution.py
+++ b/solution.py
@@ -50,45 +50,85 @@
     )(*arrays)
 
 
-def late_kernel(_, after, down, up, reflect, first, second):
-    top = lax.axis_index("layer") == 0
-    first[...] = jnp.where(top, up[...], down[...])
-    second[...] = jnp.where(top, reflect[...], up[...])
-
-
-def near_kernel(plan, own, near, received, sources, new, down_in):
+def near_kernel(plan, own, near, received, sources, new):
     core = lax.axis_index("shot") % 2
-    down_in[...] = injected(received[...], sources[plan[0, 0]])
-    for k, block in enumerate((own, near)):
-        new[band(core ^ k, block.shape[0]), :] = dot(block[...], down_in[...]).astype(BF16)
-
-
-def far_kernel(_, far, cross, down_in, *new):
-    core = lax.axis_index("shot") % 2
-    for k, block in enumerate((far, cross)):
-        rows = band(core ^ k, block.shape[0])
-        for chunk, ref in enumerate(new):
-            cols = columns(down_in, chunk, ref.shape[1])
-            ref[rows, :] = dot(block[...], down_in[:, cols]).astype(BF16)
+
+    @pl.when(lax.axis_index("layer") == 0)
+    def _():
+        down_in = injected(received[...], sources[plan[0, 0]])
+        for k, block in enumerate((own, near)):
+            new[band(core ^ k, block.shape[0]), :] = dot(block[...], down_in).astype(BF16)
+
+
+def far_kernel(_, first, second, new):
+    rows = band(1 - lax.axis_index("shot") // 2, new.shape[0])
+
+    @pl.when(lax.axis_index("layer") == 0)
+    def _():
+        for chunk, ref in enumerate((first, second)):
+            new[:, columns(new, chunk, ref.shape[1])] = ref[rows, :]
+
+
+def products(blocks, down_in, new):
+    spot = lax.axis_index("shot")
+    for k, block in enumerate(blocks):
+        new[band(spot ^ k, block.shape[0]), :] = dot(block[...], down_in[...]).astype(BF16)
+
+
+def fix_kernel(plan, b0, b1, b2, b3, received, sources, *refs):
+    n = len(refs) // 2
+    inside = lax.axis_index("layer") == lax.axis_size("layer") // 2
+
+    @pl.when(inside)
+    def _():
+        for chunk in range(n // 2):
+            new, down_in = refs[n + 2 * chunk : n + 2 * chunk + 2]
+            cols = columns(sources, chunk, new.shape[1])
+            down_in[...] = injected(received[:, cols], sources[plan[0, 0], :, cols])
+            products((b0, b1, b2, b3), down_in, new)
+
+    @pl.when(jnp.logical_not(inside))
+    def _():
+        for old, new in zip(refs[:n], refs[n:]):
+            new[...] = old[...]
 
 
 def columns(ref, chunk, width):
     return slice(chunk * width, (chunk + 1) * width) if ref.shape[-1] > width else slice(None)
 
 
-def down_kernel(moment, chunk, n, last, plan, b0, b1, b2, b3, *rest):
-    received, sources, late, (new, down_in) = rest[:n], rest[n], rest[n + 1 : -2], rest[-2:]
-    end = lax.axis_index("layer") == lax.axis_size("layer") - 1
+def down_kernel(moment, chunk, plan, b0, b1, b2, b3, received, sources, *rest):
+    others, (new, down_in) = rest[:-2], rest[-2:]
+    layer, count = lax.axis_index("layer"), lax.axis_size("layer")
     spot = lax.axis_index("shot")
-    width = down_in.shape[1]
-    cols, picked = columns(sources, chunk, width), plan[0, moment]
-    for k, ref in enumerate(received):
-        rows = band((spot // 2) ^ k, ref.shape[0]) if n > 1 else slice(None)
-        down_in[rows, :] = injected(ref[:, columns(ref, chunk, width)], sources[picked, rows, cols])
+    cols = columns(sources, chunk, down_in.shape[1])
+
+    def take(ref, rows=slice(None)):
+        value = ref[:, columns(ref, chunk, down_in.shape[1])]
+        down_in[rows, :] = injected(value, sources[plan[0, moment], rows, cols])
+
+    if moment == 1:
+        near, far, middle = others
+
+        @pl.when(layer == 1)
+        def _():
+            for k, ref in enumerate((near, far)):
+                take(ref, band((spot // 2) ^ k, ref.shape[0]))
+
+        @pl.when(layer == count // 2)
+        def _():
+            take(middle)
+
+        @pl.when(jnp.logical_and(layer != 1, layer != count // 2))
+        def _():
+            take(received)
+
+    else:
+        take(received)
     for k, block in enumerate((b0, b1, b2, b3)):
         high, value = block.shape[0], block[...]
-        if last and k >= 2:
-            value = jnp.where(end, late[k - 2][...], value)
+        if moment == TICKS - 1 and k >= 2:
+            value = jnp.where(layer == count - 1, others[k - 2][...], value)
         new[band(spot ^ k, high), :] = dot(value, down_in[...]).astype(BF16)
 
 
@@ -106,9 +146,8 @@
         up, reflect = blocks[k][...], blocks[4 + k][...]
         high = up.shape[0]
         if last and k >= 2:
-            first, second = late[k - 2][...], late[k][...]
-            up = jnp.where(top, first, jnp.where(end, second, up))
-            reflect = jnp.where(top, second, reflect)
+            up = jnp.where(jnp.logical_or(top, end), late[k - 2][...], up)
+            reflect = jnp.where(top, late[k][...], reflect)
         rows = band(spot ^ k, high)
         total = dot(up, gathered) + dot(reflect, injection)
         total = total + sources[pick[0], rows, columns(sources, chunk, width)].astype(F32)
@@ -167,18 +206,26 @@
 
     every = range(layers)
 
-    def shift(value, steps, lowest=0):
+    def shift(value, steps, without=()):
         return sent(value, [
-            (at(l, s), at(l + steps, s)) for l in every for s in range(shots) if lowest <= l + steps < layers
+            (at(l, s), at(l + steps, s))
+            for l in every for s in range(shots) if 0 <= l + steps < layers and l not in without
         ])
+
+    def link(value, pairs, bit):
+        return sent(value, [(at(a, s), at(b, s ^ bit)) for a, b in pairs for s in range(shots)])
 
     def swap(value, bit, members):
         return sent(value, [(at(l, s), at(l, s ^ bit)) for l in members for s in range(shots)])
 
     middle = [l for l in every if 0 < l < layers - 1]
-    down_0 = shift(down_state[0], 1)
+    cut = layers // 2
+    down_0b = link(down_state[0], [(cut - 1, cut)], 0)
+    down_0 = shift(down_state[0], 1, [cut - 1])
     far_d = swap(down_op, 2, [0] + middle)
-    up_0 = shift(up_state[0], -1, 1)
+    up_0 = shift(up_state[0], -1, [1])
+    far_e = swap(down_op, 2, [layers - 1])
+    cross_e = swap(far_e, 1, [layers - 1])
     near_d = swap(down_op, 1, every)
     far_u = swap(up_op, 2, middle)
     far_r = swap(reflect_op, 2, middle + [layers - 1])
@@ -193,21 +240,27 @@
     d_blocks = [down_op, near_d, far_d, cross_d]
     u_blocks = [up_op, near_u, far_u, cross_u, reflect_op, near_r, far_r, cross_r]
     ends = ((0, layers - 4), (layers - 1, 3))
-    out = [(at(a, s), at(b, s)) for a, b in ends for s in range(shots)]
-    back = [(at(b, s), at(a, s ^ 2)) for a, b in ends for s in range(shots)]
-    half = height // 2
-    near, down_in = call(near_kernel, plan, [down_op, near_d, down_0, sources], [(half, wide), (height, wide)], one)
-    far = call(far_kernel, layer_source, [far_d, cross_d, down_in], [(half, width)] * CHUNKS, one)
-    near = shift(near, 1)
-    downs = [[near, shift(a, 1)] for a in far]
-    pair = call(
-        late_kernel, layer_source, [far[-1], down_op, up_op, reflect_op],
-        [down_op.shape] * 2, one // 8,
-    )
     late = []
-    for a in pair:
-        a = sent(sent(a, out), back)
-        late += [a, swap(a, 1, (0, layers - 1))]
+    for op, pairs in ((up_op, ends), (reflect_op, ends[:1])):
+        op = link(op, pairs, 0)
+        op = link(op, [(b, a) for a, b in pairs], 2)
+        late += [op, link(op, [(a, a) for a, _ in pairs], 1)]
+    half = (height // 2, wide)
+    piece = (height, width)
+    (near,) = call(near_kernel, plan, [down_op, near_d, down_0, sources], [half], one // 8)
+    near = link(near, [(0, 1)], 0)
+    firsts, middles = [], []
+    for chunk in range(CHUNKS):
+        new, down_in = call(
+            functools.partial(down_kernel, 0, chunk), plan,
+            [*d_blocks, down_0, sources], [piece] * 2, one,
+        )
+        firsts += [new, down_in]
+        middles.append(link(new, [(cut - 1, cut)], 0))
+    (far,) = call(far_kernel, layer_source, [firsts[0], firsts[2]], [half], one // 8)
+    far = link(far, [(0, 1)], 0)
+    firsts = call(fix_kernel, plan, [*d_blocks, down_0b, sources, *firsts], [piece] * (2 * CHUNKS), one // 8)
+    downs = [shift(firsts[2 * i], 1, [0, cut - 1]) for i in range(CHUNKS)]
     ups = [up_0] * CHUNKS
     for moment in range(TICKS):
         last = moment == TICKS - 1
@@ -215,25 +268,27 @@
         for chunk in range(CHUNKS):
             full = (chunk, wide) if last else None
             if moment:
+                more = [near, far, middles[chunk]] if moment == 1 else [far_e, cross_e] if last else []
                 new, down_in = call(
-                    functools.partial(down_kernel, moment, chunk, len(downs[chunk]), last),
-                    plan, [*d_blocks, *downs[chunk], sources],
-                    [(height, width)] * 2, one,
-                    full=full, into=new if last else None, more=late[:2] if last else (),
+                    functools.partial(down_kernel, moment, chunk), plan,
+                    [*d_blocks, downs[chunk], sources], [piece] * 2, one,
+                    full=full, into=new if last else None, more=more,
                 )
                 new_downs.append(new)
+            else:
+                down_in = firsts[2 * chunk + 1]
             (up,) = call(
                 functools.partial(up_kernel, chunk, last), layer_source,
-                [*u_blocks, ups[chunk], down_in, sources], [(height, width)], 2 * one,
+                [*u_blocks, ups[chunk], down_in, sources], [piece], 2 * one,
                 full=full, into=up if last else None, more=late if last else (),
             )
             new_ups.append(up)
         if last:
             return (new[None], up[None])
         if moment:
-            downs = [[shift(a, 1)] for a in new_downs]
-        lowest = 0 if moment == TICKS - 2 else 1
-        ups = [shift(a, -1, lowest) for a in new_ups]
+            downs = [shift(a, 1) for a in new_downs]
+        without_top = [] if moment == TICKS - 2 else [1]
+        ups = [shift(a, -1, without_top) for a in new_ups]
 
 
 def solution(mesh):

time: 150 us -> 166 us (1.11)
  the two profiles are of different devices: /device:TPU:24 before, /device:TPU:8 now
where the time goes in v3:
time: 166 us; the launch traced here: 164 us
  starting transfers between devices  79.4 us (48%)
  waiting for transfers between devices  51 us (31%)
  Pallas kernels  26.5 us (16%)
  local copies, waits for them, and re-layouts  4.72 us (3%)
  between operations  1.87 us (1%)
    ppermute x36, starting transfers between devices, sent(): return lax.ppermute(value, ('layer', 'shot'), pairs)  79.4 us
    ppermute x36, waiting for transfers between devices, sent(): return lax.ppermute(value, ('layer', 'shot'), pairs)  51 us
    pallas_call x19, Pallas kernels, call(): pl.pallas_call(kernel, grid=(1,), in_specs=in_specs, out_specs=out_specs,...  26.2 us
    unnamed x10, local copies, waits for them, and re-layouts  4.72 us
  transfers between devices with their start and end apart: 36, of which 9 were waited for; matrix products, arithmetic and copies ran while one was open for 0% of the time, Pallas kernels for 15%

profile of v3, /device:TPU:8, one launch (start us, length us, event | category | flops | bytes accessed | tf_op | source)
XLA Modules:
  0.0 163.5 jit_solution(6413790674794148597)
XLA Ops:
  0.7 4.1 %collective-permute-start.1 = (bf16[256,1024]{1,0:T(8,128)(2,1)}, bf16[256,1024]{1,0:T(8,128)(2,1)S(1)}, u32[]{:S(2)}, u32[]{:S(2)}) collective-permute-start(bf16[256,1024]{1,0:T(8,128)(2,1)} %bitcast.11), channel_id=1, source_target_pairs={{0,2},{1,3},{2,0},{3,1},{4,6},{5,7},{6,4},{7,5},{8,10},{9,11},{10,... | collective-permute-start | bytes 1572872 | tf_op jit(solution)/shard_map/ppermute | solution.py:194
  5.8 1.7 %collective-permute-start.4 = (bf16[1024,512]{1,0:T(8,128)(2,1)}, bf16[1024,512]{1,0:T(8,128)(2,1)S(1)}, u32[]{:S(2)}, u32[]{:S(2)}) collective-permute-start(bf16[1024,512]{1,0:T(8,128)(2,1)} %bitcast.32), channel_id=1, source_target_pairs={{0,4},{1,5},{2,6},{3,7},{4,8},{5,9},{6,10},{7,11},{8,12},{9,13},{1... | collective-permute-start | bytes 3145736 | tf_op jit(solution)/shard_map/ppermute | solution.py:194
  8.3 9.3 %collective-permute-done.1.b2.refs_3_ = bf16[256,1024]{1,0:T(8,128)(2,1)S(1)} collective-permute-done((bf16[256,1024]{1,0:T(8,128)(2,1)}, bf16[256,1024]{1,0:T(8,128)(2,1)S(1)}, u32[]{:S(2)}, u32[]{:S(2)}) %collective-permute-start.1) | collective-permute-done | bytes 524320 | tf_op jit(solution)/shard_map/ppermute | solution.py:194
  18.3 0.7 collective-permute-start.3
  19.1 0.7 collective-permute-start.23
  21.2 1.6 copy-done
  22.8 1.0 copy-done.1
  23.8 1.0 copy-done.2
  24.8 1.0 copy-done.3
  26.8 3.9 %collective-permute-done.4.received = bf16[1024,512]{1,0:T(8,128)(2,1)S(1)} collective-permute-done((bf16[1024,512]{1,0:T(8,128)(2,1)}, bf16[1024,512]{1,0:T(8,128)(2,1)S(1)}, u32[]{:S(2)}, u32[]{:S(2)}) %collective-permute-start.4) | collective-permute-done | bytes 1048608 | tf_op jit(solution)/shard_map/ppermute | solution.py:194
  30.7 1.3 shard_map.95
  32.0 1.3 shard_map.96
  33.3 1.3 shard_map.98
  34.6 17.9 %collective-permute-start.6 = (bf16[512,512]{1,0:T(8,128)(2,1)S(1)}, bf16[512,512]{1,0:T(8,128)(2,1)S(1)}, u32[]{:S(2)}, u32[]{:S(2)}) collective-permute-start(bf16[512,512]{1,0:T(8,128)(2,1)S(1)} %shard_map.98), channel_id=1, source_target_pairs={{0,4},{1,5},{2,6},{3,7}} | collective-permute-start | bytes 1572872 | tf_op jit(solution)/shard_map/ppermute | solution.py:194
  52.6 1.3 collective-permute-start.7
  53.9 0.7 shard_map.97
  54.6 0.7 collective-permute-start.13
  56.0 9.5 %collective-permute-start.27 = (bf16[256,1024]{1,0:T(8,128)(2,1)S(1)}, bf16[256,1024]{1,0:T(8,128)(2,1)S(1)}, u32[]{:S(2)}, u32[]{:S(2)}) collective-permute-start(bf16[256,1024]{1,0:T(8,128)(2,1)S(1)} %get-tuple-element.40.refs_1_), channel_id=1, source_target_pairs={{0,240},{1,241},{2,242},{3,243},{252,12},{253,13},{254,14},{255,15}} | collective-permute-start | bytes 1572872 | tf_op jit(solution)/shard_map/ppermute | solution.py:194
  66.2 9.3 %collective-permute-done.7.rest_1_ = bf16[512,512]{1,0:T(8,128)(2,1)S(1)} collective-permute-done((bf16[512,512]{1,0:T(8,128)(2,1)S(1)}, bf16[512,512]{1,0:T(8,128)(2,1)S(1)}, u32[]{:S(2)}, u32[]{:S(2)}) %collective-permute-start.7) | collective-permute-done | bytes 524320 | tf_op jit(solution)/shard_map/ppermute | solution.py:194
  76.3 1.3 shard_map.109
  78.3 1.3 shard_map.106
  80.2 1.4 shard_map.102
  81.7 6.4 %collective-permute-start.30 = (bf16[256,1024]{1,0:T(8,128)(2,1)S(1)}, bf16[256,1024]{1,0:T(8,128)(2,1)S(1)}, u32[]{:S(2)}, u32[]{:S(2)}) collective-permute-start(bf16[256,1024]{1,0:T(8,128)(2,1)S(1)} %get-tuple-element.41.refs_5_), channel_id=1, source_target_pairs={{0,240},{1,241},{2,242},{3,243}} | collective-permute-start | bytes 1572872 | tf_op jit(solution)/shard_map/ppermute | solution.py:194
  88.8 4.4 %collective-permute-start.15 = (bf16[1024,256]{1,0:T(8,128)(2,1)S(1)}, bf16[1024,256]{1,0:T(8,128)(2,1)S(1)}, u32[]{:S(2)}, u32[]{:S(2)}) collective-permute-start(bf16[1024,256]{1,0:T(8,128)(2,1)S(1)} %get-tuple-element.36), channel_id=1, source_target_pairs={{0,4},{1,5},{2,6},{3,7},{4,8},{5,9},{6,10},{7,11},{8,12},{9,13},{1... | collective-permute-start | bytes 1572872 | tf_op jit(solution)/shard_map/ppermute | solution.py:194
  93.2 1.6 shard_map.100
  94.8 4.5 %collective-permute-start.9 = (bf16[1024,256]{1,0:T(8,128)(2,1)S(1)}, bf16[1024,256]{1,0:T(8,128)(2,1)S(1)}, u32[]{:S(2)}, u32[]{:S(2)}) collective-permute-start(bf16[1024,256]{1,0:T(8,128)(2,1)S(1)} %get-tuple-element.33), channel_id=1, source_target_pairs={{0,4},{1,5},{2,6},{3,7},{4,8},{5,9},{6,10},{7,11},{8,12},{9,13},{1... | collective-permute-start | bytes 1572872 | tf_op jit(solution)/shard_map/ppermute | solution.py:194
  99.3 1.3 shard_map.110
  101.3 1.3 shard_map.107
  102.6 1.3 collective-permute-start.28
  103.9 1.3 collective-permute-start.31
  106.2 1.3 shard_map.103
  107.5 7.3 %collective-permute-done.9.received = bf16[1024,256]{1,0:T(8,128)(2,1)S(1)} collective-permute-done((bf16[1024,256]{1,0:T(8,128)(2,1)S(1)}, bf16[1024,256]{1,0:T(8,128)(2,1)S(1)}, u32[]{:S(2)}, u32[]{:S(2)}) %collective-permute-start.9) | collective-permute-done | bytes 524320 | tf_op jit(solution)/shard_map/ppermute | solution.py:194
  114.8 4.4 %collective-permute-start.16 = (bf16[1024,256]{1,0:T(8,128)(2,1)S(1)}, bf16[1024,256]{1,0:T(8,128)(2,1)S(1)}, u32[]{:S(2)}, u32[]{:S(2)}) collective-permute-start(bf16[1024,256]{1,0:T(8,128)(2,1)S(1)} %get-tuple-element.37), channel_id=1, source_target_pairs={{0,4},{1,5},{2,6},{3,7},{4,8},{5,9},{6,10},{7,11},{8,12},{9,13},{1... | collective-permute-start | bytes 1572872 | tf_op jit(solution)/shard_map/ppermute | solution.py:194
  119.2 1.3 shard_map.101
  120.5 5.3 %collective-permute-start.10 = (bf16[1024,256]{1,0:T(8,128)(2,1)S(1)}, bf16[1024,256]{1,0:T(8,128)(2,1)S(1)}, u32[]{:S(2)}, u32[]{:S(2)}) collective-permute-start(bf16[1024,256]{1,0:T(8,128)(2,1)S(1)} %get-tuple-element.34), channel_id=1, source_target_pairs={{0,4},{1,5},{2,6},{3,7},{4,8},{5,9},{6,10},{7,11},{8,12},{9,13},{1... | collective-permute-start | bytes 1572872 | tf_op jit(solution)/shard_map/ppermute | solution.py:194
  125.8 1.3 shard_map.111
  127.1 1.9 %collective-permute-start.29 = (bf16[256,1024]{1,0:T(8,128)(2,1)S(1)}, bf16[256,1024]{1,0:T(8,128)(2,1)S(1)}, u32[]{:S(2)}, u32[]{:S(2)}) collective-permute-start(bf16[256,1024]{1,0:T(8,128)(2,1)S(1)} %collective-permute-done.28.refs_12_), channel_id=1, source_target_pairs={{0,1},{1,0},{2,3},{3,2},{252,253},{253,252},{254,255},{255,254}} | collective-permute-start | bytes 1572872 | tf_op jit(solution)/shard_map/ppermute | solution.py:194
  129.1 2.9 %collective-permute-done.31.refs_14_ = bf16[256,1024]{1,0:T(8,128)(2,1)S(1)} collective-permute-done((bf16[256,1024]{1,0:T(8,128)(2,1)S(1)}, bf16[256,1024]{1,0:T(8,128)(2,1)S(1)}, u32[]{:S(2)}, u32[]{:S(2)}) %collective-permute-start.31) | collective-permute-done | bytes 524320 | tf_op jit(solution)/shard_map/ppermute | solution.py:194
  132.0 1.9 %collective-permute-start.32 = (bf16[256,1024]{1,0:T(8,128)(2,1)S(1)}, bf16[256,1024]{1,0:T(8,128)(2,1)S(1)}, u32[]{:S(2)}, u32[]{:S(2)}) collective-permute-start(bf16[256,1024]{1,0:T(8,128)(2,1)S(1)} %collective-permute-done.31.refs_14_), channel_id=1, source_target_pairs={{0,1},{1,0},{2,3},{3,2}} | collective-permute-start | bytes 1572872 | tf_op jit(solution)/shard_map/ppermute | solution.py:194
  133.9 1.3 collective-permute-start.35
  135.2 1.3 shard_map.108
  136.5 1.3 collective-permute-start.26
  137.8 2.1 %shard_map.104 = (bf16[1024,512]{1,0:T(8,128)(2,1)}, bf16[1024,256]{1,0:T(8,128)(2,1)S(1)}) custom-call(s32[1,4]{1,0:T(1,128)S(1)} %bitcast.28, bf16[256,1024]{1,0:T(8,128)(2,1)S(1)} %get-tuple-element.26.b0.own.refs_1_, bf16[256,1024]{1,0:T(8,128)(2,1)S(1)} %collective-permute-done.b1.near.refs_2_, bf16[256,1024]{1,0:T(8,128)(2,1)S(1)} %collective-permute-done.1.b2.refs_3_, ...), custom_call_target="tpu_custom_call" | custom-call | flops 536870912 | bytes 1048576 | tf_op jit(solution)/shard_map/pallas_call | solution.py:174
  139.9 2.1 %shard_map.105 = (bf16[1024,512]{1,0:T(8,128)(2,1)}, bf16[1024,256]{1,0:T(8,128)(2,1)S(1)}) custom-call(s32[1,4]{1,0:T(1,128)S(1)} %bitcast.29, bf16[256,1024]{1,0:T(8,128)(2,1)S(1)} %get-tuple-element.26.b0.own.refs_1_, bf16[256,1024]{1,0:T(8,128)(2,1)S(1)} %collective-permute-done.b1.near.refs_2_, ...), custom_call_target="tpu_custom_call", output_to_operand_aliasing={{0}: (9, {})} | custom-call | flops 536870912 | bytes 1048576 | tf_op jit(solution)/shard_map/pallas_call | solution.py:174
  142.0 8.6 %collective-permute-done.35.refs_9_ = bf16[1024,256]{1,0:T(8,128)(2,1)S(1)} collective-permute-done((bf16[1024,256]{1,0:T(8,128)(2,1)S(1)}, bf16[1024,256]{1,0:T(8,128)(2,1)S(1)}, u32[]{:S(2)}, u32[]{:S(2)}) %collective-permute-start.35) | collective-permute-done | bytes 524320 | tf_op jit(solution)/shard_map/ppermute | solution.py:194
  150.6 2.1 %shard_map.112.refs_16_ = bf16[1024,512]{1,0:T(8,128)(2,1)} custom-call(s32[1]{0:T(128)S(6)} %copy.14._.refs_0_, bf16[256,1024]{1,0:T(8,128)(2,1)S(1)} %get-tuple-element.40.refs_1_, bf16[256,1024]{1,0:T(8,128)(2,1)S(1)} %collective-permute-done.17.refs_2_, bf16[256,1024]{1,0:T(8,128)(2,1)S(1)} %collective-permute-done.18.refs_3_, ...), custom_call_target="tpu_custom_call" | custom-call | flops 1073741824 | bytes 1048576 | tf_op jit(solution)/shard_map/pallas_call | solution.py:174
  152.7 8.7 %collective-permute-done.26.refs_9_ = bf16[1024,256]{1,0:T(8,128)(2,1)S(1)} collective-permute-done((bf16[1024,256]{1,0:T(8,128)(2,1)S(1)}, bf16[1024,256]{1,0:T(8,128)(2,1)S(1)}, u32[]{:S(2)}, u32[]{:S(2)}) %collective-permute-start.26) | collective-permute-done | bytes 524320 | tf_op jit(solution)/shard_map/ppermute | solution.py:194
  161.4 2.1 %shard_map.113 = bf16[1024,512]{1,0:T(8,128)(2,1)} custom-call(s32[1]{0:T(128)S(6)} %copy.14._.refs_0_, bf16[256,1024]{1,0:T(8,128)(2,1)S(1)} %get-tuple-element.40.refs_1_, bf16[256,1024]{1,0:T(8,128)(2,1)S(1)} %collective-permute-done.17.refs_2_, bf16[256,1024]{1,0:T(8,128)(2,1)S(1)} %collective-permute-done.18.refs_3_, ...), custom_call_target="tpu_custom_call", output_to_operand_aliasing={{}: (16, {})} | custom-call | flops 1073741824 | bytes 1048576 | tf_op jit(solution)/shard_map/pallas_call | solution.py:174
  (54 shorter events, 10.1 us)
Async XLA Ops:
  0.6 30.1 %copy-start.4 = (s32[4,1]{0,1:T(1,128)S(1)}, s32[4,1]{0,1:T(1,128)}, u32[]{:S(2)}) copy-start(s32[4,1]{0,1:T(1,128)} %param.14) | copy-start | bytes 52
  0.6 6.9 %collective-permute-start = (bf16[256,1024]{1,0:T(8,128)(2,1)}, bf16[256,1024]{1,0:T(8,128)(2,1)S(1)}, u32[]{:S(2)}, u32[]{:S(2)}) collective-permute-start(bf16[256,1024]{1,0:T(8,128)(2,1)} %bitcast.10), channel_id=1, source_target_pairs={{0,1},{1,0},{2,3},{3,2},{4,5},{5,4},{6,7},{7,6},{8,9},{9,8},{10,11... | collective-permute-start | bytes 1572872 | tf_op jit(solution)/shard_map/ppermute | solution.py:194
  0.7 16.8 %collective-permute-start.1 = (bf16[256,1024]{1,0:T(8,128)(2,1)}, bf16[256,1024]{1,0:T(8,128)(2,1)S(1)}, u32[]{:S(2)}, u32[]{:S(2)}) collective-permute-start(bf16[256,1024]{1,0:T(8,128)(2,1)} %bitcast.11), channel_id=1, source_target_pairs={{0,2},{1,3},{2,0},{3,1},{4,6},{5,7},{6,4},{7,5},{8,10},{9,11},{10,... | collective-permute-start | bytes 1572872 | tf_op jit(solution)/shard_map/ppermute | solution.py:194
  4.8 13.5 %collective-permute-start.11 = (bf16[256,1024]{1,0:T(8,128)(2,1)}, bf16[256,1024]{1,0:T(8,128)(2,1)S(1)}, u32[]{:S(2)}, u32[]{:S(2)}) collective-permute-start(bf16[256,1024]{1,0:T(8,128)(2,1)} %bitcast.12), channel_id=1, source_target_pairs={{252,254},{253,255},{254,252},{255,253}} | collective-permute-start | bytes 1572872 | tf_op jit(solution)/shard_map/ppermute | solution.py:194
  5.5 13.5 %collective-permute-start.17 = (bf16[256,1024]{1,0:T(8,128)(2,1)}, bf16[256,1024]{1,0:T(8,128)(2,1)S(1)}, u32[]{:S(2)}, u32[]{:S(2)}) collective-permute-start(bf16[256,1024]{1,0:T(8,128)(2,1)} %bitcast.14), channel_id=1, source_target_pairs={{0,1},{1,0},{2,3},{3,2},{4,5},{5,4},{6,7},{7,6},{8,9},{9,8},{10,11... | collective-permute-start | bytes 1572872 | tf_op jit(solution)/shard_map/ppermute | solution.py:194
  5.8 24.9 %collective-permute-start.4 = (bf16[1024,512]{1,0:T(8,128)(2,1)}, bf16[1024,512]{1,0:T(8,128)(2,1)S(1)}, u32[]{:S(2)}, u32[]{:S(2)}) collective-permute-start(bf16[1024,512]{1,0:T(8,128)(2,1)} %bitcast.32), channel_id=1, source_target_pairs={{0,4},{1,5},{2,6},{3,7},{4,8},{5,9},{6,10},{7,11},{8,12},{9,13},{1... | collective-permute-start | bytes 3145736 | tf_op jit(solution)/shard_map/ppermute | solution.py:194
  7.6 11.6 %collective-permute-start.18 = (bf16[256,1024]{1,0:T(8,128)(2,1)}, bf16[256,1024]{1,0:T(8,128)(2,1)S(1)}, u32[]{:S(2)}, u32[]{:S(2)}) collective-permute-start(bf16[256,1024]{1,0:T(8,128)(2,1)} %bitcast.15), channel_id=1, source_target_pairs={{4,6},{5,7},{6,4},{7,5},{8,10},{9,11},{10,8},{11,9},{12,14},{13,15... | collective-permute-start | bytes 1572872 | tf_op jit(solution)/shard_map/ppermute | solution.py:194
  17.6 2.3 %collective-permute-start.21 = (bf16[256,1024]{1,0:T(8,128)(2,1)}, bf16[256,1024]{1,0:T(8,128)(2,1)S(1)}, u32[]{:S(2)}, u32[]{:S(2)}) collective-permute-start(bf16[256,1024]{1,0:T(8,128)(2,1)} %bitcast.17), channel_id=1, source_target_pairs={{4,6},{5,7},{6,4},{7,5},{8,10},{9,11},{10,8},{11,9},{12,14},{13,15... | collective-permute-start | bytes 1572872 | tf_op jit(solution)/shard_map/ppermute | solution.py:194
  18.3 34.3 %collective-permute-start.3 = (bf16[1024,512]{1,0:T(8,128)(2,1)}, bf16[1024,512]{1,0:T(8,128)(2,1)S(1)}, u32[]{:S(2)}, u32[]{:S(2)}) collective-permute-start(bf16[1024,512]{1,0:T(8,128)(2,1)} %bitcast.33), channel_id=1, source_target_pairs={{124,128},{125,129},{126,130},{127,131}} | collective-permute-start | bytes 3145736 | tf_op jit(solution)/shard_map/ppermute | solution.py:194
  19.0 2.0 %collective-permute-start.2 = (bf16[256,1024]{1,0:T(8,128)(2,1)S(1)}, bf16[256,1024]{1,0:T(8,128)(2,1)S(1)}, u32[]{:S(2)}, u32[]{:S(2)}) collective-permute-start(bf16[256,1024]{1,0:T(8,128)(2,1)S(1)} %collective-permute-done.1.b2.refs_3_), channel_id=1, source_target_pairs={{0,1},{1,0},{2,3},{3,2},{4,5},{5,4},{6,7},{7,6},{8,9},{9,8},{10,11... | collective-permute-start | bytes 1572872 | tf_op jit(solution)/shard_map/ppermute | solution.py:194
  19.1 36.9 %collective-permute-start.23 = (bf16[1024,512]{1,0:T(8,128)(2,1)}, bf16[1024,512]{1,0:T(8,128)(2,1)S(1)}, u32[]{:S(2)}, u32[]{:S(2)}) collective-permute-start(bf16[1024,512]{1,0:T(8,128)(2,1)} %bitcast.34), channel_id=1, source_target_pairs={{8,4},{9,5},{10,6},{11,7},{12,8},{13,9},{14,10},{15,11},{16,12},{1... | collective-permute-start | bytes 3145736 | tf_op jit(solution)/shard_map/ppermute | solution.py:194
  19.9 14.7 %collective-permute-start.20 = (bf16[256,1024]{1,0:T(8,128)(2,1)}, bf16[256,1024]{1,0:T(8,128)(2,1)S(1)}, u32[]{:S(2)}, u32[]{:S(2)}) collective-permute-start(bf16[256,1024]{1,0:T(8,128)(2,1)} %bitcast.18), channel_id=1, source_target_pairs={{0,1},{1,0},{2,3},{3,2},{4,5},{5,4},{6,7},{7,6},{8,9},{9,8},{10,11... | collective-permute-start | bytes 1572872 | tf_op jit(solution)/shard_map/ppermute | solution.py:194
  21.0 33.6 %collective-permute-start.19 = (bf16[256,1024]{1,0:T(8,128)(2,1)S(1)}, bf16[256,1024]{1,0:T(8,128)(2,1)S(1)}, u32[]{:S(2)}, u32[]{:S(2)}) collective-permute-start(bf16[256,1024]{1,0:T(8,128)(2,1)S(1)} %collective-permute-done.18.refs_3_), channel_id=1, source_target_pairs={{0,1},{1,0},{2,3},{3,2},{4,5},{5,4},{6,7},{7,6},{8,9},{9,8},{10,11... | collective-permute-start | bytes 1572872 | tf_op jit(solution)/shard_map/ppermute | solution.py:194
  21.2 1.6 copy-start
  22.8 1.0 copy-start.1
  23.8 1.0 copy-start.2
  24.8 1.0 copy-start.3
  30.7 24.6 %collective-permute-start.22 = (bf16[256,1024]{1,0:T(8,128)(2,1)S(1)}, bf16[256,1024]{1,0:T(8,128)(2,1)S(1)}, u32[]{:S(2)}, u32[]{:S(2)}) collective-permute-start(bf16[256,1024]{1,0:T(8,128)(2,1)S(1)} %collective-permute-done.21.refs_7_), channel_id=1, source_target_pairs={{0,1},{1,0},{2,3},{3,2},{4,5},{5,4},{6,7},{7,6},{8,9},{9,8},{10,11... | collective-permute-start | bytes 1572872 | tf_op jit(solution)/shard_map/ppermute | solution.py:194
  34.6 30.9 %collective-permute-start.6 = (bf16[512,512]{1,0:T(8,128)(2,1)S(1)}, bf16[512,512]{1,0:T(8,128)(2,1)S(1)}, u32[]{:S(2)}, u32[]{:S(2)}) collective-permute-start(bf16[512,512]{1,0:T(8,128)(2,1)S(1)} %shard_map.98), channel_id=1, source_target_pairs={{0,4},{1,5},{2,6},{3,7}} | collective-permute-start | bytes 1572872 | tf_op jit(solution)/shard_map/ppermute | solution.py:194
  52.6 23.0 %collective-permute-start.7 = (bf16[512,512]{1,0:T(8,128)(2,1)S(1)}, bf16[512,512]{1,0:T(8,128)(2,1)S(1)}, u32[]{:S(2)}, u32[]{:S(2)}) collective-permute-start(bf16[512,512]{1,0:T(8,128)(2,1)S(1)} %shard_map.99), channel_id=1, source_target_pairs={{0,4},{1,5},{2,6},{3,7}} | collective-permute-start | bytes 1572872 | tf_op jit(solution)/shard_map/ppermute | solution.py:194
  54.6 22.9 %collective-permute-start.13 = (bf16[1024,256]{1,0:T(8,128)(2,1)S(1)}, bf16[1024,256]{1,0:T(8,128)(2,1)S(1)}, u32[]{:S(2)}, u32[]{:S(2)}) collective-permute-start(bf16[1024,256]{1,0:T(8,128)(2,1)S(1)} %get-tuple-element.35), channel_id=1, source_target_pairs={{4,8},{5,9},{6,10},{7,11},{8,12},{9,13},{10,14},{11,15},{12,16},{1... | collective-permute-start | bytes 1572872 | tf_op jit(solution)/shard_map/ppermute | solution.py:194
  55.3 24.2 %collective-permute-start.14 = (bf16[1024,256]{1,0:T(8,128)(2,1)S(1)}, bf16[1024,256]{1,0:T(8,128)(2,1)S(1)}, u32[]{:S(2)}, u32[]{:S(2)}) collective-permute-start(bf16[1024,256]{1,0:T(8,128)(2,1)S(1)} %get-tuple-element.28.refs_0_.first), channel_id=1, source_target_pairs={{124,128},{125,129},{126,130},{127,131}} | collective-permute-start | bytes 1572872 | tf_op jit(solution)/shard_map/ppermute | solution.py:194
  56.0 25.6 %collective-permute-start.27 = (bf16[256,1024]{1,0:T(8,128)(2,1)S(1)}, bf16[256,1024]{1,0:T(8,128)(2,1)S(1)}, u32[]{:S(2)}, u32[]{:S(2)}) collective-permute-start(bf16[256,1024]{1,0:T(8,128)(2,1)S(1)} %get-tuple-element.40.refs_1_), channel_id=1, source_target_pairs={{0,240},{1,241},{2,242},{3,243},{252,12},{253,13},{254,14},{255,15}} | collective-permute-start | bytes 1572872 | tf_op jit(solution)/shard_map/ppermute | solution.py:194
  65.5 23.2 %collective-permute-start.8 = (bf16[1024,256]{1,0:T(8,128)(2,1)S(1)}, bf16[1024,256]{1,0:T(8,128)(2,1)S(1)}, u32[]{:S(2)}, u32[]{:S(2)}) collective-permute-start(bf16[1024,256]{1,0:T(8,128)(2,1)S(1)} %get-tuple-element.30.refs_2_.second), channel_id=1, source_target_pairs={{124,128},{125,129},{126,130},{127,131}} | collective-permute-start | bytes 1572872 | tf_op jit(solution)/shard_map/ppermute | solution.py:194
  75.6 12.5 %collective-permute-start.5 = (bf16[1024,256]{1,0:T(8,128)(2,1)S(1)}, bf16[1024,256]{1,0:T(8,128)(2,1)S(1)}, u32[]{:S(2)}, u32[]{:S(2)}) collective-permute-start(bf16[1024,256]{1,0:T(8,128)(2,1)S(1)} %get-tuple-element.32), channel_id=1, source_target_pairs={{4,8},{5,9},{6,10},{7,11},{8,12},{9,13},{10,14},{11,15},{12,16},{1... | collective-permute-start | bytes 1572872 | tf_op jit(solution)/shard_map/ppermute | solution.py:194
  77.5 17.3 %collective-permute-start.33 = (bf16[1024,256]{1,0:T(8,128)(2,1)S(1)}, bf16[1024,256]{1,0:T(8,128)(2,1)S(1)}, u32[]{:S(2)}, u32[]{:S(2)}) collective-permute-start(bf16[1024,256]{1,0:T(8,128)(2,1)S(1)} %shard_map.109), channel_id=1, source_target_pairs={{8,4},{9,5},{10,6},{11,7},{12,8},{13,9},{14,10},{15,11},{16,12},{1... | collective-permute-start | bytes 1572872 | tf_op jit(solution)/shard_map/ppermute | solution.py:194
  79.5 21.0 %collective-permute-start.24 = (bf16[1024,256]{1,0:T(8,128)(2,1)S(1)}, bf16[1024,256]{1,0:T(8,128)(2,1)S(1)}, u32[]{:S(2)}, u32[]{:S(2)}) collective-permute-start(bf16[1024,256]{1,0:T(8,128)(2,1)S(1)} %shard_map.106), channel_id=1, source_target_pairs={{8,4},{9,5},{10,6},{11,7},{12,8},{13,9},{14,10},{15,11},{16,12},{1... | collective-permute-start | bytes 1572872 | tf_op jit(solution)/shard_map/ppermute | solution.py:194
  81.7 20.9 %collective-permute-start.30 = (bf16[256,1024]{1,0:T(8,128)(2,1)S(1)}, bf16[256,1024]{1,0:T(8,128)(2,1)S(1)}, u32[]{:S(2)}, u32[]{:S(2)}) collective-permute-start(bf16[256,1024]{1,0:T(8,128)(2,1)S(1)} %get-tuple-element.41.refs_5_), channel_id=1, source_target_pairs={{0,240},{1,241},{2,242},{3,243}} | collective-permute-start | bytes 1572872 | tf_op jit(solution)/shard_map/ppermute | solution.py:194
  88.1 15.8 %collective-permute-start.12 = (bf16[256,1024]{1,0:T(8,128)(2,1)S(1)}, bf16[256,1024]{1,0:T(8,128)(2,1)S(1)}, u32[]{:S(2)}, u32[]{:S(2)}) collective-permute-start(bf16[256,1024]{1,0:T(8,128)(2,1)S(1)} %collective-permute-done.11.rest_0_.refs_7_), channel_id=1, source_target_pairs={{252,253},{253,252},{254,255},{255,254}} | collective-permute-start | bytes 1572872 | tf_op jit(solution)/shard_map/ppermute | solution.py:194
  88.8 16.7 %collective-permute-start.15 = (bf16[1024,256]{1,0:T(8,128)(2,1)S(1)}, bf16[1024,256]{1,0:T(8,128)(2,1)S(1)}, u32[]{:S(2)}, u32[]{:S(2)}) collective-permute-start(bf16[1024,256]{1,0:T(8,128)(2,1)S(1)} %get-tuple-element.36), channel_id=1, source_target_pairs={{0,4},{1,5},{2,6},{3,7},{4,8},{5,9},{6,10},{7,11},{8,12},{9,13},{1... | collective-permute-start | bytes 1572872 | tf_op jit(solution)/shard_map/ppermute | solution.py:194
  94.8 20.0 %collective-permute-start.9 = (bf16[1024,256]{1,0:T(8,128)(2,1)S(1)}, bf16[1024,256]{1,0:T(8,128)(2,1)S(1)}, u32[]{:S(2)}, u32[]{:S(2)}) collective-permute-start(bf16[1024,256]{1,0:T(8,128)(2,1)S(1)} %get-tuple-element.33), channel_id=1, source_target_pairs={{0,4},{1,5},{2,6},{3,7},{4,8},{5,9},{6,10},{7,11},{8,12},{9,13},{1... | collective-permute-start | bytes 1572872 | tf_op jit(solution)/shard_map/ppermute | solution.py:194
  100.6 19.9 %collective-permute-start.34 = (bf16[1024,256]{1,0:T(8,128)(2,1)S(1)}, bf16[1024,256]{1,0:T(8,128)(2,1)S(1)}, u32[]{:S(2)}, u32[]{:S(2)}) collective-permute-start(bf16[1024,256]{1,0:T(8,128)(2,1)S(1)} %shard_map.110), channel_id=1, source_target_pairs={{8,4},{9,5},{10,6},{11,7},{12,8},{13,9},{14,10},{15,11},{16,12},{1... | collective-permute-start | bytes 1572872 | tf_op jit(solution)/shard_map/ppermute | solution.py:194
  102.6 24.6 %collective-permute-start.28 = (bf16[256,1024]{1,0:T(8,128)(2,1)S(1)}, bf16[256,1024]{1,0:T(8,128)(2,1)S(1)}, u32[]{:S(2)}, u32[]{:S(2)}) collective-permute-start(bf16[256,1024]{1,0:T(8,128)(2,1)S(1)} %collective-permute-done.27), channel_id=1, source_target_pairs={{240,2},{241,3},{242,0},{243,1},{12,254},{13,255},{14,252},{15,253}} | collective-permute-start | bytes 1572872 | tf_op jit(solution)/shard_map/ppermute | solution.py:194
  103.9 28.1 %collective-permute-start.31 = (bf16[256,1024]{1,0:T(8,128)(2,1)S(1)}, bf16[256,1024]{1,0:T(8,128)(2,1)S(1)}, u32[]{:S(2)}, u32[]{:S(2)}) collective-permute-start(bf16[256,1024]{1,0:T(8,128)(2,1)S(1)} %collective-permute-done.30), channel_id=1, source_target_pairs={{240,2},{241,3},{242,0},{243,1}} | collective-permute-start | bytes 1572872 | tf_op jit(solution)/shard_map/ppermute | solution.py:194
  105.5 28.4 %collective-permute-start.25 = (bf16[1024,256]{1,0:T(8,128)(2,1)S(1)}, bf16[1024,256]{1,0:T(8,128)(2,1)S(1)}, u32[]{:S(2)}, u32[]{:S(2)}) collective-permute-start(bf16[1024,256]{1,0:T(8,128)(2,1)S(1)} %shard_map.107), channel_id=1, source_target_pairs={{8,4},{9,5},{10,6},{11,7},{12,8},{13,9},{14,10},{15,11},{16,12},{1... | collective-permute-start | bytes 1572872 | tf_op jit(solution)/shard_map/ppermute | solution.py:194
  114.8 21.7 %collective-permute-start.16 = (bf16[1024,256]{1,0:T(8,128)(2,1)S(1)}, bf16[1024,256]{1,0:T(8,128)(2,1)S(1)}, u32[]{:S(2)}, u32[]{:S(2)}) collective-permute-start(bf16[1024,256]{1,0:T(8,128)(2,1)S(1)} %get-tuple-element.37), channel_id=1, source_target_pairs={{0,4},{1,5},{2,6},{3,7},{4,8},{5,9},{6,10},{7,11},{8,12},{9,13},{1... | collective-permute-start | bytes 1572872 | tf_op jit(solution)/shard_map/ppermute | solution.py:194
  120.5 19.4 %collective-permute-start.10 = (bf16[1024,256]{1,0:T(8,128)(2,1)S(1)}, bf16[1024,256]{1,0:T(8,128)(2,1)S(1)}, u32[]{:S(2)}, u32[]{:S(2)}) collective-permute-start(bf16[1024,256]{1,0:T(8,128)(2,1)S(1)} %get-tuple-element.34), channel_id=1, source_target_pairs={{0,4},{1,5},{2,6},{3,7},{4,8},{5,9},{6,10},{7,11},{8,12},{9,13},{1... | collective-permute-start | bytes 1572872 | tf_op jit(solution)/shard_map/ppermute | solution.py:194
  127.1 14.9 %collective-permute-start.29 = (bf16[256,1024]{1,0:T(8,128)(2,1)S(1)}, bf16[256,1024]{1,0:T(8,128)(2,1)S(1)}, u32[]{:S(2)}, u32[]{:S(2)}) collective-permute-start(bf16[256,1024]{1,0:T(8,128)(2,1)S(1)} %collective-permute-done.28.refs_12_), channel_id=1, source_target_pairs={{0,1},{1,0},{2,3},{3,2},{252,253},{253,252},{254,255},{255,254}} | collective-permute-start | bytes 1572872 | tf_op jit(solution)/shard_map/ppermute | solution.py:194
  132.0 10.0 %collective-permute-start.32 = (bf16[256,1024]{1,0:T(8,128)(2,1)S(1)}, bf16[256,1024]{1,0:T(8,128)(2,1)S(1)}, u32[]{:S(2)}, u32[]{:S(2)}) collective-permute-start(bf16[256,1024]{1,0:T(8,128)(2,1)S(1)} %collective-permute-done.31.refs_14_), channel_id=1, source_target_pairs={{0,1},{1,0},{2,3},{3,2}} | collective-permute-start | bytes 1572872 | tf_op jit(solution)/shard_map/ppermute | solution.py:194
  133.9 16.7 %collective-permute-start.35 = (bf16[1024,256]{1,0:T(8,128)(2,1)S(1)}, bf16[1024,256]{1,0:T(8,128)(2,1)S(1)}, u32[]{:S(2)}, u32[]{:S(2)}) collective-permute-start(bf16[1024,256]{1,0:T(8,128)(2,1)S(1)} %shard_map.111), channel_id=1, source_target_pairs={{4,0},{5,1},{6,2},{7,3},{8,4},{9,5},{10,6},{11,7},{12,8},{13,9},{1... | collective-permute-start | bytes 1572872 | tf_op jit(solution)/shard_map/ppermute | solution.py:194
  136.5 24.9 %collective-permute-start.26 = (bf16[1024,256]{1,0:T(8,128)(2,1)S(1)}, bf16[1024,256]{1,0:T(8,128)(2,1)S(1)}, u32[]{:S(2)}, u32[]{:S(2)}) collective-permute-start(bf16[1024,256]{1,0:T(8,128)(2,1)S(1)} %shard_map.108), channel_id=1, source_target_pairs={{4,0},{5,1},{6,2},{7,3},{8,4},{9,5},{10,6},{11,7},{12,8},{13,9},{1... | collective-permute-start | bytes 1572872 | tf_op jit(solution)/shard_map/ppermute | solution.py:194

commit v4 on v3

--- a/solution.py
+++ b/solution.py
@@ -50,29 +50,33 @@
     )(*arrays)
 
 
-def near_kernel(plan, own, near, received, sources, new):
-    core = lax.axis_index("shot") % 2
-
-    @pl.when(lax.axis_index("layer") == 0)
-    def _():
-        down_in = injected(received[...], sources[plan[0, 0]])
-        for k, block in enumerate((own, near)):
-            new[band(core ^ k, block.shape[0]), :] = dot(block[...], down_in).astype(BF16)
-
-
-def far_kernel(_, first, second, new):
-    rows = band(1 - lax.axis_index("shot") // 2, new.shape[0])
-
-    @pl.when(lax.axis_index("layer") == 0)
-    def _():
-        for chunk, ref in enumerate((first, second)):
-            new[:, columns(new, chunk, ref.shape[1])] = ref[rows, :]
-
-
 def products(blocks, down_in, new):
     spot = lax.axis_index("shot")
     for k, block in enumerate(blocks):
         new[band(spot ^ k, block.shape[0]), :] = dot(block[...], down_in[...]).astype(BF16)
+
+
+def first_kernel(chunk, plan, b0, b1, b2, b3, received, sources, *rest):
+    pair, (new, down_in) = rest[:-2], rest[-2:]
+    layer, core = lax.axis_index("layer"), lax.axis_index("shot") % 2
+    width = down_in.shape[1]
+
+    def injection(cols):
+        return injected(received[:, cols], sources[plan[0, 0], :, cols])
+
+    down_in[...] = injection(columns(sources, chunk, width))
+
+    @pl.when(layer == 0)
+    def _():
+        for other in range(CHUNKS):
+            value = injection(columns(sources, other, width))
+            for k, block in enumerate(pair or (b0, b1)):
+                high = block.shape[0]
+                new[band(other * 2 + (core ^ k), high), :] = dot(block[...], value).astype(BF16)
+
+    @pl.when(layer != 0)
+    def _():
+        products((b0, b1, b2, b3), down_in, new)
 
 
 def fix_kernel(plan, b0, b1, b2, b3, received, sources, *refs):
@@ -103,21 +107,23 @@
     spot = lax.axis_index("shot")
     cols = columns(sources, chunk, down_in.shape[1])
 
-    def take(ref, rows=slice(None)):
+    def take(ref):
         value = ref[:, columns(ref, chunk, down_in.shape[1])]
-        down_in[rows, :] = injected(value, sources[plan[0, moment], rows, cols])
+        down_in[...] = injected(value, sources[plan[0, moment], :, cols])
 
     if moment == 1:
-        near, far, middle = others
 
         @pl.when(layer == 1)
         def _():
-            for k, ref in enumerate((near, far)):
-                take(ref, band((spot // 2) ^ k, ref.shape[0]))
+            for k, ref in enumerate(others[:2]):
+                half = ref.shape[0] // 2
+                rows = band((spot // 2) ^ k, half)
+                value = ref[chunk * half : (chunk + 1) * half, :]
+                down_in[rows, :] = injected(value, sources[plan[0, moment], rows, cols])
 
         @pl.when(layer == count // 2)
         def _():
-            take(middle)
+            take(others[chunk])
 
         @pl.when(jnp.logical_and(layer != 1, layer != count // 2))
         def _():
@@ -127,6 +133,8 @@
         take(received)
     for k, block in enumerate((b0, b1, b2, b3)):
         high, value = block.shape[0], block[...]
+        if k >= 2:
+            value = jnp.where(layer == 0, others[k - 4][...], value)
         if moment == TICKS - 1 and k >= 2:
             value = jnp.where(layer == count - 1, others[k - 2][...], value)
         new[band(spot ^ k, high), :] = dot(value, down_in[...]).astype(BF16)
@@ -222,8 +230,10 @@
     cut = layers // 2
     down_0b = link(down_state[0], [(cut - 1, cut)], 0)
     down_0 = shift(down_state[0], 1, [cut - 1])
-    far_d = swap(down_op, 2, [0] + middle)
-    up_0 = shift(up_state[0], -1, [1])
+    far_d = swap(down_op, 2, middle)
+    far_0 = swap(down_op, 2, [0])
+    cross_0 = swap(far_0, 1, [0])
+    up_0 = shift(up_state[0], -1, [1, 2, 3])
     far_e = swap(down_op, 2, [layers - 1])
     cross_e = swap(far_e, 1, [layers - 1])
     near_d = swap(down_op, 1, every)
@@ -245,21 +255,18 @@
         op = link(op, pairs, 0)
         op = link(op, [(b, a) for a, b in pairs], 2)
         late += [op, link(op, [(a, a) for a, _ in pairs], 1)]
-    half = (height // 2, wide)
     piece = (height, width)
-    (near,) = call(near_kernel, plan, [down_op, near_d, down_0, sources], [half], one // 8)
-    near = link(near, [(0, 1)], 0)
-    firsts, middles = [], []
+    firsts, specials = [], []
     for chunk in range(CHUNKS):
         new, down_in = call(
-            functools.partial(down_kernel, 0, chunk), plan,
-            [*d_blocks, down_0, sources], [piece] * 2, one,
+            functools.partial(first_kernel, chunk), plan,
+            [*d_blocks, down_0, sources], [piece] * 2, one, more=[far_0, cross_0] if chunk else [],
         )
         firsts += [new, down_in]
-        middles.append(link(new, [(cut - 1, cut)], 0))
-    (far,) = call(far_kernel, layer_source, [firsts[0], firsts[2]], [half], one // 8)
-    far = link(far, [(0, 1)], 0)
-    firsts = call(fix_kernel, plan, [*d_blocks, down_0b, sources, *firsts], [piece] * (2 * CHUNKS), one // 8)
+        specials.append(link(new, [(0, 1), (cut - 1, cut)], 0))
+    firsts = call(
+        fix_kernel, plan, [*d_blocks, down_0b, sources, *firsts], [piece] * (2 * CHUNKS), one // 8
+    )
     downs = [shift(firsts[2 * i], 1, [0, cut - 1]) for i in range(CHUNKS)]
     ups = [up_0] * CHUNKS
     for moment in range(TICKS):
@@ -268,11 +275,11 @@
         for chunk in range(CHUNKS):
             full = (chunk, wide) if last else None
             if moment:
-                more = [near, far, middles[chunk]] if moment == 1 else [far_e, cross_e] if last else []
+                more = specials if moment == 1 else [far_e, cross_e] if last else []
                 new, down_in = call(
                     functools.partial(down_kernel, moment, chunk), plan,
                     [*d_blocks, downs[chunk], sources], [piece] * 2, one,
-                    full=full, into=new if last else None, more=more,
+                    full=full, into=new if last else None, more=[*more, far_0, cross_0],
                 )
                 new_downs.append(new)
             else:
@@ -287,7 +294,7 @@
             return (new[None], up[None])
         if moment:
             downs = [shift(a, 1) for a in new_downs]
-        without_top = [] if moment == TICKS - 2 else [1]
+        without_top = range(1, TICKS - 1 - moment)
         ups = [shift(a, -1, without_top) for a in new_ups]
 
 

time: 166 us -> 170 us (1.024)
  the two profiles are of different devices: /device:TPU:8 before, /device:TPU:24 now
where the time goes in v4:
time: 170 us; the launch traced here: 169 us
  starting transfers between devices  74.5 us (44%)
  waiting for transfers between devices  61.7 us (36%)
  Pallas kernels  26.6 us (16%)
  local copies, waits for them, and re-layouts  4.72 us (3%)
  between operations  1.81 us (1%)
    ppermute x36, starting transfers between devices, sent(): return lax.ppermute(value, ('layer', 'shot'), pairs)  74.5 us
    ppermute x36, waiting for transfers between devices, sent(): return lax.ppermute(value, ('layer', 'shot'), pairs)  61.7 us
    pallas_call x17, Pallas kernels, call(): pl.pallas_call(kernel, grid=(1,), in_specs=in_specs, out_specs=out_specs,...  26.3 us
    unnamed x12, local copies, waits for them, and re-layouts  4.72 us
  transfers between devices with their start and end apart: 36, of which 14 were waited for; matrix products, arithmetic and copies ran while one was open for 0% of the time, Pallas kernels for 14%

profile of v4, /device:TPU:24, one launch (start us, length us, event | category | flops | bytes accessed | tf_op | source)
XLA Modules:
  0.0 169.3 jit_solution(12944511898621740273)
XLA Ops:
  0.7 2.7 %collective-permute-start.1 = (bf16[256,1024]{1,0:T(8,128)(2,1)}, bf16[256,1024]{1,0:T(8,128)(2,1)S(1)}, u32[]{:S(2)}, u32[]{:S(2)}) collective-permute-start(bf16[256,1024]{1,0:T(8,128)(2,1)} %bitcast.17), channel_id=1, source_target_pairs={{4,6},{5,7},{6,4},{7,5},{8,10},{9,11},{10,8},{11,9},{12,14},{13,15... | collective-permute-start | bytes 1572872 | tf_op jit(solution)/shard_map/ppermute | solution.py:202
  4.4 3.2 %collective-permute-start.18 = (bf16[256,1024]{1,0:T(8,128)(2,1)}, bf16[256,1024]{1,0:T(8,128)(2,1)S(1)}, u32[]{:S(2)}, u32[]{:S(2)}) collective-permute-start(bf16[256,1024]{1,0:T(8,128)(2,1)} %bitcast.11), channel_id=1, source_target_pairs={{4,6},{5,7},{6,4},{7,5},{8,10},{9,11},{10,8},{11,9},{12,14},{13,15... | collective-permute-start | bytes 1572872 | tf_op jit(solution)/shard_map/ppermute | solution.py:202
  7.6 3.5 %collective-permute-start.4 = (bf16[1024,512]{1,0:T(8,128)(2,1)}, bf16[1024,512]{1,0:T(8,128)(2,1)S(1)}, u32[]{:S(2)}, u32[]{:S(2)}) collective-permute-start(bf16[1024,512]{1,0:T(8,128)(2,1)} %bitcast.32), channel_id=1, source_target_pairs={{0,4},{1,5},{2,6},{3,7},{4,8},{5,9},{6,10},{7,11},{8,12},{9,13},{1... | collective-permute-start | bytes 3145736 | tf_op jit(solution)/shard_map/ppermute | solution.py:202
  11.1 6.6 %collective-permute-done.1.b2.refs_3_ = bf16[256,1024]{1,0:T(8,128)(2,1)S(1)} collective-permute-done((bf16[256,1024]{1,0:T(8,128)(2,1)}, bf16[256,1024]{1,0:T(8,128)(2,1)S(1)}, u32[]{:S(2)}, u32[]{:S(2)}) %collective-permute-start.1) | collective-permute-done | bytes 524320 | tf_op jit(solution)/shard_map/ppermute | solution.py:202
  17.7 2.6 %collective-permute-start.21 = (bf16[256,1024]{1,0:T(8,128)(2,1)}, bf16[256,1024]{1,0:T(8,128)(2,1)S(1)}, u32[]{:S(2)}, u32[]{:S(2)}) collective-permute-start(bf16[256,1024]{1,0:T(8,128)(2,1)} %bitcast.14), channel_id=1, source_target_pairs={{4,6},{5,7},{6,4},{7,5},{8,10},{9,11},{10,8},{11,9},{12,14},{13,15... | collective-permute-start | bytes 1572872 | tf_op jit(solution)/shard_map/ppermute | solution.py:202
  20.3 1.3 collective-permute-start.3
  21.6 7.3 %collective-permute-done.18.refs_3_ = bf16[256,1024]{1,0:T(8,128)(2,1)S(1)} collective-permute-done((bf16[256,1024]{1,0:T(8,128)(2,1)}, bf16[256,1024]{1,0:T(8,128)(2,1)S(1)}, u32[]{:S(2)}, u32[]{:S(2)}) %collective-permute-start.18) | collective-permute-done | bytes 524320 | tf_op jit(solution)/shard_map/ppermute | solution.py:202
  28.9 10.6 %collective-permute-start.23 = (bf16[1024,512]{1,0:T(8,128)(2,1)}, bf16[1024,512]{1,0:T(8,128)(2,1)S(1)}, u32[]{:S(2)}, u32[]{:S(2)}) collective-permute-start(bf16[1024,512]{1,0:T(8,128)(2,1)} %bitcast.34), channel_id=1, source_target_pairs={{16,12},{17,13},{18,14},{19,15},{20,16},{21,17},{22,18},{23,19},{2... | collective-permute-start | bytes 3145736 | tf_op jit(solution)/shard_map/ppermute | solution.py:202
  40.6 1.6 copy-done
  46.0 1.4 shard_map.95
  47.4 1.3 collective-permute-start.8
  48.7 1.4 shard_map.96
  50.1 3.6 %collective-permute-done.3.received = bf16[1024,512]{1,0:T(8,128)(2,1)S(1)} collective-permute-done((bf16[1024,512]{1,0:T(8,128)(2,1)}, bf16[1024,512]{1,0:T(8,128)(2,1)S(1)}, u32[]{:S(2)}, u32[]{:S(2)}) %collective-permute-start.3) | collective-permute-done | bytes 1048608 | tf_op jit(solution)/shard_map/ppermute | solution.py:202
  53.8 1.3 collective-permute-start.9
  55.1 1.9 %shard_map.97 = (bf16[1024,256]{1,0:T(8,128)(2,1)S(1)}, bf16[1024,256]{1,0:T(8,128)(2,1)S(1)}, bf16[1024,256]{1,0:T(8,128)(2,1)S(1)}, bf16[1024,256]{1,0:T(8,128)(2,1)S(1)}) custom-call(s32[1,4]{1,0:T(1,128)S(1)} %bitcast.23, bf16[256,1024]{1,0:T(8,128)(2,1)S(1)} %get-tuple-element.26.b0.refs_1_, bf16[256,1024]{1,0:T(8,128)(2,1)S(1)} %collective-permute-done.b1.refs_2_, ...), custom_call_target="tpu_custom_call" | custom-call | flops 67108864 | bytes 1048576 | tf_op jit(solution)/shard_map/pallas_call | solution.py:182
  56.9 1.3 collective-permute-start.14
  59.6 3.2 %collective-permute-done.23.refs_9_ = bf16[1024,512]{1,0:T(8,128)(2,1)S(1)} collective-permute-done((bf16[1024,512]{1,0:T(8,128)(2,1)}, bf16[1024,512]{1,0:T(8,128)(2,1)S(1)}, u32[]{:S(2)}, u32[]{:S(2)}) %collective-permute-start.23) | collective-permute-done | bytes 1048608 | tf_op jit(solution)/shard_map/ppermute | solution.py:202
  63.6 6.6 %collective-permute-done.8.rest_0_ = bf16[1024,256]{1,0:T(8,128)(2,1)S(1)} collective-permute-done((bf16[1024,256]{1,0:T(8,128)(2,1)S(1)}, bf16[1024,256]{1,0:T(8,128)(2,1)S(1)}, u32[]{:S(2)}, u32[]{:S(2)}) %collective-permute-start.8) | collective-permute-done | bytes 524320 | tf_op jit(solution)/shard_map/ppermute | solution.py:202
  70.2 1.3 collective-permute-start.7
  71.5 1.3 shard_map.107
  72.8 8.0 %collective-permute-done.9.rest_1_ = bf16[1024,256]{1,0:T(8,128)(2,1)S(1)} collective-permute-done((bf16[1024,256]{1,0:T(8,128)(2,1)S(1)}, bf16[1024,256]{1,0:T(8,128)(2,1)S(1)}, u32[]{:S(2)}, u32[]{:S(2)}) %collective-permute-start.9) | collective-permute-done | bytes 524320 | tf_op jit(solution)/shard_map/ppermute | solution.py:202
  80.8 1.9 %collective-permute-start.33 = (bf16[1024,256]{1,0:T(8,128)(2,1)S(1)}, bf16[1024,256]{1,0:T(8,128)(2,1)S(1)}, u32[]{:S(2)}, u32[]{:S(2)}) collective-permute-start(bf16[1024,256]{1,0:T(8,128)(2,1)S(1)} %shard_map.107), channel_id=1, source_target_pairs={{12,8},{13,9},{14,10},{15,11},{16,12},{17,13},{18,14},{19,15},{20,... | collective-permute-start | bytes 1572872 | tf_op jit(solution)/shard_map/ppermute | solution.py:202
  82.7 1.3 shard_map.104
  84.0 1.9 %collective-permute-start.24 = (bf16[1024,256]{1,0:T(8,128)(2,1)S(1)}, bf16[1024,256]{1,0:T(8,128)(2,1)S(1)}, u32[]{:S(2)}, u32[]{:S(2)}) collective-permute-start(bf16[1024,256]{1,0:T(8,128)(2,1)S(1)} %shard_map.104), channel_id=1, source_target_pairs={{12,8},{13,9},{14,10},{15,11},{16,12},{17,13},{18,14},{19,15},{20,... | collective-permute-start | bytes 1572872 | tf_op jit(solution)/shard_map/ppermute | solution.py:202
  85.9 1.4 shard_map.100
  89.0 3.9 %collective-permute-start.15 = (bf16[1024,256]{1,0:T(8,128)(2,1)S(1)}, bf16[1024,256]{1,0:T(8,128)(2,1)S(1)}, u32[]{:S(2)}, u32[]{:S(2)}) collective-permute-start(bf16[1024,256]{1,0:T(8,128)(2,1)S(1)} %get-tuple-element.36), channel_id=1, source_target_pairs={{0,4},{1,5},{2,6},{3,7},{4,8},{5,9},{6,10},{7,11},{8,12},{9,13},{1... | collective-permute-start | bytes 1572872 | tf_op jit(solution)/shard_map/ppermute | solution.py:202
  92.9 1.4 shard_map.98
  94.3 3.1 %collective-permute-done.33.refs_9_ = bf16[1024,256]{1,0:T(8,128)(2,1)S(1)} collective-permute-done((bf16[1024,256]{1,0:T(8,128)(2,1)S(1)}, bf16[1024,256]{1,0:T(8,128)(2,1)S(1)}, u32[]{:S(2)}, u32[]{:S(2)}) %collective-permute-start.33) | collective-permute-done | bytes 524320 | tf_op jit(solution)/shard_map/ppermute | solution.py:202
  97.5 1.9 %collective-permute-start.10 = (bf16[1024,256]{1,0:T(8,128)(2,1)S(1)}, bf16[1024,256]{1,0:T(8,128)(2,1)S(1)}, u32[]{:S(2)}, u32[]{:S(2)}) collective-permute-start(bf16[1024,256]{1,0:T(8,128)(2,1)S(1)} %get-tuple-element.33), channel_id=1, source_target_pairs={{0,4},{1,5},{2,6},{3,7},{4,8},{5,9},{6,10},{7,11},{8,12},{9,13},{1... | collective-permute-start | bytes 1572872 | tf_op jit(solution)/shard_map/ppermute | solution.py:202
  99.4 1.3 shard_map.108
  100.7 6.5 %collective-permute-done.24.refs_9_ = bf16[1024,256]{1,0:T(8,128)(2,1)S(1)} collective-permute-done((bf16[1024,256]{1,0:T(8,128)(2,1)S(1)}, bf16[1024,256]{1,0:T(8,128)(2,1)S(1)}, u32[]{:S(2)}, u32[]{:S(2)}) %collective-permute-start.24) | collective-permute-done | bytes 524320 | tf_op jit(solution)/shard_map/ppermute | solution.py:202
  107.2 7.9 %collective-permute-start.34 = (bf16[1024,256]{1,0:T(8,128)(2,1)S(1)}, bf16[1024,256]{1,0:T(8,128)(2,1)S(1)}, u32[]{:S(2)}, u32[]{:S(2)}) collective-permute-start(bf16[1024,256]{1,0:T(8,128)(2,1)S(1)} %shard_map.108), channel_id=1, source_target_pairs={{8,4},{9,5},{10,6},{11,7},{12,8},{13,9},{14,10},{15,11},{16,12},{1... | collective-permute-start | bytes 1572872 | tf_op jit(solution)/shard_map/ppermute | solution.py:202
  117.8 1.9 %collective-permute-start.25 = (bf16[1024,256]{1,0:T(8,128)(2,1)S(1)}, bf16[1024,256]{1,0:T(8,128)(2,1)S(1)}, u32[]{:S(2)}, u32[]{:S(2)}) collective-permute-start(bf16[1024,256]{1,0:T(8,128)(2,1)S(1)} %shard_map.105), channel_id=1, source_target_pairs={{8,4},{9,5},{10,6},{11,7},{12,8},{13,9},{14,10},{15,11},{16,12},{1... | collective-permute-start | bytes 1572872 | tf_op jit(solution)/shard_map/ppermute | solution.py:202
  119.7 1.3 shard_map.101
  121.1 3.9 %collective-permute-start.16 = (bf16[1024,256]{1,0:T(8,128)(2,1)S(1)}, bf16[1024,256]{1,0:T(8,128)(2,1)S(1)}, u32[]{:S(2)}, u32[]{:S(2)}) collective-permute-start(bf16[1024,256]{1,0:T(8,128)(2,1)S(1)} %get-tuple-element.37), channel_id=1, source_target_pairs={{0,4},{1,5},{2,6},{3,7},{4,8},{5,9},{6,10},{7,11},{8,12},{9,13},{1... | collective-permute-start | bytes 1572872 | tf_op jit(solution)/shard_map/ppermute | solution.py:202
  125.0 1.3 shard_map.99
  127.4 1.9 %collective-permute-start.11 = (bf16[1024,256]{1,0:T(8,128)(2,1)S(1)}, bf16[1024,256]{1,0:T(8,128)(2,1)S(1)}, u32[]{:S(2)}, u32[]{:S(2)}) collective-permute-start(bf16[1024,256]{1,0:T(8,128)(2,1)S(1)} %get-tuple-element.34), channel_id=1, source_target_pairs={{0,4},{1,5},{2,6},{3,7},{4,8},{5,9},{6,10},{7,11},{8,12},{9,13},{1... | collective-permute-start | bytes 1572872 | tf_op jit(solution)/shard_map/ppermute | solution.py:202
  129.3 1.3 shard_map.109
  132.0 4.5 %collective-permute-done.25.refs_9_ = bf16[1024,256]{1,0:T(8,128)(2,1)S(1)} collective-permute-done((bf16[1024,256]{1,0:T(8,128)(2,1)S(1)}, bf16[1024,256]{1,0:T(8,128)(2,1)S(1)}, u32[]{:S(2)}, u32[]{:S(2)}) %collective-permute-start.25) | collective-permute-done | bytes 524320 | tf_op jit(solution)/shard_map/ppermute | solution.py:202
  136.5 10.1 %collective-permute-start.35 = (bf16[1024,256]{1,0:T(8,128)(2,1)S(1)}, bf16[1024,256]{1,0:T(8,128)(2,1)S(1)}, u32[]{:S(2)}, u32[]{:S(2)}) collective-permute-start(bf16[1024,256]{1,0:T(8,128)(2,1)S(1)} %shard_map.109), channel_id=1, source_target_pairs={{4,0},{5,1},{6,2},{7,3},{8,4},{9,5},{10,6},{11,7},{12,8},{13,9},{1... | collective-permute-start | bytes 1572872 | tf_op jit(solution)/shard_map/ppermute | solution.py:202
  146.6 1.3 shard_map.106
  147.9 1.9 %collective-permute-start.26 = (bf16[1024,256]{1,0:T(8,128)(2,1)S(1)}, bf16[1024,256]{1,0:T(8,128)(2,1)S(1)}, u32[]{:S(2)}, u32[]{:S(2)}) collective-permute-start(bf16[1024,256]{1,0:T(8,128)(2,1)S(1)} %shard_map.106), channel_id=1, source_target_pairs={{4,0},{5,1},{6,2},{7,3},{8,4},{9,5},{10,6},{11,7},{12,8},{13,9},{1... | collective-permute-start | bytes 1572872 | tf_op jit(solution)/shard_map/ppermute | solution.py:202
  149.9 2.2 %shard_map.102 = (bf16[1024,512]{1,0:T(8,128)(2,1)}, bf16[1024,256]{1,0:T(8,128)(2,1)S(1)}) custom-call(s32[1,4]{1,0:T(1,128)S(1)} %bitcast.28, bf16[256,1024]{1,0:T(8,128)(2,1)S(1)} %get-tuple-element.26.b0.refs_1_, bf16[256,1024]{1,0:T(8,128)(2,1)S(1)} %collective-permute-done.b1.refs_2_, bf16[256,1024]{1,0:T(8,128)(2,1)S(1)} %collective-permute-done.1.b2.refs_3_, ...), custom_call_target="tpu_custom_call" | custom-call | flops 536870912 | bytes 1048576 | tf_op jit(solution)/shard_map/pallas_call | solution.py:182
  152.3 2.2 %shard_map.103 = (bf16[1024,512]{1,0:T(8,128)(2,1)}, bf16[1024,256]{1,0:T(8,128)(2,1)S(1)}) custom-call(s32[1,4]{1,0:T(1,128)S(1)} %bitcast.29, bf16[256,1024]{1,0:T(8,128)(2,1)S(1)} %get-tuple-element.26.b0.refs_1_, bf16[256,1024]{1,0:T(8,128)(2,1)S(1)} %collective-permute-done.b1.refs_2_, ...), custom_call_target="tpu_custom_call", output_to_operand_aliasing={{0}: (11, {})} | custom-call | flops 536870912 | bytes 1048576 | tf_op jit(solution)/shard_map/pallas_call | solution.py:182
  154.5 4.4 %collective-permute-done.35.refs_9_ = bf16[1024,256]{1,0:T(8,128)(2,1)S(1)} collective-permute-done((bf16[1024,256]{1,0:T(8,128)(2,1)S(1)}, bf16[1024,256]{1,0:T(8,128)(2,1)S(1)}, u32[]{:S(2)}, u32[]{:S(2)}) %collective-permute-start.35) | collective-permute-done | bytes 524320 | tf_op jit(solution)/shard_map/ppermute | solution.py:202
  158.9 2.1 %shard_map.110.refs_16_ = bf16[1024,512]{1,0:T(8,128)(2,1)} custom-call(s32[1]{0:T(128)S(6)} %copy.14.refs_0_, bf16[256,1024]{1,0:T(8,128)(2,1)S(1)} %get-tuple-element.40.refs_1_, bf16[256,1024]{1,0:T(8,128)(2,1)S(1)} %collective-permute-done.17.refs_2_, bf16[256,1024]{1,0:T(8,128)(2,1)S(1)} %collective-permute-done.18.refs_3_, ...), custom_call_target="tpu_custom_call" | custom-call | flops 1073741824 | bytes 1048576 | tf_op jit(solution)/shard_map/pallas_call | solution.py:182
  161.0 6.2 %collective-permute-done.26.refs_9_ = bf16[1024,256]{1,0:T(8,128)(2,1)S(1)} collective-permute-done((bf16[1024,256]{1,0:T(8,128)(2,1)S(1)}, bf16[1024,256]{1,0:T(8,128)(2,1)S(1)}, u32[]{:S(2)}, u32[]{:S(2)}) %collective-permute-start.26) | collective-permute-done | bytes 524320 | tf_op jit(solution)/shard_map/ppermute | solution.py:202
  167.2 2.1 %shard_map.111 = bf16[1024,512]{1,0:T(8,128)(2,1)} custom-call(s32[1]{0:T(128)S(6)} %copy.14.refs_0_, bf16[256,1024]{1,0:T(8,128)(2,1)S(1)} %get-tuple-element.40.refs_1_, bf16[256,1024]{1,0:T(8,128)(2,1)S(1)} %collective-permute-done.17.refs_2_, bf16[256,1024]{1,0:T(8,128)(2,1)S(1)} %collective-permute-done.18.refs_3_, ...), custom_call_target="tpu_custom_call", output_to_operand_aliasing={{}: (16, {})} | custom-call | flops 1073741824 | bytes 1048576 | tf_op jit(solution)/shard_map/pallas_call | solution.py:182
  (54 shorter events, 14.5 us)
Async XLA Ops:
  0.6 45.4 %copy-start.5 = (s32[4,1]{0,1:T(1,128)S(1)}, s32[4,1]{0,1:T(1,128)}, u32[]{:S(2)}) copy-start(s32[4,1]{0,1:T(1,128)} %param.14) | copy-start | bytes 52
  0.6 6.9 %collective-permute-start = (bf16[256,1024]{1,0:T(8,128)(2,1)}, bf16[256,1024]{1,0:T(8,128)(2,1)S(1)}, u32[]{:S(2)}, u32[]{:S(2)}) collective-permute-start(bf16[256,1024]{1,0:T(8,128)(2,1)} %bitcast.16), channel_id=1, source_target_pairs={{0,1},{1,0},{2,3},{3,2},{4,5},{5,4},{6,7},{7,6},{8,9},{9,8},{10,11... | collective-permute-start | bytes 1572872 | tf_op jit(solution)/shard_map/ppermute | solution.py:202
  0.7 16.9 %collective-permute-start.1 = (bf16[256,1024]{1,0:T(8,128)(2,1)}, bf16[256,1024]{1,0:T(8,128)(2,1)S(1)}, u32[]{:S(2)}, u32[]{:S(2)}) collective-permute-start(bf16[256,1024]{1,0:T(8,128)(2,1)} %bitcast.17), channel_id=1, source_target_pairs={{4,6},{5,7},{6,4},{7,5},{8,10},{9,11},{10,8},{11,9},{12,14},{13,15... | collective-permute-start | bytes 1572872 | tf_op jit(solution)/shard_map/ppermute | solution.py:202
  3.4 14.2 %collective-permute-start.5 = (bf16[256,1024]{1,0:T(8,128)(2,1)}, bf16[256,1024]{1,0:T(8,128)(2,1)S(1)}, u32[]{:S(2)}, u32[]{:S(2)}) collective-permute-start(bf16[256,1024]{1,0:T(8,128)(2,1)} %bitcast.18), channel_id=1, source_target_pairs={{0,2},{1,3},{2,0},{3,1}} | collective-permute-start | bytes 1572872 | tf_op jit(solution)/shard_map/ppermute | solution.py:202
  4.1 16.2 %collective-permute-start.17 = (bf16[256,1024]{1,0:T(8,128)(2,1)}, bf16[256,1024]{1,0:T(8,128)(2,1)S(1)}, u32[]{:S(2)}, u32[]{:S(2)}) collective-permute-start(bf16[256,1024]{1,0:T(8,128)(2,1)} %bitcast.10), channel_id=1, source_target_pairs={{0,1},{1,0},{2,3},{3,2},{4,5},{5,4},{6,7},{7,6},{8,9},{9,8},{10,11... | collective-permute-start | bytes 1572872 | tf_op jit(solution)/shard_map/ppermute | solution.py:202
  4.4 24.5 %collective-permute-start.18 = (bf16[256,1024]{1,0:T(8,128)(2,1)}, bf16[256,1024]{1,0:T(8,128)(2,1)S(1)}, u32[]{:S(2)}, u32[]{:S(2)}) collective-permute-start(bf16[256,1024]{1,0:T(8,128)(2,1)} %bitcast.11), channel_id=1, source_target_pairs={{4,6},{5,7},{6,4},{7,5},{8,10},{9,11},{10,8},{11,9},{12,14},{13,15... | collective-permute-start | bytes 1572872 | tf_op jit(solution)/shard_map/ppermute | solution.py:202
  7.6 38.0 %collective-permute-start.4 = (bf16[1024,512]{1,0:T(8,128)(2,1)}, bf16[1024,512]{1,0:T(8,128)(2,1)S(1)}, u32[]{:S(2)}, u32[]{:S(2)}) collective-permute-start(bf16[1024,512]{1,0:T(8,128)(2,1)} %bitcast.32), channel_id=1, source_target_pairs={{0,4},{1,5},{2,6},{3,7},{4,8},{5,9},{6,10},{7,11},{8,12},{9,13},{1... | collective-permute-start | bytes 3145736 | tf_op jit(solution)/shard_map/ppermute | solution.py:202
  17.6 11.2 %collective-permute-start.20 = (bf16[256,1024]{1,0:T(8,128)(2,1)}, bf16[256,1024]{1,0:T(8,128)(2,1)S(1)}, u32[]{:S(2)}, u32[]{:S(2)}) collective-permute-start(bf16[256,1024]{1,0:T(8,128)(2,1)} %bitcast.13), channel_id=1, source_target_pairs={{0,1},{1,0},{2,3},{3,2},{4,5},{5,4},{6,7},{7,6},{8,9},{9,8},{10,11... | collective-permute-start | bytes 1572872 | tf_op jit(solution)/shard_map/ppermute | solution.py:202
  17.7 22.0 %collective-permute-start.21 = (bf16[256,1024]{1,0:T(8,128)(2,1)}, bf16[256,1024]{1,0:T(8,128)(2,1)S(1)}, u32[]{:S(2)}, u32[]{:S(2)}) collective-permute-start(bf16[256,1024]{1,0:T(8,128)(2,1)} %bitcast.14), channel_id=1, source_target_pairs={{4,6},{5,7},{6,4},{7,5},{8,10},{9,11},{10,8},{11,9},{12,14},{13,15... | collective-permute-start | bytes 1572872 | tf_op jit(solution)/shard_map/ppermute | solution.py:202
  20.3 33.5 %collective-permute-start.3 = (bf16[1024,512]{1,0:T(8,128)(2,1)}, bf16[1024,512]{1,0:T(8,128)(2,1)S(1)}, u32[]{:S(2)}, u32[]{:S(2)}) collective-permute-start(bf16[1024,512]{1,0:T(8,128)(2,1)} %bitcast.33), channel_id=1, source_target_pairs={{124,128},{125,129},{126,130},{127,131}} | collective-permute-start | bytes 3145736 | tf_op jit(solution)/shard_map/ppermute | solution.py:202
  28.9 11.4 %collective-permute-start.2 = (bf16[256,1024]{1,0:T(8,128)(2,1)S(1)}, bf16[256,1024]{1,0:T(8,128)(2,1)S(1)}, u32[]{:S(2)}, u32[]{:S(2)}) collective-permute-start(bf16[256,1024]{1,0:T(8,128)(2,1)S(1)} %collective-permute-done.1.b2.refs_3_), channel_id=1, source_target_pairs={{0,1},{1,0},{2,3},{3,2},{4,5},{5,4},{6,7},{7,6},{8,9},{9,8},{10,11... | collective-permute-start | bytes 1572872 | tf_op jit(solution)/shard_map/ppermute | solution.py:202
  28.9 34.0 %collective-permute-start.23 = (bf16[1024,512]{1,0:T(8,128)(2,1)}, bf16[1024,512]{1,0:T(8,128)(2,1)S(1)}, u32[]{:S(2)}, u32[]{:S(2)}) collective-permute-start(bf16[1024,512]{1,0:T(8,128)(2,1)} %bitcast.34), channel_id=1, source_target_pairs={{16,12},{17,13},{18,14},{19,15},{20,16},{21,17},{22,18},{23,19},{2... | collective-permute-start | bytes 3145736 | tf_op jit(solution)/shard_map/ppermute | solution.py:202
  39.6 7.8 %collective-permute-start.6 = (bf16[256,1024]{1,0:T(8,128)(2,1)S(1)}, bf16[256,1024]{1,0:T(8,128)(2,1)S(1)}, u32[]{:S(2)}, u32[]{:S(2)}) collective-permute-start(bf16[256,1024]{1,0:T(8,128)(2,1)S(1)} %collective-permute-done.5.rest_0_.rest_2_.refs_9_), channel_id=1, source_target_pairs={{0,1},{1,0},{2,3},{3,2}} | collective-permute-start | bytes 1572872 | tf_op jit(solution)/shard_map/ppermute | solution.py:202
  40.3 16.6 %collective-permute-start.19 = (bf16[256,1024]{1,0:T(8,128)(2,1)S(1)}, bf16[256,1024]{1,0:T(8,128)(2,1)S(1)}, u32[]{:S(2)}, u32[]{:S(2)}) collective-permute-start(bf16[256,1024]{1,0:T(8,128)(2,1)S(1)} %collective-permute-done.18.refs_3_), channel_id=1, source_target_pairs={{0,1},{1,0},{2,3},{3,2},{4,5},{5,4},{6,7},{7,6},{8,9},{9,8},{10,11... | collective-permute-start | bytes 1572872 | tf_op jit(solution)/shard_map/ppermute | solution.py:202
  40.6 1.6 copy-start
  42.1 1.0 copy-start.1
  43.2 1.0 copy-start.2
  44.2 1.0 copy-start.3
  45.6 13.4 %collective-permute-start.22 = (bf16[256,1024]{1,0:T(8,128)(2,1)S(1)}, bf16[256,1024]{1,0:T(8,128)(2,1)S(1)}, u32[]{:S(2)}, u32[]{:S(2)}) collective-permute-start(bf16[256,1024]{1,0:T(8,128)(2,1)S(1)} %collective-permute-done.21.refs_7_), channel_id=1, source_target_pairs={{0,1},{1,0},{2,3},{3,2},{4,5},{5,4},{6,7},{7,6},{8,9},{9,8},{10,11... | collective-permute-start | bytes 1572872 | tf_op jit(solution)/shard_map/ppermute | solution.py:202
  47.4 22.8 %collective-permute-start.8 = (bf16[1024,256]{1,0:T(8,128)(2,1)S(1)}, bf16[1024,256]{1,0:T(8,128)(2,1)S(1)}, u32[]{:S(2)}, u32[]{:S(2)}) collective-permute-start(bf16[1024,256]{1,0:T(8,128)(2,1)S(1)} %get-tuple-element.28.refs_0_), channel_id=1, source_target_pairs={{0,4},{1,5},{2,6},{3,7},{124,128},{125,129},{126,130},{127,131}} | collective-permute-start | bytes 1572872 | tf_op jit(solution)/shard_map/ppermute | solution.py:202
  53.8 27.0 %collective-permute-start.9 = (bf16[1024,256]{1,0:T(8,128)(2,1)S(1)}, bf16[1024,256]{1,0:T(8,128)(2,1)S(1)}, u32[]{:S(2)}, u32[]{:S(2)}) collective-permute-start(bf16[1024,256]{1,0:T(8,128)(2,1)S(1)} %get-tuple-element.30.refs_2_), channel_id=1, source_target_pairs={{0,4},{1,5},{2,6},{3,7},{124,128},{125,129},{126,130},{127,131}} | collective-permute-start | bytes 1572872 | tf_op jit(solution)/shard_map/ppermute | solution.py:202
  55.1 3.9 %copy-start.4 = (bf16[1,256,1024]{2,1,0:T(8,128)(2,1)S(1)}, bf16[1,256,1024]{2,1,0:T(8,128)(2,1)}, u32[]{:S(2)}) copy-start(bf16[1,256,1024]{2,1,0:T(8,128)(2,1)} %param.10) | copy-start | bytes 1572868
  56.9 27.0 %collective-permute-start.14 = (bf16[1024,256]{1,0:T(8,128)(2,1)S(1)}, bf16[1024,256]{1,0:T(8,128)(2,1)S(1)}, u32[]{:S(2)}, u32[]{:S(2)}) collective-permute-start(bf16[1024,256]{1,0:T(8,128)(2,1)S(1)} %get-tuple-element.35), channel_id=1, source_target_pairs={{4,8},{5,9},{6,10},{7,11},{8,12},{9,13},{10,14},{11,15},{12,16},{1... | collective-permute-start | bytes 1572872 | tf_op jit(solution)/shard_map/ppermute | solution.py:202
  58.9 28.4 %collective-permute-start.12 = (bf16[256,1024]{1,0:T(8,128)(2,1)S(1)}, bf16[256,1024]{1,0:T(8,128)(2,1)S(1)}, u32[]{:S(2)}, u32[]{:S(2)}) collective-permute-start(bf16[256,1024]{1,0:T(8,128)(2,1)S(1)} %bitcast.20), channel_id=1, source_target_pairs={{252,254},{253,255},{254,252},{255,253}} | collective-permute-start | bytes 1572872 | tf_op jit(solution)/shard_map/ppermute | solution.py:202
  62.9 25.3 %collective-permute-start.27 = (bf16[256,1024]{1,0:T(8,128)(2,1)S(1)}, bf16[256,1024]{1,0:T(8,128)(2,1)S(1)}, u32[]{:S(2)}, u32[]{:S(2)}) collective-permute-start(bf16[256,1024]{1,0:T(8,128)(2,1)S(1)} %get-tuple-element.40.refs_1_), channel_id=1, source_target_pairs={{0,240},{1,241},{2,242},{3,243},{252,12},{253,13},{254,14},{255,15}} | collective-permute-start | bytes 1572872 | tf_op jit(solution)/shard_map/ppermute | solution.py:202
  70.2 18.7 %collective-permute-start.7 = (bf16[1024,256]{1,0:T(8,128)(2,1)S(1)}, bf16[1024,256]{1,0:T(8,128)(2,1)S(1)}, u32[]{:S(2)}, u32[]{:S(2)}) collective-permute-start(bf16[1024,256]{1,0:T(8,128)(2,1)S(1)} %get-tuple-element.32), channel_id=1, source_target_pairs={{4,8},{5,9},{6,10},{7,11},{8,12},{9,13},{10,14},{11,15},{12,16},{1... | collective-permute-start | bytes 1572872 | tf_op jit(solution)/shard_map/ppermute | solution.py:202
  80.8 16.7 %collective-permute-start.33 = (bf16[1024,256]{1,0:T(8,128)(2,1)S(1)}, bf16[1024,256]{1,0:T(8,128)(2,1)S(1)}, u32[]{:S(2)}, u32[]{:S(2)}) collective-permute-start(bf16[1024,256]{1,0:T(8,128)(2,1)S(1)} %shard_map.107), channel_id=1, source_target_pairs={{12,8},{13,9},{14,10},{15,11},{16,12},{17,13},{18,14},{19,15},{20,... | collective-permute-start | bytes 1572872 | tf_op jit(solution)/shard_map/ppermute | solution.py:202
  84.0 23.2 %collective-permute-start.24 = (bf16[1024,256]{1,0:T(8,128)(2,1)S(1)}, bf16[1024,256]{1,0:T(8,128)(2,1)S(1)}, u32[]{:S(2)}, u32[]{:S(2)}) collective-permute-start(bf16[1024,256]{1,0:T(8,128)(2,1)S(1)} %shard_map.104), channel_id=1, source_target_pairs={{12,8},{13,9},{14,10},{15,11},{16,12},{17,13},{18,14},{19,15},{20,... | collective-permute-start | bytes 1572872 | tf_op jit(solution)/shard_map/ppermute | solution.py:202
  87.4 29.0 %collective-permute-start.30 = (bf16[256,1024]{1,0:T(8,128)(2,1)S(1)}, bf16[256,1024]{1,0:T(8,128)(2,1)S(1)}, u32[]{:S(2)}, u32[]{:S(2)}) collective-permute-start(bf16[256,1024]{1,0:T(8,128)(2,1)S(1)} %get-tuple-element.41.refs_5_), channel_id=1, source_target_pairs={{0,240},{1,241},{2,242},{3,243}} | collective-permute-start | bytes 1572872 | tf_op jit(solution)/shard_map/ppermute | solution.py:202
  88.3 28.8 %collective-permute-start.13 = (bf16[256,1024]{1,0:T(8,128)(2,1)S(1)}, bf16[256,1024]{1,0:T(8,128)(2,1)S(1)}, u32[]{:S(2)}, u32[]{:S(2)}) collective-permute-start(bf16[256,1024]{1,0:T(8,128)(2,1)S(1)} %collective-permute-done.12.rest_0_.refs_7_), channel_id=1, source_target_pairs={{252,253},{253,252},{254,255},{255,254}} | collective-permute-start | bytes 1572872 | tf_op jit(solution)/shard_map/ppermute | solution.py:202
  89.0 28.8 %collective-permute-start.15 = (bf16[1024,256]{1,0:T(8,128)(2,1)S(1)}, bf16[1024,256]{1,0:T(8,128)(2,1)S(1)}, u32[]{:S(2)}, u32[]{:S(2)}) collective-permute-start(bf16[1024,256]{1,0:T(8,128)(2,1)S(1)} %get-tuple-element.36), channel_id=1, source_target_pairs={{0,4},{1,5},{2,6},{3,7},{4,8},{5,9},{6,10},{7,11},{8,12},{9,13},{1... | collective-permute-start | bytes 1572872 | tf_op jit(solution)/shard_map/ppermute | solution.py:202
  97.5 23.6 %collective-permute-start.10 = (bf16[1024,256]{1,0:T(8,128)(2,1)S(1)}, bf16[1024,256]{1,0:T(8,128)(2,1)S(1)}, u32[]{:S(2)}, u32[]{:S(2)}) collective-permute-start(bf16[1024,256]{1,0:T(8,128)(2,1)S(1)} %get-tuple-element.33), channel_id=1, source_target_pairs={{0,4},{1,5},{2,6},{3,7},{4,8},{5,9},{6,10},{7,11},{8,12},{9,13},{1... | collective-permute-start | bytes 1572872 | tf_op jit(solution)/shard_map/ppermute | solution.py:202
  107.2 20.2 %collective-permute-start.34 = (bf16[1024,256]{1,0:T(8,128)(2,1)S(1)}, bf16[1024,256]{1,0:T(8,128)(2,1)S(1)}, u32[]{:S(2)}, u32[]{:S(2)}) collective-permute-start(bf16[1024,256]{1,0:T(8,128)(2,1)S(1)} %shard_map.108), channel_id=1, source_target_pairs={{8,4},{9,5},{10,6},{11,7},{12,8},{13,9},{14,10},{15,11},{16,12},{1... | collective-permute-start | bytes 1572872 | tf_op jit(solution)/shard_map/ppermute | solution.py:202
  116.4 14.2 %collective-permute-start.28 = (bf16[256,1024]{1,0:T(8,128)(2,1)S(1)}, bf16[256,1024]{1,0:T(8,128)(2,1)S(1)}, u32[]{:S(2)}, u32[]{:S(2)}) collective-permute-start(bf16[256,1024]{1,0:T(8,128)(2,1)S(1)} %collective-permute-done.27), channel_id=1, source_target_pairs={{240,2},{241,3},{242,0},{243,1},{12,254},{13,255},{14,252},{15,253}} | collective-permute-start | bytes 1572872 | tf_op jit(solution)/shard_map/ppermute | solution.py:202
  117.1 14.2 %collective-permute-start.31 = (bf16[256,1024]{1,0:T(8,128)(2,1)S(1)}, bf16[256,1024]{1,0:T(8,128)(2,1)S(1)}, u32[]{:S(2)}, u32[]{:S(2)}) collective-permute-start(bf16[256,1024]{1,0:T(8,128)(2,1)S(1)} %collective-permute-done.30), channel_id=1, source_target_pairs={{240,2},{241,3},{242,0},{243,1}} | collective-permute-start | bytes 1572872 | tf_op jit(solution)/shard_map/ppermute | solution.py:202
  117.8 18.7 %collective-permute-start.25 = (bf16[1024,256]{1,0:T(8,128)(2,1)S(1)}, bf16[1024,256]{1,0:T(8,128)(2,1)S(1)}, u32[]{:S(2)}, u32[]{:S(2)}) collective-permute-start(bf16[1024,256]{1,0:T(8,128)(2,1)S(1)} %shard_map.105), channel_id=1, source_target_pairs={{8,4},{9,5},{10,6},{11,7},{12,8},{13,9},{14,10},{15,11},{16,12},{1... | collective-permute-start | bytes 1572872 | tf_op jit(solution)/shard_map/ppermute | solution.py:202
  121.1 26.8 %collective-permute-start.16 = (bf16[1024,256]{1,0:T(8,128)(2,1)S(1)}, bf16[1024,256]{1,0:T(8,128)(2,1)S(1)}, u32[]{:S(2)}, u32[]{:S(2)}) collective-permute-start(bf16[1024,256]{1,0:T(8,128)(2,1)S(1)} %get-tuple-element.37), channel_id=1, source_target_pairs={{0,4},{1,5},{2,6},{3,7},{4,8},{5,9},{6,10},{7,11},{8,12},{9,13},{1... | collective-permute-start | bytes 1572872 | tf_op jit(solution)/shard_map/ppermute | solution.py:202
  127.4 25.0 %collective-permute-start.11 = (bf16[1024,256]{1,0:T(8,128)(2,1)S(1)}, bf16[1024,256]{1,0:T(8,128)(2,1)S(1)}, u32[]{:S(2)}, u32[]{:S(2)}) collective-permute-start(bf16[1024,256]{1,0:T(8,128)(2,1)S(1)} %get-tuple-element.34), channel_id=1, source_target_pairs={{0,4},{1,5},{2,6},{3,7},{4,8},{5,9},{6,10},{7,11},{8,12},{9,13},{1... | collective-permute-start | bytes 1572872 | tf_op jit(solution)/shard_map/ppermute | solution.py:202
  130.6 23.9 %collective-permute-start.29 = (bf16[256,1024]{1,0:T(8,128)(2,1)S(1)}, bf16[256,1024]{1,0:T(8,128)(2,1)S(1)}, u32[]{:S(2)}, u32[]{:S(2)}) collective-permute-start(bf16[256,1024]{1,0:T(8,128)(2,1)S(1)} %collective-permute-done.28.refs_12_), channel_id=1, source_target_pairs={{0,1},{1,0},{2,3},{3,2},{252,253},{253,252},{254,255},{255,254}} | collective-permute-start | bytes 1572872 | tf_op jit(solution)/shard_map/ppermute | solution.py:202
  131.3 23.2 %collective-permute-start.32 = (bf16[256,1024]{1,0:T(8,128)(2,1)S(1)}, bf16[256,1024]{1,0:T(8,128)(2,1)S(1)}, u32[]{:S(2)}, u32[]{:S(2)}) collective-permute-start(bf16[256,1024]{1,0:T(8,128)(2,1)S(1)} %collective-permute-done.31.refs_14_), channel_id=1, source_target_pairs={{0,1},{1,0},{2,3},{3,2}} | collective-permute-start | bytes 1572872 | tf_op jit(solution)/shard_map/ppermute | solution.py:202
  136.5 22.4 %collective-permute-start.35 = (bf16[1024,256]{1,0:T(8,128)(2,1)S(1)}, bf16[1024,256]{1,0:T(8,128)(2,1)S(1)}, u32[]{:S(2)}, u32[]{:S(2)}) collective-permute-start(bf16[1024,256]{1,0:T(8,128)(2,1)S(1)} %shard_map.109), channel_id=1, source_target_pairs={{4,0},{5,1},{6,2},{7,3},{8,4},{9,5},{10,6},{11,7},{12,8},{13,9},{1... | collective-permute-start | bytes 1572872 | tf_op jit(solution)/shard_map/ppermute | solution.py:202
  147.9 19.3 %collective-permute-start.26 = (bf16[1024,256]{1,0:T(8,128)(2,1)S(1)}, bf16[1024,256]{1,0:T(8,128)(2,1)S(1)}, u32[]{:S(2)}, u32[]{:S(2)}) collective-permute-start(bf16[1024,256]{1,0:T(8,128)(2,1)S(1)} %shard_map.106), channel_id=1, source_target_pairs={{4,0},{5,1},{6,2},{7,3},{8,4},{9,5},{10,6},{11,7},{12,8},{13,9},{1... | collective-permute-start | bytes 1572872 | tf_op jit(solution)/shard_map/ppermute | solution.py:202

commit v5 on v4

--- a/solution.py
+++ b/solution.py
@@ -41,7 +41,7 @@
     return pl.pallas_call(
         stage_kernel,
         name="stage",
-        in_specs=[pl.BlockSpec(memory_space=pl.ANY)] * n,
+        in_specs=[pl.BlockSpec(memory_space=pltpu.HBM)] * n,
         out_specs=[WHOLE] * n,
         out_shape=[jax.ShapeDtypeStruct(a.shape, a.dtype) for a in arrays],
         scratch_shapes=[pltpu.SemaphoreType.DMA((n,))],
@@ -54,29 +54,6 @@
     spot = lax.axis_index("shot")
     for k, block in enumerate(blocks):
         new[band(spot ^ k, block.shape[0]), :] = dot(block[...], down_in[...]).astype(BF16)
-
-
-def first_kernel(chunk, plan, b0, b1, b2, b3, received, sources, *rest):
-    pair, (new, down_in) = rest[:-2], rest[-2:]
-    layer, core = lax.axis_index("layer"), lax.axis_index("shot") % 2
-    width = down_in.shape[1]
-
-    def injection(cols):
-        return injected(received[:, cols], sources[plan[0, 0], :, cols])
-
-    down_in[...] = injection(columns(sources, chunk, width))
-
-    @pl.when(layer == 0)
-    def _():
-        for other in range(CHUNKS):
-            value = injection(columns(sources, other, width))
-            for k, block in enumerate(pair or (b0, b1)):
-                high = block.shape[0]
-                new[band(other * 2 + (core ^ k), high), :] = dot(block[...], value).astype(BF16)
-
-    @pl.when(layer != 0)
-    def _():
-        products((b0, b1, b2, b3), down_in, new)
 
 
 def fix_kernel(plan, b0, b1, b2, b3, received, sources, *refs):
@@ -113,19 +90,11 @@
 
     if moment == 1:
 
-        @pl.when(layer == 1)
-        def _():
-            for k, ref in enumerate(others[:2]):
-                half = ref.shape[0] // 2
-                rows = band((spot // 2) ^ k, half)
-                value = ref[chunk * half : (chunk + 1) * half, :]
-                down_in[rows, :] = injected(value, sources[plan[0, moment], rows, cols])
-
         @pl.when(layer == count // 2)
         def _():
-            take(others[chunk])
-
-        @pl.when(jnp.logical_and(layer != 1, layer != count // 2))
+            take(others[0])
+
+        @pl.when(layer != count // 2)
         def _():
             take(received)
 
@@ -133,8 +102,6 @@
         take(received)
     for k, block in enumerate((b0, b1, b2, b3)):
         high, value = block.shape[0], block[...]
-        if k >= 2:
-            value = jnp.where(layer == 0, others[k - 4][...], value)
         if moment == TICKS - 1 and k >= 2:
             value = jnp.where(layer == count - 1, others[k - 2][...], value)
         new[band(spot ^ k, high), :] = dot(value, down_in[...]).astype(BF16)
@@ -230,9 +197,7 @@
     cut = layers // 2
     down_0b = link(down_state[0], [(cut - 1, cut)], 0)
     down_0 = shift(down_state[0], 1, [cut - 1])
-    far_d = swap(down_op, 2, middle)
-    far_0 = swap(down_op, 2, [0])
-    cross_0 = swap(far_0, 1, [0])
+    far_d = swap(down_op, 2, [0] + middle)
     up_0 = shift(up_state[0], -1, [1, 2, 3])
     far_e = swap(down_op, 2, [layers - 1])
     cross_e = swap(far_e, 1, [layers - 1])
@@ -259,15 +224,15 @@
     firsts, specials = [], []
     for chunk in range(CHUNKS):
         new, down_in = call(
-            functools.partial(first_kernel, chunk), plan,
-            [*d_blocks, down_0, sources], [piece] * 2, one, more=[far_0, cross_0] if chunk else [],
+            functools.partial(down_kernel, 0, chunk), plan,
+            [*d_blocks, down_0, sources], [piece] * 2, one,
         )
         firsts += [new, down_in]
-        specials.append(link(new, [(0, 1), (cut - 1, cut)], 0))
+        specials.append(link(new, [(cut - 1, cut)], 0))
     firsts = call(
         fix_kernel, plan, [*d_blocks, down_0b, sources, *firsts], [piece] * (2 * CHUNKS), one // 8
     )
-    downs = [shift(firsts[2 * i], 1, [0, cut - 1]) for i in range(CHUNKS)]
+    downs = [shift(firsts[2 * i], 1, [cut - 1]) for i in range(CHUNKS)]
     ups = [up_0] * CHUNKS
     for moment in range(TICKS):
         last = moment == TICKS - 1
@@ -275,11 +240,11 @@
         for chunk in range(CHUNKS):
             full = (chunk, wide) if last else None
             if moment:
-                more = specials if moment == 1 else [far_e, cross_e] if last else []
+                more = [specials[chunk]] if moment == 1 else [far_e, cross_e] if last else []
                 new, down_in = call(
                     functools.partial(down_kernel, moment, chunk), plan,
                     [*d_blocks, downs[chunk], sources], [piece] * 2, one,
-                    full=full, into=new if last else None, more=[*more, far_0, cross_0],
+                    full=full, into=new if last else None, more=more,
                 )
                 new_downs.append(new)
             else:

time: 170 us -> 163 us (0.959)
  the two profiles are of different devices: /device:TPU:24 before, /device:TPU:8 now
where the time goes in v5:
time: 163 us; the launch traced here: 160 us
  waiting for transfers between devices  71.7 us (44%)
  starting transfers between devices  56.7 us (35%)
  Pallas kernels  25 us (15%)
  local copies, waits for them, and re-layouts  4.72 us (3%)
  between operations  1.81 us (1%)
    ppermute x34, waiting for transfers between devices, sent(): return lax.ppermute(value, ('layer', 'shot'), pairs)  71.7 us
    ppermute x34, starting transfers between devices, sent(): return lax.ppermute(value, ('layer', 'shot'), pairs)  56.7 us
    pallas_call x17, Pallas kernels, call(): pl.pallas_call(kernel, grid=(1,), in_specs=in_specs, out_specs=out_specs,...  24.7 us
    unnamed x10, local copies, waits for them, and re-layouts  4.72 us
  transfers between devices with their start and end apart: 34, of which 10 were waited for; matrix products, arithmetic and copies ran while one was open for 0% of the time, Pallas kernels for 14%

profile of v5, /device:TPU:8, one launch (start us, length us, event | category | flops | bytes accessed | tf_op | source)
XLA Modules:
  0.0 159.8 jit_solution(9061970834111875472)
XLA Ops:
  0.7 4.1 %collective-permute-start.1 = (bf16[256,1024]{1,0:T(8,128)(2,1)}, bf16[256,1024]{1,0:T(8,128)(2,1)S(1)}, u32[]{:S(2)}, u32[]{:S(2)}) collective-permute-start(bf16[256,1024]{1,0:T(8,128)(2,1)} %bitcast.11), channel_id=1, source_target_pairs={{0,2},{1,3},{2,0},{3,1},{4,6},{5,7},{6,4},{7,5},{8,10},{9,11},{10,... | collective-permute-start | bytes 1572872 | tf_op jit(solution)/shard_map/ppermute | solution.py:169
  5.5 0.7 collective-permute-start.3
  6.3 1.8 %collective-permute-start.4 = (bf16[1024,512]{1,0:T(8,128)(2,1)}, bf16[1024,512]{1,0:T(8,128)(2,1)S(1)}, u32[]{:S(2)}, u32[]{:S(2)}) collective-permute-start(bf16[1024,512]{1,0:T(8,128)(2,1)} %bitcast.32), channel_id=1, source_target_pairs={{0,4},{1,5},{2,6},{3,7},{4,8},{5,9},{6,10},{7,11},{8,12},{9,13},{1... | collective-permute-start | bytes 3145736 | tf_op jit(solution)/shard_map/ppermute | solution.py:169
  8.7 31.3 %collective-permute-done.1.b2.refs_3_ = bf16[256,1024]{1,0:T(8,128)(2,1)S(1)} collective-permute-done((bf16[256,1024]{1,0:T(8,128)(2,1)}, bf16[256,1024]{1,0:T(8,128)(2,1)S(1)}, u32[]{:S(2)}, u32[]{:S(2)}) %collective-permute-start.1) | collective-permute-done | bytes 524320 | tf_op jit(solution)/shard_map/ppermute | solution.py:169
  40.9 0.7 collective-permute-start.21
  42.9 1.6 copy-done
  44.5 1.0 copy-done.1
  45.5 1.0 copy-done.2
  46.6 1.0 copy-done.3
  48.5 1.3 shard_map.95
  49.8 1.3 shard_map.96
  51.1 0.7 shard_map.97
  51.8 1.3 collective-permute-start.11
  54.5 8.8 %collective-permute-start.25 = (bf16[256,1024]{1,0:T(8,128)(2,1)S(1)}, bf16[256,1024]{1,0:T(8,128)(2,1)S(1)}, u32[]{:S(2)}, u32[]{:S(2)}) collective-permute-start(bf16[256,1024]{1,0:T(8,128)(2,1)S(1)} %get-tuple-element.40.refs_1_), channel_id=1, source_target_pairs={{0,240},{1,241},{2,242},{3,243},{252,12},{253,13},{254,14},{255,15}} | collective-permute-start | bytes 1572872 | tf_op jit(solution)/shard_map/ppermute | solution.py:169
  64.1 1.3 collective-permute-start.5
  65.4 1.3 shard_map.107
  67.4 1.3 shard_map.104
  69.4 1.4 shard_map.100
  70.8 3.7 %collective-permute-done.25 = bf16[256,1024]{1,0:T(8,128)(2,1)S(1)} collective-permute-done((bf16[256,1024]{1,0:T(8,128)(2,1)S(1)}, bf16[256,1024]{1,0:T(8,128)(2,1)S(1)}, u32[]{:S(2)}, u32[]{:S(2)}) %collective-permute-start.25) | collective-permute-done | bytes 524320 | tf_op jit(solution)/shard_map/ppermute | solution.py:169
  74.5 11.4 %collective-permute-start.28 = (bf16[256,1024]{1,0:T(8,128)(2,1)S(1)}, bf16[256,1024]{1,0:T(8,128)(2,1)S(1)}, u32[]{:S(2)}, u32[]{:S(2)}) collective-permute-start(bf16[256,1024]{1,0:T(8,128)(2,1)S(1)} %get-tuple-element.41.refs_5_), channel_id=1, source_target_pairs={{0,240},{1,241},{2,242},{3,243}} | collective-permute-start | bytes 1572872 | tf_op jit(solution)/shard_map/ppermute | solution.py:169
  86.6 1.3 collective-permute-start.13
  87.9 1.4 shard_map.98
  89.3 1.5 collective-permute-start.7
  90.9 1.3 shard_map.108
  92.8 1.3 shard_map.105
  94.1 0.9 collective-permute-done.28
  95.0 1.3 collective-permute-start.26
  96.3 1.3 collective-permute-start.29
  97.6 2.6 %collective-permute-done.13.received = bf16[1024,256]{1,0:T(8,128)(2,1)S(1)} collective-permute-done((bf16[1024,256]{1,0:T(8,128)(2,1)S(1)}, bf16[1024,256]{1,0:T(8,128)(2,1)S(1)}, u32[]{:S(2)}, u32[]{:S(2)}) %collective-permute-start.13) | collective-permute-done | bytes 524320 | tf_op jit(solution)/shard_map/ppermute | solution.py:169
  100.9 1.3 shard_map.101
  102.2 6.1 %collective-permute-done.7.received = bf16[1024,256]{1,0:T(8,128)(2,1)S(1)} collective-permute-done((bf16[1024,256]{1,0:T(8,128)(2,1)S(1)}, bf16[1024,256]{1,0:T(8,128)(2,1)S(1)}, u32[]{:S(2)}, u32[]{:S(2)}) %collective-permute-start.7) | collective-permute-done | bytes 524320 | tf_op jit(solution)/shard_map/ppermute | solution.py:169
  108.3 4.4 %collective-permute-start.14 = (bf16[1024,256]{1,0:T(8,128)(2,1)S(1)}, bf16[1024,256]{1,0:T(8,128)(2,1)S(1)}, u32[]{:S(2)}, u32[]{:S(2)}) collective-permute-start(bf16[1024,256]{1,0:T(8,128)(2,1)S(1)} %get-tuple-element.37), channel_id=1, source_target_pairs={{0,4},{1,5},{2,6},{3,7},{4,8},{5,9},{6,10},{7,11},{8,12},{9,13},{1... | collective-permute-start | bytes 1572872 | tf_op jit(solution)/shard_map/ppermute | solution.py:169
  112.7 1.3 shard_map.99
  114.0 1.9 %collective-permute-start.8 = (bf16[1024,256]{1,0:T(8,128)(2,1)S(1)}, bf16[1024,256]{1,0:T(8,128)(2,1)S(1)}, u32[]{:S(2)}, u32[]{:S(2)}) collective-permute-start(bf16[1024,256]{1,0:T(8,128)(2,1)S(1)} %get-tuple-element.34), channel_id=1, source_target_pairs={{0,4},{1,5},{2,6},{3,7},{4,8},{5,9},{6,10},{7,11},{8,12},{9,13},{1... | collective-permute-start | bytes 1572872 | tf_op jit(solution)/shard_map/ppermute | solution.py:169
  115.9 1.3 shard_map.109
  117.2 3.3 %collective-permute-done.26.refs_12_ = bf16[256,1024]{1,0:T(8,128)(2,1)S(1)} collective-permute-done((bf16[256,1024]{1,0:T(8,128)(2,1)S(1)}, bf16[256,1024]{1,0:T(8,128)(2,1)S(1)}, u32[]{:S(2)}, u32[]{:S(2)}) %collective-permute-start.26) | collective-permute-done | bytes 524320 | tf_op jit(solution)/shard_map/ppermute | solution.py:169
  120.5 1.9 %collective-permute-start.27 = (bf16[256,1024]{1,0:T(8,128)(2,1)S(1)}, bf16[256,1024]{1,0:T(8,128)(2,1)S(1)}, u32[]{:S(2)}, u32[]{:S(2)}) collective-permute-start(bf16[256,1024]{1,0:T(8,128)(2,1)S(1)} %collective-permute-done.26.refs_12_), channel_id=1, source_target_pairs={{0,1},{1,0},{2,3},{3,2},{252,253},{253,252},{254,255},{255,254}} | collective-permute-start | bytes 1572872 | tf_op jit(solution)/shard_map/ppermute | solution.py:169
  122.4 5.9 %collective-permute-done.29.refs_14_ = bf16[256,1024]{1,0:T(8,128)(2,1)S(1)} collective-permute-done((bf16[256,1024]{1,0:T(8,128)(2,1)S(1)}, bf16[256,1024]{1,0:T(8,128)(2,1)S(1)}, u32[]{:S(2)}, u32[]{:S(2)}) %collective-permute-start.29) | collective-permute-done | bytes 524320 | tf_op jit(solution)/shard_map/ppermute | solution.py:169
  128.3 1.9 %collective-permute-start.30 = (bf16[256,1024]{1,0:T(8,128)(2,1)S(1)}, bf16[256,1024]{1,0:T(8,128)(2,1)S(1)}, u32[]{:S(2)}, u32[]{:S(2)}) collective-permute-start(bf16[256,1024]{1,0:T(8,128)(2,1)S(1)} %collective-permute-done.29.refs_14_), channel_id=1, source_target_pairs={{0,1},{1,0},{2,3},{3,2}} | collective-permute-start | bytes 1572872 | tf_op jit(solution)/shard_map/ppermute | solution.py:169
  130.3 1.3 collective-permute-start.33
  131.6 1.3 shard_map.106
  132.8 1.3 collective-permute-start.24
  134.1 2.1 %shard_map.102 = (bf16[1024,512]{1,0:T(8,128)(2,1)}, bf16[1024,256]{1,0:T(8,128)(2,1)S(1)}) custom-call(s32[1,4]{1,0:T(1,128)S(1)} %bitcast.27, bf16[256,1024]{1,0:T(8,128)(2,1)S(1)} %get-tuple-element.26.b0.refs_1_, bf16[256,1024]{1,0:T(8,128)(2,1)S(1)} %collective-permute-done.b1.refs_2_, bf16[256,1024]{1,0:T(8,128)(2,1)S(1)} %collective-permute-done.1.b2.refs_3_, ...), custom_call_target="tpu_custom_call" | custom-call | flops 536870912 | bytes 1048576 | tf_op jit(solution)/shard_map/pallas_call | solution.py:149
  136.2 2.1 %shard_map.103 = (bf16[1024,512]{1,0:T(8,128)(2,1)}, bf16[1024,256]{1,0:T(8,128)(2,1)S(1)}) custom-call(s32[1,4]{1,0:T(1,128)S(1)} %bitcast.28, bf16[256,1024]{1,0:T(8,128)(2,1)S(1)} %get-tuple-element.26.b0.refs_1_, bf16[256,1024]{1,0:T(8,128)(2,1)S(1)} %collective-permute-done.b1.refs_2_, ...), custom_call_target="tpu_custom_call", output_to_operand_aliasing={{0}: (9, {})} | custom-call | flops 536870912 | bytes 1048576 | tf_op jit(solution)/shard_map/pallas_call | solution.py:149
  138.3 8.6 %collective-permute-done.33.refs_9_ = bf16[1024,256]{1,0:T(8,128)(2,1)S(1)} collective-permute-done((bf16[1024,256]{1,0:T(8,128)(2,1)S(1)}, bf16[1024,256]{1,0:T(8,128)(2,1)S(1)}, u32[]{:S(2)}, u32[]{:S(2)}) %collective-permute-start.33) | collective-permute-done | bytes 524320 | tf_op jit(solution)/shard_map/ppermute | solution.py:169
  146.9 2.1 %shard_map.110.refs_16_ = bf16[1024,512]{1,0:T(8,128)(2,1)} custom-call(s32[1]{0:T(128)S(6)} %copy.14.refs_0_, bf16[256,1024]{1,0:T(8,128)(2,1)S(1)} %get-tuple-element.40.refs_1_, bf16[256,1024]{1,0:T(8,128)(2,1)S(1)} %collective-permute-done.15.refs_2_, bf16[256,1024]{1,0:T(8,128)(2,1)S(1)} %collective-permute-done.16.refs_3_, ...), custom_call_target="tpu_custom_call" | custom-call | flops 1073741824 | bytes 1048576 | tf_op jit(solution)/shard_map/pallas_call | solution.py:149
  149.0 8.7 %collective-permute-done.24.refs_9_ = bf16[1024,256]{1,0:T(8,128)(2,1)S(1)} collective-permute-done((bf16[1024,256]{1,0:T(8,128)(2,1)S(1)}, bf16[1024,256]{1,0:T(8,128)(2,1)S(1)}, u32[]{:S(2)}, u32[]{:S(2)}) %collective-permute-start.24) | collective-permute-done | bytes 524320 | tf_op jit(solution)/shard_map/ppermute | solution.py:169
  157.7 2.1 %shard_map.111 = bf16[1024,512]{1,0:T(8,128)(2,1)} custom-call(s32[1]{0:T(128)S(6)} %copy.14.refs_0_, bf16[256,1024]{1,0:T(8,128)(2,1)S(1)} %get-tuple-element.40.refs_1_, bf16[256,1024]{1,0:T(8,128)(2,1)S(1)} %collective-permute-done.15.refs_2_, bf16[256,1024]{1,0:T(8,128)(2,1)S(1)} %collective-permute-done.16.refs_3_, ...), custom_call_target="tpu_custom_call", output_to_operand_aliasing={{}: (16, {})} | custom-call | flops 1073741824 | bytes 1048576 | tf_op jit(solution)/shard_map/pallas_call | solution.py:149
  (48 shorter events, 9.3 us)
Async XLA Ops:
  0.6 47.9 %copy-start.4 = (s32[4,1]{0,1:T(1,128)S(1)}, s32[4,1]{0,1:T(1,128)}, u32[]{:S(2)}) copy-start(s32[4,1]{0,1:T(1,128)} %param.14) | copy-start | bytes 52
  0.6 7.4 %collective-permute-start = (bf16[256,1024]{1,0:T(8,128)(2,1)}, bf16[256,1024]{1,0:T(8,128)(2,1)S(1)}, u32[]{:S(2)}, u32[]{:S(2)}) collective-permute-start(bf16[256,1024]{1,0:T(8,128)(2,1)} %bitcast.10), channel_id=1, source_target_pairs={{0,1},{1,0},{2,3},{3,2},{4,5},{5,4},{6,7},{7,6},{8,9},{9,8},{10,11... | collective-permute-start | bytes 1572872 | tf_op jit(solution)/shard_map/ppermute | solution.py:169
  0.7 39.3 %collective-permute-start.1 = (bf16[256,1024]{1,0:T(8,128)(2,1)}, bf16[256,1024]{1,0:T(8,128)(2,1)S(1)}, u32[]{:S(2)}, u32[]{:S(2)}) collective-permute-start(bf16[256,1024]{1,0:T(8,128)(2,1)} %bitcast.11), channel_id=1, source_target_pairs={{0,2},{1,3},{2,0},{3,1},{4,6},{5,7},{6,4},{7,5},{8,10},{9,11},{10,... | collective-permute-start | bytes 1572872 | tf_op jit(solution)/shard_map/ppermute | solution.py:169
  4.8 35.9 %collective-permute-start.9 = (bf16[256,1024]{1,0:T(8,128)(2,1)}, bf16[256,1024]{1,0:T(8,128)(2,1)S(1)}, u32[]{:S(2)}, u32[]{:S(2)}) collective-permute-start(bf16[256,1024]{1,0:T(8,128)(2,1)} %bitcast.12), channel_id=1, source_target_pairs={{252,254},{253,255},{254,252},{255,253}} | collective-permute-start | bytes 1572872 | tf_op jit(solution)/shard_map/ppermute | solution.py:169
  5.5 42.4 %collective-permute-start.3 = (bf16[1024,512]{1,0:T(8,128)(2,1)}, bf16[1024,512]{1,0:T(8,128)(2,1)S(1)}, u32[]{:S(2)}, u32[]{:S(2)}) collective-permute-start(bf16[1024,512]{1,0:T(8,128)(2,1)} %bitcast.31), channel_id=1, source_target_pairs={{124,128},{125,129},{126,130},{127,131}} | collective-permute-start | bytes 3145736 | tf_op jit(solution)/shard_map/ppermute | solution.py:169
  6.3 42.1 %collective-permute-start.4 = (bf16[1024,512]{1,0:T(8,128)(2,1)}, bf16[1024,512]{1,0:T(8,128)(2,1)S(1)}, u32[]{:S(2)}, u32[]{:S(2)}) collective-permute-start(bf16[1024,512]{1,0:T(8,128)(2,1)} %bitcast.32), channel_id=1, source_target_pairs={{0,4},{1,5},{2,6},{3,7},{4,8},{5,9},{6,10},{7,11},{8,12},{9,13},{1... | collective-permute-start | bytes 3145736 | tf_op jit(solution)/shard_map/ppermute | solution.py:169
  8.0 32.8 %collective-permute-start.16 = (bf16[256,1024]{1,0:T(8,128)(2,1)}, bf16[256,1024]{1,0:T(8,128)(2,1)S(1)}, u32[]{:S(2)}, u32[]{:S(2)}) collective-permute-start(bf16[256,1024]{1,0:T(8,128)(2,1)} %bitcast.14), channel_id=1, source_target_pairs={{4,6},{5,7},{6,4},{7,5},{8,10},{9,11},{10,8},{11,9},{12,14},{13,15... | collective-permute-start | bytes 1572872 | tf_op jit(solution)/shard_map/ppermute | solution.py:169
  40.1 1.6 collective-permute-start.19
  40.8 2.0 %collective-permute-start.2 = (bf16[256,1024]{1,0:T(8,128)(2,1)S(1)}, bf16[256,1024]{1,0:T(8,128)(2,1)S(1)}, u32[]{:S(2)}, u32[]{:S(2)}) collective-permute-start(bf16[256,1024]{1,0:T(8,128)(2,1)S(1)} %collective-permute-done.1.b2.refs_3_), channel_id=1, source_target_pairs={{0,1},{1,0},{2,3},{3,2},{4,5},{5,4},{6,7},{7,6},{8,9},{9,8},{10,11... | collective-permute-start | bytes 1572872 | tf_op jit(solution)/shard_map/ppermute | solution.py:169
  40.9 23.2 %collective-permute-start.21 = (bf16[1024,512]{1,0:T(8,128)(2,1)}, bf16[1024,512]{1,0:T(8,128)(2,1)S(1)}, u32[]{:S(2)}, u32[]{:S(2)}) collective-permute-start(bf16[1024,512]{1,0:T(8,128)(2,1)} %bitcast.33), channel_id=1, source_target_pairs={{16,12},{17,13},{18,14},{19,15},{20,16},{21,17},{22,18},{23,19},{2... | collective-permute-start | bytes 3145736 | tf_op jit(solution)/shard_map/ppermute | solution.py:169
  41.6 10.2 %collective-permute-start.15 = (bf16[256,1024]{1,0:T(8,128)(2,1)}, bf16[256,1024]{1,0:T(8,128)(2,1)S(1)}, u32[]{:S(2)}, u32[]{:S(2)}) collective-permute-start(bf16[256,1024]{1,0:T(8,128)(2,1)} %bitcast.15), channel_id=1, source_target_pairs={{0,1},{1,0},{2,3},{3,2},{4,5},{5,4},{6,7},{7,6},{8,9},{9,8},{10,11... | collective-permute-start | bytes 1572872 | tf_op jit(solution)/shard_map/ppermute | solution.py:169
  42.8 10.4 %collective-permute-start.18 = (bf16[256,1024]{1,0:T(8,128)(2,1)}, bf16[256,1024]{1,0:T(8,128)(2,1)S(1)}, u32[]{:S(2)}, u32[]{:S(2)}) collective-permute-start(bf16[256,1024]{1,0:T(8,128)(2,1)} %bitcast.18), channel_id=1, source_target_pairs={{0,1},{1,0},{2,3},{3,2},{4,5},{5,4},{6,7},{7,6},{8,9},{9,8},{10,11... | collective-permute-start | bytes 1572872 | tf_op jit(solution)/shard_map/ppermute | solution.py:169
  42.9 1.6 copy-start
  44.5 1.0 copy-start.1
  45.5 1.0 copy-start.2
  46.6 1.0 copy-start.3
  47.9 6.6 %collective-permute-start.17 = (bf16[256,1024]{1,0:T(8,128)(2,1)S(1)}, bf16[256,1024]{1,0:T(8,128)(2,1)S(1)}, u32[]{:S(2)}, u32[]{:S(2)}) collective-permute-start(bf16[256,1024]{1,0:T(8,128)(2,1)S(1)} %collective-permute-done.16.refs_3_), channel_id=1, source_target_pairs={{0,1},{1,0},{2,3},{3,2},{4,5},{5,4},{6,7},{7,6},{8,9},{9,8},{10,11... | collective-permute-start | bytes 1572872 | tf_op jit(solution)/shard_map/ppermute | solution.py:169
  48.4 15.0 %collective-permute-start.20 = (bf16[256,1024]{1,0:T(8,128)(2,1)S(1)}, bf16[256,1024]{1,0:T(8,128)(2,1)S(1)}, u32[]{:S(2)}, u32[]{:S(2)}) collective-permute-start(bf16[256,1024]{1,0:T(8,128)(2,1)S(1)} %collective-permute-done.19.refs_7_), channel_id=1, source_target_pairs={{0,1},{1,0},{2,3},{3,2},{4,5},{5,4},{6,7},{7,6},{8,9},{9,8},{10,11... | collective-permute-start | bytes 1572872 | tf_op jit(solution)/shard_map/ppermute | solution.py:169
  51.8 14.9 %collective-permute-start.11 = (bf16[1024,256]{1,0:T(8,128)(2,1)S(1)}, bf16[1024,256]{1,0:T(8,128)(2,1)S(1)}, u32[]{:S(2)}, u32[]{:S(2)}) collective-permute-start(bf16[1024,256]{1,0:T(8,128)(2,1)S(1)} %get-tuple-element.35), channel_id=1, source_target_pairs={{0,4},{1,5},{2,6},{3,7},{4,8},{5,9},{6,10},{7,11},{8,12},{9,13},{1... | collective-permute-start | bytes 1572872 | tf_op jit(solution)/shard_map/ppermute | solution.py:169
  53.2 15.5 %collective-permute-start.12 = (bf16[1024,256]{1,0:T(8,128)(2,1)S(1)}, bf16[1024,256]{1,0:T(8,128)(2,1)S(1)}, u32[]{:S(2)}, u32[]{:S(2)}) collective-permute-start(bf16[1024,256]{1,0:T(8,128)(2,1)S(1)} %get-tuple-element.28.refs_0_), channel_id=1, source_target_pairs={{124,128},{125,129},{126,130},{127,131}} | collective-permute-start | bytes 1572872 | tf_op jit(solution)/shard_map/ppermute | solution.py:169
  54.5 20.0 %collective-permute-start.25 = (bf16[256,1024]{1,0:T(8,128)(2,1)S(1)}, bf16[256,1024]{1,0:T(8,128)(2,1)S(1)}, u32[]{:S(2)}, u32[]{:S(2)}) collective-permute-start(bf16[256,1024]{1,0:T(8,128)(2,1)S(1)} %get-tuple-element.40.refs_1_), channel_id=1, source_target_pairs={{0,240},{1,241},{2,242},{3,243},{252,12},{253,13},{254,14},{255,15}} | collective-permute-start | bytes 1572872 | tf_op jit(solution)/shard_map/ppermute | solution.py:169
  63.4 23.2 %collective-permute-start.6 = (bf16[1024,256]{1,0:T(8,128)(2,1)S(1)}, bf16[1024,256]{1,0:T(8,128)(2,1)S(1)}, u32[]{:S(2)}, u32[]{:S(2)}) collective-permute-start(bf16[1024,256]{1,0:T(8,128)(2,1)S(1)} %get-tuple-element.30.refs_2_), channel_id=1, source_target_pairs={{124,128},{125,129},{126,130},{127,131}} | collective-permute-start | bytes 1572872 | tf_op jit(solution)/shard_map/ppermute | solution.py:169
  64.1 21.8 %collective-permute-start.5 = (bf16[1024,256]{1,0:T(8,128)(2,1)S(1)}, bf16[1024,256]{1,0:T(8,128)(2,1)S(1)}, u32[]{:S(2)}, u32[]{:S(2)}) collective-permute-start(bf16[1024,256]{1,0:T(8,128)(2,1)S(1)} %get-tuple-element.32), channel_id=1, source_target_pairs={{0,4},{1,5},{2,6},{3,7},{4,8},{5,9},{6,10},{7,11},{8,12},{9,13},{1... | collective-permute-start | bytes 1572872 | tf_op jit(solution)/shard_map/ppermute | solution.py:169
  66.7 22.6 %collective-permute-start.31 = (bf16[1024,256]{1,0:T(8,128)(2,1)S(1)}, bf16[1024,256]{1,0:T(8,128)(2,1)S(1)}, u32[]{:S(2)}, u32[]{:S(2)}) collective-permute-start(bf16[1024,256]{1,0:T(8,128)(2,1)S(1)} %shard_map.107), channel_id=1, source_target_pairs={{12,8},{13,9},{14,10},{15,11},{16,12},{17,13},{18,14},{19,15},{20,... | collective-permute-start | bytes 1572872 | tf_op jit(solution)/shard_map/ppermute | solution.py:169
  68.7 23.4 %collective-permute-start.22 = (bf16[1024,256]{1,0:T(8,128)(2,1)S(1)}, bf16[1024,256]{1,0:T(8,128)(2,1)S(1)}, u32[]{:S(2)}, u32[]{:S(2)}) collective-permute-start(bf16[1024,256]{1,0:T(8,128)(2,1)S(1)} %shard_map.104), channel_id=1, source_target_pairs={{12,8},{13,9},{14,10},{15,11},{16,12},{17,13},{18,14},{19,15},{20,... | collective-permute-start | bytes 1572872 | tf_op jit(solution)/shard_map/ppermute | solution.py:169
  74.5 20.5 %collective-permute-start.28 = (bf16[256,1024]{1,0:T(8,128)(2,1)S(1)}, bf16[256,1024]{1,0:T(8,128)(2,1)S(1)}, u32[]{:S(2)}, u32[]{:S(2)}) collective-permute-start(bf16[256,1024]{1,0:T(8,128)(2,1)S(1)} %get-tuple-element.41.refs_5_), channel_id=1, source_target_pairs={{0,240},{1,241},{2,242},{3,243}} | collective-permute-start | bytes 1572872 | tf_op jit(solution)/shard_map/ppermute | solution.py:169
  85.9 10.4 %collective-permute-start.10 = (bf16[256,1024]{1,0:T(8,128)(2,1)S(1)}, bf16[256,1024]{1,0:T(8,128)(2,1)S(1)}, u32[]{:S(2)}, u32[]{:S(2)}) collective-permute-start(bf16[256,1024]{1,0:T(8,128)(2,1)S(1)} %collective-permute-done.9.rest_0_.refs_7_), channel_id=1, source_target_pairs={{252,253},{253,252},{254,255},{255,254}} | collective-permute-start | bytes 1572872 | tf_op jit(solution)/shard_map/ppermute | solution.py:169
  86.6 13.6 %collective-permute-start.13 = (bf16[1024,256]{1,0:T(8,128)(2,1)S(1)}, bf16[1024,256]{1,0:T(8,128)(2,1)S(1)}, u32[]{:S(2)}, u32[]{:S(2)}) collective-permute-start(bf16[1024,256]{1,0:T(8,128)(2,1)S(1)} %get-tuple-element.36), channel_id=1, source_target_pairs={{0,4},{1,5},{2,6},{3,7},{4,8},{5,9},{6,10},{7,11},{8,12},{9,13},{1... | collective-permute-start | bytes 1572872 | tf_op jit(solution)/shard_map/ppermute | solution.py:169
  89.3 18.9 %collective-permute-start.7 = (bf16[1024,256]{1,0:T(8,128)(2,1)S(1)}, bf16[1024,256]{1,0:T(8,128)(2,1)S(1)}, u32[]{:S(2)}, u32[]{:S(2)}) collective-permute-start(bf16[1024,256]{1,0:T(8,128)(2,1)S(1)} %get-tuple-element.33), channel_id=1, source_target_pairs={{0,4},{1,5},{2,6},{3,7},{4,8},{5,9},{6,10},{7,11},{8,12},{9,13},{1... | collective-permute-start | bytes 1572872 | tf_op jit(solution)/shard_map/ppermute | solution.py:169
  92.1 21.8 %collective-permute-start.32 = (bf16[1024,256]{1,0:T(8,128)(2,1)S(1)}, bf16[1024,256]{1,0:T(8,128)(2,1)S(1)}, u32[]{:S(2)}, u32[]{:S(2)}) collective-permute-start(bf16[1024,256]{1,0:T(8,128)(2,1)S(1)} %shard_map.108), channel_id=1, source_target_pairs={{8,4},{9,5},{10,6},{11,7},{12,8},{13,9},{14,10},{15,11},{16,12},{1... | collective-permute-start | bytes 1572872 | tf_op jit(solution)/shard_map/ppermute | solution.py:169
  95.0 25.5 %collective-permute-start.26 = (bf16[256,1024]{1,0:T(8,128)(2,1)S(1)}, bf16[256,1024]{1,0:T(8,128)(2,1)S(1)}, u32[]{:S(2)}, u32[]{:S(2)}) collective-permute-start(bf16[256,1024]{1,0:T(8,128)(2,1)S(1)} %collective-permute-done.25), channel_id=1, source_target_pairs={{240,2},{241,3},{242,0},{243,1},{12,254},{13,255},{14,252},{15,253}} | collective-permute-start | bytes 1572872 | tf_op jit(solution)/shard_map/ppermute | solution.py:169
  96.3 32.0 %collective-permute-start.29 = (bf16[256,1024]{1,0:T(8,128)(2,1)S(1)}, bf16[256,1024]{1,0:T(8,128)(2,1)S(1)}, u32[]{:S(2)}, u32[]{:S(2)}) collective-permute-start(bf16[256,1024]{1,0:T(8,128)(2,1)S(1)} %collective-permute-done.28), channel_id=1, source_target_pairs={{240,2},{241,3},{242,0},{243,1}} | collective-permute-start | bytes 1572872 | tf_op jit(solution)/shard_map/ppermute | solution.py:169
  100.2 30.1 %collective-permute-start.23 = (bf16[1024,256]{1,0:T(8,128)(2,1)S(1)}, bf16[1024,256]{1,0:T(8,128)(2,1)S(1)}, u32[]{:S(2)}, u32[]{:S(2)}) collective-permute-start(bf16[1024,256]{1,0:T(8,128)(2,1)S(1)} %shard_map.105), channel_id=1, source_target_pairs={{8,4},{9,5},{10,6},{11,7},{12,8},{13,9},{14,10},{15,11},{16,12},{1... | collective-permute-start | bytes 1572872 | tf_op jit(solution)/shard_map/ppermute | solution.py:169
  108.3 24.6 %collective-permute-start.14 = (bf16[1024,256]{1,0:T(8,128)(2,1)S(1)}, bf16[1024,256]{1,0:T(8,128)(2,1)S(1)}, u32[]{:S(2)}, u32[]{:S(2)}) collective-permute-start(bf16[1024,256]{1,0:T(8,128)(2,1)S(1)} %get-tuple-element.37), channel_id=1, source_target_pairs={{0,4},{1,5},{2,6},{3,7},{4,8},{5,9},{6,10},{7,11},{8,12},{9,13},{1... | collective-permute-start | bytes 1572872 | tf_op jit(solution)/shard_map/ppermute | solution.py:169
  114.0 22.3 %collective-permute-start.8 = (bf16[1024,256]{1,0:T(8,128)(2,1)S(1)}, bf16[1024,256]{1,0:T(8,128)(2,1)S(1)}, u32[]{:S(2)}, u32[]{:S(2)}) collective-permute-start(bf16[1024,256]{1,0:T(8,128)(2,1)S(1)} %get-tuple-element.34), channel_id=1, source_target_pairs={{0,4},{1,5},{2,6},{3,7},{4,8},{5,9},{6,10},{7,11},{8,12},{9,13},{1... | collective-permute-start | bytes 1572872 | tf_op jit(solution)/shard_map/ppermute | solution.py:169
  120.5 17.8 %collective-permute-start.27 = (bf16[256,1024]{1,0:T(8,128)(2,1)S(1)}, bf16[256,1024]{1,0:T(8,128)(2,1)S(1)}, u32[]{:S(2)}, u32[]{:S(2)}) collective-permute-start(bf16[256,1024]{1,0:T(8,128)(2,1)S(1)} %collective-permute-done.26.refs_12_), channel_id=1, source_target_pairs={{0,1},{1,0},{2,3},{3,2},{252,253},{253,252},{254,255},{255,254}} | collective-permute-start | bytes 1572872 | tf_op jit(solution)/shard_map/ppermute | solution.py:169
  128.3 10.0 %collective-permute-start.30 = (bf16[256,1024]{1,0:T(8,128)(2,1)S(1)}, bf16[256,1024]{1,0:T(8,128)(2,1)S(1)}, u32[]{:S(2)}, u32[]{:S(2)}) collective-permute-start(bf16[256,1024]{1,0:T(8,128)(2,1)S(1)} %collective-permute-done.29.refs_14_), channel_id=1, source_target_pairs={{0,1},{1,0},{2,3},{3,2}} | collective-permute-start | bytes 1572872 | tf_op jit(solution)/shard_map/ppermute | solution.py:169
  130.3 16.7 %collective-permute-start.33 = (bf16[1024,256]{1,0:T(8,128)(2,1)S(1)}, bf16[1024,256]{1,0:T(8,128)(2,1)S(1)}, u32[]{:S(2)}, u32[]{:S(2)}) collective-permute-start(bf16[1024,256]{1,0:T(8,128)(2,1)S(1)} %shard_map.109), channel_id=1, source_target_pairs={{4,0},{5,1},{6,2},{7,3},{8,4},{9,5},{10,6},{11,7},{12,8},{13,9},{1... | collective-permute-start | bytes 1572872 | tf_op jit(solution)/shard_map/ppermute | solution.py:169
  132.8 24.9 %collective-permute-start.24 = (bf16[1024,256]{1,0:T(8,128)(2,1)S(1)}, bf16[1024,256]{1,0:T(8,128)(2,1)S(1)}, u32[]{:S(2)}, u32[]{:S(2)}) collective-permute-start(bf16[1024,256]{1,0:T(8,128)(2,1)S(1)} %shard_map.106), channel_id=1, source_target_pairs={{4,0},{5,1},{6,2},{7,3},{8,4},{9,5},{10,6},{11,7},{12,8},{13,9},{1... | collective-permute-start | bytes 1572872 | tf_op jit(solution)/shard_map/ppermute | solution.py:169

commit v6 on v5

--- a/solution.py
+++ b/solution.py
@@ -50,30 +50,6 @@
     )(*arrays)
 
 
-def products(blocks, down_in, new):
-    spot = lax.axis_index("shot")
-    for k, block in enumerate(blocks):
-        new[band(spot ^ k, block.shape[0]), :] = dot(block[...], down_in[...]).astype(BF16)
-
-
-def fix_kernel(plan, b0, b1, b2, b3, received, sources, *refs):
-    n = len(refs) // 2
-    inside = lax.axis_index("layer") == lax.axis_size("layer") // 2
-
-    @pl.when(inside)
-    def _():
-        for chunk in range(n // 2):
-            new, down_in = refs[n + 2 * chunk : n + 2 * chunk + 2]
-            cols = columns(sources, chunk, new.shape[1])
-            down_in[...] = injected(received[:, cols], sources[plan[0, 0], :, cols])
-            products((b0, b1, b2, b3), down_in, new)
-
-    @pl.when(jnp.logical_not(inside))
-    def _():
-        for old, new in zip(refs[:n], refs[n:]):
-            new[...] = old[...]
-
-
 def columns(ref, chunk, width):
     return slice(chunk * width, (chunk + 1) * width) if ref.shape[-1] > width else slice(None)
 
@@ -84,22 +60,8 @@
     spot = lax.axis_index("shot")
     cols = columns(sources, chunk, down_in.shape[1])
 
-    def take(ref):
-        value = ref[:, columns(ref, chunk, down_in.shape[1])]
-        down_in[...] = injected(value, sources[plan[0, moment], :, cols])
-
-    if moment == 1:
-
-        @pl.when(layer == count // 2)
-        def _():
-            take(others[0])
-
-        @pl.when(layer != count // 2)
-        def _():
-            take(received)
-
-    else:
-        take(received)
+    source = sources[plan[0, moment], :, cols]
+    down_in[...] = injected(received[:, columns(received, chunk, down_in.shape[1])], source)
     for k, block in enumerate((b0, b1, b2, b3)):
         high, value = block.shape[0], block[...]
         if moment == TICKS - 1 and k >= 2:
@@ -194,9 +156,7 @@
         return sent(value, [(at(l, s), at(l, s ^ bit)) for l in members for s in range(shots)])
 
     middle = [l for l in every if 0 < l < layers - 1]
-    cut = layers // 2
-    down_0b = link(down_state[0], [(cut - 1, cut)], 0)
-    down_0 = shift(down_state[0], 1, [cut - 1])
+    down_0 = shift(down_state[0], 1)
     far_d = swap(down_op, 2, [0] + middle)
     up_0 = shift(up_state[0], -1, [1, 2, 3])
     far_e = swap(down_op, 2, [layers - 1])
@@ -221,34 +181,18 @@
         op = link(op, [(b, a) for a, b in pairs], 2)
         late += [op, link(op, [(a, a) for a, _ in pairs], 1)]
     piece = (height, width)
-    firsts, specials = [], []
-    for chunk in range(CHUNKS):
-        new, down_in = call(
-            functools.partial(down_kernel, 0, chunk), plan,
-            [*d_blocks, down_0, sources], [piece] * 2, one,
-        )
-        firsts += [new, down_in]
-        specials.append(link(new, [(cut - 1, cut)], 0))
-    firsts = call(
-        fix_kernel, plan, [*d_blocks, down_0b, sources, *firsts], [piece] * (2 * CHUNKS), one // 8
-    )
-    downs = [shift(firsts[2 * i], 1, [cut - 1]) for i in range(CHUNKS)]
-    ups = [up_0] * CHUNKS
+    downs, ups = [down_0] * CHUNKS, [up_0] * CHUNKS
     for moment in range(TICKS):
         last = moment == TICKS - 1
         new_downs, new_ups, new, up = [], [], None, None
         for chunk in range(CHUNKS):
             full = (chunk, wide) if last else None
-            if moment:
-                more = [specials[chunk]] if moment == 1 else [far_e, cross_e] if last else []
-                new, down_in = call(
-                    functools.partial(down_kernel, moment, chunk), plan,
-                    [*d_blocks, downs[chunk], sources], [piece] * 2, one,
-                    full=full, into=new if last else None, more=more,
-                )
-                new_downs.append(new)
-            else:
-                down_in = firsts[2 * chunk + 1]
+            new, down_in = call(
+                functools.partial(down_kernel, moment, chunk), plan,
+                [*d_blocks, downs[chunk], sources], [piece] * 2, one,
+                full=full, into=new if last else None, more=[far_e, cross_e] if last else [],
+            )
+            new_downs.append(new)
             (up,) = call(
                 functools.partial(up_kernel, chunk, last), layer_source,
                 [*u_blocks, ups[chunk], down_in, sources], [piece], 2 * one,
@@ -257,8 +201,7 @@
             new_ups.append(up)
         if last:
             return (new[None], up[None])
-        if moment:
-            downs = [shift(a, 1) for a in new_downs]
+        downs = [shift(a, 1) for a in new_downs]
         without_top = range(1, TICKS - 1 - moment)
         ups = [shift(a, -1, without_top) for a in new_ups]
 

time: 163 us -> 157 us (0.963)
  starting transfers between devices: 56.7 us -> 54.3 us
  waiting for transfers between devices: 71.7 us -> 69.5 us
    ppermute x34 -> x31, starting transfers between devices: 56.7 us -> 54.3 us  [sent(): return lax.ppermute(value, ('layer', 'shot'), pairs)]
    ppermute x34 -> x31, waiting for transfers between devices: 71.7 us -> 69.5 us  [sent(): return lax.ppermute(value, ('layer', 'shot'), pairs)]
    pallas_call x17 -> x16, Pallas kernels: 24.7 us -> 23.7 us  [call(): pl.pallas_call(kernel, grid=(1,), in_specs=in_specs, out_specs=out_specs,...]
    unnamed x10 -> x12, local copies, waits for them, and re-layouts: 4.72 us -> 4.72 us
  transfers between devices with their start and end apart: 34 -> 31, of which waited for: 10 -> 9; matrix products, arithmetic and copies ran while one was open for 0% -> 0% of each run, Pallas kernels for 14% -> 14%
where the time goes in v6:
time: 157 us; the launch traced here: 154 us
  waiting for transfers between devices  69.5 us (44%)
  starting transfers between devices  54.3 us (35%)
  Pallas kernels  24 us (15%)
  local copies, waits for them, and re-layouts  4.72 us (3%)
  between operations  1.76 us (1%)
    ppermute x31, waiting for transfers between devices, sent(): return lax.ppermute(value, ('layer', 'shot'), pairs)  69.5 us
    ppermute x31, starting transfers between devices, sent(): return lax.ppermute(value, ('layer', 'shot'), pairs)  54.3 us
    pallas_call x16, Pallas kernels, call(): pl.pallas_call(kernel, grid=(1,), in_specs=in_specs, out_specs=out_specs,...  23.7 us
    unnamed x12, local copies, waits for them, and re-layouts  4.72 us
  transfers between devices with their start and end apart: 31, of which 9 were waited for; matrix products, arithmetic and copies ran while one was open for 0% of the time, Pallas kernels for 14%

profile of v6, /device:TPU:8, one launch (start us, length us, event | category | flops | bytes accessed | tf_op | source)
XLA Modules:
  0.0 154.4 jit_solution(16743024698425347601)
XLA Ops:
  0.6 4.1 %collective-permute-start.1 = (bf16[256,1024]{1,0:T(8,128)(2,1)}, bf16[256,1024]{1,0:T(8,128)(2,1)S(1)}, u32[]{:S(2)}, u32[]{:S(2)}) collective-permute-start(bf16[256,1024]{1,0:T(8,128)(2,1)} %bitcast.16), channel_id=1, source_target_pairs={{0,2},{1,3},{2,0},{3,1},{4,6},{5,7},{6,4},{7,5},{8,10},{9,11},{10,... | collective-permute-start | bytes 1572872 | tf_op jit(solution)/shard_map/ppermute | solution.py:131
  4.7 1.8 %collective-permute-start.3 = (bf16[1024,512]{1,0:T(8,128)(2,1)}, bf16[1024,512]{1,0:T(8,128)(2,1)S(1)}, u32[]{:S(2)}, u32[]{:S(2)}) collective-permute-start(bf16[1024,512]{1,0:T(8,128)(2,1)} %bitcast.30), channel_id=1, source_target_pairs={{0,4},{1,5},{2,6},{3,7},{4,8},{5,9},{6,10},{7,11},{8,12},{9,13},{1... | collective-permute-start | bytes 3145736 | tf_op jit(solution)/shard_map/ppermute | solution.py:131
  8.0 30.9 %collective-permute-done.1.b2.refs_3_ = bf16[256,1024]{1,0:T(8,128)(2,1)S(1)} collective-permute-done((bf16[256,1024]{1,0:T(8,128)(2,1)}, bf16[256,1024]{1,0:T(8,128)(2,1)S(1)}, u32[]{:S(2)}, u32[]{:S(2)}) %collective-permute-start.1) | collective-permute-done | bytes 524320 | tf_op jit(solution)/shard_map/ppermute | solution.py:131
  38.9 0.7 collective-permute-start.18
  41.3 1.6 %copy-done = bf16[1,2,1024,512]{3,2,1,0:T(8,128)(2,1)S(1)} copy-done((bf16[1,2,1024,512]{3,2,1,0:T(8,128)(2,1)S(1)}, bf16[1,2,1024,512]{3,2,1,0:T(8,128)(2,1)}, u32[]{:S(2)}) %copy-start) | copy-done | bytes 2097176
  42.9 1.0 copy-done.1
  43.9 1.0 copy-done.2
  45.0 1.0 copy-done.3
  46.3 1.3 shard_map.98
  47.6 1.6 %collective-permute-start.9 = (bf16[1024,256]{1,0:T(8,128)(2,1)S(1)}, bf16[1024,256]{1,0:T(8,128)(2,1)S(1)}, u32[]{:S(2)}, u32[]{:S(2)}) collective-permute-start(bf16[1024,256]{1,0:T(8,128)(2,1)S(1)} %get-tuple-element.27), channel_id=1, source_target_pairs={{0,4},{1,5},{2,6},{3,7},{4,8},{5,9},{6,10},{7,11},{8,12},{9,13},{1... | collective-permute-start | bytes 1572872 | tf_op jit(solution)/shard_map/ppermute | solution.py:131
  49.9 1.3 shard_map.95
  51.2 0.7 collective-permute-start.7
  51.9 9.5 %collective-permute-start.22 = (bf16[256,1024]{1,0:T(8,128)(2,1)S(1)}, bf16[256,1024]{1,0:T(8,128)(2,1)S(1)}, u32[]{:S(2)}, u32[]{:S(2)}) collective-permute-start(bf16[256,1024]{1,0:T(8,128)(2,1)S(1)} %get-tuple-element.32.refs_1_), channel_id=1, source_target_pairs={{0,240},{1,241},{2,242},{3,243},{252,12},{253,13},{254,14},{255,15}} | collective-permute-start | bytes 1572872 | tf_op jit(solution)/shard_map/ppermute | solution.py:131
  61.5 1.3 collective-permute-start.4
  62.8 1.3 shard_map.106
  64.1 0.7 collective-permute-start.28
  64.8 1.3 shard_map.103
  66.7 1.3 shard_map.99
  68.1 10.4 %collective-permute-start.25 = (bf16[256,1024]{1,0:T(8,128)(2,1)S(1)}, bf16[256,1024]{1,0:T(8,128)(2,1)S(1)}, u32[]{:S(2)}, u32[]{:S(2)}) collective-permute-start(bf16[256,1024]{1,0:T(8,128)(2,1)S(1)} %get-tuple-element.33.refs_5_), channel_id=1, source_target_pairs={{0,240},{1,241},{2,242},{3,243}} | collective-permute-start | bytes 1572872 | tf_op jit(solution)/shard_map/ppermute | solution.py:131
  79.2 1.3 collective-permute-start.10
  80.5 1.3 shard_map.96
  81.8 1.3 collective-permute-start.5
  83.2 1.3 shard_map.107
  85.2 1.3 shard_map.104
  86.4 2.1 %collective-permute-done.25 = bf16[256,1024]{1,0:T(8,128)(2,1)S(1)} collective-permute-done((bf16[256,1024]{1,0:T(8,128)(2,1)S(1)}, bf16[256,1024]{1,0:T(8,128)(2,1)S(1)}, u32[]{:S(2)}, u32[]{:S(2)}) %collective-permute-start.25) | collective-permute-done | bytes 524320 | tf_op jit(solution)/shard_map/ppermute | solution.py:131
  88.5 1.3 collective-permute-start.23
  89.8 1.3 collective-permute-start.26
  91.1 1.7 %collective-permute-done.10.received = bf16[1024,256]{1,0:T(8,128)(2,1)S(1)} collective-permute-done((bf16[1024,256]{1,0:T(8,128)(2,1)S(1)}, bf16[1024,256]{1,0:T(8,128)(2,1)S(1)}, u32[]{:S(2)}, u32[]{:S(2)}) %collective-permute-start.10) | collective-permute-done | bytes 524320 | tf_op jit(solution)/shard_map/ppermute | solution.py:131
  92.8 0.9 collective-permute-start.20
  93.7 1.3 shard_map.100
  94.9 6.8 %collective-permute-done.5.received = bf16[1024,256]{1,0:T(8,128)(2,1)S(1)} collective-permute-done((bf16[1024,256]{1,0:T(8,128)(2,1)S(1)}, bf16[1024,256]{1,0:T(8,128)(2,1)S(1)}, u32[]{:S(2)}, u32[]{:S(2)}) %collective-permute-start.5) | collective-permute-done | bytes 524320 | tf_op jit(solution)/shard_map/ppermute | solution.py:131
  101.8 4.4 %collective-permute-start.11 = (bf16[1024,256]{1,0:T(8,128)(2,1)S(1)}, bf16[1024,256]{1,0:T(8,128)(2,1)S(1)}, u32[]{:S(2)}, u32[]{:S(2)}) collective-permute-start(bf16[1024,256]{1,0:T(8,128)(2,1)S(1)} %get-tuple-element.29), channel_id=1, source_target_pairs={{0,4},{1,5},{2,6},{3,7},{4,8},{5,9},{6,10},{7,11},{8,12},{9,13},{1... | collective-permute-start | bytes 1572872 | tf_op jit(solution)/shard_map/ppermute | solution.py:131
  106.2 1.3 shard_map.97
  107.5 1.9 %collective-permute-start.6 = (bf16[1024,256]{1,0:T(8,128)(2,1)S(1)}, bf16[1024,256]{1,0:T(8,128)(2,1)S(1)}, u32[]{:S(2)}, u32[]{:S(2)}) collective-permute-start(bf16[1024,256]{1,0:T(8,128)(2,1)S(1)} %get-tuple-element.26), channel_id=1, source_target_pairs={{0,4},{1,5},{2,6},{3,7},{4,8},{5,9},{6,10},{7,11},{8,12},{9,13},{1... | collective-permute-start | bytes 1572872 | tf_op jit(solution)/shard_map/ppermute | solution.py:131
  109.4 1.3 shard_map.108
  110.7 2.9 %collective-permute-done.23.refs_12_ = bf16[256,1024]{1,0:T(8,128)(2,1)S(1)} collective-permute-done((bf16[256,1024]{1,0:T(8,128)(2,1)S(1)}, bf16[256,1024]{1,0:T(8,128)(2,1)S(1)}, u32[]{:S(2)}, u32[]{:S(2)}) %collective-permute-start.23) | collective-permute-done | bytes 524320 | tf_op jit(solution)/shard_map/ppermute | solution.py:131
  113.6 1.9 %collective-permute-start.24 = (bf16[256,1024]{1,0:T(8,128)(2,1)S(1)}, bf16[256,1024]{1,0:T(8,128)(2,1)S(1)}, u32[]{:S(2)}, u32[]{:S(2)}) collective-permute-start(bf16[256,1024]{1,0:T(8,128)(2,1)S(1)} %collective-permute-done.23.refs_12_), channel_id=1, source_target_pairs={{0,1},{1,0},{2,3},{3,2},{252,253},{253,252},{254,255},{255,254}} | collective-permute-start | bytes 1572872 | tf_op jit(solution)/shard_map/ppermute | solution.py:131
  115.5 7.4 %collective-permute-done.26.refs_14_ = bf16[256,1024]{1,0:T(8,128)(2,1)S(1)} collective-permute-done((bf16[256,1024]{1,0:T(8,128)(2,1)S(1)}, bf16[256,1024]{1,0:T(8,128)(2,1)S(1)}, u32[]{:S(2)}, u32[]{:S(2)}) %collective-permute-start.26) | collective-permute-done | bytes 524320 | tf_op jit(solution)/shard_map/ppermute | solution.py:131
  122.9 1.9 %collective-permute-start.27 = (bf16[256,1024]{1,0:T(8,128)(2,1)S(1)}, bf16[256,1024]{1,0:T(8,128)(2,1)S(1)}, u32[]{:S(2)}, u32[]{:S(2)}) collective-permute-start(bf16[256,1024]{1,0:T(8,128)(2,1)S(1)} %collective-permute-done.26.refs_14_), channel_id=1, source_target_pairs={{0,1},{1,0},{2,3},{3,2}} | collective-permute-start | bytes 1572872 | tf_op jit(solution)/shard_map/ppermute | solution.py:131
  124.8 1.3 collective-permute-start.30
  126.1 1.3 shard_map.105
  127.4 1.3 collective-permute-start.21
  128.7 2.1 %shard_map.101 = (bf16[1024,512]{1,0:T(8,128)(2,1)}, bf16[1024,256]{1,0:T(8,128)(2,1)S(1)}) custom-call(s32[1,4]{1,0:T(1,128)S(1)} %bitcast.26, bf16[256,1024]{1,0:T(8,128)(2,1)S(1)} %get-tuple-element.22.b0.refs_1_, bf16[256,1024]{1,0:T(8,128)(2,1)S(1)} %collective-permute-done.b1.refs_2_, bf16[256,1024]{1,0:T(8,128)(2,1)S(1)} %collective-permute-done.1.b2.refs_3_, ...), custom_call_target="tpu_custom_call" | custom-call | flops 536870912 | bytes 1048576 | tf_op jit(solution)/shard_map/pallas_call | solution.py:111
  130.8 2.1 %shard_map.102 = (bf16[1024,512]{1,0:T(8,128)(2,1)}, bf16[1024,256]{1,0:T(8,128)(2,1)S(1)}) custom-call(s32[1,4]{1,0:T(1,128)S(1)} %bitcast.27, bf16[256,1024]{1,0:T(8,128)(2,1)S(1)} %get-tuple-element.22.b0.refs_1_, bf16[256,1024]{1,0:T(8,128)(2,1)S(1)} %collective-permute-done.b1.refs_2_, ...), custom_call_target="tpu_custom_call", output_to_operand_aliasing={{0}: (9, {})} | custom-call | flops 536870912 | bytes 1048576 | tf_op jit(solution)/shard_map/pallas_call | solution.py:111
  132.9 8.6 %collective-permute-done.30.refs_9_ = bf16[1024,256]{1,0:T(8,128)(2,1)S(1)} collective-permute-done((bf16[1024,256]{1,0:T(8,128)(2,1)S(1)}, bf16[1024,256]{1,0:T(8,128)(2,1)S(1)}, u32[]{:S(2)}, u32[]{:S(2)}) %collective-permute-start.30) | collective-permute-done | bytes 524320 | tf_op jit(solution)/shard_map/ppermute | solution.py:131
  141.5 2.1 %shard_map.109.refs_16_ = bf16[1024,512]{1,0:T(8,128)(2,1)} custom-call(s32[1]{0:T(128)S(6)} %copy.14.refs_0_, bf16[256,1024]{1,0:T(8,128)(2,1)S(1)} %get-tuple-element.32.refs_1_, bf16[256,1024]{1,0:T(8,128)(2,1)S(1)} %collective-permute-done.12.refs_2_, bf16[256,1024]{1,0:T(8,128)(2,1)S(1)} %collective-permute-done.13.refs_3_, ...), custom_call_target="tpu_custom_call" | custom-call | flops 1073741824 | bytes 1048576 | tf_op jit(solution)/shard_map/pallas_call | solution.py:111
  143.6 8.7 %collective-permute-done.21.refs_9_ = bf16[1024,256]{1,0:T(8,128)(2,1)S(1)} collective-permute-done((bf16[1024,256]{1,0:T(8,128)(2,1)S(1)}, bf16[1024,256]{1,0:T(8,128)(2,1)S(1)}, u32[]{:S(2)}, u32[]{:S(2)}) %collective-permute-start.21) | collective-permute-done | bytes 524320 | tf_op jit(solution)/shard_map/ppermute | solution.py:131
  152.3 2.1 %shard_map.110 = bf16[1024,512]{1,0:T(8,128)(2,1)} custom-call(s32[1]{0:T(128)S(6)} %copy.14.refs_0_, bf16[256,1024]{1,0:T(8,128)(2,1)S(1)} %get-tuple-element.32.refs_1_, bf16[256,1024]{1,0:T(8,128)(2,1)S(1)} %collective-permute-done.12.refs_2_, bf16[256,1024]{1,0:T(8,128)(2,1)S(1)} %collective-permute-done.13.refs_3_, ...), custom_call_target="tpu_custom_call", output_to_operand_aliasing={{}: (16, {})} | custom-call | flops 1073741824 | bytes 1048576 | tf_op jit(solution)/shard_map/pallas_call | solution.py:111
  (43 shorter events, 5.6 us)
Async XLA Ops:
  0.6 45.7 %copy-start.5 = (s32[4,1]{0,1:T(1,128)S(1)}, s32[4,1]{0,1:T(1,128)}, u32[]{:S(2)}) copy-start(s32[4,1]{0,1:T(1,128)} %param.14) | copy-start | bytes 52
  0.6 38.2 %collective-permute-start.1 = (bf16[256,1024]{1,0:T(8,128)(2,1)}, bf16[256,1024]{1,0:T(8,128)(2,1)S(1)}, u32[]{:S(2)}, u32[]{:S(2)}) collective-permute-start(bf16[256,1024]{1,0:T(8,128)(2,1)} %bitcast.16), channel_id=1, source_target_pairs={{0,2},{1,3},{2,0},{3,1},{4,6},{5,7},{6,4},{7,5},{8,10},{9,11},{10,... | collective-permute-start | bytes 1572872 | tf_op jit(solution)/shard_map/ppermute | solution.py:131
  4.7 36.2 %collective-permute-start.3 = (bf16[1024,512]{1,0:T(8,128)(2,1)}, bf16[1024,512]{1,0:T(8,128)(2,1)S(1)}, u32[]{:S(2)}, u32[]{:S(2)}) collective-permute-start(bf16[1024,512]{1,0:T(8,128)(2,1)} %bitcast.30), channel_id=1, source_target_pairs={{0,4},{1,5},{2,6},{3,7},{4,8},{5,9},{6,10},{7,11},{8,12},{9,13},{1... | collective-permute-start | bytes 3145736 | tf_op jit(solution)/shard_map/ppermute | solution.py:131
  6.5 32.4 %collective-permute-start = (bf16[256,1024]{1,0:T(8,128)(2,1)}, bf16[256,1024]{1,0:T(8,128)(2,1)S(1)}, u32[]{:S(2)}, u32[]{:S(2)}) collective-permute-start(bf16[256,1024]{1,0:T(8,128)(2,1)} %bitcast.17), channel_id=1, source_target_pairs={{0,1},{1,0},{2,3},{3,2},{4,5},{5,4},{6,7},{7,6},{8,9},{9,8},{10,11... | collective-permute-start | bytes 1572872 | tf_op jit(solution)/shard_map/ppermute | solution.py:131
  6.6 33.0 %collective-permute-start.13 = (bf16[256,1024]{1,0:T(8,128)(2,1)}, bf16[256,1024]{1,0:T(8,128)(2,1)S(1)}, u32[]{:S(2)}, u32[]{:S(2)}) collective-permute-start(bf16[256,1024]{1,0:T(8,128)(2,1)} %bitcast.10), channel_id=1, source_target_pairs={{4,6},{5,7},{6,4},{7,5},{8,10},{9,11},{10,8},{11,9},{12,14},{13,15... | collective-permute-start | bytes 1572872 | tf_op jit(solution)/shard_map/ppermute | solution.py:131
  7.3 32.9 %collective-permute-start.16 = (bf16[256,1024]{1,0:T(8,128)(2,1)}, bf16[256,1024]{1,0:T(8,128)(2,1)S(1)}, u32[]{:S(2)}, u32[]{:S(2)}) collective-permute-start(bf16[256,1024]{1,0:T(8,128)(2,1)} %bitcast.13), channel_id=1, source_target_pairs={{4,6},{5,7},{6,4},{7,5},{8,10},{9,11},{10,8},{11,9},{12,14},{13,15... | collective-permute-start | bytes 1572872 | tf_op jit(solution)/shard_map/ppermute | solution.py:131
  38.9 1.9 %collective-permute-start.2 = (bf16[256,1024]{1,0:T(8,128)(2,1)S(1)}, bf16[256,1024]{1,0:T(8,128)(2,1)S(1)}, u32[]{:S(2)}, u32[]{:S(2)}) collective-permute-start(bf16[256,1024]{1,0:T(8,128)(2,1)S(1)} %collective-permute-done.1.b2.refs_3_), channel_id=1, source_target_pairs={{0,1},{1,0},{2,3},{3,2},{4,5},{5,4},{6,7},{7,6},{8,9},{9,8},{10,11... | collective-permute-start | bytes 1572872 | tf_op jit(solution)/shard_map/ppermute | solution.py:131
  38.9 23.9 %collective-permute-start.18 = (bf16[1024,512]{1,0:T(8,128)(2,1)}, bf16[1024,512]{1,0:T(8,128)(2,1)S(1)}, u32[]{:S(2)}, u32[]{:S(2)}) collective-permute-start(bf16[1024,512]{1,0:T(8,128)(2,1)} %bitcast.31), channel_id=1, source_target_pairs={{16,12},{17,13},{18,14},{19,15},{20,16},{21,17},{22,18},{23,19},{2... | collective-permute-start | bytes 3145736 | tf_op jit(solution)/shard_map/ppermute | solution.py:131
  39.6 8.0 %collective-permute-start.12 = (bf16[256,1024]{1,0:T(8,128)(2,1)}, bf16[256,1024]{1,0:T(8,128)(2,1)S(1)}, u32[]{:S(2)}, u32[]{:S(2)}) collective-permute-start(bf16[256,1024]{1,0:T(8,128)(2,1)} %bitcast.11), channel_id=1, source_target_pairs={{0,1},{1,0},{2,3},{3,2},{4,5},{5,4},{6,7},{7,6},{8,9},{9,8},{10,11... | collective-permute-start | bytes 1572872 | tf_op jit(solution)/shard_map/ppermute | solution.py:131
  40.2 11.0 %collective-permute-start.15 = (bf16[256,1024]{1,0:T(8,128)(2,1)}, bf16[256,1024]{1,0:T(8,128)(2,1)S(1)}, u32[]{:S(2)}, u32[]{:S(2)}) collective-permute-start(bf16[256,1024]{1,0:T(8,128)(2,1)} %bitcast.14), channel_id=1, source_target_pairs={{0,1},{1,0},{2,3},{3,2},{4,5},{5,4},{6,7},{7,6},{8,9},{9,8},{10,11... | collective-permute-start | bytes 1572872 | tf_op jit(solution)/shard_map/ppermute | solution.py:131
  40.8 11.1 %collective-permute-start.14 = (bf16[256,1024]{1,0:T(8,128)(2,1)S(1)}, bf16[256,1024]{1,0:T(8,128)(2,1)S(1)}, u32[]{:S(2)}, u32[]{:S(2)}) collective-permute-start(bf16[256,1024]{1,0:T(8,128)(2,1)S(1)} %collective-permute-done.13.refs_3_), channel_id=1, source_target_pairs={{0,1},{1,0},{2,3},{3,2},{4,5},{5,4},{6,7},{7,6},{8,9},{9,8},{10,11... | collective-permute-start | bytes 1572872 | tf_op jit(solution)/shard_map/ppermute | solution.py:131
  40.9 20.5 %collective-permute-start.17 = (bf16[256,1024]{1,0:T(8,128)(2,1)S(1)}, bf16[256,1024]{1,0:T(8,128)(2,1)S(1)}, u32[]{:S(2)}, u32[]{:S(2)}) collective-permute-start(bf16[256,1024]{1,0:T(8,128)(2,1)S(1)} %collective-permute-done.16.refs_7_), channel_id=1, source_target_pairs={{0,1},{1,0},{2,3},{3,2},{4,5},{5,4},{6,7},{7,6},{8,9},{9,8},{10,11... | collective-permute-start | bytes 1572872 | tf_op jit(solution)/shard_map/ppermute | solution.py:131
  41.3 1.6 %copy-start = (bf16[1,2,1024,512]{3,2,1,0:T(8,128)(2,1)S(1)}, bf16[1,2,1024,512]{3,2,1,0:T(8,128)(2,1)}, u32[]{:S(2)}) copy-start(bf16[1,2,1024,512]{3,2,1,0:T(8,128)(2,1)} %param.13) | copy-start | bytes 6291460
  42.9 1.0 copy-start.1
  43.9 1.0 copy-start.2
  45.0 1.0 copy-start.3
  47.6 18.4 %collective-permute-start.9 = (bf16[1024,256]{1,0:T(8,128)(2,1)S(1)}, bf16[1024,256]{1,0:T(8,128)(2,1)S(1)}, u32[]{:S(2)}, u32[]{:S(2)}) collective-permute-start(bf16[1024,256]{1,0:T(8,128)(2,1)S(1)} %get-tuple-element.27), channel_id=1, source_target_pairs={{0,4},{1,5},{2,6},{3,7},{4,8},{5,9},{6,10},{7,11},{8,12},{9,13},{1... | collective-permute-start | bytes 1572872 | tf_op jit(solution)/shard_map/ppermute | solution.py:131
  49.9 1.3 copy-start.4
  51.2 16.8 %collective-permute-start.7 = (bf16[256,1024]{1,0:T(8,128)(2,1)S(1)}, bf16[256,1024]{1,0:T(8,128)(2,1)S(1)}, u32[]{:S(2)}, u32[]{:S(2)}) collective-permute-start(bf16[256,1024]{1,0:T(8,128)(2,1)S(1)} %bitcast.19), channel_id=1, source_target_pairs={{252,254},{253,255},{254,252},{255,253}} | collective-permute-start | bytes 1572872 | tf_op jit(solution)/shard_map/ppermute | solution.py:131
  51.9 26.5 %collective-permute-start.22 = (bf16[256,1024]{1,0:T(8,128)(2,1)S(1)}, bf16[256,1024]{1,0:T(8,128)(2,1)S(1)}, u32[]{:S(2)}, u32[]{:S(2)}) collective-permute-start(bf16[256,1024]{1,0:T(8,128)(2,1)S(1)} %get-tuple-element.32.refs_1_), channel_id=1, source_target_pairs={{0,240},{1,241},{2,242},{3,243},{252,12},{253,13},{254,14},{255,15}} | collective-permute-start | bytes 1572872 | tf_op jit(solution)/shard_map/ppermute | solution.py:131
  61.5 17.7 %collective-permute-start.4 = (bf16[1024,256]{1,0:T(8,128)(2,1)S(1)}, bf16[1024,256]{1,0:T(8,128)(2,1)S(1)}, u32[]{:S(2)}, u32[]{:S(2)}) collective-permute-start(bf16[1024,256]{1,0:T(8,128)(2,1)S(1)} %get-tuple-element.24), channel_id=1, source_target_pairs={{0,4},{1,5},{2,6},{3,7},{4,8},{5,9},{6,10},{7,11},{8,12},{9,13},{1... | collective-permute-start | bytes 1572872 | tf_op jit(solution)/shard_map/ppermute | solution.py:131
  64.1 17.8 %collective-permute-start.28 = (bf16[1024,256]{1,0:T(8,128)(2,1)S(1)}, bf16[1024,256]{1,0:T(8,128)(2,1)S(1)}, u32[]{:S(2)}, u32[]{:S(2)}) collective-permute-start(bf16[1024,256]{1,0:T(8,128)(2,1)S(1)} %shard_map.106), channel_id=1, source_target_pairs={{12,8},{13,9},{14,10},{15,11},{16,12},{17,13},{18,14},{19,15},{20,... | collective-permute-start | bytes 1572872 | tf_op jit(solution)/shard_map/ppermute | solution.py:131
  66.0 18.4 %collective-permute-start.19 = (bf16[1024,256]{1,0:T(8,128)(2,1)S(1)}, bf16[1024,256]{1,0:T(8,128)(2,1)S(1)}, u32[]{:S(2)}, u32[]{:S(2)}) collective-permute-start(bf16[1024,256]{1,0:T(8,128)(2,1)S(1)} %shard_map.103), channel_id=1, source_target_pairs={{12,8},{13,9},{14,10},{15,11},{16,12},{17,13},{18,14},{19,15},{20,... | collective-permute-start | bytes 1572872 | tf_op jit(solution)/shard_map/ppermute | solution.py:131
  68.1 20.4 %collective-permute-start.25 = (bf16[256,1024]{1,0:T(8,128)(2,1)S(1)}, bf16[256,1024]{1,0:T(8,128)(2,1)S(1)}, u32[]{:S(2)}, u32[]{:S(2)}) collective-permute-start(bf16[256,1024]{1,0:T(8,128)(2,1)S(1)} %get-tuple-element.33.refs_5_), channel_id=1, source_target_pairs={{0,240},{1,241},{2,242},{3,243}} | collective-permute-start | bytes 1572872 | tf_op jit(solution)/shard_map/ppermute | solution.py:131
  78.5 11.3 %collective-permute-start.8 = (bf16[256,1024]{1,0:T(8,128)(2,1)S(1)}, bf16[256,1024]{1,0:T(8,128)(2,1)S(1)}, u32[]{:S(2)}, u32[]{:S(2)}) collective-permute-start(bf16[256,1024]{1,0:T(8,128)(2,1)S(1)} %collective-permute-done.7.rest_0_.refs_7_), channel_id=1, source_target_pairs={{252,253},{253,252},{254,255},{255,254}} | collective-permute-start | bytes 1572872 | tf_op jit(solution)/shard_map/ppermute | solution.py:131
  79.2 13.6 %collective-permute-start.10 = (bf16[1024,256]{1,0:T(8,128)(2,1)S(1)}, bf16[1024,256]{1,0:T(8,128)(2,1)S(1)}, u32[]{:S(2)}, u32[]{:S(2)}) collective-permute-start(bf16[1024,256]{1,0:T(8,128)(2,1)S(1)} %get-tuple-element.28), channel_id=1, source_target_pairs={{0,4},{1,5},{2,6},{3,7},{4,8},{5,9},{6,10},{7,11},{8,12},{9,13},{1... | collective-permute-start | bytes 1572872 | tf_op jit(solution)/shard_map/ppermute | solution.py:131
  81.8 19.9 %collective-permute-start.5 = (bf16[1024,256]{1,0:T(8,128)(2,1)S(1)}, bf16[1024,256]{1,0:T(8,128)(2,1)S(1)}, u32[]{:S(2)}, u32[]{:S(2)}) collective-permute-start(bf16[1024,256]{1,0:T(8,128)(2,1)S(1)} %get-tuple-element.25), channel_id=1, source_target_pairs={{0,4},{1,5},{2,6},{3,7},{4,8},{5,9},{6,10},{7,11},{8,12},{9,13},{1... | collective-permute-start | bytes 1572872 | tf_op jit(solution)/shard_map/ppermute | solution.py:131
  84.5 23.0 %collective-permute-start.29 = (bf16[1024,256]{1,0:T(8,128)(2,1)S(1)}, bf16[1024,256]{1,0:T(8,128)(2,1)S(1)}, u32[]{:S(2)}, u32[]{:S(2)}) collective-permute-start(bf16[1024,256]{1,0:T(8,128)(2,1)S(1)} %shard_map.107), channel_id=1, source_target_pairs={{8,4},{9,5},{10,6},{11,7},{12,8},{13,9},{14,10},{15,11},{16,12},{1... | collective-permute-start | bytes 1572872 | tf_op jit(solution)/shard_map/ppermute | solution.py:131
  88.5 25.1 %collective-permute-start.23 = (bf16[256,1024]{1,0:T(8,128)(2,1)S(1)}, bf16[256,1024]{1,0:T(8,128)(2,1)S(1)}, u32[]{:S(2)}, u32[]{:S(2)}) collective-permute-start(bf16[256,1024]{1,0:T(8,128)(2,1)S(1)} %collective-permute-done.22), channel_id=1, source_target_pairs={{240,2},{241,3},{242,0},{243,1},{12,254},{13,255},{14,252},{15,253}} | collective-permute-start | bytes 1572872 | tf_op jit(solution)/shard_map/ppermute | solution.py:131
  89.8 33.1 %collective-permute-start.26 = (bf16[256,1024]{1,0:T(8,128)(2,1)S(1)}, bf16[256,1024]{1,0:T(8,128)(2,1)S(1)}, u32[]{:S(2)}, u32[]{:S(2)}) collective-permute-start(bf16[256,1024]{1,0:T(8,128)(2,1)S(1)} %collective-permute-done.25), channel_id=1, source_target_pairs={{240,2},{241,3},{242,0},{243,1}} | collective-permute-start | bytes 1572872 | tf_op jit(solution)/shard_map/ppermute | solution.py:131
  92.8 32.0 %collective-permute-start.20 = (bf16[1024,256]{1,0:T(8,128)(2,1)S(1)}, bf16[1024,256]{1,0:T(8,128)(2,1)S(1)}, u32[]{:S(2)}, u32[]{:S(2)}) collective-permute-start(bf16[1024,256]{1,0:T(8,128)(2,1)S(1)} %shard_map.104), channel_id=1, source_target_pairs={{8,4},{9,5},{10,6},{11,7},{12,8},{13,9},{14,10},{15,11},{16,12},{1... | collective-permute-start | bytes 1572872 | tf_op jit(solution)/shard_map/ppermute | solution.py:131
  101.8 25.6 %collective-permute-start.11 = (bf16[1024,256]{1,0:T(8,128)(2,1)S(1)}, bf16[1024,256]{1,0:T(8,128)(2,1)S(1)}, u32[]{:S(2)}, u32[]{:S(2)}) collective-permute-start(bf16[1024,256]{1,0:T(8,128)(2,1)S(1)} %get-tuple-element.29), channel_id=1, source_target_pairs={{0,4},{1,5},{2,6},{3,7},{4,8},{5,9},{6,10},{7,11},{8,12},{9,13},{1... | collective-permute-start | bytes 1572872 | tf_op jit(solution)/shard_map/ppermute | solution.py:131
  107.5 23.3 %collective-permute-start.6 = (bf16[1024,256]{1,0:T(8,128)(2,1)S(1)}, bf16[1024,256]{1,0:T(8,128)(2,1)S(1)}, u32[]{:S(2)}, u32[]{:S(2)}) collective-permute-start(bf16[1024,256]{1,0:T(8,128)(2,1)S(1)} %get-tuple-element.26), channel_id=1, source_target_pairs={{0,4},{1,5},{2,6},{3,7},{4,8},{5,9},{6,10},{7,11},{8,12},{9,13},{1... | collective-permute-start | bytes 1572872 | tf_op jit(solution)/shard_map/ppermute | solution.py:131
  113.6 19.3 %collective-permute-start.24 = (bf16[256,1024]{1,0:T(8,128)(2,1)S(1)}, bf16[256,1024]{1,0:T(8,128)(2,1)S(1)}, u32[]{:S(2)}, u32[]{:S(2)}) collective-permute-start(bf16[256,1024]{1,0:T(8,128)(2,1)S(1)} %collective-permute-done.23.refs_12_), channel_id=1, source_target_pairs={{0,1},{1,0},{2,3},{3,2},{252,253},{253,252},{254,255},{255,254}} | collective-permute-start | bytes 1572872 | tf_op jit(solution)/shard_map/ppermute | solution.py:131
  122.9 10.0 %collective-permute-start.27 = (bf16[256,1024]{1,0:T(8,128)(2,1)S(1)}, bf16[256,1024]{1,0:T(8,128)(2,1)S(1)}, u32[]{:S(2)}, u32[]{:S(2)}) collective-permute-start(bf16[256,1024]{1,0:T(8,128)(2,1)S(1)} %collective-permute-done.26.refs_14_), channel_id=1, source_target_pairs={{0,1},{1,0},{2,3},{3,2}} | collective-permute-start | bytes 1572872 | tf_op jit(solution)/shard_map/ppermute | solution.py:131
  124.8 16.7 %collective-permute-start.30 = (bf16[1024,256]{1,0:T(8,128)(2,1)S(1)}, bf16[1024,256]{1,0:T(8,128)(2,1)S(1)}, u32[]{:S(2)}, u32[]{:S(2)}) collective-permute-start(bf16[1024,256]{1,0:T(8,128)(2,1)S(1)} %shard_map.108), channel_id=1, source_target_pairs={{4,0},{5,1},{6,2},{7,3},{8,4},{9,5},{10,6},{11,7},{12,8},{13,9},{1... | collective-permute-start | bytes 1572872 | tf_op jit(solution)/shard_map/ppermute | solution.py:131
  127.4 24.9 %collective-permute-start.21 = (bf16[1024,256]{1,0:T(8,128)(2,1)S(1)}, bf16[1024,256]{1,0:T(8,128)(2,1)S(1)}, u32[]{:S(2)}, u32[]{:S(2)}) collective-permute-start(bf16[1024,256]{1,0:T(8,128)(2,1)S(1)} %shard_map.105), channel_id=1, source_target_pairs={{4,0},{5,1},{6,2},{7,3},{8,4},{9,5},{10,6},{11,7},{12,8},{13,9},{1... | collective-permute-start | bytes 1572872 | tf_op jit(solution)/shard_map/ppermute | solution.py:131

commit v7 on v6

--- a/solution.py
+++ b/solution.py
@@ -54,8 +54,42 @@
     return slice(chunk * width, (chunk + 1) * width) if ref.shape[-1] > width else slice(None)
 
 
+class Result:
+    def __init__(self, new, space, done, chunk):
+        self.new, self.space, self.done, self.copies = new, space, done, []
+        self.columns = slice(chunk * space.shape[1], (chunk + 1) * space.shape[1])
+
+    def put(self, k, rows, value):
+        self.space[rows, :] = value
+        copy = pltpu.make_async_copy(
+            self.space.at[rows, :], self.new.at[rows, self.columns], self.done.at[k]
+        )
+        copy.start()
+        self.copies.append(copy)
+
+    def finish(self):
+        for copy in self.copies:
+            copy.wait()
+
+
+class Plain:
+    def __init__(self, new):
+        self.new = new
+
+    def put(self, k, rows, value):
+        self.new[rows, :] = value
+
+    def finish(self):
+        pass
+
+
 def down_kernel(moment, chunk, plan, b0, b1, b2, b3, received, sources, *rest):
-    others, (new, down_in) = rest[:-2], rest[-2:]
+    if moment == TICKS - 1:
+        others, (new, down_in, space, done) = rest[:-4], rest[-4:]
+        out = Result(new, space, done, chunk)
+    else:
+        others, (new, down_in) = rest[:-2], rest[-2:]
+        out = Plain(new)
     layer, count = lax.axis_index("layer"), lax.axis_size("layer")
     spot = lax.axis_index("shot")
     cols = columns(sources, chunk, down_in.shape[1])
@@ -66,17 +100,22 @@
         high, value = block.shape[0], block[...]
         if moment == TICKS - 1 and k >= 2:
             value = jnp.where(layer == count - 1, others[k - 2][...], value)
-        new[band(spot ^ k, high), :] = dot(value, down_in[...]).astype(BF16)
+        out.put(k, band(spot ^ k, high), dot(value, down_in[...]).astype(BF16))
+    out.finish()
 
 
 def up_kernel(chunk, last, *refs):
     pick, *blocks = refs[:9]
     received, down_in, sources = refs[9:12]
-    late, new = refs[12:-1], refs[-1]
+    if last:
+        late, (new, space, done) = refs[12:-3], refs[-3:]
+        out, width = Result(new, space, done, chunk), space.shape[1]
+    else:
+        late, new = (), refs[-1]
+        out, width = Plain(new), new.shape[1]
     top = lax.axis_index("layer") == 0
     end = lax.axis_index("layer") == lax.axis_size("layer") - 1
     spot = lax.axis_index("shot")
-    width = new.shape[1]
     gathered = received[:, columns(received, chunk, width)]
     injection = down_in[:, columns(down_in, chunk, width)]
     for k in range(4):
@@ -88,7 +127,8 @@
         rows = band(spot ^ k, high)
         total = dot(up, gathered) + dot(reflect, injection)
         total = total + sources[pick[0], rows, columns(sources, chunk, width)].astype(F32)
-        new[rows, :] = total.astype(BF16)
+        out.put(k, rows, total.astype(BF16))
+    out.finish()
 
 
 def call(kernel, scalars, arrays, out_shape, flops, full=None, into=None, more=()):
@@ -97,12 +137,13 @@
     args = [scalars, *arrays]
     in_specs += [WHOLE] * len(more)
     args += more
-    aliases = {}
+    aliases, scratch = {}, []
     if full is not None:
-        chunk, wide = full
+        _, wide = full
         height, width = out_shape[0]
         out_shape = [(height, wide), *out_shape[1:]]
-        out_specs[0] = pl.BlockSpec((height, width), lambda i: (0, chunk))
+        out_specs[0] = pl.BlockSpec(memory_space=pl.ANY)
+        scratch = [pltpu.VMEM((height, width), BF16), pltpu.SemaphoreType.DMA((4,))]
         if into is not None:
             in_specs.append(pl.BlockSpec(memory_space=pl.ANY))
             aliases = {len(args): 0}
@@ -114,6 +155,7 @@
         in_specs=in_specs,
         out_specs=out_specs,
         out_shape=[jax.ShapeDtypeStruct(s, BF16) for s in out_shape],
+        scratch_shapes=scratch,
         input_output_aliases=aliases,
         cost_estimate=pl.CostEstimate(flops=flops, transcendentals=0, bytes_accessed=2**20),
         compiler_params=pltpu.CompilerParams(vmem_limit_bytes=16 * 2**20),

time: 157 us -> 157 us (level)
  no operation moved by 1% of the time
where the time goes in v7:
time: 157 us; the launch traced here: 154 us
  waiting for transfers between devices  69.7 us (44%)
  starting transfers between devices  54.3 us (35%)
  Pallas kernels  23.7 us (15%)
  local copies, waits for them, and re-layouts  4.72 us (3%)
  between operations  1.97 us (1%)
    ppermute x31, waiting for transfers between devices, sent(): return lax.ppermute(value, ('layer', 'shot'), pairs)  69.7 us
    ppermute x31, starting transfers between devices, sent(): return lax.ppermute(value, ('layer', 'shot'), pairs)  54.3 us
    pallas_call x16, Pallas kernels, call(): pl.pallas_call(kernel, grid=(1,), in_specs=in_specs, out_specs=out_specs,...  23.4 us
    unnamed x12, local copies, waits for them, and re-layouts  4.72 us
  transfers between devices with their start and end apart: 31, of which 9 were waited for; matrix products, arithmetic and copies ran while one was open for 0% of the time, Pallas kernels for 14%

profile of v7, /device:TPU:8, one launch (start us, length us, event | category | flops | bytes accessed | tf_op | source)
XLA Modules:
  0.0 154.4 jit_solution(15022058608294019900)
XLA Ops:
  0.6 4.1 %collective-permute-start.1 = (bf16[256,1024]{1,0:T(8,128)(2,1)}, bf16[256,1024]{1,0:T(8,128)(2,1)S(1)}, u32[]{:S(2)}, u32[]{:S(2)}) collective-permute-start(bf16[256,1024]{1,0:T(8,128)(2,1)} %bitcast.16), channel_id=1, source_target_pairs={{0,2},{1,3},{2,0},{3,1},{4,6},{5,7},{6,4},{7,5},{8,10},{9,11},{10,... | collective-permute-start | bytes 1572872 | tf_op jit(solution)/shard_map/ppermute | solution.py:173
  4.7 1.8 %collective-permute-start.3 = (bf16[1024,512]{1,0:T(8,128)(2,1)}, bf16[1024,512]{1,0:T(8,128)(2,1)S(1)}, u32[]{:S(2)}, u32[]{:S(2)}) collective-permute-start(bf16[1024,512]{1,0:T(8,128)(2,1)} %bitcast.30), channel_id=1, source_target_pairs={{0,4},{1,5},{2,6},{3,7},{4,8},{5,9},{6,10},{7,11},{8,12},{9,13},{1... | collective-permute-start | bytes 3145736 | tf_op jit(solution)/shard_map/ppermute | solution.py:173
  8.0 30.9 %collective-permute-done.1.b2.refs_3_ = bf16[256,1024]{1,0:T(8,128)(2,1)S(1)} collective-permute-done((bf16[256,1024]{1,0:T(8,128)(2,1)}, bf16[256,1024]{1,0:T(8,128)(2,1)S(1)}, u32[]{:S(2)}, u32[]{:S(2)}) %collective-permute-start.1) | collective-permute-done | bytes 524320 | tf_op jit(solution)/shard_map/ppermute | solution.py:173
  38.9 0.7 collective-permute-start.18
  41.3 1.6 %copy-done = bf16[1,2,1024,512]{3,2,1,0:T(8,128)(2,1)S(1)} copy-done((bf16[1,2,1024,512]{3,2,1,0:T(8,128)(2,1)S(1)}, bf16[1,2,1024,512]{3,2,1,0:T(8,128)(2,1)}, u32[]{:S(2)}) %copy-start) | copy-done | bytes 2097176
  42.9 1.0 copy-done.1
  43.9 1.0 copy-done.2
  45.0 1.0 copy-done.3
  46.3 1.3 shard_map.98
  47.6 1.6 %collective-permute-start.9 = (bf16[1024,256]{1,0:T(8,128)(2,1)S(1)}, bf16[1024,256]{1,0:T(8,128)(2,1)S(1)}, u32[]{:S(2)}, u32[]{:S(2)}) collective-permute-start(bf16[1024,256]{1,0:T(8,128)(2,1)S(1)} %get-tuple-element.27), channel_id=1, source_target_pairs={{0,4},{1,5},{2,6},{3,7},{4,8},{5,9},{6,10},{7,11},{8,12},{9,13},{1... | collective-permute-start | bytes 1572872 | tf_op jit(solution)/shard_map/ppermute | solution.py:173
  49.9 1.3 shard_map.95
  51.2 0.7 collective-permute-start.7
  51.9 9.5 %collective-permute-start.22 = (bf16[256,1024]{1,0:T(8,128)(2,1)S(1)}, bf16[256,1024]{1,0:T(8,128)(2,1)S(1)}, u32[]{:S(2)}, u32[]{:S(2)}) collective-permute-start(bf16[256,1024]{1,0:T(8,128)(2,1)S(1)} %get-tuple-element.32.refs_1_), channel_id=1, source_target_pairs={{0,240},{1,241},{2,242},{3,243},{252,12},{253,13},{254,14},{255,15}} | collective-permute-start | bytes 1572872 | tf_op jit(solution)/shard_map/ppermute | solution.py:173
  61.5 1.3 collective-permute-start.4
  62.8 1.3 shard_map.106
  64.1 0.7 collective-permute-start.28
  64.8 1.3 shard_map.103
  66.7 1.3 shard_map.99
  68.1 10.4 %collective-permute-start.25 = (bf16[256,1024]{1,0:T(8,128)(2,1)S(1)}, bf16[256,1024]{1,0:T(8,128)(2,1)S(1)}, u32[]{:S(2)}, u32[]{:S(2)}) collective-permute-start(bf16[256,1024]{1,0:T(8,128)(2,1)S(1)} %get-tuple-element.33.refs_5_), channel_id=1, source_target_pairs={{0,240},{1,241},{2,242},{3,243}} | collective-permute-start | bytes 1572872 | tf_op jit(solution)/shard_map/ppermute | solution.py:173
  79.2 1.3 collective-permute-start.10
  80.5 1.3 shard_map.96
  81.8 1.3 collective-permute-start.5
  83.2 1.3 shard_map.107
  85.2 1.3 shard_map.104
  86.4 2.1 %collective-permute-done.25 = bf16[256,1024]{1,0:T(8,128)(2,1)S(1)} collective-permute-done((bf16[256,1024]{1,0:T(8,128)(2,1)S(1)}, bf16[256,1024]{1,0:T(8,128)(2,1)S(1)}, u32[]{:S(2)}, u32[]{:S(2)}) %collective-permute-start.25) | collective-permute-done | bytes 524320 | tf_op jit(solution)/shard_map/ppermute | solution.py:173
  88.5 1.3 collective-permute-start.23
  89.8 1.3 collective-permute-start.26
  91.1 1.7 %collective-permute-done.10.received = bf16[1024,256]{1,0:T(8,128)(2,1)S(1)} collective-permute-done((bf16[1024,256]{1,0:T(8,128)(2,1)S(1)}, bf16[1024,256]{1,0:T(8,128)(2,1)S(1)}, u32[]{:S(2)}, u32[]{:S(2)}) %collective-permute-start.10) | collective-permute-done | bytes 524320 | tf_op jit(solution)/shard_map/ppermute | solution.py:173
  92.8 0.9 collective-permute-start.20
  93.7 1.3 shard_map.100
  94.9 6.8 %collective-permute-done.5.received = bf16[1024,256]{1,0:T(8,128)(2,1)S(1)} collective-permute-done((bf16[1024,256]{1,0:T(8,128)(2,1)S(1)}, bf16[1024,256]{1,0:T(8,128)(2,1)S(1)}, u32[]{:S(2)}, u32[]{:S(2)}) %collective-permute-start.5) | collective-permute-done | bytes 524320 | tf_op jit(solution)/shard_map/ppermute | solution.py:173
  101.8 4.4 %collective-permute-start.11 = (bf16[1024,256]{1,0:T(8,128)(2,1)S(1)}, bf16[1024,256]{1,0:T(8,128)(2,1)S(1)}, u32[]{:S(2)}, u32[]{:S(2)}) collective-permute-start(bf16[1024,256]{1,0:T(8,128)(2,1)S(1)} %get-tuple-element.29), channel_id=1, source_target_pairs={{0,4},{1,5},{2,6},{3,7},{4,8},{5,9},{6,10},{7,11},{8,12},{9,13},{1... | collective-permute-start | bytes 1572872 | tf_op jit(solution)/shard_map/ppermute | solution.py:173
  106.2 1.3 shard_map.97
  107.5 1.9 %collective-permute-start.6 = (bf16[1024,256]{1,0:T(8,128)(2,1)S(1)}, bf16[1024,256]{1,0:T(8,128)(2,1)S(1)}, u32[]{:S(2)}, u32[]{:S(2)}) collective-permute-start(bf16[1024,256]{1,0:T(8,128)(2,1)S(1)} %get-tuple-element.26), channel_id=1, source_target_pairs={{0,4},{1,5},{2,6},{3,7},{4,8},{5,9},{6,10},{7,11},{8,12},{9,13},{1... | collective-permute-start | bytes 1572872 | tf_op jit(solution)/shard_map/ppermute | solution.py:173
  109.4 1.3 shard_map.108
  110.7 2.9 %collective-permute-done.23.refs_12_ = bf16[256,1024]{1,0:T(8,128)(2,1)S(1)} collective-permute-done((bf16[256,1024]{1,0:T(8,128)(2,1)S(1)}, bf16[256,1024]{1,0:T(8,128)(2,1)S(1)}, u32[]{:S(2)}, u32[]{:S(2)}) %collective-permute-start.23) | collective-permute-done | bytes 524320 | tf_op jit(solution)/shard_map/ppermute | solution.py:173
  113.6 1.9 %collective-permute-start.24 = (bf16[256,1024]{1,0:T(8,128)(2,1)S(1)}, bf16[256,1024]{1,0:T(8,128)(2,1)S(1)}, u32[]{:S(2)}, u32[]{:S(2)}) collective-permute-start(bf16[256,1024]{1,0:T(8,128)(2,1)S(1)} %collective-permute-done.23.refs_12_), channel_id=1, source_target_pairs={{0,1},{1,0},{2,3},{3,2},{252,253},{253,252},{254,255},{255,254}} | collective-permute-start | bytes 1572872 | tf_op jit(solution)/shard_map/ppermute | solution.py:173
  115.5 7.4 %collective-permute-done.26.refs_14_ = bf16[256,1024]{1,0:T(8,128)(2,1)S(1)} collective-permute-done((bf16[256,1024]{1,0:T(8,128)(2,1)S(1)}, bf16[256,1024]{1,0:T(8,128)(2,1)S(1)}, u32[]{:S(2)}, u32[]{:S(2)}) %collective-permute-start.26) | collective-permute-done | bytes 524320 | tf_op jit(solution)/shard_map/ppermute | solution.py:173
  122.9 1.9 %collective-permute-start.27 = (bf16[256,1024]{1,0:T(8,128)(2,1)S(1)}, bf16[256,1024]{1,0:T(8,128)(2,1)S(1)}, u32[]{:S(2)}, u32[]{:S(2)}) collective-permute-start(bf16[256,1024]{1,0:T(8,128)(2,1)S(1)} %collective-permute-done.26.refs_14_), channel_id=1, source_target_pairs={{0,1},{1,0},{2,3},{3,2}} | collective-permute-start | bytes 1572872 | tf_op jit(solution)/shard_map/ppermute | solution.py:173
  124.8 1.3 collective-permute-start.30
  126.1 1.3 shard_map.105
  127.4 1.3 collective-permute-start.21
  128.7 2.0 %shard_map.101 = (bf16[1024,512]{1,0:T(8,128)(2,1)}, bf16[1024,256]{1,0:T(8,128)(2,1)S(1)}) custom-call(s32[1,4]{1,0:T(1,128)S(1)} %bitcast.26, bf16[256,1024]{1,0:T(8,128)(2,1)S(1)} %get-tuple-element.22.b0.refs_1_, bf16[256,1024]{1,0:T(8,128)(2,1)S(1)} %collective-permute-done.b1.refs_2_, bf16[256,1024]{1,0:T(8,128)(2,1)S(1)} %collective-permute-done.1.b2.refs_3_, ...), custom_call_target="tpu_custom_call" | custom-call | flops 536870912 | bytes 1048576 | tf_op jit(solution)/shard_map/pallas_call | solution.py:152
  130.8 2.0 %shard_map.102 = (bf16[1024,512]{1,0:T(8,128)(2,1)}, bf16[1024,256]{1,0:T(8,128)(2,1)S(1)}) custom-call(s32[1,4]{1,0:T(1,128)S(1)} %bitcast.27, bf16[256,1024]{1,0:T(8,128)(2,1)S(1)} %get-tuple-element.22.b0.refs_1_, bf16[256,1024]{1,0:T(8,128)(2,1)S(1)} %collective-permute-done.b1.refs_2_, ...), custom_call_target="tpu_custom_call", output_to_operand_aliasing={{0}: (9, {})} | custom-call | flops 536870912 | bytes 1048576 | tf_op jit(solution)/shard_map/pallas_call | solution.py:152
  132.8 8.7 %collective-permute-done.30.refs_9_ = bf16[1024,256]{1,0:T(8,128)(2,1)S(1)} collective-permute-done((bf16[1024,256]{1,0:T(8,128)(2,1)S(1)}, bf16[1024,256]{1,0:T(8,128)(2,1)S(1)}, u32[]{:S(2)}, u32[]{:S(2)}) %collective-permute-start.30) | collective-permute-done | bytes 524320 | tf_op jit(solution)/shard_map/ppermute | solution.py:173
  141.5 2.0 %shard_map.109.refs_16_ = bf16[1024,512]{1,0:T(8,128)(2,1)} custom-call(s32[1]{0:T(128)S(6)} %copy.14.refs_0_, bf16[256,1024]{1,0:T(8,128)(2,1)S(1)} %get-tuple-element.32.refs_1_, bf16[256,1024]{1,0:T(8,128)(2,1)S(1)} %collective-permute-done.12.refs_2_, bf16[256,1024]{1,0:T(8,128)(2,1)S(1)} %collective-permute-done.13.refs_3_, ...), custom_call_target="tpu_custom_call" | custom-call | flops 1073741824 | bytes 1048576 | tf_op jit(solution)/shard_map/pallas_call | solution.py:152
  143.5 8.7 %collective-permute-done.21.refs_9_ = bf16[1024,256]{1,0:T(8,128)(2,1)S(1)} collective-permute-done((bf16[1024,256]{1,0:T(8,128)(2,1)S(1)}, bf16[1024,256]{1,0:T(8,128)(2,1)S(1)}, u32[]{:S(2)}, u32[]{:S(2)}) %collective-permute-start.21) | collective-permute-done | bytes 524320 | tf_op jit(solution)/shard_map/ppermute | solution.py:173
  152.3 2.0 %shard_map.110 = bf16[1024,512]{1,0:T(8,128)(2,1)} custom-call(s32[1]{0:T(128)S(6)} %copy.14.refs_0_, bf16[256,1024]{1,0:T(8,128)(2,1)S(1)} %get-tuple-element.32.refs_1_, bf16[256,1024]{1,0:T(8,128)(2,1)S(1)} %collective-permute-done.12.refs_2_, bf16[256,1024]{1,0:T(8,128)(2,1)S(1)} %collective-permute-done.13.refs_3_, ...), custom_call_target="tpu_custom_call", output_to_operand_aliasing={{}: (16, {})} | custom-call | flops 1073741824 | bytes 1048576 | tf_op jit(solution)/shard_map/pallas_call | solution.py:152
  (43 shorter events, 5.6 us)
Async XLA Ops:
  0.6 45.7 %copy-start.5 = (s32[4,1]{0,1:T(1,128)S(1)}, s32[4,1]{0,1:T(1,128)}, u32[]{:S(2)}) copy-start(s32[4,1]{0,1:T(1,128)} %param.14) | copy-start | bytes 52
  0.6 38.2 %collective-permute-start.1 = (bf16[256,1024]{1,0:T(8,128)(2,1)}, bf16[256,1024]{1,0:T(8,128)(2,1)S(1)}, u32[]{:S(2)}, u32[]{:S(2)}) collective-permute-start(bf16[256,1024]{1,0:T(8,128)(2,1)} %bitcast.16), channel_id=1, source_target_pairs={{0,2},{1,3},{2,0},{3,1},{4,6},{5,7},{6,4},{7,5},{8,10},{9,11},{10,... | collective-permute-start | bytes 1572872 | tf_op jit(solution)/shard_map/ppermute | solution.py:173
  4.7 36.2 %collective-permute-start.3 = (bf16[1024,512]{1,0:T(8,128)(2,1)}, bf16[1024,512]{1,0:T(8,128)(2,1)S(1)}, u32[]{:S(2)}, u32[]{:S(2)}) collective-permute-start(bf16[1024,512]{1,0:T(8,128)(2,1)} %bitcast.30), channel_id=1, source_target_pairs={{0,4},{1,5},{2,6},{3,7},{4,8},{5,9},{6,10},{7,11},{8,12},{9,13},{1... | collective-permute-start | bytes 3145736 | tf_op jit(solution)/shard_map/ppermute | solution.py:173
  6.5 32.4 %collective-permute-start = (bf16[256,1024]{1,0:T(8,128)(2,1)}, bf16[256,1024]{1,0:T(8,128)(2,1)S(1)}, u32[]{:S(2)}, u32[]{:S(2)}) collective-permute-start(bf16[256,1024]{1,0:T(8,128)(2,1)} %bitcast.17), channel_id=1, source_target_pairs={{0,1},{1,0},{2,3},{3,2},{4,5},{5,4},{6,7},{7,6},{8,9},{9,8},{10,11... | collective-permute-start | bytes 1572872 | tf_op jit(solution)/shard_map/ppermute | solution.py:173
  6.6 33.0 %collective-permute-start.13 = (bf16[256,1024]{1,0:T(8,128)(2,1)}, bf16[256,1024]{1,0:T(8,128)(2,1)S(1)}, u32[]{:S(2)}, u32[]{:S(2)}) collective-permute-start(bf16[256,1024]{1,0:T(8,128)(2,1)} %bitcast.10), channel_id=1, source_target_pairs={{4,6},{5,7},{6,4},{7,5},{8,10},{9,11},{10,8},{11,9},{12,14},{13,15... | collective-permute-start | bytes 1572872 | tf_op jit(solution)/shard_map/ppermute | solution.py:173
  7.3 32.9 %collective-permute-start.16 = (bf16[256,1024]{1,0:T(8,128)(2,1)}, bf16[256,1024]{1,0:T(8,128)(2,1)S(1)}, u32[]{:S(2)}, u32[]{:S(2)}) collective-permute-start(bf16[256,1024]{1,0:T(8,128)(2,1)} %bitcast.13), channel_id=1, source_target_pairs={{4,6},{5,7},{6,4},{7,5},{8,10},{9,11},{10,8},{11,9},{12,14},{13,15... | collective-permute-start | bytes 1572872 | tf_op jit(solution)/shard_map/ppermute | solution.py:173
  38.9 1.9 %collective-permute-start.2 = (bf16[256,1024]{1,0:T(8,128)(2,1)S(1)}, bf16[256,1024]{1,0:T(8,128)(2,1)S(1)}, u32[]{:S(2)}, u32[]{:S(2)}) collective-permute-start(bf16[256,1024]{1,0:T(8,128)(2,1)S(1)} %collective-permute-done.1.b2.refs_3_), channel_id=1, source_target_pairs={{0,1},{1,0},{2,3},{3,2},{4,5},{5,4},{6,7},{7,6},{8,9},{9,8},{10,11... | collective-permute-start | bytes 1572872 | tf_op jit(solution)/shard_map/ppermute | solution.py:173
  38.9 23.9 %collective-permute-start.18 = (bf16[1024,512]{1,0:T(8,128)(2,1)}, bf16[1024,512]{1,0:T(8,128)(2,1)S(1)}, u32[]{:S(2)}, u32[]{:S(2)}) collective-permute-start(bf16[1024,512]{1,0:T(8,128)(2,1)} %bitcast.31), channel_id=1, source_target_pairs={{16,12},{17,13},{18,14},{19,15},{20,16},{21,17},{22,18},{23,19},{2... | collective-permute-start | bytes 3145736 | tf_op jit(solution)/shard_map/ppermute | solution.py:173
  39.6 8.0 %collective-permute-start.12 = (bf16[256,1024]{1,0:T(8,128)(2,1)}, bf16[256,1024]{1,0:T(8,128)(2,1)S(1)}, u32[]{:S(2)}, u32[]{:S(2)}) collective-permute-start(bf16[256,1024]{1,0:T(8,128)(2,1)} %bitcast.11), channel_id=1, source_target_pairs={{0,1},{1,0},{2,3},{3,2},{4,5},{5,4},{6,7},{7,6},{8,9},{9,8},{10,11... | collective-permute-start | bytes 1572872 | tf_op jit(solution)/shard_map/ppermute | solution.py:173
  40.2 11.0 %collective-permute-start.15 = (bf16[256,1024]{1,0:T(8,128)(2,1)}, bf16[256,1024]{1,0:T(8,128)(2,1)S(1)}, u32[]{:S(2)}, u32[]{:S(2)}) collective-permute-start(bf16[256,1024]{1,0:T(8,128)(2,1)} %bitcast.14), channel_id=1, source_target_pairs={{0,1},{1,0},{2,3},{3,2},{4,5},{5,4},{6,7},{7,6},{8,9},{9,8},{10,11... | collective-permute-start | bytes 1572872 | tf_op jit(solution)/shard_map/ppermute | solution.py:173
  40.8 11.1 %collective-permute-start.14 = (bf16[256,1024]{1,0:T(8,128)(2,1)S(1)}, bf16[256,1024]{1,0:T(8,128)(2,1)S(1)}, u32[]{:S(2)}, u32[]{:S(2)}) collective-permute-start(bf16[256,1024]{1,0:T(8,128)(2,1)S(1)} %collective-permute-done.13.refs_3_), channel_id=1, source_target_pairs={{0,1},{1,0},{2,3},{3,2},{4,5},{5,4},{6,7},{7,6},{8,9},{9,8},{10,11... | collective-permute-start | bytes 1572872 | tf_op jit(solution)/shard_map/ppermute | solution.py:173
  40.9 20.5 %collective-permute-start.17 = (bf16[256,1024]{1,0:T(8,128)(2,1)S(1)}, bf16[256,1024]{1,0:T(8,128)(2,1)S(1)}, u32[]{:S(2)}, u32[]{:S(2)}) collective-permute-start(bf16[256,1024]{1,0:T(8,128)(2,1)S(1)} %collective-permute-done.16.refs_7_), channel_id=1, source_target_pairs={{0,1},{1,0},{2,3},{3,2},{4,5},{5,4},{6,7},{7,6},{8,9},{9,8},{10,11... | collective-permute-start | bytes 1572872 | tf_op jit(solution)/shard_map/ppermute | solution.py:173
  41.3 1.6 %copy-start = (bf16[1,2,1024,512]{3,2,1,0:T(8,128)(2,1)S(1)}, bf16[1,2,1024,512]{3,2,1,0:T(8,128)(2,1)}, u32[]{:S(2)}) copy-start(bf16[1,2,1024,512]{3,2,1,0:T(8,128)(2,1)} %param.13) | copy-start | bytes 6291460
  42.9 1.0 copy-start.1
  43.9 1.0 copy-start.2
  45.0 1.0 copy-start.3
  47.6 18.4 %collective-permute-start.9 = (bf16[1024,256]{1,0:T(8,128)(2,1)S(1)}, bf16[1024,256]{1,0:T(8,128)(2,1)S(1)}, u32[]{:S(2)}, u32[]{:S(2)}) collective-permute-start(bf16[1024,256]{1,0:T(8,128)(2,1)S(1)} %get-tuple-element.27), channel_id=1, source_target_pairs={{0,4},{1,5},{2,6},{3,7},{4,8},{5,9},{6,10},{7,11},{8,12},{9,13},{1... | collective-permute-start | bytes 1572872 | tf_op jit(solution)/shard_map/ppermute | solution.py:173
  49.9 1.3 copy-start.4
  51.2 16.8 %collective-permute-start.7 = (bf16[256,1024]{1,0:T(8,128)(2,1)S(1)}, bf16[256,1024]{1,0:T(8,128)(2,1)S(1)}, u32[]{:S(2)}, u32[]{:S(2)}) collective-permute-start(bf16[256,1024]{1,0:T(8,128)(2,1)S(1)} %bitcast.19), channel_id=1, source_target_pairs={{252,254},{253,255},{254,252},{255,253}} | collective-permute-start | bytes 1572872 | tf_op jit(solution)/shard_map/ppermute | solution.py:173
  51.9 26.5 %collective-permute-start.22 = (bf16[256,1024]{1,0:T(8,128)(2,1)S(1)}, bf16[256,1024]{1,0:T(8,128)(2,1)S(1)}, u32[]{:S(2)}, u32[]{:S(2)}) collective-permute-start(bf16[256,1024]{1,0:T(8,128)(2,1)S(1)} %get-tuple-element.32.refs_1_), channel_id=1, source_target_pairs={{0,240},{1,241},{2,242},{3,243},{252,12},{253,13},{254,14},{255,15}} | collective-permute-start | bytes 1572872 | tf_op jit(solution)/shard_map/ppermute | solution.py:173
  61.5 17.7 %collective-permute-start.4 = (bf16[1024,256]{1,0:T(8,128)(2,1)S(1)}, bf16[1024,256]{1,0:T(8,128)(2,1)S(1)}, u32[]{:S(2)}, u32[]{:S(2)}) collective-permute-start(bf16[1024,256]{1,0:T(8,128)(2,1)S(1)} %get-tuple-element.24), channel_id=1, source_target_pairs={{0,4},{1,5},{2,6},{3,7},{4,8},{5,9},{6,10},{7,11},{8,12},{9,13},{1... | collective-permute-start | bytes 1572872 | tf_op jit(solution)/shard_map/ppermute | solution.py:173
  64.1 17.8 %collective-permute-start.28 = (bf16[1024,256]{1,0:T(8,128)(2,1)S(1)}, bf16[1024,256]{1,0:T(8,128)(2,1)S(1)}, u32[]{:S(2)}, u32[]{:S(2)}) collective-permute-start(bf16[1024,256]{1,0:T(8,128)(2,1)S(1)} %shard_map.106), channel_id=1, source_target_pairs={{12,8},{13,9},{14,10},{15,11},{16,12},{17,13},{18,14},{19,15},{20,... | collective-permute-start | bytes 1572872 | tf_op jit(solution)/shard_map/ppermute | solution.py:173
  66.0 18.4 %collective-permute-start.19 = (bf16[1024,256]{1,0:T(8,128)(2,1)S(1)}, bf16[1024,256]{1,0:T(8,128)(2,1)S(1)}, u32[]{:S(2)}, u32[]{:S(2)}) collective-permute-start(bf16[1024,256]{1,0:T(8,128)(2,1)S(1)} %shard_map.103), channel_id=1, source_target_pairs={{12,8},{13,9},{14,10},{15,11},{16,12},{17,13},{18,14},{19,15},{20,... | collective-permute-start | bytes 1572872 | tf_op jit(solution)/shard_map/ppermute | solution.py:173
  68.1 20.4 %collective-permute-start.25 = (bf16[256,1024]{1,0:T(8,128)(2,1)S(1)}, bf16[256,1024]{1,0:T(8,128)(2,1)S(1)}, u32[]{:S(2)}, u32[]{:S(2)}) collective-permute-start(bf16[256,1024]{1,0:T(8,128)(2,1)S(1)} %get-tuple-element.33.refs_5_), channel_id=1, source_target_pairs={{0,240},{1,241},{2,242},{3,243}} | collective-permute-start | bytes 1572872 | tf_op jit(solution)/shard_map/ppermute | solution.py:173
  78.5 11.3 %collective-permute-start.8 = (bf16[256,1024]{1,0:T(8,128)(2,1)S(1)}, bf16[256,1024]{1,0:T(8,128)(2,1)S(1)}, u32[]{:S(2)}, u32[]{:S(2)}) collective-permute-start(bf16[256,1024]{1,0:T(8,128)(2,1)S(1)} %collective-permute-done.7.rest_0_.refs_7_), channel_id=1, source_target_pairs={{252,253},{253,252},{254,255},{255,254}} | collective-permute-start | bytes 1572872 | tf_op jit(solution)/shard_map/ppermute | solution.py:173
  79.2 13.6 %collective-permute-start.10 = (bf16[1024,256]{1,0:T(8,128)(2,1)S(1)}, bf16[1024,256]{1,0:T(8,128)(2,1)S(1)}, u32[]{:S(2)}, u32[]{:S(2)}) collective-permute-start(bf16[1024,256]{1,0:T(8,128)(2,1)S(1)} %get-tuple-element.28), channel_id=1, source_target_pairs={{0,4},{1,5},{2,6},{3,7},{4,8},{5,9},{6,10},{7,11},{8,12},{9,13},{1... | collective-permute-start | bytes 1572872 | tf_op jit(solution)/shard_map/ppermute | solution.py:173
  81.8 19.9 %collective-permute-start.5 = (bf16[1024,256]{1,0:T(8,128)(2,1)S(1)}, bf16[1024,256]{1,0:T(8,128)(2,1)S(1)}, u32[]{:S(2)}, u32[]{:S(2)}) collective-permute-start(bf16[1024,256]{1,0:T(8,128)(2,1)S(1)} %get-tuple-element.25), channel_id=1, source_target_pairs={{0,4},{1,5},{2,6},{3,7},{4,8},{5,9},{6,10},{7,11},{8,12},{9,13},{1... | collective-permute-start | bytes 1572872 | tf_op jit(solution)/shard_map/ppermute | solution.py:173
  84.5 23.0 %collective-permute-start.29 = (bf16[1024,256]{1,0:T(8,128)(2,1)S(1)}, bf16[1024,256]{1,0:T(8,128)(2,1)S(1)}, u32[]{:S(2)}, u32[]{:S(2)}) collective-permute-start(bf16[1024,256]{1,0:T(8,128)(2,1)S(1)} %shard_map.107), channel_id=1, source_target_pairs={{8,4},{9,5},{10,6},{11,7},{12,8},{13,9},{14,10},{15,11},{16,12},{1... | collective-permute-start | bytes 1572872 | tf_op jit(solution)/shard_map/ppermute | solution.py:173
  88.5 25.1 %collective-permute-start.23 = (bf16[256,1024]{1,0:T(8,128)(2,1)S(1)}, bf16[256,1024]{1,0:T(8,128)(2,1)S(1)}, u32[]{:S(2)}, u32[]{:S(2)}) collective-permute-start(bf16[256,1024]{1,0:T(8,128)(2,1)S(1)} %collective-permute-done.22), channel_id=1, source_target_pairs={{240,2},{241,3},{242,0},{243,1},{12,254},{13,255},{14,252},{15,253}} | collective-permute-start | bytes 1572872 | tf_op jit(solution)/shard_map/ppermute | solution.py:173
  89.8 33.1 %collective-permute-start.26 = (bf16[256,1024]{1,0:T(8,128)(2,1)S(1)}, bf16[256,1024]{1,0:T(8,128)(2,1)S(1)}, u32[]{:S(2)}, u32[]{:S(2)}) collective-permute-start(bf16[256,1024]{1,0:T(8,128)(2,1)S(1)} %collective-permute-done.25), channel_id=1, source_target_pairs={{240,2},{241,3},{242,0},{243,1}} | collective-permute-start | bytes 1572872 | tf_op jit(solution)/shard_map/ppermute | solution.py:173
  92.8 32.0 %collective-permute-start.20 = (bf16[1024,256]{1,0:T(8,128)(2,1)S(1)}, bf16[1024,256]{1,0:T(8,128)(2,1)S(1)}, u32[]{:S(2)}, u32[]{:S(2)}) collective-permute-start(bf16[1024,256]{1,0:T(8,128)(2,1)S(1)} %shard_map.104), channel_id=1, source_target_pairs={{8,4},{9,5},{10,6},{11,7},{12,8},{13,9},{14,10},{15,11},{16,12},{1... | collective-permute-start | bytes 1572872 | tf_op jit(solution)/shard_map/ppermute | solution.py:173
  101.8 25.6 %collective-permute-start.11 = (bf16[1024,256]{1,0:T(8,128)(2,1)S(1)}, bf16[1024,256]{1,0:T(8,128)(2,1)S(1)}, u32[]{:S(2)}, u32[]{:S(2)}) collective-permute-start(bf16[1024,256]{1,0:T(8,128)(2,1)S(1)} %get-tuple-element.29), channel_id=1, source_target_pairs={{0,4},{1,5},{2,6},{3,7},{4,8},{5,9},{6,10},{7,11},{8,12},{9,13},{1... | collective-permute-start | bytes 1572872 | tf_op jit(solution)/shard_map/ppermute | solution.py:173
  107.5 23.2 %collective-permute-start.6 = (bf16[1024,256]{1,0:T(8,128)(2,1)S(1)}, bf16[1024,256]{1,0:T(8,128)(2,1)S(1)}, u32[]{:S(2)}, u32[]{:S(2)}) collective-permute-start(bf16[1024,256]{1,0:T(8,128)(2,1)S(1)} %get-tuple-element.26), channel_id=1, source_target_pairs={{0,4},{1,5},{2,6},{3,7},{4,8},{5,9},{6,10},{7,11},{8,12},{9,13},{1... | collective-permute-start | bytes 1572872 | tf_op jit(solution)/shard_map/ppermute | solution.py:173
  113.6 19.2 %collective-permute-start.24 = (bf16[256,1024]{1,0:T(8,128)(2,1)S(1)}, bf16[256,1024]{1,0:T(8,128)(2,1)S(1)}, u32[]{:S(2)}, u32[]{:S(2)}) collective-permute-start(bf16[256,1024]{1,0:T(8,128)(2,1)S(1)} %collective-permute-done.23.refs_12_), channel_id=1, source_target_pairs={{0,1},{1,0},{2,3},{3,2},{252,253},{253,252},{254,255},{255,254}} | collective-permute-start | bytes 1572872 | tf_op jit(solution)/shard_map/ppermute | solution.py:173
  122.9 9.9 %collective-permute-start.27 = (bf16[256,1024]{1,0:T(8,128)(2,1)S(1)}, bf16[256,1024]{1,0:T(8,128)(2,1)S(1)}, u32[]{:S(2)}, u32[]{:S(2)}) collective-permute-start(bf16[256,1024]{1,0:T(8,128)(2,1)S(1)} %collective-permute-done.26.refs_14_), channel_id=1, source_target_pairs={{0,1},{1,0},{2,3},{3,2}} | collective-permute-start | bytes 1572872 | tf_op jit(solution)/shard_map/ppermute | solution.py:173
  124.8 16.7 %collective-permute-start.30 = (bf16[1024,256]{1,0:T(8,128)(2,1)S(1)}, bf16[1024,256]{1,0:T(8,128)(2,1)S(1)}, u32[]{:S(2)}, u32[]{:S(2)}) collective-permute-start(bf16[1024,256]{1,0:T(8,128)(2,1)S(1)} %shard_map.108), channel_id=1, source_target_pairs={{4,0},{5,1},{6,2},{7,3},{8,4},{9,5},{10,6},{11,7},{12,8},{13,9},{1... | collective-permute-start | bytes 1572872 | tf_op jit(solution)/shard_map/ppermute | solution.py:173
  127.4 24.9 %collective-permute-start.21 = (bf16[1024,256]{1,0:T(8,128)(2,1)S(1)}, bf16[1024,256]{1,0:T(8,128)(2,1)S(1)}, u32[]{:S(2)}, u32[]{:S(2)}) collective-permute-start(bf16[1024,256]{1,0:T(8,128)(2,1)S(1)} %shard_map.105), channel_id=1, source_target_pairs={{4,0},{5,1},{6,2},{7,3},{8,4},{9,5},{10,6},{11,7},{12,8},{13,9},{1... | collective-permute-start | bytes 1572872 | tf_op jit(solution)/shard_map/ppermute | solution.py:173

commit v8 on v7

--- a/solution.py
+++ b/solution.py
@@ -61,6 +61,9 @@
 
     def put(self, k, rows, value):
         self.space[rows, :] = value
+        self.send(k, rows)
+
+    def send(self, k, rows):
         copy = pltpu.make_async_copy(
             self.space.at[rows, :], self.new.at[rows, self.columns], self.done.at[k]
         )
@@ -119,15 +122,28 @@
     gathered = received[:, columns(received, chunk, width)]
     injection = down_in[:, columns(down_in, chunk, width)]
     for k in range(4):
-        up, reflect = blocks[k][...], blocks[4 + k][...]
-        high = up.shape[0]
+        rows = band(spot ^ k, blocks[k].shape[0])
+
+        def result(up, reflect, rows=rows):
+            total = dot(up, gathered) + dot(reflect, injection)
+            total = total + sources[pick[0], rows, columns(sources, chunk, width)].astype(F32)
+            return total.astype(BF16)
+
         if last and k >= 2:
-            up = jnp.where(jnp.logical_or(top, end), late[k - 2][...], up)
-            reflect = jnp.where(top, late[k][...], reflect)
-        rows = band(spot ^ k, high)
-        total = dot(up, gathered) + dot(reflect, injection)
-        total = total + sources[pick[0], rows, columns(sources, chunk, width)].astype(F32)
-        out.put(k, rows, total.astype(BF16))
+            outer = jnp.logical_or(top, end)
+
+            @pl.when(outer)
+            def _(k=k, rows=rows, result=result):
+                reflect = jnp.where(top, late[k][...], blocks[4 + k][...])
+                space[rows, :] = result(late[k - 2][...], reflect)
+
+            @pl.when(jnp.logical_not(outer))
+            def _(k=k, rows=rows, result=result):
+                space[rows, :] = result(blocks[k][...], blocks[4 + k][...])
+
+            out.send(k, rows)
+        else:
+            out.put(k, rows, result(blocks[k][...], blocks[4 + k][...]))
     out.finish()
 
 

time: 157 us -> 158 us (level)
  no operation moved by 1% of the time
where the time goes in v8:
time: 158 us; the launch traced here: 155 us
  waiting for transfers between devices  69.4 us (44%)
  starting transfers between devices  54.3 us (34%)
  Pallas kernels  24.3 us (15%)
  local copies, waits for them, and re-layouts  4.72 us (3%)
  between operations  1.97 us (1%)
    ppermute x31, waiting for transfers between devices, sent(): return lax.ppermute(value, ('layer', 'shot'), pairs)  69.4 us
    ppermute x31, starting transfers between devices, sent(): return lax.ppermute(value, ('layer', 'shot'), pairs)  54.3 us
    pallas_call x16, Pallas kernels, call(): pl.pallas_call(kernel, grid=(1,), in_specs=in_specs, out_specs=out_specs,...  24 us
    unnamed x12, local copies, waits for them, and re-layouts  4.72 us
  transfers between devices with their start and end apart: 31, of which 9 were waited for; matrix products, arithmetic and copies ran while one was open for 0% of the time, Pallas kernels for 14%

profile of v8, /device:TPU:8, one launch (start us, length us, event | category | flops | bytes accessed | tf_op | source)
XLA Modules:
  0.0 154.7 jit_solution(926680382904581866)
XLA Ops:
  0.6 4.1 %collective-permute-start.1 = (bf16[256,1024]{1,0:T(8,128)(2,1)}, bf16[256,1024]{1,0:T(8,128)(2,1)S(1)}, u32[]{:S(2)}, u32[]{:S(2)}) collective-permute-start(bf16[256,1024]{1,0:T(8,128)(2,1)} %bitcast.16), channel_id=1, source_target_pairs={{0,2},{1,3},{2,0},{3,1},{4,6},{5,7},{6,4},{7,5},{8,10},{9,11},{10,... | collective-permute-start | bytes 1572872 | tf_op jit(solution)/shard_map/ppermute | solution.py:189
  4.7 1.8 %collective-permute-start.3 = (bf16[1024,512]{1,0:T(8,128)(2,1)}, bf16[1024,512]{1,0:T(8,128)(2,1)S(1)}, u32[]{:S(2)}, u32[]{:S(2)}) collective-permute-start(bf16[1024,512]{1,0:T(8,128)(2,1)} %bitcast.30), channel_id=1, source_target_pairs={{0,4},{1,5},{2,6},{3,7},{4,8},{5,9},{6,10},{7,11},{8,12},{9,13},{1... | collective-permute-start | bytes 3145736 | tf_op jit(solution)/shard_map/ppermute | solution.py:189
  8.0 30.9 %collective-permute-done.1.b2.refs_3_ = bf16[256,1024]{1,0:T(8,128)(2,1)S(1)} collective-permute-done((bf16[256,1024]{1,0:T(8,128)(2,1)}, bf16[256,1024]{1,0:T(8,128)(2,1)S(1)}, u32[]{:S(2)}, u32[]{:S(2)}) %collective-permute-start.1) | collective-permute-done | bytes 524320 | tf_op jit(solution)/shard_map/ppermute | solution.py:189
  38.9 0.7 collective-permute-start.18
  41.3 1.6 %copy-done = bf16[1,2,1024,512]{3,2,1,0:T(8,128)(2,1)S(1)} copy-done((bf16[1,2,1024,512]{3,2,1,0:T(8,128)(2,1)S(1)}, bf16[1,2,1024,512]{3,2,1,0:T(8,128)(2,1)}, u32[]{:S(2)}) %copy-start) | copy-done | bytes 2097176
  42.9 1.0 copy-done.1
  43.9 1.0 copy-done.2
  45.0 1.0 copy-done.3
  46.3 1.3 shard_map.98
  47.6 1.6 %collective-permute-start.9 = (bf16[1024,256]{1,0:T(8,128)(2,1)S(1)}, bf16[1024,256]{1,0:T(8,128)(2,1)S(1)}, u32[]{:S(2)}, u32[]{:S(2)}) collective-permute-start(bf16[1024,256]{1,0:T(8,128)(2,1)S(1)} %get-tuple-element.27), channel_id=1, source_target_pairs={{0,4},{1,5},{2,6},{3,7},{4,8},{5,9},{6,10},{7,11},{8,12},{9,13},{1... | collective-permute-start | bytes 1572872 | tf_op jit(solution)/shard_map/ppermute | solution.py:189
  49.9 1.3 shard_map.95
  51.2 0.7 collective-permute-start.7
  51.9 9.5 %collective-permute-start.22 = (bf16[256,1024]{1,0:T(8,128)(2,1)S(1)}, bf16[256,1024]{1,0:T(8,128)(2,1)S(1)}, u32[]{:S(2)}, u32[]{:S(2)}) collective-permute-start(bf16[256,1024]{1,0:T(8,128)(2,1)S(1)} %get-tuple-element.32.refs_1_), channel_id=1, source_target_pairs={{0,240},{1,241},{2,242},{3,243},{252,12},{253,13},{254,14},{255,15}} | collective-permute-start | bytes 1572872 | tf_op jit(solution)/shard_map/ppermute | solution.py:189
  61.5 1.3 collective-permute-start.4
  62.8 1.3 shard_map.106
  64.1 0.7 collective-permute-start.28
  64.8 1.3 shard_map.103
  66.7 1.3 shard_map.99
  68.1 10.4 %collective-permute-start.25 = (bf16[256,1024]{1,0:T(8,128)(2,1)S(1)}, bf16[256,1024]{1,0:T(8,128)(2,1)S(1)}, u32[]{:S(2)}, u32[]{:S(2)}) collective-permute-start(bf16[256,1024]{1,0:T(8,128)(2,1)S(1)} %get-tuple-element.33.refs_5_), channel_id=1, source_target_pairs={{0,240},{1,241},{2,242},{3,243}} | collective-permute-start | bytes 1572872 | tf_op jit(solution)/shard_map/ppermute | solution.py:189
  79.2 1.3 collective-permute-start.10
  80.5 1.3 shard_map.96
  81.8 1.3 collective-permute-start.5
  83.2 1.3 shard_map.107
  85.2 1.3 shard_map.104
  86.4 2.1 %collective-permute-done.25 = bf16[256,1024]{1,0:T(8,128)(2,1)S(1)} collective-permute-done((bf16[256,1024]{1,0:T(8,128)(2,1)S(1)}, bf16[256,1024]{1,0:T(8,128)(2,1)S(1)}, u32[]{:S(2)}, u32[]{:S(2)}) %collective-permute-start.25) | collective-permute-done | bytes 524320 | tf_op jit(solution)/shard_map/ppermute | solution.py:189
  88.5 1.3 collective-permute-start.23
  89.8 1.3 collective-permute-start.26
  91.1 1.7 %collective-permute-done.10.received = bf16[1024,256]{1,0:T(8,128)(2,1)S(1)} collective-permute-done((bf16[1024,256]{1,0:T(8,128)(2,1)S(1)}, bf16[1024,256]{1,0:T(8,128)(2,1)S(1)}, u32[]{:S(2)}, u32[]{:S(2)}) %collective-permute-start.10) | collective-permute-done | bytes 524320 | tf_op jit(solution)/shard_map/ppermute | solution.py:189
  92.8 0.9 collective-permute-start.20
  93.7 1.3 shard_map.100
  94.9 6.8 %collective-permute-done.5.received = bf16[1024,256]{1,0:T(8,128)(2,1)S(1)} collective-permute-done((bf16[1024,256]{1,0:T(8,128)(2,1)S(1)}, bf16[1024,256]{1,0:T(8,128)(2,1)S(1)}, u32[]{:S(2)}, u32[]{:S(2)}) %collective-permute-start.5) | collective-permute-done | bytes 524320 | tf_op jit(solution)/shard_map/ppermute | solution.py:189
  101.8 4.4 %collective-permute-start.11 = (bf16[1024,256]{1,0:T(8,128)(2,1)S(1)}, bf16[1024,256]{1,0:T(8,128)(2,1)S(1)}, u32[]{:S(2)}, u32[]{:S(2)}) collective-permute-start(bf16[1024,256]{1,0:T(8,128)(2,1)S(1)} %get-tuple-element.29), channel_id=1, source_target_pairs={{0,4},{1,5},{2,6},{3,7},{4,8},{5,9},{6,10},{7,11},{8,12},{9,13},{1... | collective-permute-start | bytes 1572872 | tf_op jit(solution)/shard_map/ppermute | solution.py:189
  106.2 1.3 shard_map.97
  107.5 1.9 %collective-permute-start.6 = (bf16[1024,256]{1,0:T(8,128)(2,1)S(1)}, bf16[1024,256]{1,0:T(8,128)(2,1)S(1)}, u32[]{:S(2)}, u32[]{:S(2)}) collective-permute-start(bf16[1024,256]{1,0:T(8,128)(2,1)S(1)} %get-tuple-element.26), channel_id=1, source_target_pairs={{0,4},{1,5},{2,6},{3,7},{4,8},{5,9},{6,10},{7,11},{8,12},{9,13},{1... | collective-permute-start | bytes 1572872 | tf_op jit(solution)/shard_map/ppermute | solution.py:189
  109.4 1.3 shard_map.108
  110.7 2.9 %collective-permute-done.23.refs_12_ = bf16[256,1024]{1,0:T(8,128)(2,1)S(1)} collective-permute-done((bf16[256,1024]{1,0:T(8,128)(2,1)S(1)}, bf16[256,1024]{1,0:T(8,128)(2,1)S(1)}, u32[]{:S(2)}, u32[]{:S(2)}) %collective-permute-start.23) | collective-permute-done | bytes 524320 | tf_op jit(solution)/shard_map/ppermute | solution.py:189
  113.6 1.9 %collective-permute-start.24 = (bf16[256,1024]{1,0:T(8,128)(2,1)S(1)}, bf16[256,1024]{1,0:T(8,128)(2,1)S(1)}, u32[]{:S(2)}, u32[]{:S(2)}) collective-permute-start(bf16[256,1024]{1,0:T(8,128)(2,1)S(1)} %collective-permute-done.23.refs_12_), channel_id=1, source_target_pairs={{0,1},{1,0},{2,3},{3,2},{252,253},{253,252},{254,255},{255,254}} | collective-permute-start | bytes 1572872 | tf_op jit(solution)/shard_map/ppermute | solution.py:189
  115.5 7.4 %collective-permute-done.26.refs_14_ = bf16[256,1024]{1,0:T(8,128)(2,1)S(1)} collective-permute-done((bf16[256,1024]{1,0:T(8,128)(2,1)S(1)}, bf16[256,1024]{1,0:T(8,128)(2,1)S(1)}, u32[]{:S(2)}, u32[]{:S(2)}) %collective-permute-start.26) | collective-permute-done | bytes 524320 | tf_op jit(solution)/shard_map/ppermute | solution.py:189
  122.9 1.9 %collective-permute-start.27 = (bf16[256,1024]{1,0:T(8,128)(2,1)S(1)}, bf16[256,1024]{1,0:T(8,128)(2,1)S(1)}, u32[]{:S(2)}, u32[]{:S(2)}) collective-permute-start(bf16[256,1024]{1,0:T(8,128)(2,1)S(1)} %collective-permute-done.26.refs_14_), channel_id=1, source_target_pairs={{0,1},{1,0},{2,3},{3,2}} | collective-permute-start | bytes 1572872 | tf_op jit(solution)/shard_map/ppermute | solution.py:189
  124.8 1.3 collective-permute-start.30
  126.1 1.3 shard_map.105
  127.4 1.3 collective-permute-start.21
  128.7 2.0 %shard_map.101 = (bf16[1024,512]{1,0:T(8,128)(2,1)}, bf16[1024,256]{1,0:T(8,128)(2,1)S(1)}) custom-call(s32[1,4]{1,0:T(1,128)S(1)} %bitcast.26, bf16[256,1024]{1,0:T(8,128)(2,1)S(1)} %get-tuple-element.22.b0.refs_1_, bf16[256,1024]{1,0:T(8,128)(2,1)S(1)} %collective-permute-done.b1.refs_2_, bf16[256,1024]{1,0:T(8,128)(2,1)S(1)} %collective-permute-done.1.b2.refs_3_, ...), custom_call_target="tpu_custom_call" | custom-call | flops 536870912 | bytes 1048576 | tf_op jit(solution)/shard_map/pallas_call | solution.py:168
  130.8 2.0 %shard_map.102 = (bf16[1024,512]{1,0:T(8,128)(2,1)}, bf16[1024,256]{1,0:T(8,128)(2,1)S(1)}) custom-call(s32[1,4]{1,0:T(1,128)S(1)} %bitcast.27, bf16[256,1024]{1,0:T(8,128)(2,1)S(1)} %get-tuple-element.22.b0.refs_1_, bf16[256,1024]{1,0:T(8,128)(2,1)S(1)} %collective-permute-done.b1.refs_2_, ...), custom_call_target="tpu_custom_call", output_to_operand_aliasing={{0}: (9, {})} | custom-call | flops 536870912 | bytes 1048576 | tf_op jit(solution)/shard_map/pallas_call | solution.py:168
  132.8 8.7 %collective-permute-done.30.refs_9_ = bf16[1024,256]{1,0:T(8,128)(2,1)S(1)} collective-permute-done((bf16[1024,256]{1,0:T(8,128)(2,1)S(1)}, bf16[1024,256]{1,0:T(8,128)(2,1)S(1)}, u32[]{:S(2)}, u32[]{:S(2)}) %collective-permute-start.30) | collective-permute-done | bytes 524320 | tf_op jit(solution)/shard_map/ppermute | solution.py:189
  141.5 2.3 %shard_map.109.refs_16_ = bf16[1024,512]{1,0:T(8,128)(2,1)} custom-call(s32[1]{0:T(128)S(6)} %copy.14.refs_0_, bf16[256,1024]{1,0:T(8,128)(2,1)S(1)} %get-tuple-element.32.refs_1_, bf16[256,1024]{1,0:T(8,128)(2,1)S(1)} %collective-permute-done.12.refs_2_, bf16[256,1024]{1,0:T(8,128)(2,1)S(1)} %collective-permute-done.13.refs_3_, ...), custom_call_target="tpu_custom_call" | custom-call | flops 1073741824 | bytes 1048576 | tf_op jit(solution)/shard_map/pallas_call | solution.py:168
  143.8 8.5 %collective-permute-done.21.refs_9_ = bf16[1024,256]{1,0:T(8,128)(2,1)S(1)} collective-permute-done((bf16[1024,256]{1,0:T(8,128)(2,1)S(1)}, bf16[1024,256]{1,0:T(8,128)(2,1)S(1)}, u32[]{:S(2)}, u32[]{:S(2)}) %collective-permute-start.21) | collective-permute-done | bytes 524320 | tf_op jit(solution)/shard_map/ppermute | solution.py:189
  152.3 2.3 %shard_map.110 = bf16[1024,512]{1,0:T(8,128)(2,1)} custom-call(s32[1]{0:T(128)S(6)} %copy.14.refs_0_, bf16[256,1024]{1,0:T(8,128)(2,1)S(1)} %get-tuple-element.32.refs_1_, bf16[256,1024]{1,0:T(8,128)(2,1)S(1)} %collective-permute-done.12.refs_2_, bf16[256,1024]{1,0:T(8,128)(2,1)S(1)} %collective-permute-done.13.refs_3_, ...), custom_call_target="tpu_custom_call", output_to_operand_aliasing={{}: (16, {})} | custom-call | flops 1073741824 | bytes 1048576 | tf_op jit(solution)/shard_map/pallas_call | solution.py:168
  (43 shorter events, 5.6 us)
Async XLA Ops:
  0.6 45.7 %copy-start.5 = (s32[4,1]{0,1:T(1,128)S(1)}, s32[4,1]{0,1:T(1,128)}, u32[]{:S(2)}) copy-start(s32[4,1]{0,1:T(1,128)} %param.14) | copy-start | bytes 52
  0.6 38.2 %collective-permute-start.1 = (bf16[256,1024]{1,0:T(8,128)(2,1)}, bf16[256,1024]{1,0:T(8,128)(2,1)S(1)}, u32[]{:S(2)}, u32[]{:S(2)}) collective-permute-start(bf16[256,1024]{1,0:T(8,128)(2,1)} %bitcast.16), channel_id=1, source_target_pairs={{0,2},{1,3},{2,0},{3,1},{4,6},{5,7},{6,4},{7,5},{8,10},{9,11},{10,... | collective-permute-start | bytes 1572872 | tf_op jit(solution)/shard_map/ppermute | solution.py:189
  4.7 36.2 %collective-permute-start.3 = (bf16[1024,512]{1,0:T(8,128)(2,1)}, bf16[1024,512]{1,0:T(8,128)(2,1)S(1)}, u32[]{:S(2)}, u32[]{:S(2)}) collective-permute-start(bf16[1024,512]{1,0:T(8,128)(2,1)} %bitcast.30), channel_id=1, source_target_pairs={{0,4},{1,5},{2,6},{3,7},{4,8},{5,9},{6,10},{7,11},{8,12},{9,13},{1... | collective-permute-start | bytes 3145736 | tf_op jit(solution)/shard_map/ppermute | solution.py:189
  6.5 32.4 %collective-permute-start = (bf16[256,1024]{1,0:T(8,128)(2,1)}, bf16[256,1024]{1,0:T(8,128)(2,1)S(1)}, u32[]{:S(2)}, u32[]{:S(2)}) collective-permute-start(bf16[256,1024]{1,0:T(8,128)(2,1)} %bitcast.17), channel_id=1, source_target_pairs={{0,1},{1,0},{2,3},{3,2},{4,5},{5,4},{6,7},{7,6},{8,9},{9,8},{10,11... | collective-permute-start | bytes 1572872 | tf_op jit(solution)/shard_map/ppermute | solution.py:189
  6.6 33.0 %collective-permute-start.13 = (bf16[256,1024]{1,0:T(8,128)(2,1)}, bf16[256,1024]{1,0:T(8,128)(2,1)S(1)}, u32[]{:S(2)}, u32[]{:S(2)}) collective-permute-start(bf16[256,1024]{1,0:T(8,128)(2,1)} %bitcast.10), channel_id=1, source_target_pairs={{4,6},{5,7},{6,4},{7,5},{8,10},{9,11},{10,8},{11,9},{12,14},{13,15... | collective-permute-start | bytes 1572872 | tf_op jit(solution)/shard_map/ppermute | solution.py:189
  7.3 32.9 %collective-permute-start.16 = (bf16[256,1024]{1,0:T(8,128)(2,1)}, bf16[256,1024]{1,0:T(8,128)(2,1)S(1)}, u32[]{:S(2)}, u32[]{:S(2)}) collective-permute-start(bf16[256,1024]{1,0:T(8,128)(2,1)} %bitcast.13), channel_id=1, source_target_pairs={{4,6},{5,7},{6,4},{7,5},{8,10},{9,11},{10,8},{11,9},{12,14},{13,15... | collective-permute-start | bytes 1572872 | tf_op jit(solution)/shard_map/ppermute | solution.py:189
  38.9 1.9 %collective-permute-start.2 = (bf16[256,1024]{1,0:T(8,128)(2,1)S(1)}, bf16[256,1024]{1,0:T(8,128)(2,1)S(1)}, u32[]{:S(2)}, u32[]{:S(2)}) collective-permute-start(bf16[256,1024]{1,0:T(8,128)(2,1)S(1)} %collective-permute-done.1.b2.refs_3_), channel_id=1, source_target_pairs={{0,1},{1,0},{2,3},{3,2},{4,5},{5,4},{6,7},{7,6},{8,9},{9,8},{10,11... | collective-permute-start | bytes 1572872 | tf_op jit(solution)/shard_map/ppermute | solution.py:189
  38.9 23.9 %collective-permute-start.18 = (bf16[1024,512]{1,0:T(8,128)(2,1)}, bf16[1024,512]{1,0:T(8,128)(2,1)S(1)}, u32[]{:S(2)}, u32[]{:S(2)}) collective-permute-start(bf16[1024,512]{1,0:T(8,128)(2,1)} %bitcast.31), channel_id=1, source_target_pairs={{16,12},{17,13},{18,14},{19,15},{20,16},{21,17},{22,18},{23,19},{2... | collective-permute-start | bytes 3145736 | tf_op jit(solution)/shard_map/ppermute | solution.py:189
  39.6 8.0 %collective-permute-start.12 = (bf16[256,1024]{1,0:T(8,128)(2,1)}, bf16[256,1024]{1,0:T(8,128)(2,1)S(1)}, u32[]{:S(2)}, u32[]{:S(2)}) collective-permute-start(bf16[256,1024]{1,0:T(8,128)(2,1)} %bitcast.11), channel_id=1, source_target_pairs={{0,1},{1,0},{2,3},{3,2},{4,5},{5,4},{6,7},{7,6},{8,9},{9,8},{10,11... | collective-permute-start | bytes 1572872 | tf_op jit(solution)/shard_map/ppermute | solution.py:189
  40.2 11.0 %collective-permute-start.15 = (bf16[256,1024]{1,0:T(8,128)(2,1)}, bf16[256,1024]{1,0:T(8,128)(2,1)S(1)}, u32[]{:S(2)}, u32[]{:S(2)}) collective-permute-start(bf16[256,1024]{1,0:T(8,128)(2,1)} %bitcast.14), channel_id=1, source_target_pairs={{0,1},{1,0},{2,3},{3,2},{4,5},{5,4},{6,7},{7,6},{8,9},{9,8},{10,11... | collective-permute-start | bytes 1572872 | tf_op jit(solution)/shard_map/ppermute | solution.py:189
  40.8 11.1 %collective-permute-start.14 = (bf16[256,1024]{1,0:T(8,128)(2,1)S(1)}, bf16[256,1024]{1,0:T(8,128)(2,1)S(1)}, u32[]{:S(2)}, u32[]{:S(2)}) collective-permute-start(bf16[256,1024]{1,0:T(8,128)(2,1)S(1)} %collective-permute-done.13.refs_3_), channel_id=1, source_target_pairs={{0,1},{1,0},{2,3},{3,2},{4,5},{5,4},{6,7},{7,6},{8,9},{9,8},{10,11... | collective-permute-start | bytes 1572872 | tf_op jit(solution)/shard_map/ppermute | solution.py:189
  40.9 20.5 %collective-permute-start.17 = (bf16[256,1024]{1,0:T(8,128)(2,1)S(1)}, bf16[256,1024]{1,0:T(8,128)(2,1)S(1)}, u32[]{:S(2)}, u32[]{:S(2)}) collective-permute-start(bf16[256,1024]{1,0:T(8,128)(2,1)S(1)} %collective-permute-done.16.refs_7_), channel_id=1, source_target_pairs={{0,1},{1,0},{2,3},{3,2},{4,5},{5,4},{6,7},{7,6},{8,9},{9,8},{10,11... | collective-permute-start | bytes 1572872 | tf_op jit(solution)/shard_map/ppermute | solution.py:189
  41.3 1.6 %copy-start = (bf16[1,2,1024,512]{3,2,1,0:T(8,128)(2,1)S(1)}, bf16[1,2,1024,512]{3,2,1,0:T(8,128)(2,1)}, u32[]{:S(2)}) copy-start(bf16[1,2,1024,512]{3,2,1,0:T(8,128)(2,1)} %param.13) | copy-start | bytes 6291460
  42.9 1.0 copy-start.1
  43.9 1.0 copy-start.2
  45.0 1.0 copy-start.3
  47.6 18.4 %collective-permute-start.9 = (bf16[1024,256]{1,0:T(8,128)(2,1)S(1)}, bf16[1024,256]{1,0:T(8,128)(2,1)S(1)}, u32[]{:S(2)}, u32[]{:S(2)}) collective-permute-start(bf16[1024,256]{1,0:T(8,128)(2,1)S(1)} %get-tuple-element.27), channel_id=1, source_target_pairs={{0,4},{1,5},{2,6},{3,7},{4,8},{5,9},{6,10},{7,11},{8,12},{9,13},{1... | collective-permute-start | bytes 1572872 | tf_op jit(solution)/shard_map/ppermute | solution.py:189
  49.9 1.3 copy-start.4
  51.2 16.8 %collective-permute-start.7 = (bf16[256,1024]{1,0:T(8,128)(2,1)S(1)}, bf16[256,1024]{1,0:T(8,128)(2,1)S(1)}, u32[]{:S(2)}, u32[]{:S(2)}) collective-permute-start(bf16[256,1024]{1,0:T(8,128)(2,1)S(1)} %bitcast.19), channel_id=1, source_target_pairs={{252,254},{253,255},{254,252},{255,253}} | collective-permute-start | bytes 1572872 | tf_op jit(solution)/shard_map/ppermute | solution.py:189
  51.9 26.5 %collective-permute-start.22 = (bf16[256,1024]{1,0:T(8,128)(2,1)S(1)}, bf16[256,1024]{1,0:T(8,128)(2,1)S(1)}, u32[]{:S(2)}, u32[]{:S(2)}) collective-permute-start(bf16[256,1024]{1,0:T(8,128)(2,1)S(1)} %get-tuple-element.32.refs_1_), channel_id=1, source_target_pairs={{0,240},{1,241},{2,242},{3,243},{252,12},{253,13},{254,14},{255,15}} | collective-permute-start | bytes 1572872 | tf_op jit(solution)/shard_map/ppermute | solution.py:189
  61.5 17.7 %collective-permute-start.4 = (bf16[1024,256]{1,0:T(8,128)(2,1)S(1)}, bf16[1024,256]{1,0:T(8,128)(2,1)S(1)}, u32[]{:S(2)}, u32[]{:S(2)}) collective-permute-start(bf16[1024,256]{1,0:T(8,128)(2,1)S(1)} %get-tuple-element.24), channel_id=1, source_target_pairs={{0,4},{1,5},{2,6},{3,7},{4,8},{5,9},{6,10},{7,11},{8,12},{9,13},{1... | collective-permute-start | bytes 1572872 | tf_op jit(solution)/shard_map/ppermute | solution.py:189
  64.1 17.8 %collective-permute-start.28 = (bf16[1024,256]{1,0:T(8,128)(2,1)S(1)}, bf16[1024,256]{1,0:T(8,128)(2,1)S(1)}, u32[]{:S(2)}, u32[]{:S(2)}) collective-permute-start(bf16[1024,256]{1,0:T(8,128)(2,1)S(1)} %shard_map.106), channel_id=1, source_target_pairs={{12,8},{13,9},{14,10},{15,11},{16,12},{17,13},{18,14},{19,15},{20,... | collective-permute-start | bytes 1572872 | tf_op jit(solution)/shard_map/ppermute | solution.py:189
  66.0 18.4 %collective-permute-start.19 = (bf16[1024,256]{1,0:T(8,128)(2,1)S(1)}, bf16[1024,256]{1,0:T(8,128)(2,1)S(1)}, u32[]{:S(2)}, u32[]{:S(2)}) collective-permute-start(bf16[1024,256]{1,0:T(8,128)(2,1)S(1)} %shard_map.103), channel_id=1, source_target_pairs={{12,8},{13,9},{14,10},{15,11},{16,12},{17,13},{18,14},{19,15},{20,... | collective-permute-start | bytes 1572872 | tf_op jit(solution)/shard_map/ppermute | solution.py:189
  68.1 20.4 %collective-permute-start.25 = (bf16[256,1024]{1,0:T(8,128)(2,1)S(1)}, bf16[256,1024]{1,0:T(8,128)(2,1)S(1)}, u32[]{:S(2)}, u32[]{:S(2)}) collective-permute-start(bf16[256,1024]{1,0:T(8,128)(2,1)S(1)} %get-tuple-element.33.refs_5_), channel_id=1, source_target_pairs={{0,240},{1,241},{2,242},{3,243}} | collective-permute-start | bytes 1572872 | tf_op jit(solution)/shard_map/ppermute | solution.py:189
  78.5 11.3 %collective-permute-start.8 = (bf16[256,1024]{1,0:T(8,128)(2,1)S(1)}, bf16[256,1024]{1,0:T(8,128)(2,1)S(1)}, u32[]{:S(2)}, u32[]{:S(2)}) collective-permute-start(bf16[256,1024]{1,0:T(8,128)(2,1)S(1)} %collective-permute-done.7.rest_0_.refs_7_), channel_id=1, source_target_pairs={{252,253},{253,252},{254,255},{255,254}} | collective-permute-start | bytes 1572872 | tf_op jit(solution)/shard_map/ppermute | solution.py:189
  79.2 13.6 %collective-permute-start.10 = (bf16[1024,256]{1,0:T(8,128)(2,1)S(1)}, bf16[1024,256]{1,0:T(8,128)(2,1)S(1)}, u32[]{:S(2)}, u32[]{:S(2)}) collective-permute-start(bf16[1024,256]{1,0:T(8,128)(2,1)S(1)} %get-tuple-element.28), channel_id=1, source_target_pairs={{0,4},{1,5},{2,6},{3,7},{4,8},{5,9},{6,10},{7,11},{8,12},{9,13},{1... | collective-permute-start | bytes 1572872 | tf_op jit(solution)/shard_map/ppermute | solution.py:189
  81.8 19.9 %collective-permute-start.5 = (bf16[1024,256]{1,0:T(8,128)(2,1)S(1)}, bf16[1024,256]{1,0:T(8,128)(2,1)S(1)}, u32[]{:S(2)}, u32[]{:S(2)}) collective-permute-start(bf16[1024,256]{1,0:T(8,128)(2,1)S(1)} %get-tuple-element.25), channel_id=1, source_target_pairs={{0,4},{1,5},{2,6},{3,7},{4,8},{5,9},{6,10},{7,11},{8,12},{9,13},{1... | collective-permute-start | bytes 1572872 | tf_op jit(solution)/shard_map/ppermute | solution.py:189
  84.5 23.0 %collective-permute-start.29 = (bf16[1024,256]{1,0:T(8,128)(2,1)S(1)}, bf16[1024,256]{1,0:T(8,128)(2,1)S(1)}, u32[]{:S(2)}, u32[]{:S(2)}) collective-permute-start(bf16[1024,256]{1,0:T(8,128)(2,1)S(1)} %shard_map.107), channel_id=1, source_target_pairs={{8,4},{9,5},{10,6},{11,7},{12,8},{13,9},{14,10},{15,11},{16,12},{1... | collective-permute-start | bytes 1572872 | tf_op jit(solution)/shard_map/ppermute | solution.py:189
  88.5 25.1 %collective-permute-start.23 = (bf16[256,1024]{1,0:T(8,128)(2,1)S(1)}, bf16[256,1024]{1,0:T(8,128)(2,1)S(1)}, u32[]{:S(2)}, u32[]{:S(2)}) collective-permute-start(bf16[256,1024]{1,0:T(8,128)(2,1)S(1)} %collective-permute-done.22), channel_id=1, source_target_pairs={{240,2},{241,3},{242,0},{243,1},{12,254},{13,255},{14,252},{15,253}} | collective-permute-start | bytes 1572872 | tf_op jit(solution)/shard_map/ppermute | solution.py:189
  89.8 33.1 %collective-permute-start.26 = (bf16[256,1024]{1,0:T(8,128)(2,1)S(1)}, bf16[256,1024]{1,0:T(8,128)(2,1)S(1)}, u32[]{:S(2)}, u32[]{:S(2)}) collective-permute-start(bf16[256,1024]{1,0:T(8,128)(2,1)S(1)} %collective-permute-done.25), channel_id=1, source_target_pairs={{240,2},{241,3},{242,0},{243,1}} | collective-permute-start | bytes 1572872 | tf_op jit(solution)/shard_map/ppermute | solution.py:189
  92.8 32.0 %collective-permute-start.20 = (bf16[1024,256]{1,0:T(8,128)(2,1)S(1)}, bf16[1024,256]{1,0:T(8,128)(2,1)S(1)}, u32[]{:S(2)}, u32[]{:S(2)}) collective-permute-start(bf16[1024,256]{1,0:T(8,128)(2,1)S(1)} %shard_map.104), channel_id=1, source_target_pairs={{8,4},{9,5},{10,6},{11,7},{12,8},{13,9},{14,10},{15,11},{16,12},{1... | collective-permute-start | bytes 1572872 | tf_op jit(solution)/shard_map/ppermute | solution.py:189
  101.8 25.6 %collective-permute-start.11 = (bf16[1024,256]{1,0:T(8,128)(2,1)S(1)}, bf16[1024,256]{1,0:T(8,128)(2,1)S(1)}, u32[]{:S(2)}, u32[]{:S(2)}) collective-permute-start(bf16[1024,256]{1,0:T(8,128)(2,1)S(1)} %get-tuple-element.29), channel_id=1, source_target_pairs={{0,4},{1,5},{2,6},{3,7},{4,8},{5,9},{6,10},{7,11},{8,12},{9,13},{1... | collective-permute-start | bytes 1572872 | tf_op jit(solution)/shard_map/ppermute | solution.py:189
  107.5 23.2 %collective-permute-start.6 = (bf16[1024,256]{1,0:T(8,128)(2,1)S(1)}, bf16[1024,256]{1,0:T(8,128)(2,1)S(1)}, u32[]{:S(2)}, u32[]{:S(2)}) collective-permute-start(bf16[1024,256]{1,0:T(8,128)(2,1)S(1)} %get-tuple-element.26), channel_id=1, source_target_pairs={{0,4},{1,5},{2,6},{3,7},{4,8},{5,9},{6,10},{7,11},{8,12},{9,13},{1... | collective-permute-start | bytes 1572872 | tf_op jit(solution)/shard_map/ppermute | solution.py:189
  113.6 19.2 %collective-permute-start.24 = (bf16[256,1024]{1,0:T(8,128)(2,1)S(1)}, bf16[256,1024]{1,0:T(8,128)(2,1)S(1)}, u32[]{:S(2)}, u32[]{:S(2)}) collective-permute-start(bf16[256,1024]{1,0:T(8,128)(2,1)S(1)} %collective-permute-done.23.refs_12_), channel_id=1, source_target_pairs={{0,1},{1,0},{2,3},{3,2},{252,253},{253,252},{254,255},{255,254}} | collective-permute-start | bytes 1572872 | tf_op jit(solution)/shard_map/ppermute | solution.py:189
  122.9 9.9 %collective-permute-start.27 = (bf16[256,1024]{1,0:T(8,128)(2,1)S(1)}, bf16[256,1024]{1,0:T(8,128)(2,1)S(1)}, u32[]{:S(2)}, u32[]{:S(2)}) collective-permute-start(bf16[256,1024]{1,0:T(8,128)(2,1)S(1)} %collective-permute-done.26.refs_14_), channel_id=1, source_target_pairs={{0,1},{1,0},{2,3},{3,2}} | collective-permute-start | bytes 1572872 | tf_op jit(solution)/shard_map/ppermute | solution.py:189
  124.8 16.7 %collective-permute-start.30 = (bf16[1024,256]{1,0:T(8,128)(2,1)S(1)}, bf16[1024,256]{1,0:T(8,128)(2,1)S(1)}, u32[]{:S(2)}, u32[]{:S(2)}) collective-permute-start(bf16[1024,256]{1,0:T(8,128)(2,1)S(1)} %shard_map.108), channel_id=1, source_target_pairs={{4,0},{5,1},{6,2},{7,3},{8,4},{9,5},{10,6},{11,7},{12,8},{13,9},{1... | collective-permute-start | bytes 1572872 | tf_op jit(solution)/shard_map/ppermute | solution.py:189
  127.4 24.9 %collective-permute-start.21 = (bf16[1024,256]{1,0:T(8,128)(2,1)S(1)}, bf16[1024,256]{1,0:T(8,128)(2,1)S(1)}, u32[]{:S(2)}, u32[]{:S(2)}) collective-permute-start(bf16[1024,256]{1,0:T(8,128)(2,1)S(1)} %shard_map.105), channel_id=1, source_target_pairs={{4,0},{5,1},{6,2},{7,3},{8,4},{9,5},{10,6},{11,7},{12,8},{13,9},{1... | collective-permute-start | bytes 1572872 | tf_op jit(solution)/shard_map/ppermute | solution.py:189
